TPU v7x, 128 devices: a whole 4x4x4 slice. The times are simulated.
128 devices in a mesh: req: 32 (over z_hi, x, y), tp: 4 (over z_lo, core).
Axes of the slice: x: 4, y: 4, z: 4 (z_hi: 2, z_lo: 2; z = z_hi * 2 + z_lo), core: 2. Of those that a mesh axis runs over, the one named last changes fastest.
Arguments:
- hidden_in: bfloat16 [65536, 1024], P('req'), may hold values from -6 to 6
- lengths: int32 [64], replicated, may hold values from 1 to 2048, 65536 in all
- tenant: int32 [64], replicated, may hold values from 0 to 3
- shard_map: int32 [128], replicated, may hold values from 0 to 127, each once
- wq: float32 [1024, 1024], P(('req', 'tp')), as said below
- wk: float32 [1024, 1024], P(('req', 'tp')), as said below
- wv: float32 [1024, 1024], P(('req', 'tp')), may hold values from -0.75 to 0.75
- wo: float32 [1024, 1024], P(('req', 'tp')), may hold values from -0.75 to 0.75
- wi_in: float32 [1024, 2624], P(('req', 'tp')), may hold values from -0.1875 to 0.1875
- wi_gate: float32 [1024, 2624], P(('req', 'tp')), may hold values from -0.1875 to 0.1875
- wo2: float32 [1024, 2624], P(('req', 'tp')), may hold values from -0.125 to 0.125
- head: float32 [49152, 1024], P(('req', 'tp')), may hold values from -0.56 to 0.56
- attn_gain: float32 [1024], replicated, may hold values from 0.1 to 1.9
- mlp_gain: float32 [1024], replicated, may hold values from 0.1 to 1.9
- final_gain: float32 [4, 1024], replicated, may hold values from 0.1 to 1.9
Outputs:
- hidden_out: bfloat16 [65536, 1024], P('req', 'tp')
- cache: bfloat16 [2, 65536, 1024], P(None, 'req', 'tp')
- last_rms: float32 [64], replicated
- top_logit: float32 [64], replicated
Inputs may be any that keep to these rules, and one draw needn't show every extreme that they name: Prompts are packed in request order into the 65536 slots; the lengths sum to 65536 and the longest is exactly 2048. `shard_map`: A permutation: each row block is held by exactly one trainer device. `wq`: A fan-in scaled projection. `wk`: A fan-in scaled projection.
All inputs are finite; a program needn't handle non-finite values.
Results may differ from a plain program's by a relative error of at most 0.012.
The roundings to bfloat16 on the way count: a program that leaves them out, or rounds other values in their place, can miss the bound.
Values may be sent and summed in bfloat16 or wider, within the bound.
No kernel may reach another device: no remote copies, remote signals or barrier semaphores. Data moves between devices by JAX's collectives and lax.ppermute only.
A program may use at most 128 MiB of HBM per device.

v0:
```python
import jax
import jax.numpy as jnp
from jax import lax
from jax.sharding import PartitionSpec as P

HEADS = 16
HEAD_DIM = 64


THETA = 160000.0
EPS = 1e-05


def with_halo(block, sides, width):
    for axis, dim in sides:
        count = lax.axis_size(axis)
        forward = [(i, i + 1) for i in range(count - 1)]
        backward = [(target, source) for source, target in forward]
        low = lax.ppermute(
            lax.slice_in_dim(block, block.shape[dim] - width, None, axis=dim), axis, forward
        )
        high = lax.ppermute(lax.slice_in_dim(block, 0, width, axis=dim), axis, backward)
        block = jnp.concatenate([low, block, high], axis=dim)
    return block


def layer_norm(values, gain):
    center = jnp.mean(values, axis=-1, keepdims=True)
    spread = jnp.mean(values * values, axis=-1, keepdims=True) - center * center
    return (values - center) * lax.rsqrt(spread + EPS) * gain


def rotate(values, position):
    half = values.shape[-1] // 2
    freq = THETA ** (-(2.0 * jnp.arange(half, dtype=jnp.float32)) / values.shape[-1])
    angle = position.astype(jnp.float32)[:, None] * freq[None, :]
    cosine = jnp.cos(angle)[:, None, :]
    sine = jnp.sin(angle)[:, None, :]
    first = values[..., :half]
    second = values[..., half:]
    return jnp.concatenate(
        [first * cosine - second * sine, second * cosine + first * sine], axis=-1
    )


def reorder(weight, holder, shard_map, count):
    block_of = shard_map[holder]
    order = jnp.zeros((count,), jnp.int32).at[block_of].set(jnp.arange(count, dtype=jnp.int32))
    rows = weight.shape[0] // count
    return weight.reshape(count, rows, weight.shape[1])[order].reshape(
        weight.shape[0], weight.shape[1]
    )


def body(
    hidden_in,
    lengths,
    tenant,
    shard_map,
    wq,
    wk,
    wv,
    wo,
    wi_in,
    wi_gate,
    wo2,
    head,
    attn_gain,
    mlp_gain,
    final_gain,
):
    req_count = lax.axis_size("req")
    tp_count = lax.axis_size("tp")
    count = req_count * tp_count
    req_index = lax.axis_index("req")
    tp_index = lax.axis_index("tp")
    slots, width = hidden_in.shape
    local_heads = HEADS // tp_count
    share = width // tp_count
    served = (
        wq.astype(jnp.bfloat16),
        wk.astype(jnp.bfloat16),
        wv.astype(jnp.bfloat16),
        wo.astype(jnp.bfloat16),
        wi_in.astype(jnp.bfloat16),
        wi_gate.astype(jnp.bfloat16),
        wo2.astype(jnp.bfloat16),
    )
    place = jnp.arange(count, dtype=jnp.int32)
    collected = (
        lax.all_gather(served[0], "req", axis=0, tiled=True),
        lax.all_gather(served[1], "req", axis=0, tiled=True),
        lax.all_gather(served[2], "req", axis=0, tiled=True),
        lax.all_gather(served[3], "req", axis=0, tiled=True),
        lax.all_gather(served[4], "req", axis=0, tiled=True),
        lax.all_gather(served[5], "req", axis=0, tiled=True),
        lax.all_gather(served[6], "req", axis=0, tiled=True),
    )
    regrouped = (
        lax.all_to_all(collected[0], "tp", split_axis=1, concat_axis=0, tiled=True),
        lax.all_to_all(collected[1], "tp", split_axis=1, concat_axis=0, tiled=True),
        lax.all_to_all(collected[2], "tp", split_axis=1, concat_axis=0, tiled=True),
        lax.all_to_all(collected[3], "tp", split_axis=1, concat_axis=0, tiled=True),
        lax.all_to_all(collected[4], "tp", split_axis=1, concat_axis=0, tiled=True),
        lax.all_to_all(collected[5], "tp", split_axis=1, concat_axis=0, tiled=True),
        lax.all_to_all(collected[6], "tp", split_axis=1, concat_axis=0, tiled=True),
    )
    holder = place % req_count * tp_count + place // req_count
    query_w, key_w, value_w, out_w, input_w, gate_w, down_w = [
        reorder(item, holder, shard_map, count) for item in regrouped
    ]
    ends = jnp.cumsum(lengths)
    total = slots * req_count
    base = req_index * slots
    global_index = base - slots + jnp.arange(3 * slots, dtype=jnp.int32)
    before = ends[None, :] <= global_index[:, None]
    segment = jnp.sum(before.astype(jnp.int32), axis=1)
    inside = (global_index >= 0) & (global_index < total)
    segment = jnp.where(inside, segment, -1)
    own_segment = segment[slots : 2 * slots]
    own_index = global_index[slots : 2 * slots]
    own_before = before[slots : 2 * slots]
    position = own_index - jnp.sum(jnp.where(own_before, lengths[None, :], 0), axis=1)
    normed = layer_norm(hidden_in.astype(jnp.float32), attn_gain).astype(jnp.bfloat16)
    query = jnp.dot(normed, query_w, preferred_element_type=jnp.float32).reshape(
        slots, local_heads, HEAD_DIM
    )
    query = rotate(query, position).astype(jnp.bfloat16)
    keys = jnp.dot(normed, key_w, preferred_element_type=jnp.float32).reshape(
        slots, local_heads, HEAD_DIM
    )
    keys = rotate(keys, position).astype(jnp.bfloat16).reshape(slots, share)
    values = jnp.dot(normed, value_w, preferred_element_type=jnp.float32).astype(jnp.bfloat16)
    cache = jnp.stack([keys, values])
    widened = with_halo(cache, (("req", 1),), slots)
    key_heads = widened[0].reshape(3 * slots, local_heads, HEAD_DIM).transpose(1, 0, 2)
    value_heads = widened[1].reshape(3 * slots, local_heads, HEAD_DIM).transpose(1, 0, 2)
    query_heads = query.transpose(1, 0, 2)
    block = min(512, slots)
    scale = HEAD_DIM ** (-0.5)

    def head_attend(operands):
        query_head, key_head, value_head = operands

        def one_block(number):
            start = number * block
            query_block = lax.dynamic_slice_in_dim(query_head, start, block, 0)
            query_segment = lax.dynamic_slice_in_dim(own_segment, start, block, 0)
            scores = (
                lax.dot_general(
                    query_block,
                    key_head,
                    (((1,), (1,)), ((), ())),
                    preferred_element_type=jnp.float32,
                )
                * scale
            )
            scores = jnp.where(query_segment[:, None] == segment[None, :], scores, -1e30)
            highest = jnp.max(scores, axis=-1, keepdims=True)
            weights = jnp.exp(scores - highest)
            probability = (weights / jnp.sum(weights, axis=-1, keepdims=True)).astype(jnp.bfloat16)
            return jnp.dot(probability, value_head, preferred_element_type=jnp.float32)

        result = lax.map(one_block, jnp.arange(slots // block, dtype=jnp.int32))
        return result.reshape(slots, HEAD_DIM)

    attended = lax.map(head_attend, (query_heads, key_heads, value_heads))
    mixed = attended.transpose(1, 0, 2).reshape(slots, share).astype(jnp.bfloat16)
    attn_part = lax.dot_general(
        mixed, out_w, (((1,), (1,)), ((), ())), preferred_element_type=jnp.float32
    )
    summed = lax.psum(attn_part, "tp")
    first = (hidden_in.astype(jnp.float32) + summed).astype(jnp.bfloat16)
    normed2 = layer_norm(first.astype(jnp.float32), mlp_gain).astype(jnp.bfloat16)
    first_share = lax.dynamic_slice_in_dim(first, tp_index * share, share, 1)
    gate_in = jnp.dot(normed2, input_w, preferred_element_type=jnp.float32)
    gate_side = jnp.dot(normed2, gate_w, preferred_element_type=jnp.float32)
    inner = (jax.nn.gelu(gate_in, approximate=False) * gate_side).astype(jnp.bfloat16)
    down_part = lax.dot_general(
        inner, down_w, (((1,), (1,)), ((), ())), preferred_element_type=jnp.float32
    )
    down_share = lax.psum_scatter(down_part, "tp", scatter_dimension=1, tiled=True)
    hidden_out = (first_share.astype(jnp.float32) + down_share).astype(jnp.bfloat16)
    last_slot = ends - 1 - base
    holds = (last_slot >= 0) & (last_slot < slots)
    picked = hidden_out[jnp.clip(last_slot, 0, slots - 1)].astype(jnp.float32)
    picked = jnp.where(holds[:, None], picked, 0.0)
    request_count = lengths.shape[0]
    placed = lax.dynamic_update_slice(
        jnp.zeros((request_count, width), jnp.float32), picked, (jnp.int32(0), tp_index * share)
    )
    last = lax.psum(placed, ("req", "tp"))
    last_rms = jnp.sqrt(jnp.mean(last * last, axis=-1))
    choose = (tenant[:, None] == jnp.arange(final_gain.shape[0], dtype=jnp.int32)[None, :]).astype(
        jnp.float32
    )
    gain_rows = jnp.dot(
        choose, final_gain, precision=lax.Precision.HIGHEST, preferred_element_type=jnp.float32
    )
    final = layer_norm(last, gain_rows).astype(jnp.bfloat16)
    logits = lax.dot_general(
        final,
        head.astype(jnp.bfloat16),
        (((1,), (1,)), ((), ())),
        preferred_element_type=jnp.float32,
    )
    top_logit = lax.pmax(jnp.max(logits, axis=-1), ("req", "tp"))
    return (hidden_out, cache, last_rms, top_logit)


def solution(mesh):
    placed = (
        P("req", None),
        P(),
        P(),
        P(),
        P(("req", "tp"), None),
        P(("req", "tp"), None),
        P(("req", "tp"), None),
        P(("req", "tp"), None),
        P(("req", "tp"), None),
        P(("req", "tp"), None),
        P(("req", "tp"), None),
        P(("req", "tp"), None),
        P(),
        P(),
        P(),
    )
    return jax.shard_map(
        body,
        mesh=mesh,
        in_specs=placed,
        out_specs=(P("req", "tp"), P(None, "req", "tp"), P(), P()),
        check_vma=False,
    )
```

profile of v0, /device:TPU:1, one launch (start us, length us, event | category | flops | bytes accessed | tf_op | source)
XLA Modules:
  0.0 1209.6 jit_solution(8971452301709203540)
XLA Ops:
  10.4 85.3 %all_gather.22 = bf16[256,1024]{1,0:T(8,128)(2,1)S(1)} all-gather(bf16[8,1024]{1,0:T(8,128)(2,1)S(1)} %convert_element_type.94), channel_id=1, replica_groups=mesh['req'=32,'tp'=4] {'req'}, dimensions={0}, use_global_device_ids=true | all-gather | bytes 540672 | tf_op jit(solution)/shard_map/all_gather | solution.py:92
  96.7 18.5 %all-to-all-start.1 = ((bf16[256,4,256]{0,2,1:T(8,128)(2,1)}), bf16[256,4,256]{0,2,1:T(8,128)(2,1)S(1)}, u32[]{:S(2)}, u32[]{:S(2)}) async-start(bf16[256,4,256]{0,2,1:T(8,128)(2,1)} %bitcast.18), calls=%async_computation.1 | async-start | bytes 1048576 | tf_op jit(solution)/shard_map/all_to_all | solution.py:101
  118.2 3.4 convert_reduce_fusion
  124.0 76.5 %all_gather.21 = bf16[256,1024]{1,0:T(8,128)(2,1)S(1)} all-gather(bf16[8,1024]{1,0:T(8,128)(2,1)S(1)} %convert_element_type.92), channel_id=1, replica_groups=mesh['req'=32,'tp'=4] {'req'}, dimensions={0}, use_global_device_ids=true | all-gather | bytes 540672 | tf_op jit(solution)/shard_map/all_gather | solution.py:91
  200.5 78.2 %all_gather.23 = bf16[256,1024]{1,0:T(8,128)(2,1)S(1)} all-gather(bf16[8,1024]{1,0:T(8,128)(2,1)S(1)} %convert_element_type.96), channel_id=1, replica_groups=mesh['req'=32,'tp'=4] {'req'}, dimensions={0}, use_global_device_ids=true | all-gather | bytes 540672 | tf_op jit(solution)/shard_map/all_gather | solution.py:93
  279.0 4.3 fusion.12
  285.6 31.4 %all-to-all-start = ((bf16[256,4,256]{0,2,1:T(8,128)(2,1)}), bf16[256,4,256]{0,2,1:T(8,128)(2,1)S(1)}, u32[]{:S(2)}, u32[]{:S(2)}) async-start(bf16[256,4,256]{0,2,1:T(8,128)(2,1)} %bitcast.7), calls=%async_computation | async-start | bytes 1048576 | tf_op jit(solution)/shard_map/all_to_all | solution.py:100
  319.0 5.9 all-to-all-done
  325.0 4.8 all-to-all-start.2
  330.8 3.7 fusion.26
  339.1 3.4 fusion.61
  342.8 2.9 collective-permute-start
  347.1 114.9 %all_gather.24 = bf16[256,1024]{1,0:T(8,128)(2,1)S(1)} all-gather(bf16[8,1024]{1,0:T(8,128)(2,1)S(1)} %convert_element_type.102), channel_id=1, replica_groups=mesh['req'=32,'tp'=4] {'req'}, dimensions={0}, use_global_device_ids=true | all-gather | bytes 540672 | tf_op jit(solution)/shard_map/all_gather | solution.py:94
  463.0 17.3 %all-to-all-start.3 = ((bf16[256,4,256]{0,2,1:T(8,128)(2,1)}), bf16[256,4,256]{0,2,1:T(8,128)(2,1)S(1)}, u32[]{:S(2)}, u32[]{:S(2)}) async-start(bf16[256,4,256]{0,2,1:T(8,128)(2,1)} %bitcast.36), calls=%async_computation.3 | async-start | bytes 1048576 | tf_op jit(solution)/shard_map/all_to_all | solution.py:103
  481.6 6.9 all-to-all-done.3
  490.1 3.3 pad_maximum_fusion
  493.4 3.1 fusion.117
  496.5 4.8 copy.103
  501.4 3.1 copy.104
  504.5 160.4 %while.21 = (s32[]{:T(128)}, bf16[4,2048,64]{1,2,0:T(8,128)(2,1)}, bf16[4,2048,64]{1,2,0:T(8,128)(2,1)}, bf16[4,6144,64]{1,2,0:T(8,128)(2,1)}, bf16[4,6144,64]{1...) while((s32[]{:T(128)}, bf16[4,2048,64]{1,2,0:T(8,128)(2,1)}, ...), condition=%wide.region_11.12_spmd, body=%wide.region_6.0_spmd.sunk | while | flops 833616896 | bytes 53257172 | solution.py:167
  509.6 33.7 %while.22 = (s32[]{:T(128)}, bf16[4,512,64]{1,2,0:T(8,128)(2,1)S(1)}, s32[4]{0:T(128)S(1)}, s32[2048]{0:T(1024)S(1)}, s32[6144]{0:T(1024)S(1)}, /*index=5*/bf16[...) while((s32[]{:T(128)}, ...), condition=%wide.region_10.10_spmd, body=%wide.region_7.9_spmd.sunk | while | flops 833616896 | bytes 44343512 | solution.py:164
  511.0 2.1 fusion.133
  515.0 3.0 fusion.135
  523.4 3.0 fusion.135
  527.8 2.1 fusion.133
  531.8 3.0 fusion.135
  540.3 3.0 fusion.135
  549.7 33.7 %while.22 = (s32[]{:T(128)}, bf16[4,512,64]{1,2,0:T(8,128)(2,1)S(1)}, s32[4]{0:T(128)S(1)}, s32[2048]{0:T(1024)S(1)}, s32[6144]{0:T(1024)S(1)}, /*index=5*/bf16[...) while((s32[]{:T(128)}, ...), condition=%wide.region_10.10_spmd, body=%wide.region_7.9_spmd.sunk | while | flops 833616896 | bytes 44343512 | solution.py:164
  551.0 2.1 fusion.133
  555.1 3.0 fusion.135
  559.5 2.1 fusion.133
  563.5 3.0 fusion.135
  571.9 3.0 fusion.135
  576.3 2.1 fusion.133
  580.4 3.0 fusion.135
  589.8 33.7 %while.22 = (s32[]{:T(128)}, bf16[4,512,64]{1,2,0:T(8,128)(2,1)S(1)}, s32[4]{0:T(128)S(1)}, s32[2048]{0:T(1024)S(1)}, s32[6144]{0:T(1024)S(1)}, /*index=5*/bf16[...) while((s32[]{:T(128)}, ...), condition=%wide.region_10.10_spmd, body=%wide.region_7.9_spmd.sunk | while | flops 833616896 | bytes 44343512 | solution.py:164
  595.2 3.0 fusion.135
  603.6 3.0 fusion.135
  612.0 3.0 fusion.135
  616.4 2.1 fusion.133
  620.5 3.0 fusion.135
  629.9 33.7 %while.22 = (s32[]{:T(128)}, bf16[4,512,64]{1,2,0:T(8,128)(2,1)S(1)}, s32[4]{0:T(128)S(1)}, s32[2048]{0:T(1024)S(1)}, s32[6144]{0:T(1024)S(1)}, /*index=5*/bf16[...) while((s32[]{:T(128)}, ...), condition=%wide.region_10.10_spmd, body=%wide.region_7.9_spmd.sunk | while | flops 833616896 | bytes 44343512 | solution.py:164
  635.3 3.0 fusion.135
  643.7 3.0 fusion.135
  652.1 3.0 fusion.135
  656.5 2.1 fusion.133
  660.6 3.0 fusion.135
  664.8 5.9 fusion.69
  670.8 2.5 copy.111
  673.3 4.4 all-to-all-start.4
  677.7 2.5 copy.113
  680.2 21.4 %all-to-all-done.4 = bf16[256,4,656]{0,2,1:T(8,128)(2,1)S(1)} async-done(((bf16[256,4,656]{0,2,1:T(8,128)(2,1)}), bf16[256,4,656]{0,2,1:T(8,128)(2,1)S(1)}, u32[]{:S(2)}, u32[]{:S(2)}) %all-to-all-start.4) | async-done | bytes 1343520 | tf_op jit(solution)/shard_map/all_to_all | solution.py:104
  701.6 5.2 all-to-all-start.5
  706.8 2.5 copy.115
  709.3 29.3 %all-to-all-done.5 = bf16[256,4,656]{0,2,1:T(8,128)(2,1)S(1)} async-done(((bf16[256,4,656]{0,2,1:T(8,128)(2,1)}), bf16[256,4,656]{0,2,1:T(8,128)(2,1)S(1)}, u32[]{:S(2)}, u32[]{:S(2)}) %all-to-all-start.5) | async-done | bytes 1343520 | tf_op jit(solution)/shard_map/all_to_all | solution.py:105
  738.6 5.0 all-to-all-start.6
  748.8 26.2 %all-to-all-done.6 = bf16[256,4,656]{0,2,1:T(8,128)(2,1)} async-done(((bf16[256,4,656]{0,2,1:T(8,128)(2,1)}), bf16[256,4,656]{0,2,1:T(8,128)(2,1)}, u32[]{:S(2)}, u32[]{:S(2)}) %all-to-all-start.6) | async-done | bytes 1343520 | tf_op jit(solution)/shard_map/all_to_all | solution.py:106
  778.7 95.2 %all-reduce.3.cloned.1.call-done = f32[2048,1024]{1,0:T(8,128)} async-done(((f32[2048,1024]{1,0:T(8,128)}), f32[2048,1024]{1,0:T(8,128)}) %all-reduce.3.cloned.1.call-update) | async-done | bytes 8388624 | tf_op jit(solution)/shard_map/psum | solution.py:172
  873.8 5.5 convert_reduce_fusion.1
  881.3 5.4 fusion.65
  886.7 23.0 %fusion.30 = f32[2048,1024]{1,0:T(8,128)} fusion(f32[2048,656]{0,1:T(8,128)} %fusion.65, bf16[128,8,656]{2,1,0:T(8,128)(2,1)} %gather_fusion.7, bf16[128,8,656]{2,1,0:T(8,128)(2,1)S(1)} %copy-done.12, bf16[2048,1024]{1,0:T(8,128)(2,1)} %copy-done.5, f32[1024]{0:T(1024)S(1)} %copy-done.25, f32[2048]{0:T(1024)S(1)} %get-tuple-element.173, ...), kind=kOutput, calls=%fused_computation.64 | convolution fusion | flops 5602082816 | bytes 20664320 | tf_op jit(solution)/shard_map/dot_general | solution.py:179
  910.4 79.1 %reduce-scatter.2.cloned.1.call-done = f32[2048,256]{1,0:T(8,128)} async-done(((f32[2048,1024]{1,0:T(8,128)}), f32[2048,256]{1,0:T(8,128)}) %reduce-scatter.2.cloned.1.call-update) | async-done | bytes 2097168 | tf_op jit(solution)/shard_map/reduce_scatter | solution.py:182
  993.2 142.3 %all-reduce.5.cloned.1.call-done = f32[64,1024]{1,0:T(8,128)} async-done(((f32[64,1024]{1,0:T(8,128)}), f32[64,1024]{1,0:T(8,128)}) %all-reduce.5.cloned.1.call-update) | async-done | bytes 262160 | tf_op jit(solution)/shard_map/psum | solution.py:192
  1138.9 63.4 %pmax.7 = f32[64]{0:T(128)} all-reduce(f32[64]{0:T(128)S(1)} %convolution_reduce_fusion), channel_id=1, replica_groups=mesh['req'=32,'tp'=4] {'req','tp'}, use_global_device_ids=true, to_apply=%region_20.21 | all-reduce | flops 64 | bytes 512 | tf_op jit(solution)/shard_map/pmax | solution.py:207
  (264 shorter events, 128.6 us)
Async XLA Ops:
  8.0 1129.1 %copy-start = (f32[4,1024]{1,0:T(4,128)S(1)}, f32[4,1024]{1,0:T(4,128)}, u32[]{:S(2)}) copy-start(f32[4,1024]{1,0:T(4,128)} %param.33) | copy-start | bytes 49156
  8.0 113.7 %copy-start.1 = (s32[128]{0:T(128)S(1)}, s32[128]{0:T(128)}, u32[]{:S(2)}) copy-start(s32[128]{0:T(128)} %param.22) | copy-start | bytes 1540
  8.0 115.9 %copy-start.15 = (f32[8,1024]{1,0:T(8,128)S(1)}, f32[8,1024]{1,0:T(8,128)}, u32[]{:S(2)}) copy-start(f32[8,1024]{1,0:T(8,128)} %param.23) | copy-start | bytes 98308
  8.0 192.4 %copy-start.16 = (f32[8,1024]{1,0:T(8,128)S(1)}, f32[8,1024]{1,0:T(8,128)}, u32[]{:S(2)}) copy-start(f32[8,1024]{1,0:T(8,128)} %param.25) | copy-start | bytes 98308
  8.0 271.0 %copy-start.21 = (f32[1024]{0:T(1024)S(1)}, f32[1024]{0:T(1024)}, u32[]{:S(2)}) copy-start(f32[1024]{0:T(1024)} %param.31) | copy-start | bytes 12292
  8.1 662.7 %all-gather.4.cloned.1.call-start = ((), (), s32[]{:S(2)}) async-start(), calls=%async_computation.9 | async-start | bytes 1419264 | tf_op jit(solution)/shard_map/all_gather | solution.py:95
  96.7 188.8 %all-to-all-start.1 = ((bf16[256,4,256]{0,2,1:T(8,128)(2,1)}), bf16[256,4,256]{0,2,1:T(8,128)(2,1)S(1)}, u32[]{:S(2)}, u32[]{:S(2)}) async-start(bf16[256,4,256]{0,2,1:T(8,128)(2,1)} %bitcast.18), calls=%async_computation.1 | async-start | bytes 1048576 | tf_op jit(solution)/shard_map/all_to_all | solution.py:101
  115.2 562.5 %all-gather.6.cloned.1.call-start = ((), (), s32[]{:S(2)}) async-start(), calls=%async_computation.10 | async-start | bytes 1419264 | tf_op jit(solution)/shard_map/all_gather | solution.py:96
  118.2 363.1 %copy-start.19 = (s32[64]{0:T(128)}, s32[64]{0:T(128)S(1)}, u32[]{:S(2)}) copy-start(s32[64]{0:T(128)S(1)} %get-tuple-element.126) | copy-start | bytes 772
  124.0 364.7 %copy-start.18 = (s32[1024]{0:T(1024)}, s32[1024]{0:T(1024)S(1)}, u32[]{:S(2)}) copy-start(s32[1024]{0:T(1024)S(1)} %pad_clamp_fusion.1) | copy-start | bytes 12292
  279.0 6.4 copy-start.22
  285.6 39.4 %all-to-all-start = ((bf16[256,4,256]{0,2,1:T(8,128)(2,1)}), bf16[256,4,256]{0,2,1:T(8,128)(2,1)S(1)}, u32[]{:S(2)}, u32[]{:S(2)}) async-start(bf16[256,4,256]{0,2,1:T(8,128)(2,1)} %bitcast.7), calls=%async_computation | async-start | bytes 1048576 | tf_op jit(solution)/shard_map/all_to_all | solution.py:100
  325.0 13.3 %all-to-all-start.2 = ((bf16[256,4,256]{0,2,1:T(8,128)(2,1)}), bf16[256,4,256]{0,2,1:T(8,128)(2,1)S(1)}, u32[]{:S(2)}, u32[]{:S(2)}) async-start(bf16[256,4,256]{0,2,1:T(8,128)(2,1)} %bitcast.25), calls=%async_computation.2 | async-start | bytes 1048576 | tf_op jit(solution)/shard_map/all_to_all | solution.py:102
  330.8 3.7 copy-start.8
  338.2 4.6 copy-start.4
  339.1 7.9 copy-start.17
  342.6 3.2 copy-start.7
  342.6 137.7 %copy-start.14 = (f32[8,2624]{1,0:T(8,128)S(1)}, f32[8,2624]{1,0:T(8,128)}, u32[]{:S(2)}) copy-start(f32[8,2624]{1,0:T(8,128)} %param.29) | copy-start | bytes 251908
  342.8 147.3 %copy-start.9 = (bf16[2,2048,256]{2,1,0:T(8,128)(2,1)}, bf16[2,2048,256]{2,1,0:T(8,128)(2,1)S(1)}, u32[]{:S(2)}) copy-start(bf16[2,2048,256]{2,1,0:T(8,128)(2,1)S(1)} %pad_maximum_fusion.1) | copy-start | bytes 6291460
  342.8 147.3 %collective-permute-start = (bf16[2,2048,256]{2,1,0:T(8,128)(2,1)S(1)}, bf16[2,2048,256]{2,1,0:T(8,128)(2,1)}, u32[]{:S(2)}, u32[]{:S(2)}) collective-permute-start(bf16[2,2048,256]{2,1,0:T(8,128)(2,1)S(1)} %pad_maximum_fusion.1), channel_id=1, source_target_pairs={{0,4},{4,8},{8,12},{12,16},{16,20},{20,24},{24,28},{28,32},{32,36}... | collective-permute-start | bytes 6291464 | tf_op jit(solution)/shard_map/ppermute | solution.py:19
  345.7 144.4 %collective-permute-start.1 = (bf16[2,2048,256]{2,1,0:T(8,128)(2,1)S(1)}, bf16[2,2048,256]{2,1,0:T(8,128)(2,1)}, u32[]{:S(2)}, u32[]{:S(2)}) collective-permute-start(bf16[2,2048,256]{2,1,0:T(8,128)(2,1)S(1)} %pad_maximum_fusion.1), channel_id=1, source_target_pairs={{4,0},{8,4},{12,8},{16,12},{20,16},{24,20},{28,24},{32,28},{36,32}... | collective-permute-start | bytes 6291464 | tf_op jit(solution)/shard_map/ppermute | solution.py:22
  463.0 25.5 %all-to-all-start.3 = ((bf16[256,4,256]{0,2,1:T(8,128)(2,1)}), bf16[256,4,256]{0,2,1:T(8,128)(2,1)S(1)}, u32[]{:S(2)}, u32[]{:S(2)}) async-start(bf16[256,4,256]{0,2,1:T(8,128)(2,1)} %bitcast.36), calls=%async_computation.3 | async-start | bytes 1048576 | tf_op jit(solution)/shard_map/all_to_all | solution.py:103
  480.3 226.5 %all-gather.8.cloned.1.call-start = ((), (), s32[]{:S(2)}) async-start(), calls=%async_computation.11 | async-start | bytes 1419264 | tf_op jit(solution)/shard_map/all_gather | solution.py:97
  481.0 392.8 %all-reduce.3.cloned.1.call-start = ((), (), s32[]{:S(2)}) async-start(), calls=%async_computation.8 | async-start | bytes 16777216 | tf_op jit(solution)/shard_map/psum | solution.py:172
  496.5 4.8 copy-start.3
  513.1 1.9 copy-start.2
  521.5 1.9 copy-start.2
  529.9 1.9 copy-start.2
  538.4 1.9 copy-start.2
  553.2 1.9 copy-start.2
  561.6 1.9 copy-start.2
  570.0 1.9 copy-start.2
  578.5 1.9 copy-start.2
  593.3 1.9 copy-start.2
  601.7 1.9 copy-start.2
  610.1 1.9 copy-start.2
  618.6 1.9 copy-start.2
  633.4 1.9 copy-start.2
  641.8 1.9 copy-start.2
  650.2 1.9 copy-start.2
  658.7 1.9 copy-start.2
  673.3 28.3 %all-to-all-start.4 = ((bf16[256,4,656]{0,2,1:T(8,128)(2,1)}), bf16[256,4,656]{0,2,1:T(8,128)(2,1)S(1)}, u32[]{:S(2)}, u32[]{:S(2)}) async-start(bf16[256,4,656]{0,2,1:T(8,128)(2,1)} %bitcast.40), calls=%async_computation.4 | async-start | bytes 2686976 | tf_op jit(solution)/shard_map/all_to_all | solution.py:104
  701.6 37.0 %all-to-all-start.5 = ((bf16[256,4,656]{0,2,1:T(8,128)(2,1)}), bf16[256,4,656]{0,2,1:T(8,128)(2,1)S(1)}, u32[]{:S(2)}, u32[]{:S(2)}) async-start(bf16[256,4,656]{0,2,1:T(8,128)(2,1)} %bitcast.116), calls=%async_computation.5 | async-start | bytes 2686976 | tf_op jit(solution)/shard_map/all_to_all | solution.py:105
  738.6 5.2 copy-start.6
  738.6 36.5 %all-to-all-start.6 = ((bf16[256,4,656]{0,2,1:T(8,128)(2,1)}), bf16[256,4,656]{0,2,1:T(8,128)(2,1)}, u32[]{:S(2)}, u32[]{:S(2)}) async-start(bf16[256,4,656]{0,2,1:T(8,128)(2,1)} %bitcast.115), calls=%async_computation.6 | async-start | bytes 2686976 | tf_op jit(solution)/shard_map/all_to_all | solution.py:106
  743.5 246.0 %reduce-scatter.2.cloned.1.call-start = ((), (), s32[]{:S(2)}) async-start(), calls=%async_computation.12 | async-start | bytes 10485760 | tf_op jit(solution)/shard_map/reduce_scatter | solution.py:182
  778.7 102.7 %copy-start.25 = (f32[1024]{0:T(1024)S(1)}, f32[1024]{0:T(1024)}, u32[]{:S(2)}) copy-start(f32[1024]{0:T(1024)} %param.32) | copy-start | bytes 12292
  879.4 2.0 copy-start.5
  881.3 5.4 copy-start.12
  909.7 0.7 copy-start.23
  909.7 0.7 copy-start.20
  909.7 227.4 %copy-start.24 = (s32[64]{0:T(128)S(1)}, s32[64]{0:T(128)}, u32[]{:S(2)}) copy-start(s32[64]{0:T(128)} %param.21) | copy-start | bytes 772
  909.8 228.7 %copy-start.11 = (f32[384,1024]{1,0:T(8,128)S(1)}, f32[384,1024]{1,0:T(8,128)}, u32[]{:S(2)}) copy-start(f32[384,1024]{1,0:T(8,128)} %param.30) | copy-start | bytes 4718596
  909.8 225.7 %all-reduce.5.cloned.1.call-start = ((), (), s32[]{:S(2)}) async-start(), calls=%async_computation.13 | async-start | bytes 524288 | tf_op jit(solution)/shard_map/psum | solution.py:192
  991.7 210.6 %copy-start.10 = (bf16[2048,256]{1,0:T(8,128)(2,1)}, bf16[2048,256]{1,0:T(8,128)(2,1)S(1)}, u32[]{:S(2)}) copy-start(bf16[2048,256]{1,0:T(8,128)(2,1)S(1)} %add_convert_fusion) | copy-start | bytes 3145732
  992.5 0.7 copy-start.13
Sparse Core Ops, SparseCore 0:
  12.0 70.7 all-gather.3
  119.1 62.6 all-gather.5
  484.2 72.7 all-gather.7
  993.3 142.1 all-reduce.4
Sparse Core Ops, SparseCore 1:
  670.8 202.9 all-reduce.2
  909.9 79.6 reduce-scatter.1
where the time goes:
time: 1220 us; the launch traced here: 1210 us
  blocking collectives  418 us (34%)
  waiting for transfers between devices  406 us (33%)
  matrix products  127 us (10%)
  starting transfers between devices  91.3 us (7%)
  local copies, waits for them, and re-layouts  80.1 us (7%)
  other arithmetic  59.5 us (5%)
  between operations  16 us (1%)
    psum x1, waiting for transfers between devices, body(): last = lax.psum(placed, ('req', 'tp'))  142 us
    all_gather x1, blocking collectives, body(): lax.all_gather(served[3], 'req', axis=0, tiled=True)  115 us
    psum x1, waiting for transfers between devices, body(): summed = lax.psum(attn_part, 'tp')  95.2 us
    all_gather x1, blocking collectives, body(): lax.all_gather(served[1], 'req', axis=0, tiled=True)  85.3 us
    reduce_scatter x1, waiting for transfers between devices, body(): lax.psum_scatter(down_part, 'tp', scatter_dimension=1, tiled=True)  79.1 us
    all_gather x1, blocking collectives, body(): lax.all_gather(served[2], 'req', axis=0, tiled=True)  78.2 us
    all_gather x1, blocking collectives, body(): lax.all_gather(served[0], 'req', axis=0, tiled=True)  76.5 us
    pmax x1, blocking collectives, body(): top_logit = lax.pmax(jnp.max(logits, axis=-1), ('req', 'tp'))  63.4 us
  transfers between devices with their start and end apart: 15, of which 8 were waited for; matrix products, arithmetic and copies ran while one was open for 18% of the time, Pallas kernels for 0%

commit v1 on v0

v1 whole, which is shorter than its diff:
```python
import functools

import jax
import jax.numpy as jnp
from jax import lax
from jax.experimental import pallas as pl
from jax.experimental.pallas import tpu as pltpu
from jax.sharding import PartitionSpec as P

HEADS = 16
HEAD_DIM = 64
THETA = 160000.0
EPS = 1e-05
BF = jnp.bfloat16
F32 = jnp.float32
BOTH = ("req", "tp")
NEG = -1e30
FFP = 768
QB = 256
KC = 512
VMEM_LIMIT = 60 * 1024 * 1024


def vmem(*shape):
    return pl.BlockSpec(shape, lambda *_: (0,) * len(shape))


def params():
    return pltpu.CompilerParams(vmem_limit_bytes=VMEM_LIMIT)


def prep_kernel(wq, wk, wv, wo, wi, wg, w2, qkv, wob, mlp):
    row = lax.broadcasted_iota(jnp.int32, (256, 256), 0)
    col = lax.broadcasted_iota(jnp.int32, (256, 256), 1)
    source = (col % 128) // 32 * 64 + col // 128 * 32 + col % 32
    turn = jnp.where(row == source, 1.0, 0.0).astype(BF)
    trow = lax.broadcasted_iota(jnp.int32, (64, 128), 0)
    tcol = lax.broadcasted_iota(jnp.int32, (64, 128), 1)
    for t in range(4):
        at = slice(256 * t, 256 * t + 256)
        for n, w in enumerate((wq, wk)):
            qkv[t, :, 256 * n : 256 * n + 256] = jnp.dot(
                w[:, at].astype(BF), turn, preferred_element_type=F32
            ).astype(BF)
        qkv[t, :, 512:768] = wv[:, at].astype(BF)
        pick = jnp.where((trow == tcol + 16 * t) & (tcol < 16), 1.0, 0.0).astype(BF)
        for n, w in enumerate((wi, wg, w2)):
            mlp[t, :, FFP * n : FFP * n + 640] = w[:, 640 * t : 640 * t + 640].astype(BF)
            mlp[t, :, FFP * n + 640 : FFP * n + 768] = jnp.dot(
                w[:, 2560:2624].astype(BF), pick, preferred_element_type=F32
            ).astype(BF)
    wob[...] = wo[...].astype(BF)


def prep(wq, wk, wv, wo, wi, wg, w2):
    return pl.pallas_call(
        prep_kernel,
        out_shape=(
            jax.ShapeDtypeStruct((4, 8, 768), BF),
            jax.ShapeDtypeStruct((8, 1024), BF),
            jax.ShapeDtypeStruct((4, 8, 3 * FFP), BF),
        ),
        compiler_params=params(),
        name="prep",
    )(wq, wk, wv, wo, wi, wg, w2)


def layer_norm(values, gain):
    center = jnp.mean(values, axis=-1, keepdims=True)
    spread = jnp.mean(values * values, axis=-1, keepdims=True) - center * center
    return (values - center) * lax.rsqrt(spread + EPS) * gain


def norm_kernel(h, gain, out):
    out[...] = layer_norm(h[...].astype(F32), gain[...]).astype(BF)


def norm(h, gain):
    rows = h.shape[0]
    return pl.pallas_call(
        norm_kernel,
        grid=(rows // 512,),
        in_specs=[pl.BlockSpec((512, 1024), lambda i: (i, 0)), vmem(1, 1024)],
        out_specs=pl.BlockSpec((512, 1024), lambda i: (i, 0)),
        out_shape=jax.ShapeDtypeStruct((rows, 1024), BF),
        compiler_params=params(),
        name="norm",
    )(h, gain.reshape(1, 1024))


def qkv_kernel(x, w, cos, sin, q, kv, cache):
    row = lax.broadcasted_iota(jnp.int32, (256, 256), 0)
    col = lax.broadcasted_iota(jnp.int32, (256, 256), 1)
    source = (col % 128) // 32 * 64 + col // 128 * 32 + col % 32
    back = jnp.where(source == row, 1.0, 0.0).astype(BF)
    y = jnp.dot(x[...], w[...], preferred_element_type=F32)
    c = cos[...]
    s = sin[...]

    def turned(a, b):
        return jnp.concatenate([a * c - b * s, b * c + a * s], axis=1)

    q[...] = (turned(y[:, :128], y[:, 128:256]).astype(BF).astype(F32) * 0.125).astype(BF)
    k = turned(y[:, 256:384], y[:, 384:512]).astype(BF)
    v = y[:, 512:].astype(BF)
    kv[0] = k
    kv[1] = v
    cache[0] = lax.dot_general(
        k, back, (((1,), (1,)), ((), ())), preferred_element_type=F32
    ).astype(BF)
    cache[1] = v


def qkv_project(x, w, cos, sin):
    rows = x.shape[0]
    n = 512
    return pl.pallas_call(
        qkv_kernel,
        grid=(rows // n,),
        in_specs=[
            pl.BlockSpec((n, 1024), lambda i: (i, 0)),
            vmem(1024, 768),
            pl.BlockSpec((n, 128), lambda i: (i, 0)),
            pl.BlockSpec((n, 128), lambda i: (i, 0)),
        ],
        out_specs=[
            pl.BlockSpec((n, 256), lambda i: (i, 0)),
            pl.BlockSpec((2, n, 256), lambda i: (0, i, 0)),
            pl.BlockSpec((2, n, 256), lambda i: (0, i, 0)),
        ],
        out_shape=(
            jax.ShapeDtypeStruct((rows, 256), BF),
            jax.ShapeDtypeStruct((2, rows, 256), BF),
            jax.ShapeDtypeStruct((2, rows, 256), BF),
        ),
        compiler_params=params(),
        name="qkv",
    )(x, w, cos, sin)


def attend_chunk(start, q4, kv, kseg, qseg, m_sc, l_sc, acc):
    start = pl.multiple_of(start, 128)
    k = kv[0, pl.ds(start, KC), :]
    v = kv[1, pl.ds(start, KC), :]
    same = qseg[...] == kseg[0:1, pl.ds(start, KC)]
    for h in range(4):
        at = slice(h * QB, h * QB + QB)
        s = lax.dot_general(
            q4[at, :], k, (((1,), (1,)), ((), ())), preferred_element_type=F32
        )
        s = jnp.where(same, s, NEG)
        old = m_sc[at, :]
        new = jnp.maximum(old, jnp.max(s, axis=1, keepdims=True))
        p = jnp.exp(s - new)
        fade = jnp.exp(old - new)
        l_sc[at, :] = l_sc[at, :] * fade + jnp.sum(p, axis=1, keepdims=True)
        m_sc[at, :] = new
        acc[at, :] = acc[at, :] * fade + jnp.dot(
            p.astype(BF), v, preferred_element_type=F32
        )


def spread_heads(q, q4):
    lane = lax.broadcasted_iota(jnp.int32, (QB, 256), 1)
    for h in range(4):
        q4[h * QB : h * QB + QB, :] = jnp.where(
            (lane % 128) // 32 == h, q[...].astype(F32), 0.0
        ).astype(BF)


def own_kernel(table, q, qseg, kv, kseg, acc_out, ml_out, q4, m_sc, l_sc, acc):
    i = pl.program_id(0)
    spread_heads(q, q4)
    m_sc[...] = jnp.full_like(m_sc, NEG)
    l_sc[...] = jnp.zeros_like(l_sc)
    acc[...] = jnp.zeros_like(acc)

    @pl.loop(0, table[1, i])
    def _(c):
        attend_chunk(table[0, i] + c * KC, q4, kv, kseg, qseg, m_sc, l_sc, acc)

    lane = lax.broadcasted_iota(jnp.int32, (QB, 256), 1)
    mine = lax.broadcasted_iota(jnp.int32, (QB, 128), 1)
    total = jnp.zeros((QB, 256), F32)
    ml = jnp.zeros((QB, 128), F32)
    for h in range(4):
        at = slice(h * QB, h * QB + QB)
        total = jnp.where(lane // 64 == h, acc[at, :], total)
        ml = jnp.where(mine == h, m_sc[at, :], ml)
        ml = jnp.where(mine == h + 4, l_sc[at, :], ml)
    acc_out[...] = total
    ml_out[...] = ml


def halo_kernel(table, q, qseg, lkv, lseg, rkv, rseg, acc_in, ml_in, out, q4, m_sc, l_sc, acc):
    i = pl.program_id(0)
    spread_heads(q, q4)
    for h in range(4):
        at = slice(h * QB, h * QB + QB)
        m_sc[at, :] = ml_in[:, h : h + 1]
        l_sc[at, :] = ml_in[:, h + 4 : h + 5]
        acc[at, :] = acc_in[...]

    @pl.loop(0, table[3, i])
    def _(c):
        attend_chunk(table[2, i] + c * KC, q4, lkv, lseg, qseg, m_sc, l_sc, acc)

    @pl.loop(0, table[5, i])
    def _(c):
        attend_chunk(table[4, i] + c * KC, q4, rkv, rseg, qseg, m_sc, l_sc, acc)

    lane = lax.broadcasted_iota(jnp.int32, (QB, 256), 1)
    total = jnp.zeros((QB, 256), F32)
    for h in range(4):
        at = slice(h * QB, h * QB + QB)
        total = jnp.where(lane // 64 == h, acc[at, :] / l_sc[at, :], total)
    out[...] = total.astype(BF)


def attn_scratch():
    return [
        pltpu.VMEM((4 * QB, 256), BF),
        pltpu.VMEM((4 * QB, 1), F32),
        pltpu.VMEM((4 * QB, 1), F32),
        pltpu.VMEM((4 * QB, 256), F32),
    ]


def by_block(width):
    return pl.BlockSpec((QB, width), lambda i, *_: (i, 0))


def attend_own(table, q, qseg, kv, kseg):
    rows = q.shape[0]
    return pl.pallas_call(
        own_kernel,
        grid_spec=pltpu.PrefetchScalarGridSpec(
            num_scalar_prefetch=1,
            grid=(rows // QB,),
            in_specs=[by_block(256), by_block(1), vmem(2, rows, 256), vmem(1, rows)],
            out_specs=[by_block(256), by_block(128)],
            scratch_shapes=attn_scratch(),
        ),
        out_shape=(
            jax.ShapeDtypeStruct((rows, 256), F32),
            jax.ShapeDtypeStruct((rows, 128), F32),
        ),
        compiler_params=params(),
        name="attend_own",
    )(table, q, qseg, kv, kseg)


def attend_halo(table, q, qseg, lkv, lseg, rkv, rseg, acc, ml):
    rows = q.shape[0]
    return pl.pallas_call(
        halo_kernel,
        grid_spec=pltpu.PrefetchScalarGridSpec(
            num_scalar_prefetch=1,
            grid=(rows // QB,),
            in_specs=[
                by_block(256),
                by_block(1),
                vmem(2, rows, 256),
                vmem(1, rows),
                vmem(2, rows, 256),
                vmem(1, rows),
                by_block(256),
                by_block(128),
            ],
            out_specs=by_block(256),
            scratch_shapes=attn_scratch(),
        ),
        out_shape=jax.ShapeDtypeStruct((rows, 256), BF),
        compiler_params=params(),
        name="attend_halo",
    )(table, q, qseg, lkv, lseg, rkv, rseg, acc, ml)


def contract_last(a, b):
    return lax.dot_general(a, b, (((1,), (1,)), ((), ())), preferred_element_type=F32)


def mlp_kernel(order, m0, m1, m2, m3, h, o0, o1, o2, o3, gain, wi, wg, d0, d1, d2, d3, keep, send):
    mixed = (m0, m1, m2, m3)
    outs = (o0, o1, o2, o3)
    downs = (d0, d1, d2, d3)
    summed = h[...].astype(F32)
    total = contract_last(m0[...], o0[...])
    for a, b in zip(mixed[1:], outs[1:]):
        total += contract_last(a[...], b[...])
    first = (summed + total).astype(BF)
    wide = first.astype(F32)
    normed = layer_norm(wide, gain[...]).astype(BF)
    a = jnp.dot(normed, wi[...], preferred_element_type=F32)
    b = jnp.dot(normed, wg[...], preferred_element_type=F32)
    inner = (0.5 * a * (1.0 + lax.erf(a * (0.5**0.5))) * b).astype(BF)
    mine = jnp.zeros((h.shape[0], 256), F32)
    for t in range(4):
        mine = jnp.where(order[0] == t, wide[:, 256 * t : 256 * t + 256], mine)
    keep[:, :256] = contract_last(inner, downs[0][...]) + mine
    keep[:, 256:] = contract_last(inner, downs[1][...])
    send[:, :256] = contract_last(inner, downs[2][...]).astype(BF)
    send[:, 256:] = contract_last(inner, downs[3][...]).astype(BF)


def mlp(order, mixed, h, wo, gain, weights, part, parts):
    rows = h.shape[0] // parts
    n = 256
    steps = rows // n
    base = part * steps

    def rowblock(width):
        return pl.BlockSpec((n, width), lambda i, *_: (i + base, 0))

    def outblock(width):
        return pl.BlockSpec((n, width), lambda i, *_: (i, 0))

    return pl.pallas_call(
        mlp_kernel,
        grid_spec=pltpu.PrefetchScalarGridSpec(
            num_scalar_prefetch=1,
            grid=(steps,),
            in_specs=[rowblock(256)] * 4
            + [rowblock(1024)]
            + [pl.BlockSpec((1024, 256), lambda i, s, m=m: (0, s[m])) for m in range(4)]
            + [vmem(1, 1024)]
            + [
                pl.BlockSpec((1024, FFP), lambda i, s: (0, 0)),
                pl.BlockSpec((1024, FFP), lambda i, s: (0, 1)),
            ]
            + [pl.BlockSpec((256, FFP), lambda i, s, m=m: (s[m], 2)) for m in range(4)],
            out_specs=[outblock(512), outblock(512)],
        ),
        out_shape=(
            jax.ShapeDtypeStruct((rows, 512), F32),
            jax.ShapeDtypeStruct((rows, 512), BF),
        ),
        compiler_params=params(),
        name="mlp",
    )(order, *mixed, h, wo, wo, wo, wo, gain.reshape(1, 1024), weights, weights, *([weights] * 4))


def swap(x, bit):
    return lax.ppermute(x, "tp", [(i, i ^ bit) for i in range(4)])


def shift(x, by):
    count = lax.axis_size("req")
    return lax.ppermute(x, "req", [(i, i + by) for i in range(count) if 0 <= i + by < count])


def exchange(x, axes):
    return lax.all_to_all(x, axes, split_axis=0, concat_axis=0, tiled=True)


def body(
    hidden_in,
    lengths,
    tenant,
    shard_map,
    wq,
    wk,
    wv,
    wo,
    wi_in,
    wi_gate,
    wo2,
    head,
    attn_gain,
    mlp_gain,
    final_gain,
):
    req_count = lax.axis_size("req")
    tp_count = lax.axis_size("tp")
    count = req_count * tp_count
    req_index = lax.axis_index("req")
    tp_index = lax.axis_index("tp")
    slots, width = hidden_in.shape
    requests = lengths.shape[0]

    qkv_block, out_block, mlp_block = prep(wq, wk, wv, wo, wi_in, wi_gate, wo2)
    place = jnp.arange(count, dtype=jnp.int32)
    source = jnp.sum(
        jnp.where(shard_map[None, :] == place[:, None], place[None, :], 0), axis=1
    )
    qkv_all = exchange(
        jnp.broadcast_to(qkv_block[None], (req_count, 4, 8, 768)).reshape(count, 8, 768), BOTH
    )
    qkv_w = qkv_all[source].reshape(width, 768)
    mlp_rows = exchange(mlp_block, "tp")
    mlp_all = lax.all_gather(mlp_rows.reshape(4 * 8, 3 * FFP), "req", axis=0, tiled=True)
    mlp_w = mlp_all.reshape(count, 8, 3 * FFP)[source].reshape(width, 3 * FFP)

    ends = jnp.cumsum(lengths)
    base = req_index * slots
    index = base - slots + jnp.arange(3 * slots, dtype=jnp.int32)
    segment = jnp.sum((ends[None, :] <= index[:, None]).astype(jnp.int32), axis=1)
    segment = jnp.where((index >= 0) & (index < slots * req_count), segment, -1)
    own = base + jnp.arange(slots, dtype=jnp.int32)
    start_of = jnp.max(jnp.where(ends[None, :] <= own[:, None], ends[None, :], 0), axis=1)
    position = (own - start_of).astype(F32)
    half = HEAD_DIM // 2
    lane = jnp.arange(128, dtype=jnp.int32) % half
    freq = THETA ** (-(2.0 * lane.astype(F32)) / HEAD_DIM)
    angle = position[:, None] * freq[None, :]
    cos = jnp.cos(angle)
    sin = jnp.sin(angle)
    begin = base + jnp.arange(slots // QB, dtype=jnp.int32) * QB
    close = begin + QB - 1
    low = jnp.max(jnp.where(ends[None, :] <= begin[:, None], ends[None, :], 0), axis=1) - base
    high = jnp.min(jnp.where(ends[None, :] > close[:, None], ends[None, :], 1 << 30), axis=1) - base

    def span(lo, hi):
        lo = jnp.maximum(lo, 0) // 128 * 128
        n = jnp.maximum((hi - lo + KC - 1) // KC, 0)
        return jnp.minimum(lo, slots - n * KC), n

    own_lo, own_n = span(low, jnp.minimum(high, slots))
    left_lo, left_n = span(jnp.minimum(low, 0) + slots, jnp.full_like(low, slots))
    right_lo, right_n = span(jnp.zeros_like(high), high - slots)
    table = jnp.stack([own_lo, own_n, left_lo, left_n, right_lo, right_n])
    segs = segment.reshape(3, 1, slots)
    qseg = segment[slots : 2 * slots].reshape(slots, 1)

    normed = norm(hidden_in, attn_gain)
    query, kv, cache = qkv_project(normed, qkv_w, cos, sin)
    left = shift(kv, 1)
    right = shift(kv, -1)
    out_all = exchange(
        jnp.broadcast_to(out_block[None], (count, 8, width)), BOTH
    )
    out_w = out_all[source].reshape(width, width)
    acc, ml = attend_own(table, query, qseg, kv, segs[1])
    mixed = attend_halo(table, query, qseg, left, segs[0], right, segs[2], acc, ml)

    far = swap(mixed, 2)
    near = swap(mixed, 1)
    both = swap(far, 1)
    order = tp_index ^ jnp.array([0, 2, 1, 3], jnp.int32)
    parts = 2
    pieces = []
    for part in range(parts):
        keep, send = mlp(
            order, (mixed, far, near, both), hidden_in, out_w, mlp_gain, mlp_w, part, parts
        )
        got = swap(send, 1).astype(F32)
        other = swap((keep[:, 256:] + got[:, 256:]).astype(BF), 2).astype(F32)
        pieces.append((keep[:, :256] + got[:, :256] + other).astype(BF))
    hidden_out = jnp.concatenate(pieces, axis=0)

    last_slot = ends - 1 - base
    holds = (last_slot >= 0) & (last_slot < slots)
    picked = jnp.where(holds[:, None], hidden_out[jnp.clip(last_slot, 0, slots - 1)], 0)
    each = requests // req_count
    mine = exchange(picked.reshape(req_count, each, 256), "req").astype(F32).sum(axis=0).astype(BF)
    spread = exchange(jnp.broadcast_to(mine[None], (count, each, 256)), BOTH)
    last = (
        spread.reshape(req_count, tp_count, each, 256)
        .transpose(0, 2, 1, 3)
        .reshape(requests, width)
        .astype(F32)
    )
    last_rms = jnp.sqrt(jnp.mean(last * last, axis=-1))
    choose = (tenant[:, None] == jnp.arange(final_gain.shape[0], dtype=jnp.int32)[None, :]).astype(
        F32
    )
    gain_rows = jnp.dot(
        choose, final_gain, precision=lax.Precision.HIGHEST, preferred_element_type=F32
    )
    final = layer_norm(last, gain_rows).astype(BF)
    logits = contract_last(final, head.astype(BF))
    top = jnp.max(logits, axis=-1)
    tops = exchange(jnp.broadcast_to(top[None], (count, requests)), BOTH)
    top_logit = jnp.max(tops, axis=0)
    return (hidden_out, cache, last_rms, top_logit)


def solution(mesh):
    rows = P(BOTH, None)
    placed = (P("req", None), P(), P(), P()) + (rows,) * 8 + (P(), P(), P())
    return jax.shard_map(
        body,
        mesh=mesh,
        in_specs=placed,
        out_specs=(P("req", "tp"), P(None, "req", "tp"), P(), P()),
        check_vma=False,
    )
```

time: 1220 us -> 339 us (0.28)
  blocking collectives: 418 us -> 54.6 us
  waiting for transfers between devices: 406 us -> 71.7 us
  matrix products: 127 us -> 0.76 us
  Pallas kernels: 0 us -> 118 us
  local copies, waits for them, and re-layouts: 80.1 us -> 19.4 us
  starting transfers between devices: 91.3 us -> 44.6 us
  other arithmetic: 59.5 us -> 13.4 us
    all_gather x4 -> x0, blocking collectives: 355 us -> none  [the longest x1 115 us: body(): lax.all_gather(served[3], 'req', axis=0, tiled=True)]
    psum x2 -> x0, waiting for transfers between devices: 237 us -> none  [the longest x1 142 us: body(): last = lax.psum(placed, ('req', 'tp'))]
    dot_general x39 -> x1, matrix products: 126 us -> 0.45 us  [contract_last(): lax.dot_general(a, b, (((1,), (1,)), ((), ())), preferred_element_type=F32)]
    pallas_call x0 -> x7, Pallas kernels: none -> 118 us  [the longest x1 46 us: attend_own(): pl.pallas_call(own_kernel, grid_spec=pltpu.PrefetchScalarGridSpec(num_sca...]
    reduce_scatter x1 -> x0, waiting for transfers between devices: 79.1 us -> none  [body(): lax.psum_scatter(down_part, 'tp', scatter_dimension=1, tiled=True)]
    pmax x1 -> x0, blocking collectives: 63.4 us -> none  [body(): top_logit = lax.pmax(jnp.max(logits, axis=-1), ('req', 'tp'))]
    all_to_all x0 -> x4, blocking collectives: none -> 54.6 us  [exchange(): return lax.all_to_all(x, axes, split_axis=0, concat_axis=0, tiled=True)]
    all_to_all x7 -> x2, starting transfers between devices: 86.5 us -> 36.5 us  [exchange(): return lax.all_to_all(x, axes, split_axis=0, concat_axis=0, tiled=True)]
  transfers between devices with their start and end apart: 15 -> 12, of which waited for: 8 -> 6; matrix products, arithmetic and copies ran while one was open for 18% -> 8% of each run, Pallas kernels for 0% -> 30%
where the time goes in v1:
time: 339 us; the launch traced here: 337 us
  Pallas kernels  118 us (35%)
  waiting for transfers between devices  71.7 us (21%)
  blocking collectives  54.6 us (16%)
  starting transfers between devices  44.6 us (13%)
  local copies, waits for them, and re-layouts  19.4 us (6%)
  between operations  14.4 us (4%)
  other arithmetic  13.4 us (4%)
    all_to_all x4, blocking collectives, exchange(): return lax.all_to_all(x, axes, split_axis=0, concat_axis=0, tiled=True)  54.6 us
    all_to_all x2, waiting for transfers between devices, exchange(): return lax.all_to_all(x, axes, split_axis=0, concat_axis=0, tiled=True)  49.8 us
    pallas_call x1, Pallas kernels, attend_own(): pl.pallas_call(own_kernel, grid_spec=pltpu.PrefetchScalarGridSpec(num_sca...  46 us
    all_to_all x2, starting transfers between devices, exchange(): return lax.all_to_all(x, axes, split_axis=0, concat_axis=0, tiled=True)  36.5 us
    pallas_call x2, Pallas kernels, mlp(): pl.pallas_call(mlp_kernel, grid_spec=pltpu.PrefetchScalarGridSpec(num_sca...  28.3 us
    pallas_call x1, Pallas kernels, attend_halo(): pl.pallas_call(halo_kernel, grid_spec=pltpu.PrefetchScalarGridSpec(num_sc...  27.6 us
    ppermute x7, waiting for transfers between devices, swap(): return lax.ppermute(x, 'tp', [(i, i ^ bit) for i in range(4)])  19.4 us
    pallas_call x1, Pallas kernels, qkv_project(): pl.pallas_call(qkv_kernel, grid=(rows // n,), in_specs=[pl.BlockSpec((n,...  8.01 us
  transfers between devices with their start and end apart: 12, of which 6 were waited for; matrix products, arithmetic and copies ran while one was open for 8% of the time, Pallas kernels for 30%

profile of v1, /device:TPU:1, one launch (start us, length us, event | category | flops | bytes accessed | tf_op | source)
XLA Modules:
  0.0 336.9 jit_solution(36019700112133818)
XLA Ops:
  7.2 2.0 prep.1
  9.3 9.8 %all_to_all.31 = bf16[4,8,2304]{2,1,0:T(8,128)(2,1)} all-to-all(bf16[4,8,2304]{2,1,0:T(8,128)(2,1)} %get-tuple-element.22), channel_id=1, replica_groups=mesh['req'=32,'tp'=4] {'tp'}, dimensions={0} | all-to-all | bytes 294912 | tf_op jit(solution)/shard_map/all_to_all | solution.py:353
  19.1 2.1 broadcast_in_dim.64
  21.2 10.4 %all-to-all-start = ((bf16[128,8,768]{2,1,0:T(8,128)(2,1)}), bf16[128,8,768]{2,1,0:T(8,128)(2,1)S(1)}, u32[]{:S(2)}, u32[]{:S(2)}) async-start(bf16[128,8,768]{2,1,0:T(8,128)(2,1)} %bitcast.8), calls=%async_computation | async-start | bytes 3145728 | tf_op jit(solution)/shard_map/all_to_all | solution.py:353
  31.6 0.1 copy.32
  31.7 0.1 reduce-window.4
  31.8 6.0 %norm.1.x = bf16[2048,1024]{1,0:T(8,128)(2,1)} custom-call(bf16[2048,1024]{1,0:T(8,128)(2,1)} %h.5, f32[1,1024]{1,0:T(1,128)} %bitcast.124), custom_call_target="tpu_custom_call" | custom-call | tf_op jit(solution)/shard_map/norm/pallas_call | solution.py:80
  37.8 0.1 select_reduce_fusion.1
  37.9 0.1 fusion.9
  38.1 0.2 select_reduce_fusion
  38.2 5.6 %multiply_sine_fusion = (f32[2048,128]{1,0:T(8,128)}, f32[2048,128]{1,0:T(8,128)}) fusion(f32[128]{0:T(128)S(1)} %fusion.15, f32[2048]{0:T(1024)S(1)} %subtract_convert_fusion), kind=kLoop, calls=%fused_computation.5 | loop fusion | flops 262144 | bytes 2105856 | tf_op jit(solution)/shard_map/sin | solution.py:407
  43.8 13.1 %all-to-all-done = bf16[128,8,768]{2,1,0:T(8,128)(2,1)S(1)} async-done(((bf16[128,8,768]{2,1,0:T(8,128)(2,1)}), bf16[128,8,768]{2,1,0:T(8,128)(2,1)S(1)}, u32[]{:S(2)}, u32[]{:S(2)}) %all-to-all-start) | async-done | bytes 1572896 | tf_op jit(solution)/shard_map/all_to_all | solution.py:353
  56.9 1.8 gather_fusion
  58.7 8.0 %qkv.1 = (bf16[2048,256]{1,0:T(8,128)(2,1)}, bf16[2,2048,256]{2,1,0:T(8,128)(2,1)}, bf16[2,2048,256]{2,1,0:T(8,128)(2,1)}) custom-call(bf16[2048,1024]{1,0:T(8,128)(2,1)} %norm.1.x, bf16[1024,768]{1,0:T(8,128)(2,1)} %bitcast.112, f32[2048,128]{1,0:T(8,128)} %get-tuple-element.40.cos, f32[2048,128]{1,0:T(8,128)} %get-tuple-element.39.sin), custom_call_target="tpu_custom_call" | custom-call | tf_op jit(solution)/shard_map/qkv/pallas_call | solution.py:117
  66.8 3.0 collective-permute-start
  69.8 1.3 collective-permute-start.1
  71.1 0.3 convert_reduce_fusion
  71.4 0.6 fusion.24
  72.0 1.3 copy.34.qseg
  73.3 0.2 select_reduce_fusion.2
  73.6 0.6 stack.2.table
  74.2 46.0 %attend_own.1 = (f32[2048,256]{1,0:T(8,128)}, f32[2048,128]{1,0:T(8,128)}) custom-call(s32[6,8]{1,0:T(8,128)} %stack.2.table, bf16[2048,256]{1,0:T(8,128)(2,1)} %get-tuple-element.17.q, s32[2048,1]{1,0:T(8,128)} %copy.34.qseg, bf16[2,2048,256]{2,1,0:T(8,128)(2,1)} %get-tuple-element.18.kv, s32[1,2048]{1,0:T(1,128)} %bitcast.119), custom_call_target="tpu_custom_call" | custom-call | tf_op jit(solution)/shard_map/attend_own/pallas_call | solution.py:235
  120.2 2.5 collective-permute-done.1.rkv
  122.7 27.6 %attend_halo.1.m0 = bf16[2048,256]{1,0:T(8,128)(2,1)} custom-call(s32[6,8]{1,0:T(8,128)} %stack.2.table, bf16[2048,256]{1,0:T(8,128)(2,1)} %get-tuple-element.17.q, s32[2048,1]{1,0:T(8,128)} %copy.34.qseg, bf16[2,2048,256]{2,1,0:T(8,128)(2,1)} %copy-done.4, s32[1,2048]{1,0:T(1,128)} %bitcast.121, bf16[2,2048,256]{2,1,0:T(8,128)(2,1)} %collective-permute-done.1.rkv, ...), custom_call_target="tpu_custom_call" | custom-call | tf_op jit(solution)/shard_map/attend_halo/pallas_call | solution.py:255
  150.4 1.6 broadcast_in_dim.69
  152.0 26.1 %all-to-all-start.1 = ((bf16[128,8,1024]{2,1,0:T(8,128)(2,1)}), bf16[128,8,1024]{2,1,0:T(8,128)(2,1)S(1)}, u32[]{:S(2)}, u32[]{:S(2)}) async-start(bf16[128,8,1024]{2,1,0:T(8,128)(2,1)} %broadcast_in_dim.69), calls=%async_computation.1 | async-start | bytes 4194304 | tf_op jit(solution)/shard_map/all_to_all | solution.py:353
  178.1 1.1 collective-permute-start.3
  179.3 0.3 collective-permute-start.4
  179.6 0.5 broadcast_xor_fusion.order
  180.1 36.7 %all-to-all-done.1 = bf16[128,8,1024]{2,1,0:T(8,128)(2,1)S(1)} async-done(((bf16[128,8,1024]{2,1,0:T(8,128)(2,1)}), bf16[128,8,1024]{2,1,0:T(8,128)(2,1)S(1)}, u32[]{:S(2)}, u32[]{:S(2)}) %all-to-all-start.1) | async-done | bytes 2097184 | tf_op jit(solution)/shard_map/all_to_all | solution.py:353
  216.8 2.0 gather_fusion.1
  218.8 5.4 %gather_fusion.2 = bf16[128,8,2304]{2,1,0:T(8,128)(2,1)} fusion(bf16[128,8,2304]{2,1,0:T(8,128)(2,1)} %bitcast.113, s32[1024]{0:T(1024)S(1)} %pad_clamp_fusion.1), kind=kCustom, calls=%fused_computation.2 | custom fusion | bytes 9437696 | tf_op jit(solution)/shard_map/gather | solution.py:392
  224.2 14.1 %mlp.2 = (f32[1024,512]{1,0:T(8,128)}, bf16[1024,512]{1,0:T(8,128)(2,1)}) custom-call(s32[4]{0:T(128)} %broadcast_xor_fusion.order, bf16[2048,256]{1,0:T(8,128)(2,1)} %attend_halo.1.m0, bf16[2048,256]{1,0:T(8,128)(2,1)} %collective-permute-done.2.m1, bf16[2048,256]{1,0:T(8,128)(2,1)} %collective-permute-done.3.m2, ...), custom_call_target="tpu_custom_call" | custom-call | tf_op jit(solution)/shard_map/mlp/pallas_call | solution.py:318
  238.4 0.5 collective-permute-start.5
  238.8 14.1 %mlp.3 = (f32[1024,512]{1,0:T(8,128)}, bf16[1024,512]{1,0:T(8,128)(2,1)}) custom-call(s32[4]{0:T(128)} %broadcast_xor_fusion.order, bf16[2048,256]{1,0:T(8,128)(2,1)} %attend_halo.1.m0, bf16[2048,256]{1,0:T(8,128)(2,1)} %collective-permute-done.2.m1, bf16[2048,256]{1,0:T(8,128)(2,1)} %collective-permute-done.3.m2, ...), custom_call_target="tpu_custom_call" | custom-call | tf_op jit(solution)/shard_map/mlp/pallas_call | solution.py:318
  253.0 0.2 collective-permute-start.7
  253.2 0.3 convert_element_type.73
  253.5 1.1 copy-done.6
  254.5 0.3 fusion.4
  254.8 0.8 collective-permute-start.6
  255.6 0.3 collective-permute-done.7
  255.9 0.3 convert_element_type.77
  256.2 1.4 copy-done.2
  257.6 0.3 fusion.1
  257.9 0.8 collective-permute-start.8
  258.7 0.1 and_reduce_fusion
  258.8 0.1 and.170
  258.9 9.5 %collective-permute-done.6 = bf16[1024,256]{1,0:T(8,128)(2,1)} collective-permute-done((bf16[1024,256]{1,0:T(8,128)(2,1)S(1)}, bf16[1024,256]{1,0:T(8,128)(2,1)}, u32[]{:S(2)}, u32[]{:S(2)}) %collective-permute-start.6) | collective-permute-done | bytes 524320 | tf_op jit(solution)/shard_map/ppermute | solution.py:344
  268.4 1.6 fusion.6
  270.1 9.6 %collective-permute-done.8 = bf16[1024,256]{1,0:T(8,128)(2,1)} collective-permute-done((bf16[1024,256]{1,0:T(8,128)(2,1)S(1)}, bf16[1024,256]{1,0:T(8,128)(2,1)}, u32[]{:S(2)}, u32[]{:S(2)}) %collective-permute-start.8) | collective-permute-done | bytes 524320 | tf_op jit(solution)/shard_map/ppermute | solution.py:344
  279.7 1.7 fusion.3
  281.4 0.7 gather_fusion.3
  282.1 0.1 broadcast_select_fusion
  282.3 15.8 %all_to_all.32 = bf16[32,2,256]{2,1,0:T(2,128)(2,1)S(1)} all-to-all(bf16[32,2,256]{2,1,0:T(2,128)(2,1)S(1)} %broadcast_select_fusion), channel_id=1, replica_groups=mesh['req'=32,'tp'=4] {'req'}, dimensions={0} | all-to-all | bytes 65536 | tf_op jit(solution)/shard_map/all_to_all | solution.py:353
  298.2 15.3 %all_to_all.33 = bf16[128,2,256]{2,1,0:T(2,128)(2,1)S(1)} all-to-all(bf16[128,2,256]{2,1,0:T(2,128)(2,1)S(1)} %broadcast_in_dim.72), channel_id=1, replica_groups=mesh['req'=32,'tp'=4] {'req','tp'}, dimensions={0} | all-to-all | bytes 262144 | tf_op jit(solution)/shard_map/all_to_all | solution.py:353
  313.6 0.1 convert_bitcast_fusion
  313.8 0.3 fusion.8
  314.1 0.1 div.84
  314.2 0.1 div.86
  314.3 0.5 add_rsqrt_fusion
  314.8 0.3 fusion
  315.1 0.5 convolution_reduce_fusion
  315.7 13.7 %all_to_all.34 = f32[128,1,64]{2,1,0:T(1,128)S(1)} all-to-all(f32[128,1,64]{2,1,0:T(1,128)S(1)} %broadcast_in_dim.73), channel_id=1, replica_groups=mesh['req'=32,'tp'=4] {'req','tp'}, dimensions={0} | all-to-all | bytes 65536 | tf_op jit(solution)/shard_map/all_to_all | solution.py:353
  329.4 0.7 reduce_max.39
  (56 shorter events, 0.6 us)
Async XLA Ops:
  7.2 307.7 %copy-start = (f32[4,1024]{1,0:T(4,128)S(1)}, f32[4,1024]{1,0:T(4,128)}, u32[]{:S(2)}) copy-start(f32[4,1024]{1,0:T(4,128)} %param.30) | copy-start | bytes 49156
  7.2 211.6 %all-gather.2.cloned.1.call-start = ((), (), s32[]{:S(2)}) async-start(), calls=%async_computation.6 | async-start | bytes 4866048 | tf_op jit(solution)/shard_map/all_gather | solution.py:391
  19.1 12.6 %copy-start.11 = (s32[64]{0:T(128)S(1)}, s32[64]{0:T(128)}, u32[]{:S(2)}) copy-start(s32[64]{0:T(128)} %param.17) | copy-start | bytes 772
  21.2 35.7 %all-to-all-start = ((bf16[128,8,768]{2,1,0:T(8,128)(2,1)}), bf16[128,8,768]{2,1,0:T(8,128)(2,1)S(1)}, u32[]{:S(2)}, u32[]{:S(2)}) async-start(bf16[128,8,768]{2,1,0:T(8,128)(2,1)} %bitcast.8), calls=%async_computation | async-start | bytes 3145728 | tf_op jit(solution)/shard_map/all_to_all | solution.py:353
  31.8 6.0 %copy-start.13 = (s32[128]{0:T(128)S(1)}, s32[128]{0:T(128)}, u32[]{:S(2)}) copy-start(s32[128]{0:T(128)} %param.19) | copy-start | bytes 1540
  66.8 53.5 %collective-permute-start = (bf16[2,2048,256]{2,1,0:T(8,128)(2,1)}, bf16[2,2048,256]{2,1,0:T(8,128)(2,1)S(1)}, u32[]{:S(2)}, u32[]{:S(2)}) collective-permute-start(bf16[2,2048,256]{2,1,0:T(8,128)(2,1)} %get-tuple-element.18.kv), channel_id=1, source_target_pairs={{0,4},{4,8},{8,12},{12,16},{16,20},{20,24},{24,28},{28,32},{32,36}... | collective-permute-start | bytes 6291464 | tf_op jit(solution)/shard_map/ppermute | solution.py:349
  69.8 52.9 %collective-permute-start.1 = (bf16[2,2048,256]{2,1,0:T(8,128)(2,1)}, bf16[2,2048,256]{2,1,0:T(8,128)(2,1)}, u32[]{:S(2)}, u32[]{:S(2)}) collective-permute-start(bf16[2,2048,256]{2,1,0:T(8,128)(2,1)} %get-tuple-element.18.kv), channel_id=1, source_target_pairs={{4,0},{8,4},{12,8},{16,12},{20,16},{24,20},{28,24},{32,28},{36,32}... | collective-permute-start | bytes 6291464 | tf_op jit(solution)/shard_map/ppermute | solution.py:349
  72.0 2.2 copy-start.9
  120.2 2.5 copy-start.4
  122.7 27.6 %copy-start.10 = (bf16[8,1024]{1,0:T(8,128)(2,1)S(1)}, bf16[8,1024]{1,0:T(8,128)(2,1)}, u32[]{:S(2)}) copy-start(bf16[8,1024]{1,0:T(8,128)(2,1)} %get-tuple-element.21) | copy-start | bytes 49156
  150.4 28.9 %collective-permute-start.2 = (bf16[2048,256]{1,0:T(8,128)(2,1)}, bf16[2048,256]{1,0:T(8,128)(2,1)}, u32[]{:S(2)}, u32[]{:S(2)}) collective-permute-start(bf16[2048,256]{1,0:T(8,128)(2,1)} %attend_halo.1.m0), channel_id=1, source_target_pairs={{0,2},{1,3},{2,0},{3,1},{4,6},{5,7},{6,4},{7,5},{8,10},{9,11},{10,... | collective-permute-start | bytes 3145736 | tf_op jit(solution)/shard_map/ppermute | solution.py:344
  152.0 26.2 %copy-start.1 = (bf16[2048,256]{1,0:T(8,128)(2,1)S(1)}, bf16[2048,256]{1,0:T(8,128)(2,1)}, u32[]{:S(2)}) copy-start(bf16[2048,256]{1,0:T(8,128)(2,1)} %attend_halo.1.m0) | copy-start | bytes 3145732
  152.0 27.6 %copy-start.14 = (s32[4]{0:T(128)S(1)}, s32[4]{0:T(128)}, u32[]{:S(2)}) copy-start(s32[4]{0:T(128)} %constant.165.clone) | copy-start | bytes 52
  152.0 64.8 %all-to-all-start.1 = ((bf16[128,8,1024]{2,1,0:T(8,128)(2,1)}), bf16[128,8,1024]{2,1,0:T(8,128)(2,1)S(1)}, u32[]{:S(2)}, u32[]{:S(2)}) async-start(bf16[128,8,1024]{2,1,0:T(8,128)(2,1)} %broadcast_in_dim.69), calls=%async_computation.1 | async-start | bytes 4194304 | tf_op jit(solution)/shard_map/all_to_all | solution.py:353
  178.1 46.1 %collective-permute-start.3 = (bf16[2048,256]{1,0:T(8,128)(2,1)S(1)}, bf16[2048,256]{1,0:T(8,128)(2,1)}, u32[]{:S(2)}, u32[]{:S(2)}) collective-permute-start(bf16[2048,256]{1,0:T(8,128)(2,1)S(1)} %copy-done.1), channel_id=1, source_target_pairs={{0,1},{1,0},{2,3},{3,2},{4,5},{5,4},{6,7},{7,6},{8,9},{9,8},{10,11... | collective-permute-start | bytes 3145736 | tf_op jit(solution)/shard_map/ppermute | solution.py:344
  179.3 44.9 %collective-permute-start.4 = (bf16[2048,256]{1,0:T(8,128)(2,1)}, bf16[2048,256]{1,0:T(8,128)(2,1)}, u32[]{:S(2)}, u32[]{:S(2)}) collective-permute-start(bf16[2048,256]{1,0:T(8,128)(2,1)} %collective-permute-done.2.m1), channel_id=1, source_target_pairs={{0,1},{1,0},{2,3},{3,2},{4,5},{5,4},{6,7},{7,6},{8,9},{9,8},{10,11... | collective-permute-start | bytes 3145736 | tf_op jit(solution)/shard_map/ppermute | solution.py:344
  238.4 14.8 %collective-permute-start.5 = (bf16[1024,512]{1,0:T(8,128)(2,1)}, bf16[1024,512]{1,0:T(8,128)(2,1)S(1)}, u32[]{:S(2)}, u32[]{:S(2)}) collective-permute-start(bf16[1024,512]{1,0:T(8,128)(2,1)} %get-tuple-element.24), channel_id=1, source_target_pairs={{0,1},{1,0},{2,3},{3,2},{4,5},{5,4},{6,7},{7,6},{8,9},{9,8},{10,11... | collective-permute-start | bytes 3145736 | tf_op jit(solution)/shard_map/ppermute | solution.py:344
  253.0 1.6 copy-start.6
  253.0 3.0 collective-permute-start.7
  254.8 2.8 copy-start.5
  254.8 13.6 %collective-permute-start.6 = (bf16[1024,256]{1,0:T(8,128)(2,1)S(1)}, bf16[1024,256]{1,0:T(8,128)(2,1)}, u32[]{:S(2)}, u32[]{:S(2)}) collective-permute-start(bf16[1024,256]{1,0:T(8,128)(2,1)S(1)} %fusion.4), channel_id=1, source_target_pairs={{0,2},{1,3},{2,0},{3,1},{4,6},{5,7},{6,4},{7,5},{8,10},{9,11},{10,... | collective-permute-start | bytes 1572872 | tf_op jit(solution)/shard_map/ppermute | solution.py:344
  256.2 1.4 copy-start.2
  257.9 21.8 %collective-permute-start.8 = (bf16[1024,256]{1,0:T(8,128)(2,1)S(1)}, bf16[1024,256]{1,0:T(8,128)(2,1)}, u32[]{:S(2)}, u32[]{:S(2)}) collective-permute-start(bf16[1024,256]{1,0:T(8,128)(2,1)S(1)} %fusion.1), channel_id=1, source_target_pairs={{0,2},{1,3},{2,0},{3,1},{4,6},{5,7},{6,4},{7,5},{8,10},{9,11},{10,... | collective-permute-start | bytes 1572872 | tf_op jit(solution)/shard_map/ppermute | solution.py:344
  258.9 20.8 %copy-start.3 = (f32[1024,512]{1,0:T(8,128)S(1)}, f32[1024,512]{1,0:T(8,128)}, u32[]{:S(2)}) copy-start(f32[1024,512]{1,0:T(8,128)} %copy-done.2) | copy-start | bytes 6291460
  281.3 33.5 %copy-start.12 = (s32[64]{0:T(128)S(1)}, s32[64]{0:T(128)}, u32[]{:S(2)}) copy-start(s32[64]{0:T(128)} %param.18) | copy-start | bytes 772
  281.3 33.8 %copy-start.8 = (f32[384,1024]{1,0:T(8,128)S(1)}, f32[384,1024]{1,0:T(8,128)}, u32[]{:S(2)}) copy-start(f32[384,1024]{1,0:T(8,128)} %param.27) | copy-start | bytes 4718596
  281.4 34.2 %copy-start.7 = (bf16[2048,256]{1,0:T(8,128)(2,1)}, bf16[2048,256]{1,0:T(8,128)(2,1)S(1)}, u32[]{:S(2)}) copy-start(bf16[2048,256]{1,0:T(8,128)(2,1)S(1)} %pad_maximum_fusion) | copy-start | bytes 3145732
Sparse Core Ops, SparseCore 0:
  19.2 149.9 all-gather.1

commit v2 on v1

v2 whole, which is shorter than its diff:
```python
import functools

import jax
import jax.numpy as jnp
from jax import lax
from jax.experimental import pallas as pl
from jax.experimental.pallas import tpu as pltpu
from jax.sharding import PartitionSpec as P

HEADS = 16
HEAD_DIM = 64
THETA = 160000.0
EPS = 1e-05
BF = jnp.bfloat16
F32 = jnp.float32
BOTH = ("req", "tp")
NEG = -1e30
FFP = 768
REST = 3 * FFP + 1024
QB = 256
KC = 512


def vmem(*shape):
    return pl.BlockSpec(shape, lambda *_: (0,) * len(shape))


def params(mib):
    return pltpu.CompilerParams(vmem_limit_bytes=mib * 1024 * 1024)


def cost(flops, moved, transcendentals=0):
    return pl.CostEstimate(flops=flops, bytes_accessed=moved, transcendentals=transcendentals)


def prep_kernel(wq, wk, wv, wo, wi, wg, w2, qkv, rest):
    row = lax.broadcasted_iota(jnp.int32, (256, 256), 0)
    col = lax.broadcasted_iota(jnp.int32, (256, 256), 1)
    source = (col % 128) // 32 * 64 + col // 128 * 32 + col % 32
    turn = jnp.where(row == source, 1.0, 0.0).astype(BF)
    trow = lax.broadcasted_iota(jnp.int32, (64, 128), 0)
    tcol = lax.broadcasted_iota(jnp.int32, (64, 128), 1)
    for t in range(4):
        at = slice(256 * t, 256 * t + 256)
        q, k = (
            jnp.dot(w[:, at].astype(BF), turn, preferred_element_type=F32).astype(BF)
            for w in (wq, wk)
        )
        mine = jnp.concatenate([q, k, wv[:, at].astype(BF)], axis=1)
        for r in range(qkv.shape[0]):
            qkv[r, t] = mine
        pick = jnp.where((trow == tcol + 16 * t) & (tcol < 16), 1.0, 0.0).astype(BF)
        for n, w in enumerate((wi, wg, w2)):
            rest[t, :, FFP * n : FFP * n + 640] = w[:, 640 * t : 640 * t + 640].astype(BF)
            rest[t, :, FFP * n + 640 : FFP * n + 768] = jnp.dot(
                w[:, 2560:2624].astype(BF), pick, preferred_element_type=F32
            ).astype(BF)
        rest[t, :, 3 * FFP :] = wo[...].astype(BF)


def prep(req_count, *weights):
    return pl.pallas_call(
        prep_kernel,
        out_shape=(
            jax.ShapeDtypeStruct((req_count, 4, 8, 768), BF),
            jax.ShapeDtypeStruct((4, 8, REST), BF),
        ),
        compiler_params=params(24),
        name="prep",
    )(*weights)


def layer_norm(values, gain):
    center = jnp.mean(values, axis=-1, keepdims=True)
    spread = jnp.mean(values * values, axis=-1, keepdims=True) - center * center
    return (values - center) * lax.rsqrt(spread + EPS) * gain


def norm_kernel(h, gain, out):
    out[...] = layer_norm(h[...].astype(F32), gain[...]).astype(BF)


def norm(h, gain):
    rows = h.shape[0]
    return pl.pallas_call(
        norm_kernel,
        grid=(rows // 512,),
        in_specs=[pl.BlockSpec((512, 1024), lambda i: (i, 0)), vmem(1, 1024)],
        out_specs=pl.BlockSpec((512, 1024), lambda i: (i, 0)),
        out_shape=jax.ShapeDtypeStruct((rows, 1024), BF),
        compiler_params=params(24),
        cost_estimate=cost(1 << 24, 1 << 23),
        name="norm",
    )(h, gain.reshape(1, 1024))


def qkv_kernel(x, w, cos, sin, q, key, vt, cache):
    row = lax.broadcasted_iota(jnp.int32, (256, 256), 0)
    col = lax.broadcasted_iota(jnp.int32, (256, 256), 1)
    source = (col % 128) // 32 * 64 + col // 128 * 32 + col % 32
    back = jnp.where(source == row, 1.0, 0.0).astype(BF)
    y = jnp.dot(x[...], w[...], preferred_element_type=F32)
    c = cos[...]
    s = sin[...]

    def turned(a, b):
        return jnp.concatenate([a * c - b * s, b * c + a * s], axis=1)

    q[...] = (turned(y[:, :128], y[:, 128:256]).astype(BF).astype(F32) * 0.125).astype(BF)
    k = turned(y[:, 256:384], y[:, 384:512]).astype(BF)
    v = y[:, 512:].astype(BF)
    key[...] = k
    vt[...] = jnp.transpose(v)
    cache[0] = lax.dot_general(
        k, back, (((1,), (1,)), ((), ())), preferred_element_type=F32
    ).astype(BF)
    cache[1] = v


def qkv_project(x, w, cos, sin):
    rows = x.shape[0]
    n = 512
    return pl.pallas_call(
        qkv_kernel,
        grid=(rows // n,),
        in_specs=[
            pl.BlockSpec((n, 1024), lambda i: (i, 0)),
            vmem(1024, 768),
            pl.BlockSpec((n, 128), lambda i: (i, 0)),
            pl.BlockSpec((n, 128), lambda i: (i, 0)),
        ],
        out_specs=[
            pl.BlockSpec((n, 256), lambda i: (i, 0)),
            pl.BlockSpec((n, 256), lambda i: (i, 0)),
            pl.BlockSpec((256, n), lambda i: (0, i)),
            pl.BlockSpec((2, n, 256), lambda i: (0, i, 0)),
        ],
        out_shape=(
            jax.ShapeDtypeStruct((rows, 256), BF),
            jax.ShapeDtypeStruct((rows, 256), BF),
            jax.ShapeDtypeStruct((256, rows), BF),
            jax.ShapeDtypeStruct((2, rows, 256), BF),
        ),
        compiler_params=params(32),
        cost_estimate=cost(2 * rows * 1024 * 768, 12 << 20),
        name="qkv",
    )(x, w, cos, sin)


VR = HEAD_DIM + 8


def attend_chunk(start, size, qm, key, vt, kseg, qseg, m_sc, acc):
    start = pl.multiple_of(start, 128)
    k = key[pl.ds(start, size), :]
    same = kseg[pl.ds(start, size), 0:1] == qseg[...]
    ones = jnp.ones((8, size), BF)
    scores = []
    for h in range(4):
        s = contract_last(k, qm[h])
        scores.append(jnp.where(same, s, NEG))
    for h in range(4):
        old = m_sc[h]
        new = jnp.maximum(old, jnp.max(scores[h], axis=0, keepdims=True))
        p = jnp.exp(scores[h] - new).astype(BF)
        fade = jnp.exp(old - new)
        m_sc[h] = new
        v = jnp.concatenate(
            [vt[HEAD_DIM * h : HEAD_DIM * h + HEAD_DIM, pl.ds(start, size)], ones], axis=0
        )
        acc[h] = acc[h] * fade + jnp.dot(v, p, preferred_element_type=F32)


def attend_span(table, at, i, *refs):
    start = table[at, i]
    whole = table[at + 1, i] // 2

    @pl.loop(0, whole)
    def _(c):
        attend_chunk(start + c * KC, KC, *refs)

    @pl.when(table[at + 1, i] % 2 == 1)
    def _():
        attend_chunk(start + whole * KC, KC // 2, *refs)


def spread_heads(q, qm):
    lane = lax.broadcasted_iota(jnp.int32, (QB, 256), 1)
    for h in range(4):
        qm[h] = jnp.where((lane % 128) // 32 == h, q[...].astype(F32), 0.0).astype(BF)


def own_kernel(table, q, qseg, key, vt, kseg, acc_out, m_out, qm, m_sc, acc):
    i = pl.program_id(0)
    spread_heads(q, qm)
    m_sc[...] = jnp.full_like(m_sc, NEG)
    acc[...] = jnp.zeros_like(acc)
    attend_span(table, 0, i, qm, key, vt, kseg, qseg, m_sc, acc)
    acc_out[...] = acc[...]
    m_out[...] = m_sc[...]


def halo_kernel(
    base, table, q, qseg, lkey, lvt, lseg, rkey, rvt, rseg, acc_in, m_in, last, out, picked, qm, m_sc, acc
):
    i = pl.program_id(0) + base
    spread_heads(q, qm)
    m_sc[...] = m_in[...]
    acc[...] = acc_in[...]
    attend_span(table, 2, i, qm, lkey, lvt, lseg, qseg, m_sc, acc)
    attend_span(table, 4, i, qm, rkey, rvt, rseg, qseg, m_sc, acc)
    heads = [acc[h, :HEAD_DIM] / acc[h, HEAD_DIM : HEAD_DIM + 1] for h in range(4)]
    mixed = jnp.transpose(jnp.concatenate(heads, axis=0)).astype(BF)
    out[...] = mixed
    slot = lax.broadcasted_iota(jnp.int32, (last.shape[0], QB), 1) + i * QB
    mine = jnp.where(last[...] == slot, 1.0, 0.0).astype(BF)

    @pl.when(pl.program_id(0) == 0)
    def _():
        picked[...] = jnp.zeros_like(picked)

    picked[...] += jnp.dot(mine, mixed, preferred_element_type=F32)


def attn_scratch():
    return [
        pltpu.VMEM((4, QB, 256), BF),
        pltpu.VMEM((4, 1, QB), F32),
        pltpu.VMEM((4, VR, QB), F32),
    ]


def attend_own(table, q, qseg, key, vt, kseg):
    rows = q.shape[0]
    return pl.pallas_call(
        own_kernel,
        grid_spec=pltpu.PrefetchScalarGridSpec(
            num_scalar_prefetch=1,
            grid=(rows // QB,),
            in_specs=[
                pl.BlockSpec((QB, 256), lambda i, *_: (i, 0)),
                pl.BlockSpec((1, QB), lambda i, *_: (0, i)),
                vmem(rows, 256),
                vmem(256, rows),
                vmem(rows, 1),
            ],
            out_specs=[
                pl.BlockSpec((4, VR, QB), lambda i, *_: (0, 0, i)),
                pl.BlockSpec((4, 1, QB), lambda i, *_: (0, 0, i)),
            ],
            scratch_shapes=attn_scratch(),
        ),
        out_shape=(
            jax.ShapeDtypeStruct((4, VR, rows), F32),
            jax.ShapeDtypeStruct((4, 1, rows), F32),
        ),
        compiler_params=params(32),
        cost_estimate=cost(20 << 30, 8 << 20, 12 << 20),
        name="attend_own",
    )(table, q, qseg, key, vt, kseg)


def attend_halo(part, parts, table, q, qseg, lkey, lvt, lseg, rkey, rvt, rseg, acc, m, last):
    rows = q.shape[0]
    steps = rows // QB // parts
    base = part * steps
    return pl.pallas_call(
        functools.partial(halo_kernel, base),
        grid_spec=pltpu.PrefetchScalarGridSpec(
            num_scalar_prefetch=1,
            grid=(steps,),
            in_specs=[
                pl.BlockSpec((QB, 256), lambda i, *_: (i + base, 0)),
                pl.BlockSpec((1, QB), lambda i, *_: (0, i + base)),
                vmem(rows, 256),
                vmem(256, rows),
                vmem(rows, 1),
                vmem(rows, 256),
                vmem(256, rows),
                vmem(rows, 1),
                pl.BlockSpec((4, VR, QB), lambda i, *_: (0, 0, i + base)),
                pl.BlockSpec((4, 1, QB), lambda i, *_: (0, 0, i + base)),
                vmem(*last.shape),
            ],
            out_specs=[pl.BlockSpec((QB, 256), lambda i, *_: (i, 0)), vmem(last.shape[0], 256)],
            scratch_shapes=attn_scratch(),
        ),
        out_shape=(
            jax.ShapeDtypeStruct((rows // parts, 256), BF),
            jax.ShapeDtypeStruct((last.shape[0], 256), F32),
        ),
        compiler_params=params(40),
        cost_estimate=cost(8 << 30, 8 << 20, 6 << 20),
        name="attend_halo",
    )(table, q, qseg, lkey, lvt, lseg, rkey, rvt, rseg, acc, m, last)


def contract_last(a, b):
    return lax.dot_general(a, b, (((1,), (1,)), ((), ())), preferred_element_type=F32)


def mlp_kernel(table, m0, m1, m2, m3, h, gain, weights, keep, send, w, sem):
    count = weights.shape[0]

    @pl.when(pl.program_id(0) == 0)
    def _():
        @pl.loop(0, count)
        def _(k):
            pltpu.make_async_copy(weights.at[table[4 + k]], w.at[k], sem).start()

        pltpu.make_async_copy(weights, w, sem).wait()

    def rows(at, size, lo, width):
        return w[pl.ds(at, size), :, pl.ds(lo, width)].reshape(8 * size, width)

    n = h.shape[0]
    wide = h[...].astype(F32)
    total = None
    for j, m in enumerate((m0, m1, m2, m3)):
        lo = pl.multiple_of(3 * FFP + 256 * table[j], 128)
        piece = contract_last(m[...], rows(0, count, lo, 256))
        total = piece if total is None else total + piece
    first = (wide + total).astype(BF)
    wide = first.astype(F32)
    normed = layer_norm(wide, gain[...]).astype(BF)
    a = jnp.dot(normed, rows(0, count, 0, FFP), preferred_element_type=F32)
    b = jnp.dot(normed, rows(0, count, FFP, FFP), preferred_element_type=F32)
    inner = (0.5 * a * (1.0 + lax.erf(a * (0.5**0.5))) * b).astype(BF)
    mine = jnp.zeros((n, 256), F32)
    for t in range(4):
        mine = jnp.where(table[0] == t, wide[:, 256 * t : 256 * t + 256], mine)

    def down(j):
        return contract_last(inner, rows(table[j] * (count // 4), count // 4, 2 * FFP, FFP))

    keep[:, :256] = down(0) + mine
    keep[:, 256:] = down(1)
    send[:, :256] = down(2).astype(BF)
    send[:, 256:] = down(3).astype(BF)


def mlp(table, mixed, h, base, gain, weights, n):
    rows = mixed[0].shape[0]
    count = weights.shape[0]

    def block(width):
        return pl.BlockSpec((n, width), lambda i, *_: (i, 0))

    return pl.pallas_call(
        mlp_kernel,
        grid_spec=pltpu.PrefetchScalarGridSpec(
            num_scalar_prefetch=1,
            grid=(rows // n,),
            in_specs=[block(256)] * 4
            + [pl.BlockSpec((n, 1024), lambda i, *_: (i + base, 0))]
            + [vmem(1, 1024), pl.BlockSpec(memory_space=pl.ANY)],
            out_specs=[block(512), block(512)],
            scratch_shapes=[pltpu.VMEM((count, 8, REST), BF), pltpu.SemaphoreType.DMA(())],
        ),
        out_shape=(
            jax.ShapeDtypeStruct((rows, 512), F32),
            jax.ShapeDtypeStruct((rows, 512), BF),
        ),
        compiler_params=params(40),
        cost_estimate=cost(rows * 1024 * (1024 + 3 * FFP) * 2, 12 << 20, rows * FFP),
        name="mlp",
    )(table, *mixed, h, gain.reshape(1, 1024), weights)


def gather_tp(x):
    far = swap(x, 2)
    return x, far, swap(x, 1), swap(far, 1)


def reduce_tp(keep, send):
    got = swap(send, 1).astype(F32)
    other = swap((keep[:, 256:] + got[:, 256:]).astype(BF), 2).astype(F32)
    return (keep[:, :256] + got[:, :256] + other).astype(BF)


def swap(x, bit):
    return lax.ppermute(x, "tp", [(i, i ^ bit) for i in range(4)])


def shift(x, by):
    count = lax.axis_size("req")
    return lax.ppermute(x, "req", [(i, i + by) for i in range(count) if 0 <= i + by < count])


def exchange(x, axes):
    return lax.all_to_all(x, axes, split_axis=0, concat_axis=0, tiled=True)


def body(
    hidden_in,
    lengths,
    tenant,
    shard_map,
    wq,
    wk,
    wv,
    wo,
    wi_in,
    wi_gate,
    wo2,
    head,
    attn_gain,
    mlp_gain,
    final_gain,
):
    req_count = lax.axis_size("req")
    tp_count = lax.axis_size("tp")
    count = req_count * tp_count
    req_index = lax.axis_index("req")
    tp_index = lax.axis_index("tp")
    slots, width = hidden_in.shape
    requests = lengths.shape[0]

    qkv_block, rest_block = prep(req_count, wq, wk, wv, wo, wi_in, wi_gate, wo2)
    place = jnp.arange(count, dtype=jnp.int32)
    source = jnp.sum(
        jnp.where(shard_map[None, :] == place[:, None], place[None, :], 0), axis=1
    )
    qkv_all = exchange(qkv_block.reshape(count, 8, 768), BOTH)
    qkv_w = qkv_all[source].reshape(width, 768)
    rest_rows = exchange(rest_block, "tp")
    rest = lax.all_gather(rest_rows.reshape(4 * 8, REST), "req", axis=0, tiled=True)
    rest = rest.reshape(count, 8, REST)

    ends = jnp.cumsum(lengths)
    base = req_index * slots
    index = base - slots + jnp.arange(3 * slots, dtype=jnp.int32)
    segment = jnp.sum((ends[None, :] <= index[:, None]).astype(jnp.int32), axis=1)
    segment = jnp.where((index >= 0) & (index < slots * req_count), segment, -1)
    own = base + jnp.arange(slots, dtype=jnp.int32)
    start_of = jnp.max(jnp.where(ends[None, :] <= own[:, None], ends[None, :], 0), axis=1)
    position = (own - start_of).astype(F32)
    half = HEAD_DIM // 2
    lane = jnp.arange(128, dtype=jnp.int32) % half
    freq = THETA ** (-(2.0 * lane.astype(F32)) / HEAD_DIM)
    angle = position[:, None] * freq[None, :]
    cos = jnp.cos(angle)
    sin = jnp.sin(angle)
    begin = base + jnp.arange(slots // QB, dtype=jnp.int32) * QB
    close = begin + QB - 1
    low = jnp.max(jnp.where(ends[None, :] <= begin[:, None], ends[None, :], 0), axis=1) - base
    high = jnp.min(jnp.where(ends[None, :] > close[:, None], ends[None, :], 1 << 30), axis=1) - base

    def span(lo, hi):
        lo = jnp.maximum(lo, 0) // 128 * 128
        n = jnp.maximum((hi - lo + KC // 2 - 1) // (KC // 2), 0)
        return jnp.minimum(lo, slots - n * (KC // 2)), n

    own_lo, own_n = span(low, jnp.minimum(high, slots))
    left_lo, left_n = span(jnp.minimum(low, 0) + slots, jnp.full_like(low, slots))
    right_lo, right_n = span(jnp.zeros_like(high), high - slots)
    table = jnp.stack([own_lo, own_n, left_lo, left_n, right_lo, right_n])
    segs = segment.reshape(3, slots, 1)
    qseg = segment[slots : 2 * slots].reshape(1, slots)

    normed = norm(hidden_in, attn_gain)
    query, key, vt, cache = qkv_project(normed, qkv_w, cos, sin)
    halo = (shift(key, 1), shift(vt, 1), segs[0], shift(key, -1), shift(vt, -1), segs[2])
    acc, m = attend_own(table, query, qseg, key, vt, segs[1])
    last_slot = ends - 1 - base
    holds = (last_slot >= 0) & (last_slot < slots)
    parts = 2
    halves = [
        attend_halo(part, parts, table, query, qseg, *halo, acc, m, last_slot.reshape(requests, 1))
        for part in range(parts)
    ]

    order = jnp.concatenate([tp_index ^ jnp.array([0, 2, 1, 3], jnp.int32), source])
    hidden_out = jnp.concatenate(
        [
            reduce_tp(
                *mlp(
                    order,
                    gather_tp(half[0]),
                    hidden_in,
                    part * (slots // parts // 256),
                    mlp_gain,
                    rest,
                    256,
                )
            )
            for part, half in enumerate(halves)
        ],
        axis=0,
    )

    each = requests // req_count
    rows = 16
    quarter = lax.dynamic_slice_in_dim(hidden_in, tp_index * 256, 256, 1)
    picked_in = jnp.where(holds[:, None], quarter[jnp.clip(last_slot, 0, slots - 1)], 0)
    picked_mixed = sum(half[1] for half in halves).astype(BF)
    picked = jnp.concatenate([picked_mixed, picked_in], axis=1)
    taken = exchange(picked.reshape(req_count, each, 512), "req").astype(F32).sum(axis=0).astype(BF)
    taken = gather_tp(jnp.pad(taken, ((0, rows - each), (0, 0))))
    pieces = jnp.stack([piece[:, 256:] for piece in taken])
    place_of = jnp.array([0, 2, 1, 3], jnp.int32)[jnp.arange(4, dtype=jnp.int32) ^ tp_index]
    whole_in = pieces[place_of].transpose(1, 0, 2).reshape(rows, width)
    last_mine = reduce_tp(
        *mlp(order, [piece[:, :256] for piece in taken], whole_in, 0, mlp_gain, rest, rows)
    )[:each]
    spread = exchange(jnp.broadcast_to(last_mine[None], (count, each, 256)), BOTH)
    last = (
        spread.reshape(req_count, tp_count, each, 256)
        .transpose(0, 2, 1, 3)
        .reshape(requests, width)
        .astype(F32)
    )
    last_rms = jnp.sqrt(jnp.mean(last * last, axis=-1))
    choose = (tenant[:, None] == jnp.arange(final_gain.shape[0], dtype=jnp.int32)[None, :]).astype(
        F32
    )
    gain_rows = jnp.dot(
        choose, final_gain, precision=lax.Precision.HIGHEST, preferred_element_type=F32
    )
    final = layer_norm(last, gain_rows).astype(BF)
    logits = contract_last(final, head.astype(BF))
    top = jnp.max(logits, axis=-1)
    tops = exchange(jnp.broadcast_to(top[None], (count, requests)), BOTH)
    top_logit = jnp.max(tops, axis=0)
    return (hidden_out, cache, last_rms, top_logit)


def solution(mesh):
    rows = P(BOTH, None)
    placed = (P("req", None), P(), P(), P()) + (rows,) * 8 + (P(), P(), P())
    return jax.shard_map(
        body,
        mesh=mesh,
        in_specs=placed,
        out_specs=(P("req", "tp"), P(None, "req", "tp"), P(), P()),
        check_vma=False,
    )
```

time: 339 us -> 304 us (0.90)
  Pallas kernels: 118 us -> 88 us
  waiting for transfers between devices: 71.7 us -> 42.9 us
  starting transfers between devices: 44.6 us -> 68.6 us
  blocking collectives: 54.6 us -> 32 us
  local copies, waits for them, and re-layouts: 19.4 us -> 39 us
    all_to_all x2 -> x3, waiting for transfers between devices: 49.8 us -> 10.8 us  [exchange(): return lax.all_to_all(x, axes, split_axis=0, concat_axis=0, tiled=True)]
    unnamed x31 -> x79, local copies, waits for them, and re-layouts: 2.57 us -> 27.8 us
    all_to_all x4 -> x2, blocking collectives: 54.6 us -> 32 us  [exchange(): return lax.all_to_all(x, axes, split_axis=0, concat_axis=0, tiled=True)]
    pallas_call x2 -> x3, Pallas kernels: 29.7 us -> 7.52 us  [the longest x2 6.01 us: attend_halo(): pl.pallas_call(functools.partial(halo_kernel, base), grid_spec=pltpu.Pref...]
    pallas_call x1, Pallas kernels: 46 us -> 33.2 us  [attend_own(): pl.pallas_call(own_kernel, grid_spec=pltpu.PrefetchScalarGridSpec(num_sca...]
    all_to_all x2 -> x3, starting transfers between devices: 36.5 us -> 48.4 us  [exchange(): return lax.all_to_all(x, axes, split_axis=0, concat_axis=0, tiled=True)]
    ppermute x2 -> x4, waiting for transfers between devices: 2.48 us -> 14.1 us  [shift(): lax.ppermute(x, 'req', [(i, i + by) for i in range(count) if 0 <= i + by...]
    pallas_call x2 -> x3, Pallas kernels: 28.3 us -> 39.3 us  [mlp(): pl.pallas_call(mlp_kernel, grid_spec=pltpu.PrefetchScalarGridSpec(num_sca...]
  transfers between devices with their start and end apart: 12 -> 23, of which waited for: 6 -> 7; matrix products, arithmetic and copies ran while one was open for 8% -> 9% of each run, Pallas kernels for 30% -> 29%
where the time goes in v2:
time: 304 us; the launch traced here: 302 us
  Pallas kernels  88 us (29%)
  starting transfers between devices  68.6 us (23%)
  waiting for transfers between devices  42.9 us (14%)
  local copies, waits for them, and re-layouts  39 us (13%)
  blocking collectives  32 us (11%)
  other arithmetic  16.3 us (5%)
  between operations  14.7 us (5%)
    all_to_all x3, starting transfers between devices, exchange(): return lax.all_to_all(x, axes, split_axis=0, concat_axis=0, tiled=True)  48.4 us
    pallas_call x3, Pallas kernels, mlp(): pl.pallas_call(mlp_kernel, grid_spec=pltpu.PrefetchScalarGridSpec(num_sca...  39.3 us
    pallas_call x1, Pallas kernels, attend_own(): pl.pallas_call(own_kernel, grid_spec=pltpu.PrefetchScalarGridSpec(num_sca...  33.2 us
    all_to_all x2, blocking collectives, exchange(): return lax.all_to_all(x, axes, split_axis=0, concat_axis=0, tiled=True)  32 us
    unnamed x79, local copies, waits for them, and re-layouts  27.8 us
    ppermute x15, waiting for transfers between devices, swap(): return lax.ppermute(x, 'tp', [(i, i ^ bit) for i in range(4)])  18 us
    ppermute x4, waiting for transfers between devices, shift(): lax.ppermute(x, 'req', [(i, i + by) for i in range(count) if 0 <= i + by...  14.1 us
    all_to_all x3, waiting for transfers between devices, exchange(): return lax.all_to_all(x, axes, split_axis=0, concat_axis=0, tiled=True)  10.8 us
  transfers between devices with their start and end apart: 23, of which 7 were waited for; matrix products, arithmetic and copies ran while one was open for 9% of the time, Pallas kernels for 29%

profile of v2, /device:TPU:1, one launch (start us, length us, event | category | flops | bytes accessed | tf_op | source)
XLA Modules:
  0.0 302.5 jit_solution(4739108023842688893)
XLA Ops:
  7.3 0.9 copy-done.14
  8.1 0.9 copy-done.15
  9.0 0.9 copy-done.16
  9.9 0.8 copy-done.17
  10.7 0.8 copy-done.18
  11.4 0.8 copy-done.19
  12.2 0.8 copy-done.20
  12.9 1.5 prep.1
  14.5 9.3 %all_to_all.26 = bf16[4,8,3328]{2,1,0:T(8,128)(2,1)} all-to-all(bf16[4,8,3328]{2,1,0:T(8,128)(2,1)S(1)} %get-tuple-element.29), channel_id=1, replica_groups=mesh['req'=32,'tp'=4] {'tp'}, dimensions={0} | all-to-all | bytes 425984 | tf_op jit(solution)/shard_map/all_to_all | solution.py:391
  23.7 11.0 %all-to-all-start = ((bf16[128,8,768]{2,1,0:T(8,128)(2,1)}), bf16[128,8,768]{2,1,0:T(8,128)(2,1)}, u32[]{:S(2)}, u32[]{:S(2)}) async-start(bf16[128,8,768]{2,1,0:T(8,128)(2,1)} %bitcast.8), calls=%async_computation | async-start | bytes 3145728 | tf_op jit(solution)/shard_map/all_to_all | solution.py:391
  36.5 1.3 constant_dynamic-slice_fusion
  37.9 1.4 copy.47.kseg
  39.3 1.4 copy.48.lseg
  40.7 1.3 copy.49.rseg
  42.7 2.2 copy-done.2
  44.9 2.7 norm.1.x
  47.6 2.1 copy-done.5
  50.0 5.4 %multiply_sine_fusion = (f32[2048,128]{1,0:T(8,128)S(1)}, f32[2048,128]{1,0:T(8,128)}) fusion(f32[128]{0:T(128)S(1)} %fusion.19, f32[2048]{0:T(1024)S(1)} %subtract_convert_fusion), kind=kLoop, calls=%fused_computation.5 | loop fusion | flops 262144 | bytes 2105856 | tf_op jit(solution)/shard_map/sin | solution.py:443
  55.3 4.9 %all-to-all-done = bf16[128,8,768]{2,1,0:T(8,128)(2,1)} async-done(((bf16[128,8,768]{2,1,0:T(8,128)(2,1)}), bf16[128,8,768]{2,1,0:T(8,128)(2,1)}, u32[]{:S(2)}, u32[]{:S(2)}) %all-to-all-start) | async-done | bytes 1572896 | tf_op jit(solution)/shard_map/all_to_all | solution.py:391
  60.2 2.1 gather_fusion
  62.3 2.2 copy-done.6
  64.5 1.2 copy-done.10
  65.7 5.3 %qkv.1 = (bf16[2048,256]{1,0:T(8,128)(2,1)S(1)}, bf16[2048,256]{1,0:T(8,128)(2,1)S(1)}, bf16[256,2048]{1,0:T(8,128)(2,1)S(1)}, bf16[2,2048,256]{2,1,0:T(8,128)(2,1)}) custom-call(bf16[2048,1024]{1,0:T(8,128)(2,1)S(1)} %copy-done.6, bf16[1024,768]{1,0:T(8,128)(2,1)S(1)} %bitcast.110, f32[2048,128]{1,0:T(8,128)S(1)} %copy-done.10, ...), custom_call_target="tpu_custom_call" | custom-call | flops 3221225472 | bytes 12582912 | tf_op jit(solution)/shard_map/qkv/pallas_call | solution.py:123
  71.1 2.8 collective-permute-start
  73.9 1.3 collective-permute-start.2
  75.2 4.1 %collective-permute-start.1 = (bf16[256,2048]{1,0:T(8,128)(2,1)S(1)}, bf16[256,2048]{1,0:T(8,128)(2,1)S(1)}, u32[]{:S(2)}, u32[]{:S(2)}) collective-permute-start(bf16[256,2048]{1,0:T(8,128)(2,1)S(1)} %get-tuple-element.25.vt), channel_id=1, source_target_pairs={{0,4},{4,8},{8,12},{12,16},{16,20},{20,24},{24,28},{28,32},{32,36}... | collective-permute-start | bytes 3145736 | tf_op jit(solution)/shard_map/ppermute | solution.py:387
  79.2 1.5 collective-permute-start.3
  80.8 33.2 %attend_own.1 = (f32[4,72,2048]{2,1,0:T(8,128)S(1)}, f32[4,1,2048]{2,1,0:T(1,128)S(1)}) custom-call(s32[6,8]{1,0:T(8,128)S(1)} %stack.24.table, bf16[2048,256]{1,0:T(8,128)(2,1)S(1)} %get-tuple-element.23.q, s32[1,2048]{1,0:T(1,128)S(1)} %bitcast.113, bf16[2048,256]{1,0:T(8,128)(2,1)S(1)} %get-tuple-element.24.key, ...), custom_call_target="tpu_custom_call" | custom-call | flops 21474836480 | bytes 8388608 | tf_op jit(solution)/shard_map/attend_own/pallas_call | solution.py:235
  113.9 10.9 %collective-permute-done.1.lvt = bf16[256,2048]{1,0:T(8,128)(2,1)S(1)} collective-permute-done((bf16[256,2048]{1,0:T(8,128)(2,1)S(1)}, bf16[256,2048]{1,0:T(8,128)(2,1)S(1)}, u32[]{:S(2)}, u32[]{:S(2)}) %collective-permute-start.1) | collective-permute-done | bytes 1048608 | tf_op jit(solution)/shard_map/ppermute | solution.py:387
  124.8 3.2 %collective-permute-done.3.rvt = bf16[256,2048]{1,0:T(8,128)(2,1)S(1)} collective-permute-done((bf16[256,2048]{1,0:T(8,128)(2,1)S(1)}, bf16[256,2048]{1,0:T(8,128)(2,1)S(1)}, u32[]{:S(2)}, u32[]{:S(2)}) %collective-permute-start.3) | collective-permute-done | bytes 1048608 | tf_op jit(solution)/shard_map/ppermute | solution.py:387
  128.0 2.4 attend_halo.2
  130.4 3.6 %attend_halo.3 = (bf16[1024,256]{1,0:T(8,128)(2,1)}, f32[64,256]{1,0:T(8,128)S(1)}) custom-call(s32[6,8]{1,0:T(8,128)S(1)} %stack.24.table, bf16[2048,256]{1,0:T(8,128)(2,1)S(1)} %get-tuple-element.23.q, s32[1,2048]{1,0:T(1,128)S(1)} %bitcast.115, bf16[2048,256]{1,0:T(8,128)(2,1)S(1)} %collective-permute-done.lkey, ...), custom_call_target="tpu_custom_call" | custom-call | flops 8589934592 | bytes 8388608 | tf_op jit(solution)/shard_map/attend_halo/pallas_call | solution.py:267
  134.7 28.1 %all-to-all-start.2 = ((bf16[32,2,512]{2,1,0:T(2,128)(2,1)}), bf16[32,2,512]{2,1,0:T(2,128)(2,1)S(1)}, u32[]{:S(2)}, u32[]{:S(2)}) async-start(bf16[32,2,512]{2,1,0:T(2,128)(2,1)} %reshape.528), calls=%async_computation.2 | async-start | bytes 131072 | tf_op jit(solution)/shard_map/all_to_all | solution.py:391
  163.0 1.3 collective-permute-start.5
  164.3 1.3 collective-permute-start.9
  165.6 5.9 %all-to-all-done.2 = bf16[32,2,512]{2,1,0:T(2,128)(2,1)S(1)} async-done(((bf16[32,2,512]{2,1,0:T(2,128)(2,1)}), bf16[32,2,512]{2,1,0:T(2,128)(2,1)S(1)}, u32[]{:S(2)}, u32[]{:S(2)}) %all-to-all-start.2) | async-done | bytes 65568 | tf_op jit(solution)/shard_map/all_to_all | solution.py:391
  171.8 2.5 collective-permute-start.15
  174.3 16.9 %collective-permute-done.14 = bf16[16,512]{1,0:T(8,128)(2,1)S(1)} collective-permute-done((bf16[16,512]{1,0:T(8,128)(2,1)S(1)}, bf16[16,512]{1,0:T(8,128)(2,1)S(1)}, u32[]{:S(2)}, u32[]{:S(2)}) %collective-permute-start.14) | collective-permute-done | bytes 16416 | tf_op jit(solution)/shard_map/ppermute | solution.py:382
  192.0 0.7 collective-permute-done.16
  193.3 2.9 copy-done.1
  196.3 12.2 %mlp.5 = (f32[16,512]{1,0:T(8,128)S(1)}, bf16[16,512]{1,0:T(8,128)(2,1)S(1)}) custom-call(s32[132]{0:T(256)S(1)} %pad_add_fusion.table, bf16[16,256]{1,0:T(8,128)(2,1)S(1)} %get-tuple-element.63.m0, bf16[16,256]{1,0:T(8,128)(2,1)S(1)} %get-tuple-element.55.m1, bf16[16,256]{1,0:T(8,128)(2,1)S(1)} %get-tuple-element.57.m2, ...), custom_call_target="tpu_custom_call" | custom-call | flops 109051904 | bytes 12582912 | tf_op jit(solution)/shard_map/mlp/pallas_call | solution.py:349
  210.1 0.8 copy-done.27
  210.9 0.8 copy-done.29
  211.7 1.0 copy-done.26
  212.8 1.0 copy-done.28
  213.8 1.0 copy-done.30
  214.8 12.7 %mlp.3 = (f32[1024,512]{1,0:T(8,128)S(1)}, bf16[1024,512]{1,0:T(8,128)(2,1)S(1)}) custom-call(s32[132]{0:T(256)S(1)} %pad_add_fusion.table, bf16[1024,256]{1,0:T(8,128)(2,1)S(1)} %copy-done.24, bf16[1024,256]{1,0:T(8,128)(2,1)S(1)} %copy-done.26, bf16[1024,256]{1,0:T(8,128)(2,1)S(1)} %copy-done.28, bf16[1024,256]{1,0:T(8,128)(2,1)S(1)} %copy-done.30, ...), custom_call_target="tpu_custom_call" | custom-call | flops 6979321856 | bytes 12582912 | tf_op jit(solution)/shard_map/mlp/pallas_call | solution.py:349
  228.2 0.7 broadcast_in_dim.66
  228.9 9.2 %all-to-all-start.3 = ((bf16[128,2,256]{2,1,0:T(2,128)(2,1)}), bf16[128,2,256]{2,1,0:T(2,128)(2,1)S(1)}, u32[]{:S(2)}, u32[]{:S(2)}) async-start(bf16[128,2,256]{2,1,0:T(2,128)(2,1)} %broadcast_in_dim.66), calls=%async_computation.3 | async-start | bytes 262144 | tf_op jit(solution)/shard_map/all_to_all | solution.py:391
  238.2 2.2 copy-done.4
  240.4 14.4 %mlp.4 = (f32[1024,512]{1,0:T(8,128)S(1)}, bf16[1024,512]{1,0:T(8,128)(2,1)}) custom-call(s32[132]{0:T(256)S(1)} %pad_add_fusion.table, bf16[1024,256]{1,0:T(8,128)(2,1)} %get-tuple-element.32.m0, bf16[1024,256]{1,0:T(8,128)(2,1)} %collective-permute-done.9.m1, bf16[1024,256]{1,0:T(8,128)(2,1)} %collective-permute-done.10.m2, ...), custom_call_target="tpu_custom_call" | custom-call | flops 6979321856 | bytes 12582912 | tf_op jit(solution)/shard_map/mlp/pallas_call | solution.py:349
  254.8 1.3 copy-done.7
  256.1 1.0 collective-permute-start.12
  257.4 0.7 copy.57
  259.2 1.5 convert_element_type.90
  260.7 1.4 copy-done.32
  262.3 0.9 collective-permute-start.8
  263.2 1.5 convert_element_type.94
  265.1 0.7 collective-permute-start.13
  266.2 0.8 copy-done.34
  267.5 22.7 %all_to_all.27 = f32[128,1,64]{2,1,0:T(1,128)S(1)} all-to-all(f32[128,1,64]{2,1,0:T(1,128)S(1)} %broadcast_in_dim.100), channel_id=1, replica_groups=mesh['req'=32,'tp'=4] {'req','tp'}, dimensions={0} | all-to-all | bytes 65536 | tf_op jit(solution)/shard_map/all_to_all | solution.py:391
  290.9 1.8 fusion.6
  293.0 1.6 fusion.3
  294.6 1.0 pad_maximum_fusion
  (144 shorter events, 10.8 us)
Async XLA Ops:
  7.2 258.6 %copy-start = (f32[4,1024]{1,0:T(4,128)S(1)}, f32[4,1024]{1,0:T(4,128)}, u32[]{:S(2)}) copy-start(f32[4,1024]{1,0:T(4,128)} %param.31) | copy-start | bytes 49156
  7.2 27.8 %copy-start.31 = (s32[4]{0:T(128)S(1)}, s32[4]{0:T(128)}, u32[]{:S(2)}) copy-start(s32[4]{0:T(128)} %constant.167.clone) | copy-start | bytes 52
  7.2 186.1 %all-gather.2.cloned.1.call-start = ((), (), s32[]{:S(2)}) async-start(), calls=%async_computation.5 | async-start | bytes 7028736 | tf_op jit(solution)/shard_map/all_gather | solution.py:427
  7.2 0.9 copy-start.14
  8.1 0.9 copy-start.15
  9.0 0.9 copy-start.16
  9.9 0.8 copy-start.17
  10.7 0.8 copy-start.18
  11.4 0.8 copy-start.19
  12.2 0.8 copy-start.20
  12.9 21.9 %copy-start.36 = (s32[64]{0:T(128)S(1)}, s32[64]{0:T(128)}, u32[]{:S(2)}) copy-start(s32[64]{0:T(128)} %param.18) | copy-start | bytes 772
  23.7 12.0 %copy-start.38 = (s32[128]{0:T(128)S(1)}, s32[128]{0:T(128)}, u32[]{:S(2)}) copy-start(s32[128]{0:T(128)} %param.20) | copy-start | bytes 1540
  23.7 36.5 %all-to-all-start = ((bf16[128,8,768]{2,1,0:T(8,128)(2,1)}), bf16[128,8,768]{2,1,0:T(8,128)(2,1)}, u32[]{:S(2)}, u32[]{:S(2)}) async-start(bf16[128,8,768]{2,1,0:T(8,128)(2,1)} %bitcast.8), calls=%async_computation | async-start | bytes 3145728 | tf_op jit(solution)/shard_map/all_to_all | solution.py:391
  37.9 4.8 %copy-start.21 = (f32[1024]{0:T(1024)S(1)}, f32[1024]{0:T(1024)}, u32[]{:S(2)}) copy-start(f32[1024]{0:T(1024)} %param.29) | copy-start | bytes 12292
  42.7 2.2 copy-start.2
  47.6 2.1 copy-start.5
  62.3 2.2 copy-start.6
  64.5 1.2 copy-start.10
  65.7 15.0 %copy-start.13 = (s32[2048,1]{1,0:T(8,128)S(1)}, s32[2048,1]{1,0:T(8,128)}, u32[]{:S(2)}) copy-start(s32[2048,1]{1,0:T(8,128)} %copy.47.kseg) | copy-start | bytes 24580
  71.1 42.9 %collective-permute-start = (bf16[2048,256]{1,0:T(8,128)(2,1)S(1)}, bf16[2048,256]{1,0:T(8,128)(2,1)S(1)}, u32[]{:S(2)}, u32[]{:S(2)}) collective-permute-start(bf16[2048,256]{1,0:T(8,128)(2,1)S(1)} %get-tuple-element.24.key), channel_id=1, source_target_pairs={{0,4},{4,8},{8,12},{12,16},{16,20},{20,24},{24,28},{28,32},{32,36}... | collective-permute-start | bytes 3145736 | tf_op jit(solution)/shard_map/ppermute | solution.py:387
  73.9 51.0 %collective-permute-start.2 = (bf16[2048,256]{1,0:T(8,128)(2,1)S(1)}, bf16[2048,256]{1,0:T(8,128)(2,1)S(1)}, u32[]{:S(2)}, u32[]{:S(2)}) collective-permute-start(bf16[2048,256]{1,0:T(8,128)(2,1)S(1)} %get-tuple-element.24.key), channel_id=1, source_target_pairs={{4,0},{8,4},{12,8},{16,12},{20,16},{24,20},{28,24},{32,28},{36,32}... | collective-permute-start | bytes 3145736 | tf_op jit(solution)/shard_map/ppermute | solution.py:387
  75.2 49.7 %collective-permute-start.1 = (bf16[256,2048]{1,0:T(8,128)(2,1)S(1)}, bf16[256,2048]{1,0:T(8,128)(2,1)S(1)}, u32[]{:S(2)}, u32[]{:S(2)}) collective-permute-start(bf16[256,2048]{1,0:T(8,128)(2,1)S(1)} %get-tuple-element.25.vt), channel_id=1, source_target_pairs={{0,4},{4,8},{8,12},{12,16},{16,20},{20,24},{24,28},{28,32},{32,36}... | collective-permute-start | bytes 3145736 | tf_op jit(solution)/shard_map/ppermute | solution.py:387
  79.2 48.8 %collective-permute-start.3 = (bf16[256,2048]{1,0:T(8,128)(2,1)S(1)}, bf16[256,2048]{1,0:T(8,128)(2,1)S(1)}, u32[]{:S(2)}, u32[]{:S(2)}) collective-permute-start(bf16[256,2048]{1,0:T(8,128)(2,1)S(1)} %get-tuple-element.25.vt), channel_id=1, source_target_pairs={{4,0},{8,4},{12,8},{16,12},{20,16},{24,20},{28,24},{32,28},{36,32}... | collective-permute-start | bytes 3145736 | tf_op jit(solution)/shard_map/ppermute | solution.py:387
  80.7 47.3 %copy-start.11 = (s32[2048,1]{1,0:T(8,128)S(1)}, s32[2048,1]{1,0:T(8,128)}, u32[]{:S(2)}) copy-start(s32[2048,1]{1,0:T(8,128)} %copy.48.lseg) | copy-start | bytes 24580
  80.7 47.3 %copy-start.12 = (s32[2048,1]{1,0:T(8,128)S(1)}, s32[2048,1]{1,0:T(8,128)}, u32[]{:S(2)}) copy-start(s32[2048,1]{1,0:T(8,128)} %copy.49.rseg) | copy-start | bytes 24580
  130.4 32.6 %copy-start.23 = (bf16[1024,256]{1,0:T(8,128)(2,1)}, bf16[1024,256]{1,0:T(8,128)(2,1)S(1)}, u32[]{:S(2)}) copy-start(bf16[1024,256]{1,0:T(8,128)(2,1)S(1)} %get-tuple-element.28.m0) | copy-start | bytes 1572868
  130.4 62.9 %copy-start.22 = (f32[1024]{0:T(1024)S(1)}, f32[1024]{0:T(1024)}, u32[]{:S(2)}) copy-start(f32[1024]{0:T(1024)} %param.30) | copy-start | bytes 12292
  134.7 36.8 %all-to-all-start.2 = ((bf16[32,2,512]{2,1,0:T(2,128)(2,1)}), bf16[32,2,512]{2,1,0:T(2,128)(2,1)S(1)}, u32[]{:S(2)}, u32[]{:S(2)}) async-start(bf16[32,2,512]{2,1,0:T(2,128)(2,1)} %reshape.528), calls=%async_computation.2 | async-start | bytes 131072 | tf_op jit(solution)/shard_map/all_to_all | solution.py:391
  162.9 28.9 %collective-permute-start.4 = (bf16[1024,256]{1,0:T(8,128)(2,1)S(1)}, bf16[1024,256]{1,0:T(8,128)(2,1)S(1)}, u32[]{:S(2)}, u32[]{:S(2)}) collective-permute-start(bf16[1024,256]{1,0:T(8,128)(2,1)S(1)} %get-tuple-element.28.m0), channel_id=1, source_target_pairs={{0,2},{1,3},{2,0},{3,1},{4,6},{5,7},{6,4},{7,5},{8,10},{9,11},{10,... | collective-permute-start | bytes 1572872 | tf_op jit(solution)/shard_map/ppermute | solution.py:382
  163.0 47.1 %collective-permute-start.5 = (bf16[1024,256]{1,0:T(8,128)(2,1)S(1)}, bf16[1024,256]{1,0:T(8,128)(2,1)S(1)}, u32[]{:S(2)}, u32[]{:S(2)}) collective-permute-start(bf16[1024,256]{1,0:T(8,128)(2,1)S(1)} %get-tuple-element.28.m0), channel_id=1, source_target_pairs={{0,1},{1,0},{2,3},{3,2},{4,5},{5,4},{6,7},{7,6},{8,9},{9,8},{10,11... | collective-permute-start | bytes 1572872 | tf_op jit(solution)/shard_map/ppermute | solution.py:382
  164.3 44.7 %collective-permute-start.9 = (bf16[1024,256]{1,0:T(8,128)(2,1)}, bf16[1024,256]{1,0:T(8,128)(2,1)}, u32[]{:S(2)}, u32[]{:S(2)}) collective-permute-start(bf16[1024,256]{1,0:T(8,128)(2,1)} %get-tuple-element.32.m0), channel_id=1, source_target_pairs={{0,2},{1,3},{2,0},{3,1},{4,6},{5,7},{6,4},{7,5},{8,10},{9,11},{10,... | collective-permute-start | bytes 1572872 | tf_op jit(solution)/shard_map/ppermute | solution.py:382
  171.7 19.5 %collective-permute-start.14 = (bf16[16,512]{1,0:T(8,128)(2,1)S(1)}, bf16[16,512]{1,0:T(8,128)(2,1)S(1)}, u32[]{:S(2)}, u32[]{:S(2)}) collective-permute-start(bf16[16,512]{1,0:T(8,128)(2,1)S(1)} %pad.4), channel_id=1, source_target_pairs={{0,2},{1,3},{2,0},{3,1},{4,6},{5,7},{6,4},{7,5},{8,10},{9,11},{10,... | collective-permute-start | bytes 49160 | tf_op jit(solution)/shard_map/ppermute | solution.py:382
  171.8 20.1 %collective-permute-start.15 = (bf16[16,512]{1,0:T(8,128)(2,1)S(1)}, bf16[16,512]{1,0:T(8,128)(2,1)S(1)}, u32[]{:S(2)}, u32[]{:S(2)}) collective-permute-start(bf16[16,512]{1,0:T(8,128)(2,1)S(1)} %pad.4), channel_id=1, source_target_pairs={{0,1},{1,0},{2,3},{3,2},{4,5},{5,4},{6,7},{7,6},{8,9},{9,8},{10,11... | collective-permute-start | bytes 49160 | tf_op jit(solution)/shard_map/ppermute | solution.py:382
  191.2 1.5 collective-permute-start.16
  191.9 16.6 %copy-start.25 = (bf16[1024,256]{1,0:T(8,128)(2,1)}, bf16[1024,256]{1,0:T(8,128)(2,1)S(1)}, u32[]{:S(2)}) copy-start(bf16[1024,256]{1,0:T(8,128)(2,1)S(1)} %collective-permute-done.4.m1) | copy-start | bytes 1572868
  191.9 19.0 %collective-permute-start.6 = (bf16[1024,256]{1,0:T(8,128)(2,1)S(1)}, bf16[1024,256]{1,0:T(8,128)(2,1)S(1)}, u32[]{:S(2)}, u32[]{:S(2)}) collective-permute-start(bf16[1024,256]{1,0:T(8,128)(2,1)S(1)} %collective-permute-done.4.m1), channel_id=1, source_target_pairs={{0,1},{1,0},{2,3},{3,2},{4,5},{5,4},{6,7},{7,6},{8,9},{9,8},{10,11... | collective-permute-start | bytes 1572872 | tf_op jit(solution)/shard_map/ppermute | solution.py:382
  193.3 2.9 copy-start.1
  196.3 15.5 %copy-start.3 = (bf16[2048,1024]{1,0:T(8,128)(2,1)S(1)}, bf16[2048,1024]{1,0:T(8,128)(2,1)}, u32[]{:S(2)}) copy-start(bf16[2048,1024]{1,0:T(8,128)(2,1)} %h.5) | copy-start | bytes 12582916
  196.3 15.5 %copy-start.24 = (bf16[1024,256]{1,0:T(8,128)(2,1)S(1)}, bf16[1024,256]{1,0:T(8,128)(2,1)}, u32[]{:S(2)}) copy-start(bf16[1024,256]{1,0:T(8,128)(2,1)} %copy-done.23) | copy-start | bytes 1572868
  208.5 1.3 collective-permute-start.17
  208.9 29.3 %collective-permute-start.10 = (bf16[1024,256]{1,0:T(8,128)(2,1)}, bf16[1024,256]{1,0:T(8,128)(2,1)}, u32[]{:S(2)}, u32[]{:S(2)}) collective-permute-start(bf16[1024,256]{1,0:T(8,128)(2,1)} %get-tuple-element.32.m0), channel_id=1, source_target_pairs={{0,1},{1,0},{2,3},{3,2},{4,5},{5,4},{6,7},{7,6},{8,9},{9,8},{10,11... | collective-permute-start | bytes 1572872 | tf_op jit(solution)/shard_map/ppermute | solution.py:382
  209.1 29.1 %collective-permute-start.11 = (bf16[1024,256]{1,0:T(8,128)(2,1)}, bf16[1024,256]{1,0:T(8,128)(2,1)}, u32[]{:S(2)}, u32[]{:S(2)}) collective-permute-start(bf16[1024,256]{1,0:T(8,128)(2,1)} %collective-permute-done.9.m1), channel_id=1, source_target_pairs={{0,1},{1,0},{2,3},{3,2},{4,5},{5,4},{6,7},{7,6},{8,9},{9,8},{10,11... | collective-permute-start | bytes 1572872 | tf_op jit(solution)/shard_map/ppermute | solution.py:382
  209.7 18.4 %collective-permute-start.18 = (bf16[16,256]{1,0:T(8,128)(2,1)S(1)}, bf16[16,256]{1,0:T(8,128)(2,1)S(1)}, u32[]{:S(2)}, u32[]{:S(2)}) collective-permute-start(bf16[16,256]{1,0:T(8,128)(2,1)S(1)} %get-tuple-element.48), channel_id=1, source_target_pairs={{0,2},{1,3},{2,0},{3,1},{4,6},{5,7},{6,4},{7,5},{8,10},{9,11},{10,... | collective-permute-start | bytes 24584 | tf_op jit(solution)/shard_map/ppermute | solution.py:382
  210.1 0.8 copy-start.27
  210.9 0.8 copy-start.29
  211.7 1.0 copy-start.26
  212.8 1.0 copy-start.28
  213.8 1.0 copy-start.30
  227.5 31.6 %collective-permute-start.7 = (bf16[1024,512]{1,0:T(8,128)(2,1)S(1)}, bf16[1024,512]{1,0:T(8,128)(2,1)}, u32[]{:S(2)}, u32[]{:S(2)}) collective-permute-start(bf16[1024,512]{1,0:T(8,128)(2,1)S(1)} %get-tuple-element.31), channel_id=1, source_target_pairs={{0,1},{1,0},{2,3},{3,2},{4,5},{5,4},{6,7},{7,6},{8,9},{9,8},{10,11... | collective-permute-start | bytes 3145736 | tf_op jit(solution)/shard_map/ppermute | solution.py:382
  228.9 28.3 %all-to-all-start.3 = ((bf16[128,2,256]{2,1,0:T(2,128)(2,1)}), bf16[128,2,256]{2,1,0:T(2,128)(2,1)S(1)}, u32[]{:S(2)}, u32[]{:S(2)}) async-start(bf16[128,2,256]{2,1,0:T(2,128)(2,1)} %broadcast_in_dim.66), calls=%async_computation.3 | async-start | bytes 262144 | tf_op jit(solution)/shard_map/all_to_all | solution.py:391
  238.2 2.2 copy-start.4
  254.8 1.3 copy-start.7
  256.1 7.1 %collective-permute-start.12 = (bf16[1024,512]{1,0:T(8,128)(2,1)}, bf16[1024,512]{1,0:T(8,128)(2,1)}, u32[]{:S(2)}, u32[]{:S(2)}) collective-permute-start(bf16[1024,512]{1,0:T(8,128)(2,1)} %get-tuple-element.34), channel_id=1, source_target_pairs={{0,1},{1,0},{2,3},{3,2},{4,5},{5,4},{6,7},{7,6},{8,9},{9,8},{10,11... | collective-permute-start | bytes 3145736 | tf_op jit(solution)/shard_map/ppermute | solution.py:382
  260.7 1.4 copy-start.32
  262.3 2.5 copy-start.8
  262.3 28.6 %collective-permute-start.8 = (bf16[1024,256]{1,0:T(8,128)(2,1)S(1)}, bf16[1024,256]{1,0:T(8,128)(2,1)}, u32[]{:S(2)}, u32[]{:S(2)}) collective-permute-start(bf16[1024,256]{1,0:T(8,128)(2,1)S(1)} %fusion.4), channel_id=1, source_target_pairs={{0,2},{1,3},{2,0},{3,1},{4,6},{5,7},{6,4},{7,5},{8,10},{9,11},{10,... | collective-permute-start | bytes 1572872 | tf_op jit(solution)/shard_map/ppermute | solution.py:382
  264.7 2.7 copy-start.33
  264.7 1.1 copy-start.35
  264.7 1.1 copy-start.37
  264.8 2.2 copy-start.34
  265.1 27.7 %collective-permute-start.13 = (bf16[1024,256]{1,0:T(8,128)(2,1)S(1)}, bf16[1024,256]{1,0:T(8,128)(2,1)}, u32[]{:S(2)}, u32[]{:S(2)}) collective-permute-start(bf16[1024,256]{1,0:T(8,128)(2,1)S(1)} %fusion.1), channel_id=1, source_target_pairs={{0,2},{1,3},{2,0},{3,1},{4,6},{5,7},{6,4},{7,5},{8,10},{9,11},{10,... | collective-permute-start | bytes 1572872 | tf_op jit(solution)/shard_map/ppermute | solution.py:382
  290.9 2.1 copy-start.9
Sparse Core Ops, SparseCore 0:
  23.9 158.8 all-gather.1

commit v3 on v2

v3 whole, which is shorter than its diff:
```python
import functools

import jax
import jax.numpy as jnp
from jax import lax
from jax.experimental import pallas as pl
from jax.experimental.pallas import tpu as pltpu
from jax.sharding import PartitionSpec as P

HEADS = 16
HEAD_DIM = 64
THETA = 160000.0
EPS = 1e-05
BF = jnp.bfloat16
F32 = jnp.float32
BOTH = ("req", "tp")
NEG = -1e30
FFP = 768
REST = 3 * FFP + 1024
QB = 256
KB = 256


def vmem(*shape):
    return pl.BlockSpec(shape, lambda *_: (0,) * len(shape))


def params():
    return pltpu.CompilerParams(vmem_limit_bytes=60 * 1024 * 1024)


def cost(flops, moved, transcendentals=0):
    return pl.CostEstimate(flops=flops, bytes_accessed=moved, transcendentals=transcendentals)


def prep_kernel(order, wq, wk, wv, wo, wi, wg, w2, qkv, rest):
    row = lax.broadcasted_iota(jnp.int32, (256, 256), 0)
    col = lax.broadcasted_iota(jnp.int32, (256, 256), 1)
    source = (col % 128) // 32 * 64 + col // 128 * 32 + col % 32
    turn = jnp.where(row == source, 1.0, 0.0).astype(BF)
    trow = lax.broadcasted_iota(jnp.int32, (64, 128), 0)
    tcol = lax.broadcasted_iota(jnp.int32, (64, 128), 1)
    for t in range(4):
        at = slice(256 * t, 256 * t + 256)
        q, k = (
            jnp.dot(w[:, at].astype(BF), turn, preferred_element_type=F32).astype(BF)
            for w in (wq, wk)
        )
        mine = jnp.concatenate([q, k, wv[:, at].astype(BF)], axis=1)
        for r in range(qkv.shape[0]):
            qkv[r, t] = mine
        pick = jnp.where((trow == tcol + 16 * t) & (tcol < 16), 1.0, 0.0).astype(BF)
        to = order[t]
        for n, w in enumerate((wi, wg, w2)):
            rest[to, :, FFP * n : FFP * n + 640] = w[:, 640 * t : 640 * t + 640].astype(BF)
            rest[to, :, FFP * n + 640 : FFP * n + 768] = jnp.dot(
                w[:, 2560:2624].astype(BF), pick, preferred_element_type=F32
            ).astype(BF)
        rest[to, :, 3 * FFP :] = wo[...].astype(BF)


def prep(req_count, order, *weights):
    return pl.pallas_call(
        prep_kernel,
        in_specs=[pl.BlockSpec(memory_space=pltpu.SMEM)] + [vmem(*w.shape) for w in weights],
        out_shape=(
            jax.ShapeDtypeStruct((req_count, 4, 8, 768), BF),
            jax.ShapeDtypeStruct((4, 8, REST), BF),
        ),
        compiler_params=params(),
        name="prep",
    )(order, *weights)


def layer_norm(values, gain):
    center = jnp.mean(values, axis=-1, keepdims=True)
    spread = jnp.mean(values * values, axis=-1, keepdims=True) - center * center
    return (values - center) * lax.rsqrt(spread + EPS) * gain


def norm_kernel(h, gain, out):
    out[...] = layer_norm(h[...].astype(F32), gain[...]).astype(BF)


def norm(h, gain):
    rows = h.shape[0]
    return pl.pallas_call(
        norm_kernel,
        grid=(rows // 512,),
        in_specs=[pl.BlockSpec((512, 1024), lambda i: (i, 0)), vmem(1, 1024)],
        out_specs=pl.BlockSpec((512, 1024), lambda i: (i, 0)),
        out_shape=jax.ShapeDtypeStruct((rows, 1024), BF),
        compiler_params=params(),
        cost_estimate=cost(1 << 24, 1 << 23),
        name="norm",
    )(h, gain.reshape(1, 1024))


def qkv_kernel(x, w, cos, sin, q, low, high, cache):
    row = lax.broadcasted_iota(jnp.int32, (256, 256), 0)
    col = lax.broadcasted_iota(jnp.int32, (256, 256), 1)
    source = (col % 128) // 32 * 64 + col // 128 * 32 + col % 32
    back = jnp.where(source == row, 1.0, 0.0).astype(BF)
    y = jnp.dot(x[...], w[...], preferred_element_type=F32)
    c = cos[...]
    s = sin[...]

    def turned(a, b):
        return jnp.concatenate([a * c - b * s, b * c + a * s], axis=1)

    q[...] = (turned(y[:, :128], y[:, 128:256]).astype(BF).astype(F32) * 0.125).astype(BF)
    k = turned(y[:, 256:384], y[:, 384:512]).astype(BF)
    v = y[:, 512:].astype(BF)
    i = pl.program_id(0)
    half = pl.num_programs(0) // 2
    blocks = x.shape[0] // KB
    for part, ref in enumerate((low, high)):

        @pl.when(i // half == part)
        def _():
            for n in range(blocks):
                at = (i - part * half) * blocks + n
                ref[at, 0] = k[KB * n : KB * n + KB]
                ref[at, 1] = jnp.transpose(v[KB * n : KB * n + KB])

    cache[0] = lax.dot_general(
        k, back, (((1,), (1,)), ((), ())), preferred_element_type=F32
    ).astype(BF)
    cache[1] = v


def qkv_project(x, w, cos, sin):
    rows = x.shape[0]
    n = 512
    pairs = (rows // KB // 2, 2, KB, 256)
    return pl.pallas_call(
        qkv_kernel,
        grid=(rows // n,),
        in_specs=[
            pl.BlockSpec((n, 1024), lambda i: (i, 0)),
            vmem(1024, 768),
            pl.BlockSpec((n, 128), lambda i: (i, 0)),
            pl.BlockSpec((n, 128), lambda i: (i, 0)),
        ],
        out_specs=[
            pl.BlockSpec((n, 256), lambda i: (i, 0)),
            vmem(*pairs),
            vmem(*pairs),
            pl.BlockSpec((2, n, 256), lambda i: (0, i, 0)),
        ],
        out_shape=(
            jax.ShapeDtypeStruct((rows, 256), BF),
            jax.ShapeDtypeStruct(pairs, BF),
            jax.ShapeDtypeStruct(pairs, BF),
            jax.ShapeDtypeStruct((2, rows, 256), BF),
        ),
        compiler_params=params(),
        cost_estimate=cost(2 * rows * 1024 * 768, 12 << 20),
        name="qkv",
    )(x, w, cos, sin)


VR = HEAD_DIM + 8


def attend_chunk(at, blocks, qm, kv, kseg, qseg, m_sc, acc):
    size = blocks * KB
    k = kv[pl.ds(at, blocks), 0].reshape(size, 256)
    same = kseg[pl.ds(pl.multiple_of(at * KB, KB), size), 0:1] == qseg[...]
    ones = jnp.ones((8, size), BF)
    scores = []
    for h in range(4):
        s = contract_last(k, qm[h])
        scores.append(jnp.where(same, s, NEG))
    for h in range(4):
        old = m_sc[h]
        new = jnp.maximum(old, jnp.max(scores[h], axis=0, keepdims=True))
        p = jnp.exp(scores[h] - new).astype(BF)
        fade = jnp.exp(old - new)
        m_sc[h] = new
        v = [kv[at + n, 1, HEAD_DIM * h : HEAD_DIM * h + HEAD_DIM, :] for n in range(blocks)]
        v = jnp.concatenate([jnp.concatenate(v, axis=1), ones], axis=0)
        acc[h] = acc[h] * fade + jnp.dot(v, p, preferred_element_type=F32)


def attend_span(short, table, at, i, *refs):
    start = table[at, i]
    if short:

        @pl.loop(0, table[at + 1, i])
        def _(c):
            attend_chunk(start + c, 1, *refs)

        return
    pairs = table[at + 1, i] // 2

    @pl.loop(0, pairs)
    def _(c):
        attend_chunk(start + 2 * c, 2, *refs)

    @pl.when(table[at + 1, i] % 2 == 1)
    def _():
        attend_chunk(start + 2 * pairs, 1, *refs)


def attend_kernel(stage, base, table, q, qseg, kv0, seg0, kv1, seg1, *refs):
    i = pl.program_id(0) + base
    if stage == 0:
        acc_out, m_out, qm, m_sc, acc = refs
    elif stage == 1:
        acc_in, m_in, acc_out, m_out, qm, m_sc, acc = refs
    else:
        acc_in, m_in, out, qm, m_sc, acc = refs
    lane = lax.broadcasted_iota(jnp.int32, (QB, 256), 1)
    for h in range(4):
        qm[h] = jnp.where((lane % 128) // 32 == h, q[...].astype(F32), 0.0).astype(BF)
    if stage == 0:
        m_sc[...] = jnp.full_like(m_sc, NEG)
        acc[...] = jnp.zeros_like(acc)
    else:
        m_sc[...] = m_in[...]
        acc[...] = acc_in[...]
    attend_span(stage == 2, table, 4 * stage, i, qm, kv0, seg0, qseg, m_sc, acc)
    attend_span(stage == 2, table, 4 * stage + 2, i, qm, kv1, seg1, qseg, m_sc, acc)
    if stage < 2:
        acc_out[...] = acc[...]
        m_out[...] = m_sc[...]
    else:
        heads = [acc[h, :HEAD_DIM] / acc[h, HEAD_DIM : HEAD_DIM + 1] for h in range(4)]
        out[...] = jnp.transpose(jnp.concatenate(heads, axis=0)).astype(BF)


def attend(stage, part, parts, table, q, qseg, kv0, seg0, kv1, seg1, *state):
    rows = q.shape[0]
    steps = rows // QB // parts
    base = part * steps
    state_specs = [
        pl.BlockSpec((4, VR, QB), lambda i, *_: (0, 0, i + base)),
        pl.BlockSpec((4, 1, QB), lambda i, *_: (0, 0, i + base)),
    ]
    if stage < 2:
        out_specs = state_specs
        out_shape = (
            jax.ShapeDtypeStruct((4, VR, rows), F32),
            jax.ShapeDtypeStruct((4, 1, rows), F32),
        )
    else:
        out_specs = pl.BlockSpec((QB, 256), lambda i, *_: (i, 0))
        out_shape = jax.ShapeDtypeStruct((rows // parts, 256), BF)
    return pl.pallas_call(
        functools.partial(attend_kernel, stage, base),
        grid_spec=pltpu.PrefetchScalarGridSpec(
            num_scalar_prefetch=1,
            grid=(steps,),
            in_specs=[
                pl.BlockSpec((QB, 256), lambda i, *_: (i + base, 0)),
                pl.BlockSpec((1, QB), lambda i, *_: (0, i + base)),
                vmem(*kv0.shape),
                vmem(*seg0.shape),
                vmem(*kv1.shape),
                vmem(*seg1.shape),
            ]
            + state_specs[: len(state)],
            out_specs=out_specs,
            scratch_shapes=[
                pltpu.VMEM((4, QB, 256), BF),
                pltpu.VMEM((4, 1, QB), F32),
                pltpu.VMEM((4, VR, QB), F32),
            ],
        ),
        out_shape=out_shape,
        compiler_params=params(),
        cost_estimate=cost((20 << 30, 10 << 30, 5 << 30)[stage], 8 << 20, 12 << 20),
        name=("attend_own", "attend_near", "attend_far")[stage],
    )(table, q, qseg, kv0, seg0, kv1, seg1, *state)


def contract_last(a, b):
    return lax.dot_general(a, b, (((1,), (1,)), ((), ())), preferred_element_type=F32)


def mlp_kernel(base, table, m0, m1, m2, m3, h, gain, last, before, weights, keep, send, picked, w, sem):
    count = weights.shape[0]

    @pl.when(pl.program_id(0) == 0)
    def _():
        @pl.loop(0, count)
        def _(k):
            pltpu.make_async_copy(weights.at[table[4 + k]], w.at[k], sem).start()

        pltpu.make_async_copy(weights, w, sem).wait()

    def rows(at, size, lo, width):
        return w[pl.ds(at, size), :, pl.ds(lo, width)].reshape(8 * size, width)

    n = h.shape[0]
    wide = h[...].astype(F32)
    total = None
    for j, m in enumerate((m0, m1, m2, m3)):
        lo = pl.multiple_of(3 * FFP + 256 * table[j], 128)
        piece = contract_last(m[...], rows(0, count, lo, 256))
        total = piece if total is None else total + piece
    first = (wide + total).astype(BF)
    wide = first.astype(F32)
    normed = layer_norm(wide, gain[...]).astype(BF)
    a = jnp.dot(normed, rows(0, count, 0, FFP), preferred_element_type=F32)
    b = jnp.dot(normed, rows(0, count, FFP, FFP), preferred_element_type=F32)
    inner = (0.5 * a * (1.0 + lax.erf(a * (0.5**0.5))) * b).astype(BF)
    mine = jnp.zeros((n, 256), F32)
    for t in range(4):
        mine = jnp.where(table[0] == t, wide[:, 256 * t : 256 * t + 256], mine)

    def down(j):
        return contract_last(inner, rows(table[j] * (count // 4), count // 4, 2 * FFP, FFP))

    kept = jnp.concatenate([down(0) + mine, down(1)], axis=1)
    sent = jnp.concatenate([down(2), down(3)], axis=1).astype(BF)
    keep[...] = kept
    send[...] = sent
    slot = lax.broadcasted_iota(jnp.int32, (last.shape[0], n), 1) + (pl.program_id(0) + base) * n
    ends_here = jnp.where(last[...] == slot, 1.0, 0.0).astype(BF)
    coarse = kept.astype(BF)
    fine = (kept - coarse.astype(F32)).astype(BF)

    def pick(x):
        return jnp.dot(ends_here, x, preferred_element_type=F32)

    @pl.when(pl.program_id(0) == 0)
    def _():
        picked[...] = before[...]

    picked[0] += pick(coarse) + pick(fine)
    picked[1] += pick(sent)


def mlp(table, mixed, h, base, gain, last, before, weights):
    n = 256
    rows = mixed[0].shape[0]
    count = weights.shape[0]

    def block(width):
        return pl.BlockSpec((n, width), lambda i, *_: (i, 0))

    return pl.pallas_call(
        functools.partial(mlp_kernel, base),
        grid_spec=pltpu.PrefetchScalarGridSpec(
            num_scalar_prefetch=1,
            grid=(rows // n,),
            in_specs=[block(256)] * 4
            + [pl.BlockSpec((n, 1024), lambda i, *_: (i + base, 0))]
            + [vmem(1, 1024), vmem(*last.shape), vmem(*before.shape)]
            + [pl.BlockSpec(memory_space=pl.ANY)],
            out_specs=[block(512), block(512), vmem(*before.shape)],
            scratch_shapes=[pltpu.VMEM((count, 8, REST), BF), pltpu.SemaphoreType.DMA(())],
        ),
        out_shape=(
            jax.ShapeDtypeStruct((rows, 512), F32),
            jax.ShapeDtypeStruct((rows, 512), BF),
            jax.ShapeDtypeStruct(before.shape, F32),
        ),
        compiler_params=params(),
        cost_estimate=cost(rows * 1024 * (1024 + 3 * FFP) * 2, 12 << 20, rows * FFP),
        name="mlp",
    )(table, *mixed, h, gain.reshape(1, 1024), last, before, weights)


def gather_tp(x, after=None):
    far = swap(x, 2)
    near = swap(x, 1)
    if after is not None:
        far, _ = lax.optimization_barrier((far, after))
    return x, far, near, swap(far, 1)


def reduce_tp(keep, send):
    got = swap(send, 1).astype(F32)
    other = swap((keep[:, 256:] + got[:, 256:]).astype(BF), 2).astype(F32)
    return (keep[:, :256] + got[:, :256] + other).astype(BF)


def swap(x, bit):
    return lax.ppermute(x, "tp", [(i, i ^ bit) for i in range(4)])


def shift(x, by):
    count = lax.axis_size("req")
    return lax.ppermute(x, "req", [(i, i + by) for i in range(count) if 0 <= i + by < count])


def exchange(x, axes):
    return lax.all_to_all(x, axes, split_axis=0, concat_axis=0, tiled=True)


def body(
    hidden_in,
    lengths,
    tenant,
    shard_map,
    wq,
    wk,
    wv,
    wo,
    wi_in,
    wi_gate,
    wo2,
    head,
    attn_gain,
    mlp_gain,
    final_gain,
):
    req_count = lax.axis_size("req")
    tp_count = lax.axis_size("tp")
    count = req_count * tp_count
    req_index = lax.axis_index("req")
    tp_index = lax.axis_index("tp")
    slots, width = hidden_in.shape
    requests = lengths.shape[0]

    tp_order = jnp.array([0, 2, 1, 3], jnp.int32)
    place_of = tp_order[jnp.arange(4, dtype=jnp.int32) ^ tp_index]
    qkv_block, rest_block = prep(req_count, place_of, wq, wk, wv, wo, wi_in, wi_gate, wo2)
    place = jnp.arange(count, dtype=jnp.int32)
    source = jnp.sum(
        jnp.where(shard_map[None, :] == place[:, None], place[None, :], 0), axis=1
    )
    qkv_all = exchange(qkv_block.reshape(count, 8, 768), BOTH)
    qkv_w = qkv_all[source].reshape(width, 768)
    ends = jnp.cumsum(lengths)
    base = req_index * slots
    index = base - slots + jnp.arange(3 * slots, dtype=jnp.int32)
    segment = jnp.sum((ends[None, :] <= index[:, None]).astype(jnp.int32), axis=1)
    segment = jnp.where((index >= 0) & (index < slots * req_count), segment, -1)
    own = base + jnp.arange(slots, dtype=jnp.int32)
    start_of = jnp.max(jnp.where(ends[None, :] <= own[:, None], ends[None, :], 0), axis=1)
    position = (own - start_of).astype(F32)
    half = HEAD_DIM // 2
    lane = jnp.arange(128, dtype=jnp.int32) % half
    freq = THETA ** (-(2.0 * lane.astype(F32)) / HEAD_DIM)
    angle = position[:, None] * freq[None, :]
    cos = jnp.cos(angle)
    sin = jnp.sin(angle)
    begin = base + jnp.arange(slots // QB, dtype=jnp.int32) * QB
    close = begin + QB - 1
    low = jnp.max(jnp.where(ends[None, :] <= begin[:, None], ends[None, :], 0), axis=1) - base
    high = jnp.min(jnp.where(ends[None, :] > close[:, None], ends[None, :], 1 << 30), axis=1) - base

    half = slots // KB // 2
    own_0 = jnp.maximum(low, 0) // KB
    own_1 = (jnp.minimum(high, slots) + KB - 1) // KB
    left_0 = (jnp.minimum(low, 0) + slots) // KB
    right_1 = (jnp.maximum(high - slots, 0) + KB - 1) // KB
    spans = (
        (own_0, jnp.minimum(own_1, half)),
        (jnp.maximum(own_0 - half, 0), own_1 - half),
        (jnp.maximum(left_0 - half, 0), half),
        (jnp.zeros_like(right_1), jnp.minimum(right_1, half)),
        (left_0, half),
        (jnp.zeros_like(right_1), right_1 - half),
    )
    table = jnp.stack(
        [row for first, end in spans for row in (first, jnp.maximum(end - first, 0))]
    )
    segs = segment.reshape(6, slots // 2, 1)
    qseg = segment[slots : 2 * slots].reshape(1, slots)

    normed = norm(hidden_in, attn_gain)
    rest_block, normed = lax.optimization_barrier((rest_block, normed))
    rest_rows = jnp.concatenate(
        [rest_block[0], swap(rest_block[1], 2), swap(rest_block[2], 1), swap(rest_block[3], 3)], axis=0
    )
    rest = lax.all_gather(rest_rows, "req", axis=0, tiled=True).reshape(count, 8, REST)
    rest_source = source // tp_count * tp_count + place_of[source % tp_count]
    query, kv_low, kv_high, cache = qkv_project(normed, qkv_w, cos, sin)
    left_near = shift(kv_high, 1)
    right_near = shift(kv_low, -1)
    left_far = shift(kv_low, 1)
    right_far = shift(kv_high, -1)
    parts = 2
    state = attend(0, 0, 1, table, query, qseg, kv_low, segs[2], kv_high, segs[3])
    state = attend(1, 0, 1, table, query, qseg, left_near, segs[1], right_near, segs[4], *state)
    mixed = [
        attend(2, part, parts, table, query, qseg, left_far, segs[0], right_far, segs[5], *state)
        for part in range(parts)
    ]

    last_slot = (ends - 1 - base).reshape(requests, 1)
    order = jnp.concatenate([tp_index ^ tp_order, rest_source])
    picked = jnp.zeros((2, requests, 512), F32)
    bulk = []
    for part in range(parts):
        keep, send, picked = mlp(
            order,
            gather_tp(mixed[part], bulk[-1] if bulk else None),
            hidden_in,
            part * (slots // parts // 256),
            mlp_gain,
            last_slot,
            picked,
            rest,
        )
        bulk.append((keep, send))

    each = requests // req_count
    last_mine = reduce_tp(picked[0], picked[1].astype(BF))
    taken = exchange(last_mine.reshape(req_count, each, 256), "req").astype(F32).sum(axis=0)
    spread = exchange(jnp.broadcast_to(taken.astype(BF)[None], (count, each, 256)), BOTH)
    hidden_out = jnp.concatenate([reduce_tp(*pair) for pair in bulk], axis=0)
    last = (
        spread.reshape(req_count, tp_count, each, 256)
        .transpose(0, 2, 1, 3)
        .reshape(requests, width)
        .astype(F32)
    )
    last_rms = jnp.sqrt(jnp.mean(last * last, axis=-1))
    choose = (tenant[:, None] == jnp.arange(final_gain.shape[0], dtype=jnp.int32)[None, :]).astype(
        F32
    )
    gain_rows = jnp.dot(
        choose, final_gain, precision=lax.Precision.HIGHEST, preferred_element_type=F32
    )
    final = layer_norm(last, gain_rows).astype(BF)
    logits = contract_last(final, head.astype(BF))
    top = jnp.max(logits, axis=-1)
    tops = exchange(jnp.broadcast_to(top[None], (count, requests)), BOTH)
    top_logit = jnp.max(tops, axis=0)
    return (hidden_out, cache, last_rms, top_logit)


def solution(mesh):
    rows = P(BOTH, None)
    placed = (P("req", None), P(), P(), P()) + (rows,) * 8 + (P(), P(), P())
    return jax.shard_map(
        body,
        mesh=mesh,
        in_specs=placed,
        out_specs=(P("req", "tp"), P(None, "req", "tp"), P(), P()),
        check_vma=False,
    )
```

time: 304 us -> 309 us (1.016)
  waiting for transfers between devices: 42.9 us -> 75 us
  starting transfers between devices: 68.6 us -> 41 us
  local copies, waits for them, and re-layouts: 39 us -> 20.2 us
  Pallas kernels: 88 us -> 98.9 us
  blocking collectives: 32 us -> 36.7 us
  other arithmetic: 16.3 us -> 20 us
    all_to_all x3 -> x2, starting transfers between devices: 48.4 us -> 17.3 us  [exchange(): return lax.all_to_all(x, axes, split_axis=0, concat_axis=0, tiled=True)]
    unnamed x79 -> x43, local copies, waits for them, and re-layouts: 27.8 us -> 3.35 us
    all_gather x1, waiting for transfers between devices: 0.02 us -> 10.4 us  [body(): lax.all_gather(rest_rows, 'req', axis=0, tiled=True).reshape(count, 8, REST)]
    ppermute x15, waiting for transfers between devices: 18 us -> 26.1 us  [swap(): return lax.ppermute(x, 'tp', [(i, i ^ bit) for i in range(4)])]
    all_to_all x3 -> x2, waiting for transfers between devices: 10.8 us -> 18.9 us  [exchange(): return lax.all_to_all(x, axes, split_axis=0, concat_axis=0, tiled=True)]
    ppermute x4, waiting for transfers between devices: 14.1 us -> 19.6 us  [shift(): lax.ppermute(x, 'req', [(i, i + by) for i in range(count) if 0 <= i + by...]
    all_to_all x2, blocking collectives: 32 us -> 36.7 us  [exchange(): return lax.all_to_all(x, axes, split_axis=0, concat_axis=0, tiled=True)]
    squeeze x1 -> x6, local copies, waits for them, and re-layouts: 1.39 us -> 5.96 us  [the longest x1 1.05 us: body(): segs[5]]
  transfers between devices with their start and end apart: 23 -> 22, of which waited for: 7 -> 9; matrix products, arithmetic and copies ran while one was open for 9% -> 10% of each run, Pallas kernels for 29% -> 24%
where the time goes in v3:
time: 309 us; the launch traced here: 307 us
  Pallas kernels  98.9 us (32%)
  waiting for transfers between devices  75 us (24%)
  starting transfers between devices  41 us (13%)
  blocking collectives  36.7 us (12%)
  local copies, waits for them, and re-layouts  20.2 us (7%)
  other arithmetic  20 us (6%)
  between operations  14.5 us (5%)
    pallas_call x4, Pallas kernels, attend(): pl.pallas_call(functools.partial(attend_kernel, stage, base), grid_spec=p...  48.8 us
    all_to_all x2, blocking collectives, exchange(): return lax.all_to_all(x, axes, split_axis=0, concat_axis=0, tiled=True)  36.7 us
    pallas_call x2, Pallas kernels, mlp(): pl.pallas_call(functools.partial(mlp_kernel, base), grid_spec=pltpu.Prefe...  32.3 us
    ppermute x15, waiting for transfers between devices, swap(): return lax.ppermute(x, 'tp', [(i, i ^ bit) for i in range(4)])  26.1 us
    ppermute x4, waiting for transfers between devices, shift(): lax.ppermute(x, 'req', [(i, i + by) for i in range(count) if 0 <= i + by...  19.6 us
    all_to_all x2, waiting for transfers between devices, exchange(): return lax.all_to_all(x, axes, split_axis=0, concat_axis=0, tiled=True)  18.9 us
    all_to_all x2, starting transfers between devices, exchange(): return lax.all_to_all(x, axes, split_axis=0, concat_axis=0, tiled=True)  17.3 us
    ppermute x15, starting transfers between devices, swap(): return lax.ppermute(x, 'tp', [(i, i ^ bit) for i in range(4)])  14 us
  transfers between devices with their start and end apart: 22, of which 9 were waited for; matrix products, arithmetic and copies ran while one was open for 10% of the time, Pallas kernels for 24%

profile of v3, /device:TPU:1, one launch (start us, length us, event | category | flops | bytes accessed | tf_op | source)
XLA Modules:
  0.0 307.2 jit_solution(17135051035479378096)
XLA Ops:
  7.3 1.8 gather_fusion
  9.1 5.9 %norm.1.x = bf16[2048,1024]{1,0:T(8,128)(2,1)} custom-call(bf16[2048,1024]{1,0:T(8,128)(2,1)} %h.5, f32[1,1024]{1,0:T(1,128)} %bitcast.108), custom_call_target="tpu_custom_call" | custom-call | flops 16777216 | bytes 8388608 | tf_op jit(solution)/shard_map/norm/pallas_call | solution.py:87
  14.9 2.6 prep.1
  17.6 0.9 slice_bitcast_fusion.4
  18.5 3.1 %collective-permute-start.9 = (bf16[8,3328]{1,0:T(8,128)(2,1)S(1)}, bf16[8,3328]{1,0:T(8,128)(2,1)S(1)}, u32[]{:S(2)}, u32[]{:S(2)}) collective-permute-start(bf16[8,3328]{1,0:T(8,128)(2,1)S(1)} %get-tuple-element.51), channel_id=1, source_target_pairs={{0,3},{1,2},{2,1},{3,0},{4,7},{5,6},{6,5},{7,4},{8,11},{9,10},{10,... | collective-permute-start | bytes 159752 | tf_op jit(solution)/shard_map/ppermute | solution.py:382
  21.8 1.6 collective-permute-done.9
  23.4 1.1 collective-permute-done.7
  24.6 0.7 pad_maximum_fusion.1
  25.3 11.2 %all-to-all-start = ((bf16[128,8,768]{2,1,0:T(8,128)(2,1)}), bf16[128,8,768]{2,1,0:T(8,128)(2,1)S(1)}, u32[]{:S(2)}, u32[]{:S(2)}) async-start(bf16[128,8,768]{2,1,0:T(8,128)(2,1)} %bitcast.93), calls=%async_computation | async-start | bytes 3145728 | tf_op jit(solution)/shard_map/all_to_all | solution.py:391
  36.8 0.7 add_subtract_fusion
  38.1 0.6 slice.118
  38.7 1.0 copy.55.seg0
  39.7 1.0 copy.56.seg1
  40.8 1.0 copy.53.seg0
  41.8 1.0 copy.54.seg1
  42.8 1.0 copy.51.seg0
  43.9 1.0 copy.52.seg1
  44.9 1.2 stack.2.table
  46.5 5.5 %multiply_sine_fusion = (f32[2048,128]{1,0:T(8,128)}, f32[2048,128]{1,0:T(8,128)}) fusion(f32[128]{0:T(128)S(1)} %fusion.18, f32[2048]{0:T(1024)S(1)} %subtract_convert_fusion), kind=kLoop, calls=%fused_computation.3 | loop fusion | flops 262144 | bytes 2105856 | tf_op jit(solution)/shard_map/sin | solution.py:441
  52.0 10.2 %all-to-all-done = bf16[128,8,768]{2,1,0:T(8,128)(2,1)S(1)} async-done(((bf16[128,8,768]{2,1,0:T(8,128)(2,1)}), bf16[128,8,768]{2,1,0:T(8,128)(2,1)S(1)}, u32[]{:S(2)}, u32[]{:S(2)}) %all-to-all-start) | async-done | bytes 1572896 | tf_op jit(solution)/shard_map/all_to_all | solution.py:391
  62.2 1.8 gather_fusion.1
  64.0 9.3 %qkv.1 = (bf16[2048,256]{1,0:T(8,128)(2,1)}, bf16[4,2,256,256]{3,2,1,0:T(8,128)(2,1)}, bf16[4,2,256,256]{3,2,1,0:T(8,128)(2,1)}, bf16[2,2048,256]{2,1,0:T(8,128)(2,1)}) custom-call(bf16[2048,1024]{1,0:T(8,128)(2,1)} %norm.1.x, bf16[1024,768]{1,0:T(8,128)(2,1)} %bitcast.94, f32[2048,128]{1,0:T(8,128)} %get-tuple-element.63.cos, f32[2048,128]{1,0:T(8,128)} %get-tuple-element.62.sin), custom_call_target="tpu_custom_call" | custom-call | flops 3221225472 | bytes 12582912 | tf_op jit(solution)/shard_map/qkv/pallas_call | solution.py:136
  73.3 1.3 collective-permute-start.1
  74.6 4.1 %collective-permute-start.2 = (bf16[4,2,256,256]{3,2,1,0:T(8,128)(2,1)}, bf16[4,2,256,256]{3,2,1,0:T(8,128)(2,1)S(1)}, u32[]{:S(2)}, u32[]{:S(2)}) collective-permute-start(bf16[4,2,256,256]{3,2,1,0:T(8,128)(2,1)} %get-tuple-element.28.kv1), channel_id=1, source_target_pairs={{0,4},{4,8},{8,12},{12,16},{16,20},{20,24},{24,28},{28,32},{32,36}... | collective-permute-start | bytes 3145736 | tf_op jit(solution)/shard_map/ppermute | solution.py:387
  78.7 2.9 collective-permute-start
  81.5 1.5 collective-permute-start.3
  83.0 26.8 %attend_own.1 = (f32[4,72,2048]{2,1,0:T(8,128)}, f32[4,1,2048]{2,1,0:T(1,128)}) custom-call(s32[12,8]{1,0:T(8,128)} %stack.2.table, bf16[2048,256]{1,0:T(8,128)(2,1)} %get-tuple-element.26.q, s32[1,2048]{1,0:T(1,128)} %bitcast.104, bf16[4,2,256,256]{3,2,1,0:T(8,128)(2,1)} %get-tuple-element.27.kv0, s32[1024,1]{1,0:T(8,128)} %copy.51.seg0, ...), custom_call_target="tpu_custom_call" | custom-call | flops 21474836480 | bytes 8388608 | tf_op jit(solution)/shard_map/attend_own/pallas_call | solution.py:250
  109.9 19.6 %collective-permute-done.3.kv1 = bf16[4,2,256,256]{3,2,1,0:T(8,128)(2,1)} collective-permute-done((bf16[4,2,256,256]{3,2,1,0:T(8,128)(2,1)}, bf16[4,2,256,256]{3,2,1,0:T(8,128)(2,1)}, u32[]{:S(2)}, u32[]{:S(2)}) %collective-permute-start.3) | collective-permute-done | bytes 1048608 | tf_op jit(solution)/shard_map/ppermute | solution.py:387
  129.4 10.6 %attend_near.1 = (f32[4,72,2048]{2,1,0:T(8,128)}, f32[4,1,2048]{2,1,0:T(1,128)}) custom-call(s32[12,8]{1,0:T(8,128)} %stack.2.table, bf16[2048,256]{1,0:T(8,128)(2,1)} %get-tuple-element.26.q, s32[1,2048]{1,0:T(1,128)} %bitcast.105, bf16[4,2,256,256]{3,2,1,0:T(8,128)(2,1)} %copy-done.13, s32[1024,1]{1,0:T(8,128)} %copy.53.seg0, ...), custom_call_target="tpu_custom_call" | custom-call | flops 10737418240 | bytes 8388608 | tf_op jit(solution)/shard_map/attend_near/pallas_call | solution.py:250
  140.1 0.9 copy-done.12
  141.3 5.7 %attend_far.2.m0 = bf16[1024,256]{1,0:T(8,128)(2,1)} custom-call(s32[12,8]{1,0:T(8,128)} %stack.2.table, bf16[2048,256]{1,0:T(8,128)(2,1)} %get-tuple-element.26.q, s32[1,2048]{1,0:T(1,128)} %bitcast.106, bf16[4,2,256,256]{3,2,1,0:T(8,128)(2,1)} %copy-done.12, s32[1024,1]{1,0:T(8,128)} %copy.55.seg0, bf16[4,2,256,256]{3,2,1,0:T(8,128)(2,1)} %copy-done.11, ...), custom_call_target="tpu_custom_call" | custom-call | flops 5368709120 | bytes 8388608 | tf_op jit(solution)/shard_map/attend_far/pallas_call | solution.py:250
  147.1 1.3 collective-permute-start.4
  148.4 0.6 fusion.25
  149.0 2.5 fusion.20
  151.5 1.2 collective-permute-start.5
  152.7 19.4 %collective-permute-done.4.m1 = bf16[1024,256]{1,0:T(8,128)(2,1)S(1)} collective-permute-done((bf16[1024,256]{1,0:T(8,128)(2,1)}, bf16[1024,256]{1,0:T(8,128)(2,1)S(1)}, u32[]{:S(2)}, u32[]{:S(2)}) %collective-permute-start.4) | collective-permute-done | bytes 524320 | tf_op jit(solution)/shard_map/ppermute | solution.py:382
  172.1 1.6 collective-permute-start.6
  173.7 0.6 pad_add_fusion.table
  174.3 5.6 %attend_far.3.m0 = bf16[1024,256]{1,0:T(8,128)(2,1)} custom-call(s32[12,8]{1,0:T(8,128)} %stack.2.table, bf16[2048,256]{1,0:T(8,128)(2,1)} %get-tuple-element.26.q, s32[1,2048]{1,0:T(1,128)} %bitcast.107, bf16[4,2,256,256]{3,2,1,0:T(8,128)(2,1)} %copy-done.12, s32[1024,1]{1,0:T(8,128)} %copy.55.seg0, bf16[4,2,256,256]{3,2,1,0:T(8,128)(2,1)} %copy-done.11, ...), custom_call_target="tpu_custom_call" | custom-call | flops 5368709120 | bytes 8388608 | tf_op jit(solution)/shard_map/attend_far/pallas_call | solution.py:250
  179.9 1.4 collective-permute-start.12
  181.7 10.4 %all-gather.2.cloned.1.call-done = bf16[1024,3328]{1,0:T(8,128)(2,1)} async-done(((bf16[32,3328]{1,0:T(8,128)(2,1)}), bf16[1024,3328]{1,0:T(8,128)(2,1)}) %all-gather.2.cloned.1.call-update) | async-done | bytes 6815760 | tf_op jit(solution)/shard_map/all_gather | solution.py:471
  192.0 0.7 broadcast_in_dim.54.before
  192.8 16.1 %mlp.2 = (f32[1024,512]{1,0:T(8,128)}, bf16[1024,512]{1,0:T(8,128)(2,1)}, f32[2,64,512]{2,1,0:T(8,128)}) custom-call(s32[132]{0:T(256)} %pad_add_fusion.table, bf16[1024,256]{1,0:T(8,128)(2,1)} %attend_far.2.m0, bf16[1024,256]{1,0:T(8,128)(2,1)} %copy-done.14, bf16[1024,256]{1,0:T(8,128)(2,1)} %copy-done.16, bf16[1024,256]{1,0:T(8,128)(2,1)} %copy-done.18, ...), custom_call_target="tpu_custom_call" | custom-call | flops 6979321856 | bytes 12582912 | tf_op jit(solution)/shard_map/mlp/pallas_call | solution.py:344
  208.9 1.4 collective-permute-start.14
  210.2 1.5 collective-permute-done.14.m3
  211.7 0.8 copy-done.19
  212.5 16.2 %mlp.3 = (f32[1024,512]{1,0:T(8,128)}, bf16[1024,512]{1,0:T(8,128)(2,1)}, f32[2,64,512]{2,1,0:T(8,128)}) custom-call(s32[132]{0:T(256)} %pad_add_fusion.table, bf16[1024,256]{1,0:T(8,128)(2,1)} %attend_far.3.m0, bf16[1024,256]{1,0:T(8,128)(2,1)} %copy-done.15, bf16[1024,256]{1,0:T(8,128)(2,1)} %copy-done.17, bf16[1024,256]{1,0:T(8,128)(2,1)} %copy-done.19, ...), custom_call_target="tpu_custom_call" | custom-call | flops 6979321856 | bytes 12582912 | tf_op jit(solution)/shard_map/mlp/pallas_call | solution.py:344
  228.8 0.9 fusion.9
  230.1 0.9 slice_bitcast_fusion
  231.6 2.4 collective-permute-done.18
  234.0 14.2 %all_to_all.21 = bf16[32,2,256]{2,1,0:T(2,128)(2,1)S(1)} all-to-all(bf16[32,2,256]{2,1,0:T(2,128)(2,1)S(1)} %reshape.542), channel_id=1, replica_groups=mesh['req'=32,'tp'=4] {'req'}, dimensions={0} | all-to-all | bytes 65536 | tf_op jit(solution)/shard_map/all_to_all | solution.py:391
  248.2 0.7 broadcast_in_dim.55
  248.9 6.1 %all-to-all-start.2 = ((bf16[128,2,256]{2,1,0:T(2,128)(2,1)}), bf16[128,2,256]{2,1,0:T(2,128)(2,1)S(1)}, u32[]{:S(2)}, u32[]{:S(2)}) async-start(bf16[128,2,256]{2,1,0:T(2,128)(2,1)} %broadcast_in_dim.55), calls=%async_computation.2 | async-start | bytes 262144 | tf_op jit(solution)/shard_map/all_to_all | solution.py:391
  255.1 1.3 collective-permute-start.10
  256.4 8.7 %all-to-all-done.2 = bf16[128,2,256]{2,1,0:T(2,128)(2,1)S(1)} async-done(((bf16[128,2,256]{2,1,0:T(2,128)(2,1)}), bf16[128,2,256]{2,1,0:T(2,128)(2,1)S(1)}, u32[]{:S(2)}, u32[]{:S(2)}) %all-to-all-start.2) | async-done | bytes 131104 | tf_op jit(solution)/shard_map/all_to_all | solution.py:391
  266.4 1.5 convert_element_type.87
  268.0 1.0 fusion.4
  269.8 0.7 copy-done.5
  270.8 0.7 collective-permute-start.16
  272.5 22.5 %all_to_all.22 = f32[128,1,64]{2,1,0:T(1,128)S(1)} all-to-all(f32[128,1,64]{2,1,0:T(1,128)S(1)} %broadcast_in_dim.56), channel_id=1, replica_groups=mesh['req'=32,'tp'=4] {'req','tp'}, dimensions={0} | all-to-all | bytes 65536 | tf_op jit(solution)/shard_map/all_to_all | solution.py:391
  295.1 0.7 reduce_max.39
  295.7 1.8 fusion.6
  297.8 1.5 fusion.3
  299.3 1.0 pad_maximum_fusion
  (102 shorter events, 6.9 us)
Async XLA Ops:
  7.2 264.3 %copy-start = (f32[4,1024]{1,0:T(4,128)S(1)}, f32[4,1024]{1,0:T(4,128)}, u32[]{:S(2)}) copy-start(f32[4,1024]{1,0:T(4,128)} %param.30) | copy-start | bytes 49156
  7.2 184.9 %all-gather.2.cloned.1.call-start = ((), (), s32[]{:S(2)}) async-start(), calls=%async_computation.4 | async-start | bytes 7028736 | tf_op jit(solution)/shard_map/all_gather | solution.py:471
  17.6 19.0 %copy-start.8 = (s32[64]{0:T(128)S(1)}, s32[64]{0:T(128)}, u32[]{:S(2)}) copy-start(s32[64]{0:T(128)} %param.17) | copy-start | bytes 772
  18.5 4.9 %collective-permute-start.9 = (bf16[8,3328]{1,0:T(8,128)(2,1)S(1)}, bf16[8,3328]{1,0:T(8,128)(2,1)S(1)}, u32[]{:S(2)}, u32[]{:S(2)}) collective-permute-start(bf16[8,3328]{1,0:T(8,128)(2,1)S(1)} %get-tuple-element.51), channel_id=1, source_target_pairs={{0,3},{1,2},{2,1},{3,0},{4,7},{5,6},{6,5},{7,4},{8,11},{9,10},{10,... | collective-permute-start | bytes 159752 | tf_op jit(solution)/shard_map/ppermute | solution.py:382
  21.6 1.8 collective-permute-start.8
  21.6 3.0 collective-permute-start.7
  25.3 36.9 %all-to-all-start = ((bf16[128,8,768]{2,1,0:T(8,128)(2,1)}), bf16[128,8,768]{2,1,0:T(8,128)(2,1)S(1)}, u32[]{:S(2)}, u32[]{:S(2)}) async-start(bf16[128,8,768]{2,1,0:T(8,128)(2,1)} %bitcast.93), calls=%async_computation | async-start | bytes 3145728 | tf_op jit(solution)/shard_map/all_to_all | solution.py:391
  36.5 9.6 %copy-start.20 = (s32[128]{0:T(128)S(1)}, s32[128]{0:T(128)}, u32[]{:S(2)}) copy-start(s32[128]{0:T(128)} %param.19) | copy-start | bytes 1540
  73.3 66.7 %collective-permute-start.1 = (bf16[4,2,256,256]{3,2,1,0:T(8,128)(2,1)}, bf16[4,2,256,256]{3,2,1,0:T(8,128)(2,1)S(1)}, u32[]{:S(2)}, u32[]{:S(2)}) collective-permute-start(bf16[4,2,256,256]{3,2,1,0:T(8,128)(2,1)} %get-tuple-element.28.kv1), channel_id=1, source_target_pairs={{4,0},{8,4},{12,8},{16,12},{20,16},{24,20},{28,24},{32,28},{36,32}... | collective-permute-start | bytes 3145736 | tf_op jit(solution)/shard_map/ppermute | solution.py:387
  74.6 35.2 %collective-permute-start.2 = (bf16[4,2,256,256]{3,2,1,0:T(8,128)(2,1)}, bf16[4,2,256,256]{3,2,1,0:T(8,128)(2,1)S(1)}, u32[]{:S(2)}, u32[]{:S(2)}) collective-permute-start(bf16[4,2,256,256]{3,2,1,0:T(8,128)(2,1)} %get-tuple-element.28.kv1), channel_id=1, source_target_pairs={{0,4},{4,8},{8,12},{12,16},{16,20},{20,24},{24,28},{28,32},{32,36}... | collective-permute-start | bytes 3145736 | tf_op jit(solution)/shard_map/ppermute | solution.py:387
  78.7 61.4 %collective-permute-start = (bf16[4,2,256,256]{3,2,1,0:T(8,128)(2,1)}, bf16[4,2,256,256]{3,2,1,0:T(8,128)(2,1)S(1)}, u32[]{:S(2)}, u32[]{:S(2)}) collective-permute-start(bf16[4,2,256,256]{3,2,1,0:T(8,128)(2,1)} %get-tuple-element.27.kv0), channel_id=1, source_target_pairs={{0,4},{4,8},{8,12},{12,16},{16,20},{20,24},{24,28},{28,32},{32,36}... | collective-permute-start | bytes 3145736 | tf_op jit(solution)/shard_map/ppermute | solution.py:387
  81.5 47.9 %collective-permute-start.3 = (bf16[4,2,256,256]{3,2,1,0:T(8,128)(2,1)}, bf16[4,2,256,256]{3,2,1,0:T(8,128)(2,1)}, u32[]{:S(2)}, u32[]{:S(2)}) collective-permute-start(bf16[4,2,256,256]{3,2,1,0:T(8,128)(2,1)} %get-tuple-element.27.kv0), channel_id=1, source_target_pairs={{4,0},{8,4},{12,8},{16,12},{20,16},{24,20},{28,24},{32,28},{36,32}... | collective-permute-start | bytes 3145736 | tf_op jit(solution)/shard_map/ppermute | solution.py:387
  109.9 19.6 %copy-start.13 = (bf16[4,2,256,256]{3,2,1,0:T(8,128)(2,1)}, bf16[4,2,256,256]{3,2,1,0:T(8,128)(2,1)S(1)}, u32[]{:S(2)}) copy-start(bf16[4,2,256,256]{3,2,1,0:T(8,128)(2,1)S(1)} %collective-permute-done.2.kv0) | copy-start | bytes 3145732
  140.0 1.0 copy-start.12
  140.1 1.3 copy-start.11
  141.3 7.0 %copy-start.7 = (s32[4]{0:T(128)S(1)}, s32[4]{0:T(128)}, u32[]{:S(2)}) copy-start(s32[4]{0:T(128)} %gather_fusion) | copy-start | bytes 52
  141.3 7.6 %copy-start.1 = (s32[4]{0:T(128)S(1)}, s32[4]{0:T(128)}, u32[]{:S(2)}) copy-start(s32[4]{0:T(128)} %constant.160.clone) | copy-start | bytes 52
  147.1 25.0 %collective-permute-start.4 = (bf16[1024,256]{1,0:T(8,128)(2,1)}, bf16[1024,256]{1,0:T(8,128)(2,1)S(1)}, u32[]{:S(2)}, u32[]{:S(2)}) collective-permute-start(bf16[1024,256]{1,0:T(8,128)(2,1)} %attend_far.2.m0), channel_id=1, source_target_pairs={{0,2},{1,3},{2,0},{3,1},{4,6},{5,7},{6,4},{7,5},{8,10},{9,11},{10,... | collective-permute-start | bytes 1572872 | tf_op jit(solution)/shard_map/ppermute | solution.py:382
  151.5 30.2 %collective-permute-start.5 = (bf16[1024,256]{1,0:T(8,128)(2,1)}, bf16[1024,256]{1,0:T(8,128)(2,1)S(1)}, u32[]{:S(2)}, u32[]{:S(2)}) collective-permute-start(bf16[1024,256]{1,0:T(8,128)(2,1)} %attend_far.2.m0), channel_id=1, source_target_pairs={{0,1},{1,0},{2,3},{3,2},{4,5},{5,4},{6,7},{7,6},{8,9},{9,8},{10,11... | collective-permute-start | bytes 1572872 | tf_op jit(solution)/shard_map/ppermute | solution.py:382
  172.1 7.8 %copy-start.14 = (bf16[1024,256]{1,0:T(8,128)(2,1)}, bf16[1024,256]{1,0:T(8,128)(2,1)S(1)}, u32[]{:S(2)}) copy-start(bf16[1024,256]{1,0:T(8,128)(2,1)S(1)} %collective-permute-done.4.m1) | copy-start | bytes 1572868
  172.1 9.6 %collective-permute-start.6 = (bf16[1024,256]{1,0:T(8,128)(2,1)S(1)}, bf16[1024,256]{1,0:T(8,128)(2,1)S(1)}, u32[]{:S(2)}, u32[]{:S(2)}) collective-permute-start(bf16[1024,256]{1,0:T(8,128)(2,1)S(1)} %collective-permute-done.4.m1), channel_id=1, source_target_pairs={{0,1},{1,0},{2,3},{3,2},{4,5},{5,4},{6,7},{7,6},{8,9},{9,8},{10,11... | collective-permute-start | bytes 1572872 | tf_op jit(solution)/shard_map/ppermute | solution.py:382
  179.9 28.9 %collective-permute-start.12 = (bf16[1024,256]{1,0:T(8,128)(2,1)}, bf16[1024,256]{1,0:T(8,128)(2,1)S(1)}, u32[]{:S(2)}, u32[]{:S(2)}) collective-permute-start(bf16[1024,256]{1,0:T(8,128)(2,1)} %attend_far.3.m0), channel_id=1, source_target_pairs={{0,2},{1,3},{2,0},{3,1},{4,6},{5,7},{6,4},{7,5},{8,10},{9,11},{10,... | collective-permute-start | bytes 1572872 | tf_op jit(solution)/shard_map/ppermute | solution.py:382
  181.3 28.9 %collective-permute-start.13 = (bf16[1024,256]{1,0:T(8,128)(2,1)}, bf16[1024,256]{1,0:T(8,128)(2,1)S(1)}, u32[]{:S(2)}, u32[]{:S(2)}) collective-permute-start(bf16[1024,256]{1,0:T(8,128)(2,1)} %attend_far.3.m0), channel_id=1, source_target_pairs={{0,1},{1,0},{2,3},{3,2},{4,5},{5,4},{6,7},{7,6},{8,9},{9,8},{10,11... | collective-permute-start | bytes 1572872 | tf_op jit(solution)/shard_map/ppermute | solution.py:382
  181.6 11.1 %copy-start.16 = (bf16[1024,256]{1,0:T(8,128)(2,1)}, bf16[1024,256]{1,0:T(8,128)(2,1)S(1)}, u32[]{:S(2)}) copy-start(bf16[1024,256]{1,0:T(8,128)(2,1)S(1)} %collective-permute-done.5.m2) | copy-start | bytes 1572868
  181.7 11.1 %copy-start.18 = (bf16[1024,256]{1,0:T(8,128)(2,1)}, bf16[1024,256]{1,0:T(8,128)(2,1)S(1)}, u32[]{:S(2)}) copy-start(bf16[1024,256]{1,0:T(8,128)(2,1)S(1)} %collective-permute-done.6.m3) | copy-start | bytes 1572868
  208.8 2.9 copy-start.15
  208.9 2.9 collective-permute-start.14
  210.2 1.5 copy-start.17
  211.7 0.8 copy-start.19
  212.5 42.5 %copy-start.10 = (bf16[1024,512]{1,0:T(8,128)(2,1)S(1)}, bf16[1024,512]{1,0:T(8,128)(2,1)}, u32[]{:S(2)}) copy-start(bf16[1024,512]{1,0:T(8,128)(2,1)} %get-tuple-element.35) | copy-start | bytes 3145732
  229.7 1.4 collective-permute-start.17
  231.1 2.8 collective-permute-start.18
  248.9 16.2 %all-to-all-start.2 = ((bf16[128,2,256]{2,1,0:T(2,128)(2,1)}), bf16[128,2,256]{2,1,0:T(2,128)(2,1)S(1)}, u32[]{:S(2)}, u32[]{:S(2)}) async-start(bf16[128,2,256]{2,1,0:T(2,128)(2,1)} %broadcast_in_dim.55), calls=%async_computation.2 | async-start | bytes 262144 | tf_op jit(solution)/shard_map/all_to_all | solution.py:391
  255.1 11.4 %collective-permute-start.10 = (bf16[1024,512]{1,0:T(8,128)(2,1)S(1)}, bf16[1024,512]{1,0:T(8,128)(2,1)}, u32[]{:S(2)}, u32[]{:S(2)}) collective-permute-start(bf16[1024,512]{1,0:T(8,128)(2,1)S(1)} %copy-done.10), channel_id=1, source_target_pairs={{0,1},{1,0},{2,3},{3,2},{4,5},{5,4},{6,7},{7,6},{8,9},{9,8},{10,11... | collective-permute-start | bytes 3145736 | tf_op jit(solution)/shard_map/ppermute | solution.py:382
  256.3 13.2 %collective-permute-start.15 = (bf16[1024,512]{1,0:T(8,128)(2,1)}, bf16[1024,512]{1,0:T(8,128)(2,1)S(1)}, u32[]{:S(2)}, u32[]{:S(2)}) collective-permute-start(bf16[1024,512]{1,0:T(8,128)(2,1)} %get-tuple-element.39), channel_id=1, source_target_pairs={{0,1},{1,0},{2,3},{3,2},{4,5},{5,4},{6,7},{7,6},{8,9},{9,8},{10,11... | collective-permute-start | bytes 3145736 | tf_op jit(solution)/shard_map/ppermute | solution.py:382
  265.8 2.2 copy-start.4
  268.9 1.6 copy-start.5
  268.9 26.8 %collective-permute-start.11 = (bf16[1024,256]{1,0:T(8,128)(2,1)}, bf16[1024,256]{1,0:T(8,128)(2,1)}, u32[]{:S(2)}, u32[]{:S(2)}) collective-permute-start(bf16[1024,256]{1,0:T(8,128)(2,1)} %fusion.4), channel_id=1, source_target_pairs={{0,2},{1,3},{2,0},{3,1},{4,6},{5,7},{6,4},{7,5},{8,10},{9,11},{10,... | collective-permute-start | bytes 1572872 | tf_op jit(solution)/shard_map/ppermute | solution.py:382
  269.8 2.6 copy-start.2
  269.8 1.7 copy-start.9
  269.8 2.2 copy-start.6
  270.8 26.7 %collective-permute-start.16 = (bf16[1024,256]{1,0:T(8,128)(2,1)S(1)}, bf16[1024,256]{1,0:T(8,128)(2,1)S(1)}, u32[]{:S(2)}, u32[]{:S(2)}) collective-permute-start(bf16[1024,256]{1,0:T(8,128)(2,1)S(1)} %fusion.1), channel_id=1, source_target_pairs={{0,2},{1,3},{2,0},{3,1},{4,6},{5,7},{6,4},{7,5},{8,10},{9,11},{10,... | collective-permute-start | bytes 1572872 | tf_op jit(solution)/shard_map/ppermute | solution.py:382
  295.7 2.1 copy-start.3
Sparse Core Ops, SparseCore 0:
  25.4 166.5 all-gather.1

commit v4 on v3

--- a/solution.py
+++ b/solution.py
@@ -96,7 +96,7 @@
     )(h, gain.reshape(1, 1024))
 
 
-def qkv_kernel(x, w, cos, sin, q, low, high, cache):
+def qkv_kernel(x, w, cos, sin, q, kv, cache):
     row = lax.broadcasted_iota(jnp.int32, (256, 256), 0)
     col = lax.broadcasted_iota(jnp.int32, (256, 256), 1)
     source = (col % 128) // 32 * 64 + col // 128 * 32 + col % 32
@@ -111,18 +111,9 @@
     q[...] = (turned(y[:, :128], y[:, 128:256]).astype(BF).astype(F32) * 0.125).astype(BF)
     k = turned(y[:, 256:384], y[:, 384:512]).astype(BF)
     v = y[:, 512:].astype(BF)
-    i = pl.program_id(0)
-    half = pl.num_programs(0) // 2
-    blocks = x.shape[0] // KB
-    for part, ref in enumerate((low, high)):
-
-        @pl.when(i // half == part)
-        def _():
-            for n in range(blocks):
-                at = (i - part * half) * blocks + n
-                ref[at, 0] = k[KB * n : KB * n + KB]
-                ref[at, 1] = jnp.transpose(v[KB * n : KB * n + KB])
-
+    for n in range(x.shape[0] // KB):
+        kv[n, 0] = k[KB * n : KB * n + KB]
+        kv[n, 1] = jnp.transpose(v[KB * n : KB * n + KB])
     cache[0] = lax.dot_general(
         k, back, (((1,), (1,)), ((), ())), preferred_element_type=F32
     ).astype(BF)
@@ -132,7 +123,6 @@
 def qkv_project(x, w, cos, sin):
     rows = x.shape[0]
     n = 512
-    pairs = (rows // KB // 2, 2, KB, 256)
     return pl.pallas_call(
         qkv_kernel,
         grid=(rows // n,),
@@ -144,14 +134,12 @@
         ],
         out_specs=[
             pl.BlockSpec((n, 256), lambda i: (i, 0)),
-            vmem(*pairs),
-            vmem(*pairs),
+            pl.BlockSpec((n // KB, 2, KB, 256), lambda i: (i, 0, 0, 0)),
             pl.BlockSpec((2, n, 256), lambda i: (0, i, 0)),
         ],
         out_shape=(
             jax.ShapeDtypeStruct((rows, 256), BF),
-            jax.ShapeDtypeStruct(pairs, BF),
-            jax.ShapeDtypeStruct(pairs, BF),
+            jax.ShapeDtypeStruct((rows // KB, 2, KB, 256), BF),
             jax.ShapeDtypeStruct((2, rows, 256), BF),
         ),
         compiler_params=params(),
@@ -183,15 +171,8 @@
         acc[h] = acc[h] * fade + jnp.dot(v, p, preferred_element_type=F32)
 
 
-def attend_span(short, table, at, i, *refs):
+def attend_span(table, at, i, *refs):
     start = table[at, i]
-    if short:
-
-        @pl.loop(0, table[at + 1, i])
-        def _(c):
-            attend_chunk(start + c, 1, *refs)
-
-        return
     pairs = table[at + 1, i] // 2
 
     @pl.loop(0, pairs)
@@ -203,34 +184,34 @@
         attend_chunk(start + 2 * pairs, 1, *refs)
 
 
-def attend_kernel(stage, base, table, q, qseg, kv0, seg0, kv1, seg1, *refs):
-    i = pl.program_id(0) + base
-    if stage == 0:
-        acc_out, m_out, qm, m_sc, acc = refs
-    elif stage == 1:
-        acc_in, m_in, acc_out, m_out, qm, m_sc, acc = refs
-    else:
-        acc_in, m_in, out, qm, m_sc, acc = refs
+def spread_heads(q, qm):
     lane = lax.broadcasted_iota(jnp.int32, (QB, 256), 1)
     for h in range(4):
         qm[h] = jnp.where((lane % 128) // 32 == h, q[...].astype(F32), 0.0).astype(BF)
-    if stage == 0:
-        m_sc[...] = jnp.full_like(m_sc, NEG)
-        acc[...] = jnp.zeros_like(acc)
-    else:
-        m_sc[...] = m_in[...]
-        acc[...] = acc_in[...]
-    attend_span(stage == 2, table, 4 * stage, i, qm, kv0, seg0, qseg, m_sc, acc)
-    attend_span(stage == 2, table, 4 * stage + 2, i, qm, kv1, seg1, qseg, m_sc, acc)
-    if stage < 2:
-        acc_out[...] = acc[...]
-        m_out[...] = m_sc[...]
-    else:
-        heads = [acc[h, :HEAD_DIM] / acc[h, HEAD_DIM : HEAD_DIM + 1] for h in range(4)]
-        out[...] = jnp.transpose(jnp.concatenate(heads, axis=0)).astype(BF)
-
-
-def attend(stage, part, parts, table, q, qseg, kv0, seg0, kv1, seg1, *state):
+
+
+def own_kernel(table, q, qseg, kv, kseg, acc_out, m_out, qm, m_sc, acc):
+    i = pl.program_id(0)
+    spread_heads(q, qm)
+    m_sc[...] = jnp.full_like(m_sc, NEG)
+    acc[...] = jnp.zeros_like(acc)
+    attend_span(table, 0, i, qm, kv, kseg, qseg, m_sc, acc)
+    acc_out[...] = acc[...]
+    m_out[...] = m_sc[...]
+
+
+def halo_kernel(base, table, q, qseg, lkv, lseg, rkv, rseg, acc_in, m_in, out, qm, m_sc, acc):
+    i = pl.program_id(0) + base
+    spread_heads(q, qm)
+    m_sc[...] = m_in[...]
+    acc[...] = acc_in[...]
+    attend_span(table, 2, i, qm, lkv, lseg, qseg, m_sc, acc)
+    attend_span(table, 4, i, qm, rkv, rseg, qseg, m_sc, acc)
+    heads = [acc[h, :HEAD_DIM] / acc[h, HEAD_DIM : HEAD_DIM + 1] for h in range(4)]
+    out[...] = jnp.transpose(jnp.concatenate(heads, axis=0)).astype(BF)
+
+
+def attend(part, parts, table, q, qseg, sources, state):
     rows = q.shape[0]
     steps = rows // QB // parts
     base = part * steps
@@ -238,28 +219,27 @@
         pl.BlockSpec((4, VR, QB), lambda i, *_: (0, 0, i + base)),
         pl.BlockSpec((4, 1, QB), lambda i, *_: (0, 0, i + base)),
     ]
-    if stage < 2:
+    if state:
+        kernel = functools.partial(halo_kernel, base)
+        out_specs = pl.BlockSpec((QB, 256), lambda i, *_: (i, 0))
+        out_shape = jax.ShapeDtypeStruct((rows // parts, 256), BF)
+    else:
+        kernel = own_kernel
         out_specs = state_specs
         out_shape = (
             jax.ShapeDtypeStruct((4, VR, rows), F32),
             jax.ShapeDtypeStruct((4, 1, rows), F32),
         )
-    else:
-        out_specs = pl.BlockSpec((QB, 256), lambda i, *_: (i, 0))
-        out_shape = jax.ShapeDtypeStruct((rows // parts, 256), BF)
     return pl.pallas_call(
-        functools.partial(attend_kernel, stage, base),
+        kernel,
         grid_spec=pltpu.PrefetchScalarGridSpec(
             num_scalar_prefetch=1,
             grid=(steps,),
             in_specs=[
                 pl.BlockSpec((QB, 256), lambda i, *_: (i + base, 0)),
                 pl.BlockSpec((1, QB), lambda i, *_: (0, i + base)),
-                vmem(*kv0.shape),
-                vmem(*seg0.shape),
-                vmem(*kv1.shape),
-                vmem(*seg1.shape),
             ]
+            + [vmem(*x.shape) for x in sources]
             + state_specs[: len(state)],
             out_specs=out_specs,
             scratch_shapes=[
@@ -270,25 +250,30 @@
         ),
         out_shape=out_shape,
         compiler_params=params(),
-        cost_estimate=cost((20 << 30, 10 << 30, 5 << 30)[stage], 8 << 20, 12 << 20),
-        name=("attend_own", "attend_near", "attend_far")[stage],
-    )(table, q, qseg, kv0, seg0, kv1, seg1, *state)
+        cost_estimate=cost(12 << 30, 8 << 20, 12 << 20),
+        name="attend_halo" if state else "attend_own",
+    )(table, q, qseg, *sources, *state)
 
 
 def contract_last(a, b):
     return lax.dot_general(a, b, (((1,), (1,)), ((), ())), preferred_element_type=F32)
 
 
-def mlp_kernel(base, table, m0, m1, m2, m3, h, gain, last, before, weights, keep, send, picked, w, sem):
-    count = weights.shape[0]
+def mlp_kernel(base, table, m0, m1, m2, m3, h, gain, last, before, *refs):
+    *pieces, keep, send, picked, w, sem = refs
+    count = w.shape[0]
 
     @pl.when(pl.program_id(0) == 0)
     def _():
-        @pl.loop(0, count)
-        def _(k):
-            pltpu.make_async_copy(weights.at[table[4 + k]], w.at[k], sem).start()
-
-        pltpu.make_async_copy(weights, w, sem).wait()
+        done = 4
+        for piece in pieces:
+
+            @pl.loop(0, piece.shape[0])
+            def _(n, piece=piece, done=done):
+                pltpu.make_async_copy(piece.at[n], w.at[table[done + n]], sem).start()
+
+            done += piece.shape[0]
+        pltpu.make_async_copy(w, w, sem).wait()
 
     def rows(at, size, lo, width):
         return w[pl.ds(at, size), :, pl.ds(lo, width)].reshape(8 * size, width)
@@ -333,10 +318,10 @@
     picked[1] += pick(sent)
 
 
-def mlp(table, mixed, h, base, gain, last, before, weights):
+def mlp(table, mixed, h, base, gain, last, before, pieces):
     n = 256
     rows = mixed[0].shape[0]
-    count = weights.shape[0]
+    count = sum(piece.shape[0] for piece in pieces)
 
     def block(width):
         return pl.BlockSpec((n, width), lambda i, *_: (i, 0))
@@ -349,7 +334,7 @@
             in_specs=[block(256)] * 4
             + [pl.BlockSpec((n, 1024), lambda i, *_: (i + base, 0))]
             + [vmem(1, 1024), vmem(*last.shape), vmem(*before.shape)]
-            + [pl.BlockSpec(memory_space=pl.ANY)],
+            + [pl.BlockSpec(memory_space=pl.ANY)] * len(pieces),
             out_specs=[block(512), block(512), vmem(*before.shape)],
             scratch_shapes=[pltpu.VMEM((count, 8, REST), BF), pltpu.SemaphoreType.DMA(())],
         ),
@@ -361,7 +346,11 @@
         compiler_params=params(),
         cost_estimate=cost(rows * 1024 * (1024 + 3 * FFP) * 2, 12 << 20, rows * FFP),
         name="mlp",
-    )(table, *mixed, h, gain.reshape(1, 1024), last, before, weights)
+    )(table, *mixed, h, gain.reshape(1, 1024), last, before, *pieces)
+
+
+def swap(x, bit):
+    return lax.ppermute(x, "tp", [(i, i ^ bit) for i in range(4)])
 
 
 def gather_tp(x, after=None):
@@ -372,14 +361,25 @@
     return x, far, near, swap(far, 1)
 
 
-def reduce_tp(keep, send):
+def reduce_core(keep, send):
     got = swap(send, 1).astype(F32)
-    other = swap((keep[:, 256:] + got[:, 256:]).astype(BF), 2).astype(F32)
-    return (keep[:, :256] + got[:, :256] + other).astype(BF)
-
-
-def swap(x, bit):
-    return lax.ppermute(x, "tp", [(i, i ^ bit) for i in range(4)])
+    return keep[:, :256] + got[:, :256], (keep[:, 256:] + got[:, 256:]).astype(BF)
+
+
+def reduce_far(mine, send):
+    return (mine + swap(send, 2).astype(F32)).astype(BF)
+
+
+def from_offset(x, dx, dy, dz=0):
+    pairs = []
+    for i in range(32):
+        far = (i // 16 + dz) % 2 * 16 + (i // 4 + dx) % 4 * 4 + (i + dy) % 4
+        pairs.append((far, i))
+    return lax.ppermute(x, "req", pairs)
+
+
+def sum_req(x, moves):
+    return sum([from_offset(x, *move) for move in moves], x)
 
 
 def shift(x, by):
@@ -423,8 +423,6 @@
     source = jnp.sum(
         jnp.where(shard_map[None, :] == place[:, None], place[None, :], 0), axis=1
     )
-    qkv_all = exchange(qkv_block.reshape(count, 8, 768), BOTH)
-    qkv_w = qkv_all[source].reshape(width, 768)
     ends = jnp.cumsum(lengths)
     base = req_index * slots
     index = base - slots + jnp.arange(3 * slots, dtype=jnp.int32)
@@ -444,53 +442,67 @@
     low = jnp.max(jnp.where(ends[None, :] <= begin[:, None], ends[None, :], 0), axis=1) - base
     high = jnp.min(jnp.where(ends[None, :] > close[:, None], ends[None, :], 1 << 30), axis=1) - base
 
-    half = slots // KB // 2
+    blocks = slots // KB
     own_0 = jnp.maximum(low, 0) // KB
     own_1 = (jnp.minimum(high, slots) + KB - 1) // KB
     left_0 = (jnp.minimum(low, 0) + slots) // KB
     right_1 = (jnp.maximum(high - slots, 0) + KB - 1) // KB
-    spans = (
-        (own_0, jnp.minimum(own_1, half)),
-        (jnp.maximum(own_0 - half, 0), own_1 - half),
-        (jnp.maximum(left_0 - half, 0), half),
-        (jnp.zeros_like(right_1), jnp.minimum(right_1, half)),
-        (left_0, half),
-        (jnp.zeros_like(right_1), right_1 - half),
-    )
     table = jnp.stack(
-        [row for first, end in spans for row in (first, jnp.maximum(end - first, 0))]
-    )
-    segs = segment.reshape(6, slots // 2, 1)
+        [own_0, own_1 - own_0, left_0, blocks - left_0, jnp.zeros_like(right_1), right_1]
+    )
+    segs = segment.reshape(3, slots, 1)
     qseg = segment[slots : 2 * slots].reshape(1, slots)
 
-    normed = norm(hidden_in, attn_gain)
+    later, qkv_block = lax.optimization_barrier((hidden_in, qkv_block))
+    normed = norm(later, attn_gain)
     rest_block, normed = lax.optimization_barrier((rest_block, normed))
     rest_rows = jnp.concatenate(
         [rest_block[0], swap(rest_block[1], 2), swap(rest_block[2], 1), swap(rest_block[3], 3)], axis=0
     )
-    rest = lax.all_gather(rest_rows, "req", axis=0, tiled=True).reshape(count, 8, REST)
-    rest_source = source // tp_count * tp_count + place_of[source % tp_count]
-    query, kv_low, kv_high, cache = qkv_project(normed, qkv_w, cos, sin)
-    left_near = shift(kv_high, 1)
-    right_near = shift(kv_low, -1)
-    left_far = shift(kv_low, 1)
-    right_far = shift(kv_high, -1)
+    level = jnp.concatenate([rest_rows, from_offset(rest_rows, 0, 0, 1)], axis=0)
+    level = jnp.concatenate([level] + [from_offset(level, 0, d) for d in (1, 3, 2)], axis=0)
+    ahead = from_offset(level, 1, 0)
+    behind = from_offset(level, 3, 0)
+    far = jnp.arange(count, dtype=jnp.int32)
+    slot_x, slot_y = (jnp.array([0, 1, 3, 2], jnp.int32)[n] for n in (far // 32, far // 8 % 4))
+    from_req = (
+        (req_index // 16 + far // 4) % 2 * 16
+        + (req_index // 4 + slot_x) % 4 * 4
+        + (req_index + slot_y) % 4
+    )
+    rest_target = shard_map[from_req * tp_count + (tp_index ^ tp_order[far % 4])]
+    qkv_all = exchange(qkv_block.reshape(count, 8, 768), BOTH)
+    qkv_w = qkv_all[source].reshape(width, 768)
+    query, kv, cache = qkv_project(normed, qkv_w, cos, sin)
+    left = shift(kv, 1)
+    right = shift(kv, -1)
     parts = 2
-    state = attend(0, 0, 1, table, query, qseg, kv_low, segs[2], kv_high, segs[3])
-    state = attend(1, 0, 1, table, query, qseg, left_near, segs[1], right_near, segs[4], *state)
+    state = attend(0, 1, table, query, qseg, (kv, segs[1]), ())
+    ahead, behind, state = lax.optimization_barrier((ahead, behind, state))
+    rest = [
+        piece.reshape(-1, 8, REST)
+        for piece in (
+            level,
+            ahead,
+            behind,
+            from_offset(ahead[:128], 1, 0),
+            from_offset(behind[128:], 3, 0),
+        )
+    ]
     mixed = [
-        attend(2, part, parts, table, query, qseg, left_far, segs[0], right_far, segs[5], *state)
+        attend(part, parts, table, query, qseg, (left, segs[0], right, segs[2]), state)
         for part in range(parts)
     ]
 
     last_slot = (ends - 1 - base).reshape(requests, 1)
-    order = jnp.concatenate([tp_index ^ tp_order, rest_source])
+    order = jnp.concatenate([tp_index ^ tp_order, rest_target])
     picked = jnp.zeros((2, requests, 512), F32)
     bulk = []
+    after = mixed[1]
     for part in range(parts):
         keep, send, picked = mlp(
             order,
-            gather_tp(mixed[part], bulk[-1] if bulk else None),
+            gather_tp(mixed[part], after),
             hidden_in,
             part * (slots // parts // 256),
             mlp_gain,
@@ -498,19 +510,17 @@
             picked,
             rest,
         )
+        after = (keep, send)
         bulk.append((keep, send))
 
-    each = requests // req_count
-    last_mine = reduce_tp(picked[0], picked[1].astype(BF))
-    taken = exchange(last_mine.reshape(req_count, each, 256), "req").astype(F32).sum(axis=0)
-    spread = exchange(jnp.broadcast_to(taken.astype(BF)[None], (count, each, 256)), BOTH)
-    hidden_out = jnp.concatenate([reduce_tp(*pair) for pair in bulk], axis=0)
-    last = (
-        spread.reshape(req_count, tp_count, each, 256)
-        .transpose(0, 2, 1, 3)
-        .reshape(requests, width)
-        .astype(F32)
-    )
+    pieces = gather_tp(reduce_far(*reduce_core(picked[0], picked[1].astype(BF))))
+    wide = jnp.stack(pieces)[place_of].transpose(1, 0, 2).reshape(requests, width)
+    wide = sum_req(wide, ((0, 0, 1),))
+    bulk, wide = lax.optimization_barrier((bulk, wide))
+    hidden_out = jnp.concatenate([reduce_far(*reduce_core(*pair)) for pair in bulk], axis=0)
+    wide = sum_req(wide, tuple((0, d, 0) for d in (1, 3, 2)))
+    wide = sum_req(wide, tuple((d, 0, 0) for d in (1, 3, 2)))
+    last = wide.astype(F32)
     last_rms = jnp.sqrt(jnp.mean(last * last, axis=-1))
     choose = (tenant[:, None] == jnp.arange(final_gain.shape[0], dtype=jnp.int32)[None, :]).astype(
         F32

time: 309 us -> 327 us (1.058); the launches traced: 307 us -> 322 us
  starting transfers between devices: 41 us -> 74.9 us
  waiting for transfers between devices: 75 us -> 91.7 us
  blocking collectives: 36.7 us -> 21 us
  between operations: 14.5 us -> 1.23 us
  Pallas kernels: 98.9 us -> 92.4 us
  other arithmetic: 20 us -> 14.9 us
  local copies, waits for them, and re-layouts: 20.2 us -> 24.8 us
    ppermute x0 -> x15, waiting for transfers between devices: none -> 87.5 us  [from_offset(): return lax.ppermute(x, 'req', pairs)]
    ppermute x0 -> x15, starting transfers between devices: none -> 25.5 us  [from_offset(): return lax.ppermute(x, 'req', pairs)]
    ppermute x15 -> x18, waiting for transfers between devices: 26.1 us -> 4.27 us  [swap(): return lax.ppermute(x, 'tp', [(i, i ^ bit) for i in range(4)])]
    ppermute x15 -> x18, starting transfers between devices: 14 us -> 35.2 us  [swap(): return lax.ppermute(x, 'tp', [(i, i ^ bit) for i in range(4)])]
    ppermute x4 -> x2, waiting for transfers between devices: 19.6 us -> 0.01 us  [shift(): lax.ppermute(x, 'req', [(i, i + by) for i in range(count) if 0 <= i + by...]
    all_to_all x2 -> x1, waiting for transfers between devices: 18.9 us -> 0.01 us  [exchange(): return lax.all_to_all(x, axes, split_axis=0, concat_axis=0, tiled=True)]
    all_to_all x2 -> x1, blocking collectives: 36.7 us -> 21 us  [exchange(): return lax.all_to_all(x, axes, split_axis=0, concat_axis=0, tiled=True)]
    all_gather x1 -> x0, waiting for transfers between devices: 10.4 us -> none  [body(): lax.all_gather(rest_rows, 'req', axis=0, tiled=True).reshape(count, 8, REST)]
  transfers between devices with their start and end apart: 22 -> 36, of which waited for: 9 -> 14; matrix products, arithmetic and copies ran while one was open for 10% -> 9% of each run, Pallas kernels for 24% -> 21%
where the time goes in v4:
time: 327 us; the launch traced here: 322 us
  Pallas kernels  92.4 us (28%)
  waiting for transfers between devices  91.7 us (28%)
  starting transfers between devices  74.9 us (23%)
  local copies, waits for them, and re-layouts  24.8 us (8%)
  blocking collectives  21 us (6%)
  other arithmetic  14.9 us (5%)
    ppermute x15, waiting for transfers between devices, from_offset(): return lax.ppermute(x, 'req', pairs)  87.5 us
    pallas_call x3, Pallas kernels, attend(): pl.pallas_call(kernel, grid_spec=pltpu.PrefetchScalarGridSpec(num_scalar_...  43.3 us
    ppermute x18, starting transfers between devices, swap(): return lax.ppermute(x, 'tp', [(i, i ^ bit) for i in range(4)])  35.2 us
    pallas_call x2, Pallas kernels, mlp(): pl.pallas_call(functools.partial(mlp_kernel, base), grid_spec=pltpu.Prefe...  32.3 us
    ppermute x15, starting transfers between devices, from_offset(): return lax.ppermute(x, 'req', pairs)  25.5 us
    all_to_all x1, blocking collectives, exchange(): return lax.all_to_all(x, axes, split_axis=0, concat_axis=0, tiled=True)  21 us
    all_to_all x1, starting transfers between devices, exchange(): return lax.all_to_all(x, axes, split_axis=0, concat_axis=0, tiled=True)  10.2 us
    unnamed x48, local copies, waits for them, and re-layouts  8.95 us
  transfers between devices with their start and end apart: 36, of which 14 were waited for; matrix products, arithmetic and copies ran while one was open for 9% of the time, Pallas kernels for 21%

profile of v4, /device:TPU:1, one launch (start us, length us, event | category | flops | bytes accessed | tf_op | source)
XLA Modules:
  0.0 321.7 jit_solution(17714881695874503682)
XLA Ops:
  0.7 1.8 gather_fusion.1
  2.5 2.6 prep.1
  5.2 5.9 %norm.1.x = bf16[2048,1024]{1,0:T(8,128)(2,1)} custom-call(bf16[2048,1024]{1,0:T(8,128)(2,1)} %h.4, f32[1,1024]{1,0:T(1,128)} %bitcast.103), custom_call_target="tpu_custom_call" | custom-call | flops 16777216 | bytes 8388608 | tf_op jit(solution)/shard_map/norm/pallas_call | solution.py:87
  11.2 2.5 collective-permute-start.2
  13.7 1.0 collective-permute-start.3
  14.7 10.2 %all-to-all-start = ((bf16[128,8,768]{2,1,0:T(8,128)(2,1)}), bf16[128,8,768]{2,1,0:T(8,128)(2,1)S(1)}, u32[]{:S(2)}, u32[]{:S(2)}) async-start(bf16[128,8,768]{2,1,0:T(8,128)(2,1)} %bitcast.9), calls=%async_computation | async-start | bytes 3145728 | tf_op jit(solution)/shard_map/all_to_all | solution.py:391
  27.1 3.4 %collective-permute-start.5 = (bf16[32,3328]{1,0:T(8,128)(2,1)S(1)}, bf16[32,3328]{1,0:T(8,128)(2,1)S(1)}, u32[]{:S(2)}, u32[]{:S(2)}) collective-permute-start(bf16[32,3328]{1,0:T(8,128)(2,1)S(1)} %pad_maximum_fusion.1), channel_id=1, source_target_pairs={{64,0},{68,4},{72,8},{76,12},{80,16},{84,20},{88,24},{92,28},{96,3... | collective-permute-start | bytes 638984 | tf_op jit(solution)/shard_map/ppermute | solution.py:378
  32.4 19.5 %collective-permute-done.5 = bf16[32,3328]{1,0:T(8,128)(2,1)S(1)} collective-permute-done((bf16[32,3328]{1,0:T(8,128)(2,1)S(1)}, bf16[32,3328]{1,0:T(8,128)(2,1)S(1)}, u32[]{:S(2)}, u32[]{:S(2)}) %collective-permute-start.5) | collective-permute-done | bytes 213024 | tf_op jit(solution)/shard_map/ppermute | solution.py:378
  52.5 1.4 collective-permute-start.6
  53.9 5.5 %multiply_sine_fusion = (f32[2048,128]{1,0:T(8,128)}, f32[2048,128]{1,0:T(8,128)}) fusion(f32[128]{0:T(128)S(1)} %fusion.32, f32[2048]{0:T(1024)S(1)} %subtract_convert_fusion), kind=kLoop, calls=%fused_computation.5 | loop fusion | flops 262144 | bytes 2105856 | tf_op jit(solution)/shard_map/sin | solution.py:439
  59.5 1.5 collective-permute-start.8
  61.0 2.4 collective-permute-done.6
  63.4 0.8 constant_dynamic-update-slice_fusion.7
  64.2 8.2 %collective-permute-done.7 = bf16[64,3328]{1,0:T(8,128)(2,1)S(1)} collective-permute-done((bf16[64,3328]{1,0:T(8,128)(2,1)S(1)}, bf16[64,3328]{1,0:T(8,128)(2,1)S(1)}, u32[]{:S(2)}, u32[]{:S(2)}) %collective-permute-start.7) | collective-permute-done | bytes 426016 | tf_op jit(solution)/shard_map/ppermute | solution.py:378
  72.4 0.8 constant_dynamic-update-slice_fusion.6
  73.2 1.8 gather_fusion.2
  75.0 8.2 %qkv.1 = (bf16[2048,256]{1,0:T(8,128)(2,1)}, bf16[8,2,256,256]{3,2,1,0:T(8,128)(2,1)}, bf16[2,2048,256]{2,1,0:T(8,128)(2,1)}) custom-call(bf16[2048,1024]{1,0:T(8,128)(2,1)} %norm.1.x, bf16[1024,768]{1,0:T(8,128)(2,1)} %bitcast.85, f32[2048,128]{1,0:T(8,128)} %get-tuple-element.87.cos, f32[2048,128]{1,0:T(8,128)} %get-tuple-element.86.sin), custom_call_target="tpu_custom_call" | custom-call | flops 3221225472 | bytes 12582912 | tf_op jit(solution)/shard_map/qkv/pallas_call | solution.py:126
  83.2 2.7 collective-permute-start
  85.9 1.3 collective-permute-start.1
  87.2 0.8 constant_dynamic-update-slice_fusion.5
  88.0 5.0 %collective-permute-start.10 = (bf16[256,3328]{1,0:T(8,128)(2,1)}, bf16[256,3328]{1,0:T(8,128)(2,1)S(1)}, u32[]{:S(2)}, u32[]{:S(2)}) collective-permute-start(bf16[256,3328]{1,0:T(8,128)(2,1)} %constant_dynamic-update-slice_fusion.5), channel_id=1, source_target_pairs={{48,0},{52,4},{56,8},{60,12},{0,16},{4,20},{8,24},{12,28},{16,32},... | collective-permute-start | bytes 5111816 | tf_op jit(solution)/shard_map/ppermute | solution.py:378
  93.0 1.2 collective-permute-start.9
  94.2 1.4 copy.38.kseg
  95.5 1.3 copy.39.lseg
  96.9 1.4 copy.40.rseg
  99.1 23.2 %attend_own.1 = (f32[4,72,2048]{2,1,0:T(8,128)}, f32[4,1,2048]{2,1,0:T(1,128)}) custom-call(s32[6,8]{1,0:T(8,128)} %stack.23.table, bf16[2048,256]{1,0:T(8,128)(2,1)} %get-tuple-element.37.q, s32[1,2048]{1,0:T(1,128)} %bitcast.95, bf16[8,2,256,256]{3,2,1,0:T(8,128)(2,1)} %get-tuple-element.38.kv, s32[2048,1]{1,0:T(8,128)} %copy.38.kseg), custom_call_target="tpu_custom_call" | custom-call | flops 12884901888 | bytes 8388608 | tf_op jit(solution)/shard_map/attend_own/pallas_call | solution.py:233
  122.3 42.5 %collective-permute-done.9 = bf16[256,3328]{1,0:T(8,128)(2,1)S(1)} collective-permute-done((bf16[256,3328]{1,0:T(8,128)(2,1)}, bf16[256,3328]{1,0:T(8,128)(2,1)S(1)}, u32[]{:S(2)}, u32[]{:S(2)}) %collective-permute-start.9) | collective-permute-done | bytes 1703968 | tf_op jit(solution)/shard_map/ppermute | solution.py:378
  164.8 1.2 copy-done.9
  166.0 1.2 slice.83
  167.9 1.1 collective-permute-start.15
  169.1 8.2 %attend_halo.2.m0 = bf16[1024,256]{1,0:T(8,128)(2,1)} custom-call(s32[6,8]{1,0:T(8,128)} %stack.23.table, bf16[2048,256]{1,0:T(8,128)(2,1)} %get-tuple-element.37.q, s32[1,2048]{1,0:T(1,128)} %bitcast.96, bf16[8,2,256,256]{3,2,1,0:T(8,128)(2,1)} %collective-permute-done.lkv, s32[2048,1]{1,0:T(8,128)} %copy.39.lseg, ...), custom_call_target="tpu_custom_call" | custom-call | flops 12884901888 | bytes 8388608 | tf_op jit(solution)/shard_map/attend_halo/pallas_call | solution.py:233
  177.3 15.9 %collective-permute-start.11 = (bf16[1024,256]{1,0:T(8,128)(2,1)}, bf16[1024,256]{1,0:T(8,128)(2,1)S(1)}, u32[]{:S(2)}, u32[]{:S(2)}) collective-permute-start(bf16[1024,256]{1,0:T(8,128)(2,1)} %attend_halo.2.m0), channel_id=1, source_target_pairs={{0,2},{1,3},{2,0},{3,1},{4,6},{5,7},{6,4},{7,5},{8,10},{9,11},{10,... | collective-permute-start | bytes 1572872 | tf_op jit(solution)/shard_map/ppermute | solution.py:353
  193.2 3.7 %collective-permute-start.12 = (bf16[1024,256]{1,0:T(8,128)(2,1)}, bf16[1024,256]{1,0:T(8,128)(2,1)S(1)}, u32[]{:S(2)}, u32[]{:S(2)}) collective-permute-start(bf16[1024,256]{1,0:T(8,128)(2,1)} %attend_halo.2.m0), channel_id=1, source_target_pairs={{0,1},{1,0},{2,3},{3,2},{4,5},{5,4},{6,7},{7,6},{8,9},{9,8},{10,11... | collective-permute-start | bytes 1572872 | tf_op jit(solution)/shard_map/ppermute | solution.py:353
  196.9 12.0 %attend_halo.3.m0 = bf16[1024,256]{1,0:T(8,128)(2,1)} custom-call(s32[6,8]{1,0:T(8,128)} %stack.23.table, bf16[2048,256]{1,0:T(8,128)(2,1)} %get-tuple-element.37.q, s32[1,2048]{1,0:T(1,128)} %bitcast.97, bf16[8,2,256,256]{3,2,1,0:T(8,128)(2,1)} %collective-permute-done.lkv, s32[2048,1]{1,0:T(8,128)} %copy.39.lseg, ...), custom_call_target="tpu_custom_call" | custom-call | flops 12884901888 | bytes 8388608 | tf_op jit(solution)/shard_map/attend_halo/pallas_call | solution.py:233
  209.0 1.2 gather_fusion
  211.5 0.8 broadcast_in_dim.52.before
  212.4 16.1 %mlp.2 = (f32[1024,512]{1,0:T(8,128)}, bf16[1024,512]{1,0:T(8,128)(2,1)}, f32[2,64,512]{2,1,0:T(8,128)}) custom-call(s32[132]{0:T(256)} %pad_add_fusion.table, bf16[1024,256]{1,0:T(8,128)(2,1)} %attend_halo.2.m0, bf16[1024,256]{1,0:T(8,128)(2,1)} %copy-done.16, bf16[1024,256]{1,0:T(8,128)(2,1)} %copy-done.17, bf16[1024,256]{1,0:T(8,128)(2,1)} %collective-permute-done.13.m3, ...), custom_call_target="tpu_custom_call" | custom-call | flops 6979321856 | bytes 12582912 | tf_op jit(solution)/shard_map/mlp/pallas_call | solution.py:329
  228.6 1.9 collective-permute-done.18.m3
  230.5 0.8 copy-done.20
  231.3 16.3 %mlp.3 = (f32[1024,512]{1,0:T(8,128)}, bf16[1024,512]{1,0:T(8,128)(2,1)}, f32[2,64,512]{2,1,0:T(8,128)}) custom-call(s32[132]{0:T(256)} %pad_add_fusion.table, bf16[1024,256]{1,0:T(8,128)(2,1)} %attend_halo.3.m0, bf16[1024,256]{1,0:T(8,128)(2,1)} %copy-done.18, bf16[1024,256]{1,0:T(8,128)(2,1)} %copy-done.19, bf16[1024,256]{1,0:T(8,128)(2,1)} %copy-done.20, ...), custom_call_target="tpu_custom_call" | custom-call | flops 6979321856 | bytes 12582912 | tf_op jit(solution)/shard_map/mlp/pallas_call | solution.py:329
  247.6 1.0 fusion.14
  249.1 0.9 slice_bitcast_fusion
  250.2 1.7 collective-permute-start.20
  251.9 1.3 collective-permute-done.20
  253.2 1.5 collective-permute-start.21
  254.8 1.6 collective-permute-start.22
  256.4 2.0 collective-permute-start.23
  258.4 0.8 collective-permute-done.23
  259.9 4.9 %collective-permute-start.24 = (bf16[64,1024]{1,0:T(8,128)(2,1)S(1)}, bf16[64,1024]{1,0:T(8,128)(2,1)S(1)}, u32[]{:S(2)}, u32[]{:S(2)}) collective-permute-start(bf16[64,1024]{1,0:T(8,128)(2,1)S(1)} %bitcast.86), channel_id=1, source_target_pairs={{64,0},{68,4},{72,8},{76,12},{80,16},{84,20},{88,24},{92,28},{96,3... | collective-permute-start | bytes 393224 | tf_op jit(solution)/shard_map/ppermute | solution.py:378
  264.8 3.6 %collective-permute-done.24 = bf16[64,1024]{1,0:T(8,128)(2,1)S(1)} collective-permute-done((bf16[64,1024]{1,0:T(8,128)(2,1)S(1)}, bf16[64,1024]{1,0:T(8,128)(2,1)S(1)}, u32[]{:S(2)}, u32[]{:S(2)}) %collective-permute-start.24) | collective-permute-done | bytes 131104 | tf_op jit(solution)/shard_map/ppermute | solution.py:378
  268.4 0.9 collective-permute-start.25
  269.4 1.5 collective-permute-start.30
  271.5 3.0 collective-permute-done.29
  274.4 3.9 %collective-permute-done.30 = bf16[64,1024]{1,0:T(8,128)(2,1)S(1)} collective-permute-done((bf16[64,1024]{1,0:T(8,128)(2,1)S(1)}, bf16[64,1024]{1,0:T(8,128)(2,1)S(1)}, u32[]{:S(2)}, u32[]{:S(2)}) %collective-permute-start.30) | collective-permute-done | bytes 131104 | tf_op jit(solution)/shard_map/ppermute | solution.py:378
  278.5 2.8 collective-permute-start.33
  281.3 1.9 collective-permute-start.34
  284.4 3.6 %collective-permute-done.34 = bf16[64,1024]{1,0:T(8,128)(2,1)S(1)} collective-permute-done((bf16[64,1024]{1,0:T(8,128)(2,1)S(1)}, bf16[64,1024]{1,0:T(8,128)(2,1)S(1)}, u32[]{:S(2)}, u32[]{:S(2)}) %collective-permute-start.34) | collective-permute-done | bytes 131104 | tf_op jit(solution)/shard_map/ppermute | solution.py:378
  288.5 1.3 copy-done.5
  290.1 1.7 collective-permute-start.26
  293.7 1.1 copy-done.7
  295.3 21.0 %all_to_all.11 = f32[128,1,64]{2,1,0:T(1,128)S(1)} all-to-all(f32[128,1,64]{2,1,0:T(1,128)S(1)} %broadcast_in_dim.53), channel_id=1, replica_groups=mesh['req'=32,'tp'=4] {'req','tp'}, dimensions={0} | all-to-all | bytes 65536 | tf_op jit(solution)/shard_map/all_to_all | solution.py:391
  317.0 1.8 fusion.5
  319.0 1.7 fusion.2
  320.7 1.0 pad_maximum_fusion
  (128 shorter events, 15.3 us)
Async XLA Ops:
  0.6 282.6 %copy-start = (f32[4,1024]{1,0:T(4,128)S(1)}, f32[4,1024]{1,0:T(4,128)}, u32[]{:S(2)}) copy-start(f32[4,1024]{1,0:T(4,128)} %param.32) | copy-start | bytes 49156
  5.2 5.9 %copy-start.10 = (bf16[4,8,3328]{2,1,0:T(8,128)(2,1)S(1)}, bf16[4,8,3328]{2,1,0:T(8,128)(2,1)}, u32[]{:S(2)}) copy-start(bf16[4,8,3328]{2,1,0:T(8,128)(2,1)} %get-tuple-element.39) | copy-start | bytes 638980
  11.1 14.4 %copy-start.1 = (s32[128]{0:T(128)S(1)}, s32[128]{0:T(128)}, u32[]{:S(2)}) copy-start(s32[128]{0:T(128)} %param.21) | copy-start | bytes 1540
  11.1 14.5 %copy-start.13 = (s32[64]{0:T(128)S(1)}, s32[64]{0:T(128)}, u32[]{:S(2)}) copy-start(s32[64]{0:T(128)} %param.19) | copy-start | bytes 772
  11.2 15.9 %collective-permute-start.2 = (bf16[8,3328]{1,0:T(8,128)(2,1)S(1)}, bf16[8,3328]{1,0:T(8,128)(2,1)S(1)}, u32[]{:S(2)}, u32[]{:S(2)}) collective-permute-start(bf16[8,3328]{1,0:T(8,128)(2,1)S(1)} %get-tuple-element.74), channel_id=1, source_target_pairs={{0,2},{1,3},{2,0},{3,1},{4,6},{5,7},{6,4},{7,5},{8,10},{9,11},{10,... | collective-permute-start | bytes 159752 | tf_op jit(solution)/shard_map/ppermute | solution.py:353
  13.7 13.4 %collective-permute-start.3 = (bf16[8,3328]{1,0:T(8,128)(2,1)S(1)}, bf16[8,3328]{1,0:T(8,128)(2,1)S(1)}, u32[]{:S(2)}, u32[]{:S(2)}) collective-permute-start(bf16[8,3328]{1,0:T(8,128)(2,1)S(1)} %get-tuple-element.73), channel_id=1, source_target_pairs={{0,1},{1,0},{2,3},{3,2},{4,5},{5,4},{6,7},{7,6},{8,9},{9,8},{10,11... | collective-permute-start | bytes 159752 | tf_op jit(solution)/shard_map/ppermute | solution.py:353
  14.7 12.4 %collective-permute-start.4 = (bf16[8,3328]{1,0:T(8,128)(2,1)S(1)}, bf16[8,3328]{1,0:T(8,128)(2,1)S(1)}, u32[]{:S(2)}, u32[]{:S(2)}) collective-permute-start(bf16[8,3328]{1,0:T(8,128)(2,1)S(1)} %get-tuple-element.72), channel_id=1, source_target_pairs={{0,3},{1,2},{2,1},{3,0},{4,7},{5,6},{6,5},{7,4},{8,11},{9,10},{10,... | collective-permute-start | bytes 159752 | tf_op jit(solution)/shard_map/ppermute | solution.py:353
  14.7 58.5 %all-to-all-start = ((bf16[128,8,768]{2,1,0:T(8,128)(2,1)}), bf16[128,8,768]{2,1,0:T(8,128)(2,1)S(1)}, u32[]{:S(2)}, u32[]{:S(2)}) async-start(bf16[128,8,768]{2,1,0:T(8,128)(2,1)} %bitcast.9), calls=%async_computation | async-start | bytes 3145728 | tf_op jit(solution)/shard_map/all_to_all | solution.py:391
  27.1 24.7 %collective-permute-start.5 = (bf16[32,3328]{1,0:T(8,128)(2,1)S(1)}, bf16[32,3328]{1,0:T(8,128)(2,1)S(1)}, u32[]{:S(2)}, u32[]{:S(2)}) collective-permute-start(bf16[32,3328]{1,0:T(8,128)(2,1)S(1)} %pad_maximum_fusion.1), channel_id=1, source_target_pairs={{64,0},{68,4},{72,8},{76,12},{80,16},{84,20},{88,24},{92,28},{96,3... | collective-permute-start | bytes 638984 | tf_op jit(solution)/shard_map/ppermute | solution.py:378
  52.5 10.8 %collective-permute-start.6 = (bf16[64,3328]{1,0:T(8,128)(2,1)S(1)}, bf16[64,3328]{1,0:T(8,128)(2,1)S(1)}, u32[]{:S(2)}, u32[]{:S(2)}) collective-permute-start(bf16[64,3328]{1,0:T(8,128)(2,1)S(1)} %get-tuple-element.67), channel_id=1, source_target_pairs={{4,0},{8,4},{12,8},{0,12},{20,16},{24,20},{28,24},{16,28},{36,32},... | collective-permute-start | bytes 1277960 | tf_op jit(solution)/shard_map/ppermute | solution.py:378
  59.4 13.0 %collective-permute-start.7 = (bf16[64,3328]{1,0:T(8,128)(2,1)S(1)}, bf16[64,3328]{1,0:T(8,128)(2,1)S(1)}, u32[]{:S(2)}, u32[]{:S(2)}) collective-permute-start(bf16[64,3328]{1,0:T(8,128)(2,1)S(1)} %get-tuple-element.67), channel_id=1, source_target_pairs={{12,0},{0,4},{4,8},{8,12},{28,16},{16,20},{20,24},{24,28},{44,32},... | collective-permute-start | bytes 1277960 | tf_op jit(solution)/shard_map/ppermute | solution.py:378
  59.5 27.7 %collective-permute-start.8 = (bf16[64,3328]{1,0:T(8,128)(2,1)S(1)}, bf16[64,3328]{1,0:T(8,128)(2,1)S(1)}, u32[]{:S(2)}, u32[]{:S(2)}) collective-permute-start(bf16[64,3328]{1,0:T(8,128)(2,1)S(1)} %get-tuple-element.67), channel_id=1, source_target_pairs={{8,0},{12,4},{0,8},{4,12},{24,16},{28,20},{16,24},{20,28},{40,32},... | collective-permute-start | bytes 1277960 | tf_op jit(solution)/shard_map/ppermute | solution.py:378
  83.2 85.9 %collective-permute-start = (bf16[8,2,256,256]{3,2,1,0:T(8,128)(2,1)}, bf16[8,2,256,256]{3,2,1,0:T(8,128)(2,1)}, u32[]{:S(2)}, u32[]{:S(2)}) collective-permute-start(bf16[8,2,256,256]{3,2,1,0:T(8,128)(2,1)} %get-tuple-element.38.kv), channel_id=1, source_target_pairs={{0,4},{4,8},{8,12},{12,16},{16,20},{20,24},{24,28},{28,32},{32,36}... | collective-permute-start | bytes 6291464 | tf_op jit(solution)/shard_map/ppermute | solution.py:387
  85.9 83.2 %collective-permute-start.1 = (bf16[8,2,256,256]{3,2,1,0:T(8,128)(2,1)}, bf16[8,2,256,256]{3,2,1,0:T(8,128)(2,1)}, u32[]{:S(2)}, u32[]{:S(2)}) collective-permute-start(bf16[8,2,256,256]{3,2,1,0:T(8,128)(2,1)} %get-tuple-element.38.kv), channel_id=1, source_target_pairs={{4,0},{8,4},{12,8},{16,12},{20,16},{24,20},{28,24},{32,28},{36,32}... | collective-permute-start | bytes 6291464 | tf_op jit(solution)/shard_map/ppermute | solution.py:387
  88.0 34.3 %collective-permute-start.10 = (bf16[256,3328]{1,0:T(8,128)(2,1)}, bf16[256,3328]{1,0:T(8,128)(2,1)S(1)}, u32[]{:S(2)}, u32[]{:S(2)}) collective-permute-start(bf16[256,3328]{1,0:T(8,128)(2,1)} %constant_dynamic-update-slice_fusion.5), channel_id=1, source_target_pairs={{48,0},{52,4},{56,8},{60,12},{0,16},{4,20},{8,24},{12,28},{16,32},... | collective-permute-start | bytes 5111816 | tf_op jit(solution)/shard_map/ppermute | solution.py:378
  93.0 71.8 %collective-permute-start.9 = (bf16[256,3328]{1,0:T(8,128)(2,1)}, bf16[256,3328]{1,0:T(8,128)(2,1)S(1)}, u32[]{:S(2)}, u32[]{:S(2)}) collective-permute-start(bf16[256,3328]{1,0:T(8,128)(2,1)} %constant_dynamic-update-slice_fusion.5), channel_id=1, source_target_pairs={{16,0},{20,4},{24,8},{28,12},{32,16},{36,20},{40,24},{44,28},{48,3... | collective-permute-start | bytes 5111816 | tf_op jit(solution)/shard_map/ppermute | solution.py:378
  94.2 5.0 %copy-start.11 = (s32[2048]{0:T(1024)}, s32[2048]{0:T(1024)S(1)}, u32[]{:S(2)}) copy-start(s32[2048]{0:T(1024)S(1)} %get-tuple-element.85) | copy-start | bytes 24580
  122.3 45.6 %copy-start.8 = (bf16[256,3328]{1,0:T(8,128)(2,1)}, bf16[256,3328]{1,0:T(8,128)(2,1)S(1)}, u32[]{:S(2)}) copy-start(bf16[256,3328]{1,0:T(8,128)(2,1)S(1)} %collective-permute-done.10) | copy-start | bytes 5111812
  164.8 1.2 copy-start.9
  167.2 43.7 %collective-permute-start.14 = (bf16[128,3328]{1,0:T(8,128)(2,1)S(1)}, bf16[128,3328]{1,0:T(8,128)(2,1)}, u32[]{:S(2)}, u32[]{:S(2)}) collective-permute-start(bf16[128,3328]{1,0:T(8,128)(2,1)S(1)} %slice.83), channel_id=1, source_target_pairs={{16,0},{20,4},{24,8},{28,12},{32,16},{36,20},{40,24},{44,28},{48,3... | collective-permute-start | bytes 2555912 | tf_op jit(solution)/shard_map/ppermute | solution.py:378
  167.9 43.5 %collective-permute-start.15 = (bf16[128,3328]{1,0:T(8,128)(2,1)S(1)}, bf16[128,3328]{1,0:T(8,128)(2,1)}, u32[]{:S(2)}, u32[]{:S(2)}) collective-permute-start(bf16[128,3328]{1,0:T(8,128)(2,1)S(1)} %slice.84), channel_id=1, source_target_pairs={{48,0},{52,4},{56,8},{60,12},{0,16},{4,20},{8,24},{12,28},{16,32},... | collective-permute-start | bytes 2555912 | tf_op jit(solution)/shard_map/ppermute | solution.py:378
  177.3 33.0 %copy-start.2 = (s32[4]{0:T(128)S(1)}, s32[4]{0:T(128)}, u32[]{:S(2)}) copy-start(s32[4]{0:T(128)} %constant.222.clone) | copy-start | bytes 52
  177.3 31.6 %collective-permute-start.11 = (bf16[1024,256]{1,0:T(8,128)(2,1)}, bf16[1024,256]{1,0:T(8,128)(2,1)S(1)}, u32[]{:S(2)}, u32[]{:S(2)}) collective-permute-start(bf16[1024,256]{1,0:T(8,128)(2,1)} %attend_halo.2.m0), channel_id=1, source_target_pairs={{0,2},{1,3},{2,0},{3,1},{4,6},{5,7},{6,4},{7,5},{8,10},{9,11},{10,... | collective-permute-start | bytes 1572872 | tf_op jit(solution)/shard_map/ppermute | solution.py:353
  193.2 18.3 %collective-permute-start.12 = (bf16[1024,256]{1,0:T(8,128)(2,1)}, bf16[1024,256]{1,0:T(8,128)(2,1)S(1)}, u32[]{:S(2)}, u32[]{:S(2)}) collective-permute-start(bf16[1024,256]{1,0:T(8,128)(2,1)} %attend_halo.2.m0), channel_id=1, source_target_pairs={{0,1},{1,0},{2,3},{3,2},{4,5},{5,4},{6,7},{7,6},{8,9},{9,8},{10,11... | collective-permute-start | bytes 1572872 | tf_op jit(solution)/shard_map/ppermute | solution.py:353
  208.9 3.4 %copy-start.16 = (bf16[1024,256]{1,0:T(8,128)(2,1)}, bf16[1024,256]{1,0:T(8,128)(2,1)S(1)}, u32[]{:S(2)}) copy-start(bf16[1024,256]{1,0:T(8,128)(2,1)S(1)} %collective-permute-done.11.m1) | copy-start | bytes 1572868
  208.9 2.6 collective-permute-start.13
  210.9 17.6 %collective-permute-start.16 = (bf16[1024,256]{1,0:T(8,128)(2,1)}, bf16[1024,256]{1,0:T(8,128)(2,1)S(1)}, u32[]{:S(2)}, u32[]{:S(2)}) collective-permute-start(bf16[1024,256]{1,0:T(8,128)(2,1)} %attend_halo.3.m0), channel_id=1, source_target_pairs={{0,2},{1,3},{2,0},{3,1},{4,6},{5,7},{6,4},{7,5},{8,10},{9,11},{10,... | collective-permute-start | bytes 1572872 | tf_op jit(solution)/shard_map/ppermute | solution.py:353
  210.9 17.7 %collective-permute-start.17 = (bf16[1024,256]{1,0:T(8,128)(2,1)}, bf16[1024,256]{1,0:T(8,128)(2,1)S(1)}, u32[]{:S(2)}, u32[]{:S(2)}) collective-permute-start(bf16[1024,256]{1,0:T(8,128)(2,1)} %attend_halo.3.m0), channel_id=1, source_target_pairs={{0,1},{1,0},{2,3},{3,2},{4,5},{5,4},{6,7},{7,6},{8,9},{9,8},{10,11... | collective-permute-start | bytes 1572872 | tf_op jit(solution)/shard_map/ppermute | solution.py:353
  211.5 0.9 copy-start.17
  228.5 2.0 copy-start.18
  228.5 2.0 collective-permute-start.18
  228.6 1.9 copy-start.19
  230.5 0.8 copy-start.20
  231.3 23.5 %copy-start.12 = (s32[4]{0:T(128)S(1)}, s32[4]{0:T(128)}, u32[]{:S(2)}) copy-start(s32[4]{0:T(128)} %gather_fusion.1) | copy-start | bytes 52
  247.6 20.8 %copy-start.15 = (bf16[1024,512]{1,0:T(8,128)(2,1)S(1)}, bf16[1024,512]{1,0:T(8,128)(2,1)}, u32[]{:S(2)}) copy-start(bf16[1024,512]{1,0:T(8,128)(2,1)} %get-tuple-element.55) | copy-start | bytes 3145732
  247.6 35.6 %copy-start.14 = (s32[64]{0:T(128)S(1)}, s32[64]{0:T(128)}, u32[]{:S(2)}) copy-start(s32[64]{0:T(128)} %param.20) | copy-start | bytes 772
  248.6 1.6 collective-permute-start.19
  250.2 3.0 collective-permute-start.20
  253.2 3.2 collective-permute-start.21
  254.8 3.6 %collective-permute-start.22 = (bf16[64,256]{1,0:T(8,128)(2,1)S(1)}, bf16[64,256]{1,0:T(8,128)(2,1)S(1)}, u32[]{:S(2)}, u32[]{:S(2)}) collective-permute-start(bf16[64,256]{1,0:T(8,128)(2,1)S(1)} %fusion.17), channel_id=1, source_target_pairs={{0,1},{1,0},{2,3},{3,2},{4,5},{5,4},{6,7},{7,6},{8,9},{9,8},{10,11... | collective-permute-start | bytes 98312 | tf_op jit(solution)/shard_map/ppermute | solution.py:353
  256.4 2.9 collective-permute-start.23
  259.9 8.5 %collective-permute-start.24 = (bf16[64,1024]{1,0:T(8,128)(2,1)S(1)}, bf16[64,1024]{1,0:T(8,128)(2,1)S(1)}, u32[]{:S(2)}, u32[]{:S(2)}) collective-permute-start(bf16[64,1024]{1,0:T(8,128)(2,1)S(1)} %bitcast.86), channel_id=1, source_target_pairs={{64,0},{68,4},{72,8},{76,12},{80,16},{84,20},{88,24},{92,28},{96,3... | collective-permute-start | bytes 393224 | tf_op jit(solution)/shard_map/ppermute | solution.py:378
  268.4 19.8 %collective-permute-start.25 = (bf16[1024,512]{1,0:T(8,128)(2,1)S(1)}, bf16[1024,512]{1,0:T(8,128)(2,1)S(1)}, u32[]{:S(2)}, u32[]{:S(2)}) collective-permute-start(bf16[1024,512]{1,0:T(8,128)(2,1)S(1)} %copy-done.15), channel_id=1, source_target_pairs={{0,1},{1,0},{2,3},{3,2},{4,5},{5,4},{6,7},{7,6},{8,9},{9,8},{10,11... | collective-permute-start | bytes 3145736 | tf_op jit(solution)/shard_map/ppermute | solution.py:353
  269.4 5.1 %collective-permute-start.29 = (bf16[64,1024]{1,0:T(8,128)(2,1)S(1)}, bf16[64,1024]{1,0:T(8,128)(2,1)S(1)}, u32[]{:S(2)}, u32[]{:S(2)}) collective-permute-start(bf16[64,1024]{1,0:T(8,128)(2,1)S(1)} %add.476), channel_id=1, source_target_pairs={{4,0},{8,4},{12,8},{0,12},{20,16},{24,20},{28,24},{16,28},{36,32},... | collective-permute-start | bytes 393224 | tf_op jit(solution)/shard_map/ppermute | solution.py:378
  269.4 9.0 %collective-permute-start.30 = (bf16[64,1024]{1,0:T(8,128)(2,1)S(1)}, bf16[64,1024]{1,0:T(8,128)(2,1)S(1)}, u32[]{:S(2)}, u32[]{:S(2)}) collective-permute-start(bf16[64,1024]{1,0:T(8,128)(2,1)S(1)} %add.476), channel_id=1, source_target_pairs={{12,0},{0,4},{4,8},{8,12},{28,16},{16,20},{20,24},{24,28},{44,32},... | collective-permute-start | bytes 393224 | tf_op jit(solution)/shard_map/ppermute | solution.py:378
  270.8 7.5 %collective-permute-start.31 = (bf16[64,1024]{1,0:T(8,128)(2,1)S(1)}, bf16[64,1024]{1,0:T(8,128)(2,1)S(1)}, u32[]{:S(2)}, u32[]{:S(2)}) collective-permute-start(bf16[64,1024]{1,0:T(8,128)(2,1)S(1)} %add.476), channel_id=1, source_target_pairs={{8,0},{12,4},{0,8},{4,12},{24,16},{28,20},{16,24},{20,28},{40,32},... | collective-permute-start | bytes 393224 | tf_op jit(solution)/shard_map/ppermute | solution.py:378
  270.9 21.5 %collective-permute-start.27 = (bf16[1024,512]{1,0:T(8,128)(2,1)}, bf16[1024,512]{1,0:T(8,128)(2,1)S(1)}, u32[]{:S(2)}, u32[]{:S(2)}) collective-permute-start(bf16[1024,512]{1,0:T(8,128)(2,1)} %get-tuple-element.57), channel_id=1, source_target_pairs={{0,1},{1,0},{2,3},{3,2},{4,5},{5,4},{6,7},{7,6},{8,9},{9,8},{10,11... | collective-permute-start | bytes 3145736 | tf_op jit(solution)/shard_map/ppermute | solution.py:353
  278.4 5.7 %collective-permute-start.32 = (bf16[64,1024]{1,0:T(8,128)(2,1)S(1)}, bf16[64,1024]{1,0:T(8,128)(2,1)S(1)}, u32[]{:S(2)}, u32[]{:S(2)}) collective-permute-start(bf16[64,1024]{1,0:T(8,128)(2,1)S(1)} %add_add_fusion.1), channel_id=1, source_target_pairs={{16,0},{20,4},{24,8},{28,12},{32,16},{36,20},{40,24},{44,28},{48,3... | collective-permute-start | bytes 393224 | tf_op jit(solution)/shard_map/ppermute | solution.py:378
  278.5 5.9 %collective-permute-start.33 = (bf16[64,1024]{1,0:T(8,128)(2,1)S(1)}, bf16[64,1024]{1,0:T(8,128)(2,1)S(1)}, u32[]{:S(2)}, u32[]{:S(2)}) collective-permute-start(bf16[64,1024]{1,0:T(8,128)(2,1)S(1)} %add_add_fusion.1), channel_id=1, source_target_pairs={{48,0},{52,4},{56,8},{60,12},{0,16},{4,20},{8,24},{12,28},{16,32},... | collective-permute-start | bytes 393224 | tf_op jit(solution)/shard_map/ppermute | solution.py:378
  281.3 6.7 %collective-permute-start.34 = (bf16[64,1024]{1,0:T(8,128)(2,1)S(1)}, bf16[64,1024]{1,0:T(8,128)(2,1)S(1)}, u32[]{:S(2)}, u32[]{:S(2)}) collective-permute-start(bf16[64,1024]{1,0:T(8,128)(2,1)S(1)} %add_add_fusion.1), channel_id=1, source_target_pairs={{32,0},{36,4},{40,8},{44,12},{48,16},{52,20},{56,24},{60,28},{0,32... | collective-permute-start | bytes 393224 | tf_op jit(solution)/shard_map/ppermute | solution.py:378
  288.2 1.6 copy-start.5
  290.0 2.5 copy-start.6
  290.1 26.9 %collective-permute-start.26 = (bf16[1024,256]{1,0:T(8,128)(2,1)S(1)}, bf16[1024,256]{1,0:T(8,128)(2,1)}, u32[]{:S(2)}, u32[]{:S(2)}) collective-permute-start(bf16[1024,256]{1,0:T(8,128)(2,1)S(1)} %fusion.3), channel_id=1, source_target_pairs={{0,2},{1,3},{2,0},{3,1},{4,6},{5,7},{6,4},{7,5},{8,10},{9,11},{10,... | collective-permute-start | bytes 1572872 | tf_op jit(solution)/shard_map/ppermute | solution.py:353
  292.6 2.6 copy-start.3
  292.6 2.2 copy-start.7
  292.9 25.8 %collective-permute-start.28 = (bf16[1024,256]{1,0:T(8,128)(2,1)S(1)}, bf16[1024,256]{1,0:T(8,128)(2,1)}, u32[]{:S(2)}, u32[]{:S(2)}) collective-permute-start(bf16[1024,256]{1,0:T(8,128)(2,1)S(1)} %fusion), channel_id=1, source_target_pairs={{0,2},{1,3},{2,0},{3,1},{4,6},{5,7},{6,4},{7,5},{8,10},{9,11},{10,... | collective-permute-start | bytes 1572872 | tf_op jit(solution)/shard_map/ppermute | solution.py:353
  317.0 2.1 copy-start.4

commit v5 on v4

--- a/solution.py
+++ b/solution.py
@@ -146,6 +146,49 @@
         cost_estimate=cost(2 * rows * 1024 * 768, 12 << 20),
         name="qkv",
     )(x, w, cos, sin)
+
+
+def halo_kv_kernel(order, x0, x1, w, cos, sin, kv):
+    x = jnp.where(pl.program_id(0) < 2, x0[...], x1[...])
+    y = jnp.dot(x, w[...], preferred_element_type=F32)
+    c = cos[...]
+    s = sin[...]
+    k = jnp.concatenate(
+        [y[:, :128] * c - y[:, 128:256] * s, y[:, 128:256] * c + y[:, :128] * s], axis=1
+    ).astype(BF)
+    v = y[:, 256:].astype(BF)
+    for n in range(x.shape[0] // KB):
+        kv[n, 0] = k[KB * n : KB * n + KB]
+        kv[n, 1] = jnp.transpose(v[KB * n : KB * n + KB])
+
+
+def halo_project(order, x0, x1, w, cos, sin):
+    rows = 2 * x0.shape[0]
+    n = 512
+    half = rows // n // 2
+
+    def place(i, order):
+        return (i // half ^ order[0]) * half + i % half
+
+    return pl.pallas_call(
+        halo_kv_kernel,
+        grid_spec=pltpu.PrefetchScalarGridSpec(
+            num_scalar_prefetch=1,
+            grid=(rows // n,),
+            in_specs=[
+                pl.BlockSpec((n, 1024), lambda i, o: (jnp.minimum(i, half - 1), 0)),
+                pl.BlockSpec((n, 1024), lambda i, o: (jnp.maximum(i - half, 0), 0)),
+                vmem(1024, 512),
+                pl.BlockSpec((n, 128), lambda i, o: (place(i, o), 0)),
+                pl.BlockSpec((n, 128), lambda i, o: (place(i, o), 0)),
+            ],
+            out_specs=pl.BlockSpec((n // KB, 2, KB, 256), lambda i, o: (place(i, o), 0, 0, 0)),
+        ),
+        out_shape=jax.ShapeDtypeStruct((rows // KB, 2, KB, 256), BF),
+        compiler_params=params(),
+        cost_estimate=cost(2 * rows * 1024 * 512, 12 << 20),
+        name="halo_kv",
+    )(order, x0, x1, w, cos, sin)
 
 
 VR = HEAD_DIM + 8
@@ -370,18 +413,6 @@
     return (mine + swap(send, 2).astype(F32)).astype(BF)
 
 
-def from_offset(x, dx, dy, dz=0):
-    pairs = []
-    for i in range(32):
-        far = (i // 16 + dz) % 2 * 16 + (i // 4 + dx) % 4 * 4 + (i + dy) % 4
-        pairs.append((far, i))
-    return lax.ppermute(x, "req", pairs)
-
-
-def sum_req(x, moves):
-    return sum([from_offset(x, *move) for move in moves], x)
-
-
 def shift(x, by):
     count = lax.axis_size("req")
     return lax.ppermute(x, "req", [(i, i + by) for i in range(count) if 0 <= i + by < count])
@@ -428,15 +459,15 @@
     index = base - slots + jnp.arange(3 * slots, dtype=jnp.int32)
     segment = jnp.sum((ends[None, :] <= index[:, None]).astype(jnp.int32), axis=1)
     segment = jnp.where((index >= 0) & (index < slots * req_count), segment, -1)
-    own = base + jnp.arange(slots, dtype=jnp.int32)
-    start_of = jnp.max(jnp.where(ends[None, :] <= own[:, None], ends[None, :], 0), axis=1)
-    position = (own - start_of).astype(F32)
-    half = HEAD_DIM // 2
-    lane = jnp.arange(128, dtype=jnp.int32) % half
+    start_of = jnp.max(jnp.where(ends[None, :] <= index[:, None], ends[None, :], 0), axis=1)
+    position = (index - start_of).astype(F32)
+    lane = jnp.arange(128, dtype=jnp.int32) % (HEAD_DIM // 2)
     freq = THETA ** (-(2.0 * lane.astype(F32)) / HEAD_DIM)
-    angle = position[:, None] * freq[None, :]
-    cos = jnp.cos(angle)
-    sin = jnp.sin(angle)
+    turns = []
+    for n in range(3):
+        angle = position[n * slots : (n + 1) * slots, None] * freq[None, :]
+        turns.append((jnp.cos(angle), jnp.sin(angle)))
+
     begin = base + jnp.arange(slots // QB, dtype=jnp.int32) * QB
     close = begin + QB - 1
     low = jnp.max(jnp.where(ends[None, :] <= begin[:, None], ends[None, :], 0), axis=1) - base
@@ -456,39 +487,34 @@
     later, qkv_block = lax.optimization_barrier((hidden_in, qkv_block))
     normed = norm(later, attn_gain)
     rest_block, normed = lax.optimization_barrier((rest_block, normed))
+    half = slots // 2
+    mine = lax.dynamic_slice_in_dim(normed, tp_index % 2 * half, half, 0)
+    sides = (shift(mine, 1), shift(mine, -1))
     rest_rows = jnp.concatenate(
         [rest_block[0], swap(rest_block[1], 2), swap(rest_block[2], 1), swap(rest_block[3], 3)], axis=0
     )
-    level = jnp.concatenate([rest_rows, from_offset(rest_rows, 0, 0, 1)], axis=0)
-    level = jnp.concatenate([level] + [from_offset(level, 0, d) for d in (1, 3, 2)], axis=0)
-    ahead = from_offset(level, 1, 0)
-    behind = from_offset(level, 3, 0)
+    grid = [[[z * 16 + x * 4 + y for x in range(4)] for y in range(4)] for z in range(2)]
+    plane = [[grid[z][y][x] for z in range(2) for y in range(4)] for x in range(4)]
+    column = [grid[z][y] for z in range(2) for y in range(4)]
+    rest = lax.all_gather(rest_rows, "req", axis=0, tiled=True, axis_index_groups=plane)
+    qkv_all = exchange(qkv_block.reshape(count, 8, 768), BOTH)
+    rest, qkv_all = lax.optimization_barrier((rest, qkv_all))
+    rest = lax.all_gather(rest, "req", axis=0, tiled=True, axis_index_groups=column)
+    rest = [rest.reshape(count, 8, REST)]
     far = jnp.arange(count, dtype=jnp.int32)
-    slot_x, slot_y = (jnp.array([0, 1, 3, 2], jnp.int32)[n] for n in (far // 32, far // 8 % 4))
-    from_req = (
-        (req_index // 16 + far // 4) % 2 * 16
-        + (req_index // 4 + slot_x) % 4 * 4
-        + (req_index + slot_y) % 4
-    )
+    from_req = far // 16 % 2 * 16 + far // 32 * 4 + far // 4 % 4
     rest_target = shard_map[from_req * tp_count + (tp_index ^ tp_order[far % 4])]
-    qkv_all = exchange(qkv_block.reshape(count, 8, 768), BOTH)
     qkv_w = qkv_all[source].reshape(width, 768)
-    query, kv, cache = qkv_project(normed, qkv_w, cos, sin)
-    left = shift(kv, 1)
-    right = shift(kv, -1)
+    query, kv, cache = qkv_project(normed, qkv_w, *turns[1])
     parts = 2
     state = attend(0, 1, table, query, qseg, (kv, segs[1]), ())
-    ahead, behind, state = lax.optimization_barrier((ahead, behind, state))
-    rest = [
-        piece.reshape(-1, 8, REST)
-        for piece in (
-            level,
-            ahead,
-            behind,
-            from_offset(ahead[:128], 1, 0),
-            from_offset(behind[128:], 3, 0),
-        )
-    ]
+    core = (tp_index % 2).reshape(1)
+    others = [swap(side, 1) for side in sides]
+    others, state = lax.optimization_barrier((others, state))
+    left, right = (
+        halo_project(core, side, other, qkv_w[:, 256:], *turn)
+        for side, other, turn in zip(sides, others, (turns[0], turns[2]))
+    )
     mixed = [
         attend(part, parts, table, query, qseg, (left, segs[0], right, segs[2]), state)
         for part in range(parts)
@@ -513,14 +539,18 @@
         after = (keep, send)
         bulk.append((keep, send))
 
-    pieces = gather_tp(reduce_far(*reduce_core(picked[0], picked[1].astype(BF))))
-    wide = jnp.stack(pieces)[place_of].transpose(1, 0, 2).reshape(requests, width)
-    wide = sum_req(wide, ((0, 0, 1),))
-    bulk, wide = lax.optimization_barrier((bulk, wide))
+    each = requests // req_count
+    last_mine = reduce_far(*reduce_core(picked[0], picked[1].astype(BF)))
+    bulk, last_mine = lax.optimization_barrier((bulk, last_mine))
+    taken = exchange(last_mine.reshape(req_count, each, 256), "req").astype(F32).sum(axis=0)
+    spread = exchange(jnp.broadcast_to(taken.astype(BF)[None], (count, each, 256)), BOTH)
     hidden_out = jnp.concatenate([reduce_far(*reduce_core(*pair)) for pair in bulk], axis=0)
-    wide = sum_req(wide, tuple((0, d, 0) for d in (1, 3, 2)))
-    wide = sum_req(wide, tuple((d, 0, 0) for d in (1, 3, 2)))
-    last = wide.astype(F32)
+    last = (
+        spread.reshape(req_count, tp_count, each, 256)
+        .transpose(0, 2, 1, 3)
+        .reshape(requests, width)
+        .astype(F32)
+    )
     last_rms = jnp.sqrt(jnp.mean(last * last, axis=-1))
     choose = (tenant[:, None] == jnp.arange(final_gain.shape[0], dtype=jnp.int32)[None, :]).astype(
         F32

time: 327 us -> 410 us (1.25); the launches traced: 322 us -> 410 us
  blocking collectives: 21 us -> 132 us
  starting transfers between devices: 74.9 us -> 28.4 us
  between operations: 1.23 us -> 14.5 us
  Pallas kernels: 92.4 us -> 104 us
  other arithmetic: 14.9 us -> 25.5 us
  waiting for transfers between devices: 91.7 us -> 84.4 us
  local copies, waits for them, and re-layouts: 24.8 us -> 19.9 us
    all_to_all x1 -> x3, blocking collectives: 21 us -> 132 us  [exchange(): return lax.all_to_all(x, axes, split_axis=0, concat_axis=0, tiled=True)]
    ppermute x15 -> x0, waiting for transfers between devices: 87.5 us -> none  [from_offset(): return lax.ppermute(x, 'req', pairs)]
    ppermute x2, waiting for transfers between devices: 0.01 us -> 35.1 us  [shift(): lax.ppermute(x, 'req', [(i, i + by) for i in range(count) if 0 <= i + by...]
    all_gather x0 -> x2, waiting for transfers between devices: none -> 32.4 us  [the longest x1 32.4 us: body(): lax.all_gather(rest_rows, 'req', axis=0, tiled=True, axis_index_groups=pl...]
    ppermute x15 -> x0, starting transfers between devices: 25.5 us -> none  [from_offset(): return lax.ppermute(x, 'req', pairs)]
    ppermute x18 -> x17, starting transfers between devices: 35.2 us -> 16.7 us  [swap(): return lax.ppermute(x, 'tp', [(i, i ^ bit) for i in range(4)])]
    pallas_call x0 -> x2, Pallas kernels: none -> 13.6 us  [halo_project(): pl.pallas_call(halo_kv_kernel, grid_spec=pltpu.PrefetchScalarGridSpec(num...]
    all_to_all x1, waiting for transfers between devices: 0.01 us -> 8.72 us  [exchange(): return lax.all_to_all(x, axes, split_axis=0, concat_axis=0, tiled=True)]
  transfers between devices with their start and end apart: 36 -> 22, of which waited for: 14 -> 10; matrix products, arithmetic and copies ran while one was open for 9% -> 9% of each run, Pallas kernels for 21% -> 19%
where the time goes in v5:
time: 410 us
  blocking collectives  132 us (32%)
  Pallas kernels  104 us (25%)
  waiting for transfers between devices  84.4 us (21%)
  starting transfers between devices  28.4 us (7%)
  other arithmetic  25.5 us (6%)
  local copies, waits for them, and re-layouts  19.9 us (5%)
  between operations  14.5 us (4%)
    all_to_all x3, blocking collectives, exchange(): return lax.all_to_all(x, axes, split_axis=0, concat_axis=0, tiled=True)  132 us
    pallas_call x3, Pallas kernels, attend(): pl.pallas_call(kernel, grid_spec=pltpu.PrefetchScalarGridSpec(num_scalar_...  41.6 us
    ppermute x2, waiting for transfers between devices, shift(): lax.ppermute(x, 'req', [(i, i + by) for i in range(count) if 0 <= i + by...  35.1 us
    all_gather x1, waiting for transfers between devices, body(): lax.all_gather(rest_rows, 'req', axis=0, tiled=True, axis_index_groups=pl...  32.4 us
    pallas_call x2, Pallas kernels, mlp(): pl.pallas_call(functools.partial(mlp_kernel, base), grid_spec=pltpu.Prefe...  32.3 us
    ppermute x17, starting transfers between devices, swap(): return lax.ppermute(x, 'tp', [(i, i ^ bit) for i in range(4)])  16.7 us
    pallas_call x2, Pallas kernels, halo_project(): pl.pallas_call(halo_kv_kernel, grid_spec=pltpu.PrefetchScalarGridSpec(num...  13.6 us
    sin x1, other arithmetic, body(): turns.append((jnp.cos(angle), jnp.sin(angle)))  13.4 us
  transfers between devices with their start and end apart: 22, of which 10 were waited for; matrix products, arithmetic and copies ran while one was open for 9% of the time, Pallas kernels for 19%

profile of v5, /device:TPU:1, one launch (start us, length us, event | category | flops | bytes accessed | tf_op | source)
XLA Modules:
  0.0 409.9 jit_solution(12340447746870862966)
XLA Ops:
  7.3 1.8 gather_fusion.1
  9.1 2.6 prep.1
  11.7 6.0 %norm.1.x = bf16[2048,1024]{1,0:T(8,128)(2,1)} custom-call(bf16[2048,1024]{1,0:T(8,128)(2,1)} %h.4, f32[1,1024]{1,0:T(1,128)} %bitcast.92), custom_call_target="tpu_custom_call" | custom-call | flops 16777216 | bytes 8388608 | tf_op jit(solution)/shard_map/norm/pallas_call | solution.py:87
  17.7 2.5 collective-permute-start
  20.3 1.0 collective-permute-start.1
  21.2 0.6 collective-permute-done
  22.1 2.7 collective-permute-done.2
  24.8 0.7 pad_maximum_fusion.1
  25.6 34.1 %all_to_all.21 = bf16[128,8,768]{2,1,0:T(8,128)(2,1)S(1)} all-to-all(bf16[128,8,768]{2,1,0:T(8,128)(2,1)S(1)} %bitcast.82), channel_id=1, replica_groups=mesh['req'=32,'tp'=4] {'req','tp'}, dimensions={0} | all-to-all | bytes 3145728 | tf_op jit(solution)/shard_map/all_to_all | solution.py:422
  59.6 32.4 %all-gather.3.cloned.1.call-done = bf16[256,3328]{1,0:T(8,128)(2,1)} async-done(((bf16[32,3328]{1,0:T(8,128)(2,1)}), bf16[256,3328]{1,0:T(8,128)(2,1)}) %all-gather.3.cloned.1.call-update) | async-done | bytes 1703952 | tf_op jit(solution)/shard_map/all_gather | solution.py:499
  92.1 3.1 constant_dynamic-slice_fusion
  95.1 4.1 %collective-permute-start.3 = (bf16[1024,1024]{1,0:T(8,128)(2,1)}, bf16[1024,1024]{1,0:T(8,128)(2,1)}, u32[]{:S(2)}, u32[]{:S(2)}) collective-permute-start(bf16[1024,1024]{1,0:T(8,128)(2,1)} %constant_dynamic-slice_fusion), channel_id=1, source_target_pairs={{0,4},{4,8},{8,12},{12,16},{16,20},{20,24},{24,28},{28,32},{32,36}... | collective-permute-start | bytes 6291464 | tf_op jit(solution)/shard_map/ppermute | solution.py:418
  99.3 1.3 collective-permute-start.5
  100.8 0.7 add_subtract_fusion
  101.5 0.5 fusion.1
  102.0 1.4 copy.42.kseg
  103.4 1.4 copy.43.lseg
  104.8 1.3 copy.44.rseg
  106.4 0.6 stack.2.table
  107.2 33.3 %collective-permute-done.3.x0 = bf16[1024,1024]{1,0:T(8,128)(2,1)} collective-permute-done((bf16[1024,1024]{1,0:T(8,128)(2,1)}, bf16[1024,1024]{1,0:T(8,128)(2,1)}, u32[]{:S(2)}, u32[]{:S(2)}) %collective-permute-start.3) | collective-permute-done | bytes 2097184 | tf_op jit(solution)/shard_map/ppermute | solution.py:418
  140.5 3.4 collective-permute-start.4
  144.0 1.8 collective-permute-done.5.x0
  145.8 3.7 collective-permute-start.6
  149.5 13.4 %multiply_sine_fusion = (f32[2048,128]{1,0:T(8,128)}, f32[2048,128]{1,0:T(8,128)}, f32[2048,128]{1,0:T(8,128)}, f32[2048,128]{1,0:T(8,128)}, f32[2048,128]{1,0:T(8,128)}, /*index=5*/f32[2048,128]{1,0:T(8,128)}) fusion(f32[2048]{0:T(1024)S(1)} %get-tuple-element.81, f32[128]{0:T(128)S(1)} %fusion.29, f32[2048]{0:T(1024)S(1)} %get-tuple-element.82, ...), kind=kLoop, calls=%fused_computation.7 | loop fusion | flops 786432 | bytes 6316544 | tf_op jit(solution)/shard_map/sin | solution.py:469
  162.9 0.7 gather_fusion.2
  163.6 1.1 slice.121.w
  165.1 8.2 %qkv.1 = (bf16[2048,256]{1,0:T(8,128)(2,1)}, bf16[8,2,256,256]{3,2,1,0:T(8,128)(2,1)}, bf16[2,2048,256]{2,1,0:T(8,128)(2,1)}) custom-call(bf16[2048,1024]{1,0:T(8,128)(2,1)} %norm.1.x, bf16[1024,768]{1,0:T(8,128)(2,1)} %bitcast.81, f32[2048,128]{1,0:T(8,128)} %get-tuple-element.94.cos, f32[2048,128]{1,0:T(8,128)} %get-tuple-element.95.sin), custom_call_target="tpu_custom_call" | custom-call | flops 3221225472 | bytes 12582912 | tf_op jit(solution)/shard_map/qkv/pallas_call | solution.py:126
  173.3 21.6 %attend_own.1 = (f32[4,72,2048]{2,1,0:T(8,128)}, f32[4,1,2048]{2,1,0:T(1,128)}) custom-call(s32[6,8]{1,0:T(8,128)} %stack.2.table, bf16[2048,256]{1,0:T(8,128)(2,1)} %get-tuple-element.41.q, s32[1,2048]{1,0:T(1,128)} %bitcast.87, bf16[8,2,256,256]{3,2,1,0:T(8,128)(2,1)} %get-tuple-element.42.kv, s32[2048,1]{1,0:T(8,128)} %copy.42.kseg), custom_call_target="tpu_custom_call" | custom-call | flops 12884901888 | bytes 8388608 | tf_op jit(solution)/shard_map/attend_own/pallas_call | solution.py:276
  195.0 6.8 %halo_kv.3.rkv = bf16[8,2,256,256]{3,2,1,0:T(8,128)(2,1)} custom-call(s32[1]{0:T(128)} %bitcast.18.order, bf16[1024,1024]{1,0:T(8,128)(2,1)} %collective-permute-done.5.x0, bf16[1024,1024]{1,0:T(8,128)(2,1)} %collective-permute-done.6.x1, bf16[1024,512]{1,0:T(8,128)(2,1)} %slice.121.w, f32[2048,128]{1,0:T(8,128)} %get-tuple-element.85.cos, ...), custom_call_target="tpu_custom_call" | custom-call | flops 2147483648 | bytes 12582912 | tf_op jit(solution)/shard_map/halo_kv/pallas_call | solution.py:173
  201.8 6.8 %halo_kv.2.lkv = bf16[8,2,256,256]{3,2,1,0:T(8,128)(2,1)} custom-call(s32[1]{0:T(128)} %bitcast.18.order, bf16[1024,1024]{1,0:T(8,128)(2,1)} %collective-permute-done.3.x0, bf16[1024,1024]{1,0:T(8,128)(2,1)} %collective-permute-done.4.x1, bf16[1024,512]{1,0:T(8,128)(2,1)} %slice.121.w, f32[2048,128]{1,0:T(8,128)} %get-tuple-element.92.cos, ...), custom_call_target="tpu_custom_call" | custom-call | flops 2147483648 | bytes 12582912 | tf_op jit(solution)/shard_map/halo_kv/pallas_call | solution.py:173
  208.6 6.6 %attend_halo.2.m0 = bf16[1024,256]{1,0:T(8,128)(2,1)} custom-call(s32[6,8]{1,0:T(8,128)} %stack.2.table, bf16[2048,256]{1,0:T(8,128)(2,1)} %get-tuple-element.41.q, s32[1,2048]{1,0:T(1,128)} %bitcast.88, bf16[8,2,256,256]{3,2,1,0:T(8,128)(2,1)} %halo_kv.2.lkv, s32[2048,1]{1,0:T(8,128)} %copy.43.lseg, bf16[8,2,256,256]{3,2,1,0:T(8,128)(2,1)} %halo_kv.3.rkv, ...), custom_call_target="tpu_custom_call" | custom-call | flops 12884901888 | bytes 8388608 | tf_op jit(solution)/shard_map/attend_halo/pallas_call | solution.py:276
  215.2 0.5 collective-permute-start.7
  215.7 13.4 %attend_halo.3.m0 = bf16[1024,256]{1,0:T(8,128)(2,1)} custom-call(s32[6,8]{1,0:T(8,128)} %stack.2.table, bf16[2048,256]{1,0:T(8,128)(2,1)} %get-tuple-element.41.q, s32[1,2048]{1,0:T(1,128)} %bitcast.89, bf16[8,2,256,256]{3,2,1,0:T(8,128)(2,1)} %halo_kv.2.lkv, s32[2048,1]{1,0:T(8,128)} %copy.43.lseg, bf16[8,2,256,256]{3,2,1,0:T(8,128)(2,1)} %halo_kv.3.rkv, ...), custom_call_target="tpu_custom_call" | custom-call | flops 12884901888 | bytes 8388608 | tf_op jit(solution)/shard_map/attend_halo/pallas_call | solution.py:276
  229.9 1.2 gather_fusion
  231.1 0.7 pad_add_fusion.table
  231.8 0.9 collective-permute-start.10
  232.7 0.6 collective-permute-start.11
  233.4 0.8 broadcast_in_dim.54.before
  234.5 16.1 %mlp.2 = (f32[1024,512]{1,0:T(8,128)}, bf16[1024,512]{1,0:T(8,128)(2,1)}, f32[2,64,512]{2,1,0:T(8,128)}) custom-call(s32[132]{0:T(256)} %pad_add_fusion.table, bf16[1024,256]{1,0:T(8,128)(2,1)} %attend_halo.2.m0, bf16[1024,256]{1,0:T(8,128)(2,1)} %copy-done.16, bf16[1024,256]{1,0:T(8,128)(2,1)} %copy-done.18, bf16[1024,256]{1,0:T(8,128)(2,1)} %copy-done.20, ...), custom_call_target="tpu_custom_call" | custom-call | flops 6979321856 | bytes 12582912 | tf_op jit(solution)/shard_map/mlp/pallas_call | solution.py:372
  250.7 1.9 collective-permute-done.12.m3
  252.5 0.8 copy-done.21
  253.3 16.2 %mlp.3 = (f32[1024,512]{1,0:T(8,128)}, bf16[1024,512]{1,0:T(8,128)(2,1)}, f32[2,64,512]{2,1,0:T(8,128)}) custom-call(s32[132]{0:T(256)} %pad_add_fusion.table, bf16[1024,256]{1,0:T(8,128)(2,1)} %attend_halo.3.m0, bf16[1024,256]{1,0:T(8,128)(2,1)} %copy-done.17, bf16[1024,256]{1,0:T(8,128)(2,1)} %copy-done.19, bf16[1024,256]{1,0:T(8,128)(2,1)} %copy-done.21, ...), custom_call_target="tpu_custom_call" | custom-call | flops 6979321856 | bytes 12582912 | tf_op jit(solution)/shard_map/mlp/pallas_call | solution.py:372
  269.6 0.9 fusion.11
  270.7 0.9 slice_bitcast_fusion
  271.9 0.4 collective-permute-start.14
  272.3 2.5 collective-permute-done.14
  274.8 76.1 %all_to_all.22 = bf16[32,2,256]{2,1,0:T(2,128)(2,1)S(1)} all-to-all(bf16[32,2,256]{2,1,0:T(2,128)(2,1)S(1)} %reshape.629), channel_id=1, replica_groups=mesh['req'=32,'tp'=4] {'req'}, dimensions={0} | all-to-all | bytes 65536 | tf_op jit(solution)/shard_map/all_to_all | solution.py:422
  350.9 0.7 broadcast_in_dim.55
  351.6 6.2 %all-to-all-start.2 = ((bf16[128,2,256]{2,1,0:T(2,128)(2,1)}), bf16[128,2,256]{2,1,0:T(2,128)(2,1)S(1)}, u32[]{:S(2)}, u32[]{:S(2)}) async-start(bf16[128,2,256]{2,1,0:T(2,128)(2,1)} %broadcast_in_dim.55), calls=%async_computation.2 | async-start | bytes 262144 | tf_op jit(solution)/shard_map/all_to_all | solution.py:422
  357.8 1.3 collective-permute-start.15
  359.2 8.7 %all-to-all-done.2 = bf16[128,2,256]{2,1,0:T(2,128)(2,1)S(1)} async-done(((bf16[128,2,256]{2,1,0:T(2,128)(2,1)}), bf16[128,2,256]{2,1,0:T(2,128)(2,1)S(1)}, u32[]{:S(2)}, u32[]{:S(2)}) %all-to-all-start.2) | async-done | bytes 131104 | tf_op jit(solution)/shard_map/all_to_all | solution.py:422
  368.7 0.5 add_rsqrt_fusion
  369.2 1.5 convert_element_type.92
  370.7 1.0 fusion.6
  371.7 0.6 collective-permute-start.16
  372.6 0.7 copy-done.7
  373.6 0.7 collective-permute-start.18
  374.6 0.9 copy-done.8
  375.5 0.5 convolution_reduce_fusion
  376.0 21.8 %all_to_all.23 = f32[128,1,64]{2,1,0:T(1,128)S(1)} all-to-all(f32[128,1,64]{2,1,0:T(1,128)S(1)} %broadcast_in_dim.56), channel_id=1, replica_groups=mesh['req'=32,'tp'=4] {'req','tp'}, dimensions={0} | all-to-all | bytes 65536 | tf_op jit(solution)/shard_map/all_to_all | solution.py:422
  397.8 0.7 reduce_max.39
  398.5 1.8 fusion.8
  400.6 1.5 fusion.5
  402.1 1.0 pad_maximum_fusion
  (102 shorter events, 5.1 us)
Async XLA Ops:
  7.2 367.1 %copy-start = (f32[4,1024]{1,0:T(4,128)S(1)}, f32[4,1024]{1,0:T(4,128)}, u32[]{:S(2)}) copy-start(f32[4,1024]{1,0:T(4,128)} %param.30) | copy-start | bytes 49156
  7.2 84.8 %all-gather.3.cloned.1.call-start = ((), (), s32[]{:S(2)}) async-start(), calls=%async_computation.4 | async-start | bytes 1916928 | tf_op jit(solution)/shard_map/all_gather | solution.py:499
  11.7 6.0 %copy-start.10 = (bf16[4,8,3328]{2,1,0:T(8,128)(2,1)S(1)}, bf16[4,8,3328]{2,1,0:T(8,128)(2,1)}, u32[]{:S(2)}) copy-start(bf16[4,8,3328]{2,1,0:T(8,128)(2,1)} %get-tuple-element.38) | copy-start | bytes 638980
  11.7 13.9 %copy-start.9 = (bf16[32,4,8,768]{3,2,1,0:T(8,128)(2,1)S(1)}, bf16[32,4,8,768]{3,2,1,0:T(8,128)(2,1)}, u32[]{:S(2)}) copy-start(bf16[32,4,8,768]{3,2,1,0:T(8,128)(2,1)} %get-tuple-element.39) | copy-start | bytes 4718596
  17.7 4.1 collective-permute-start
  20.3 1.8 collective-permute-start.1
  21.2 3.6 collective-permute-start.2
  25.5 207.8 %all-gather.5.cloned.1.call-start = ((), (), s32[]{:S(2)}) async-start(), calls=%async_computation.5 | async-start | bytes 8519680 | tf_op jit(solution)/shard_map/all_gather | solution.py:502
  92.0 8.5 %copy-start.12 = (s32[64]{0:T(128)S(1)}, s32[64]{0:T(128)}, u32[]{:S(2)}) copy-start(s32[64]{0:T(128)} %param.17) | copy-start | bytes 772
  95.1 11.9 %copy-start.1 = (s32[128]{0:T(128)S(1)}, s32[128]{0:T(128)}, u32[]{:S(2)}) copy-start(s32[128]{0:T(128)} %param.19) | copy-start | bytes 1540
  95.1 45.4 %collective-permute-start.3 = (bf16[1024,1024]{1,0:T(8,128)(2,1)}, bf16[1024,1024]{1,0:T(8,128)(2,1)}, u32[]{:S(2)}, u32[]{:S(2)}) collective-permute-start(bf16[1024,1024]{1,0:T(8,128)(2,1)} %constant_dynamic-slice_fusion), channel_id=1, source_target_pairs={{0,4},{4,8},{8,12},{12,16},{16,20},{20,24},{24,28},{28,32},{32,36}... | collective-permute-start | bytes 6291464 | tf_op jit(solution)/shard_map/ppermute | solution.py:418
  99.3 46.5 %collective-permute-start.5 = (bf16[1024,1024]{1,0:T(8,128)(2,1)}, bf16[1024,1024]{1,0:T(8,128)(2,1)}, u32[]{:S(2)}, u32[]{:S(2)}) collective-permute-start(bf16[1024,1024]{1,0:T(8,128)(2,1)} %constant_dynamic-slice_fusion), channel_id=1, source_target_pairs={{4,0},{8,4},{12,8},{16,12},{20,16},{24,20},{28,24},{32,28},{36,32}... | collective-permute-start | bytes 6291464 | tf_op jit(solution)/shard_map/ppermute | solution.py:418
  102.0 60.9 %copy-start.11 = (s32[2048]{0:T(1024)}, s32[2048]{0:T(1024)S(1)}, u32[]{:S(2)}) copy-start(s32[2048]{0:T(1024)S(1)} %get-tuple-element.80) | copy-start | bytes 24580
  140.5 54.5 %collective-permute-start.4 = (bf16[1024,1024]{1,0:T(8,128)(2,1)}, bf16[1024,1024]{1,0:T(8,128)(2,1)}, u32[]{:S(2)}, u32[]{:S(2)}) collective-permute-start(bf16[1024,1024]{1,0:T(8,128)(2,1)} %collective-permute-done.3.x0), channel_id=1, source_target_pairs={{0,1},{1,0},{2,3},{3,2},{4,5},{5,4},{6,7},{7,6},{8,9},{9,8},{10,11... | collective-permute-start | bytes 6291464 | tf_op jit(solution)/shard_map/ppermute | solution.py:396
  145.8 49.2 %collective-permute-start.6 = (bf16[1024,1024]{1,0:T(8,128)(2,1)}, bf16[1024,1024]{1,0:T(8,128)(2,1)}, u32[]{:S(2)}, u32[]{:S(2)}) collective-permute-start(bf16[1024,1024]{1,0:T(8,128)(2,1)} %collective-permute-done.5.x0), channel_id=1, source_target_pairs={{0,1},{1,0},{2,3},{3,2},{4,5},{5,4},{6,7},{7,6},{8,9},{9,8},{10,11... | collective-permute-start | bytes 6291464 | tf_op jit(solution)/shard_map/ppermute | solution.py:396
  163.6 1.5 copy-start.5
  215.2 13.9 %copy-start.15 = (bf16[1024,256]{1,0:T(8,128)(2,1)S(1)}, bf16[1024,256]{1,0:T(8,128)(2,1)}, u32[]{:S(2)}) copy-start(bf16[1024,256]{1,0:T(8,128)(2,1)} %attend_halo.2.m0) | copy-start | bytes 1572868
  215.2 15.9 %copy-start.2 = (s32[4]{0:T(128)S(1)}, s32[4]{0:T(128)}, u32[]{:S(2)}) copy-start(s32[4]{0:T(128)} %constant.203.clone) | copy-start | bytes 52
  215.2 14.2 %collective-permute-start.7 = (bf16[1024,256]{1,0:T(8,128)(2,1)}, bf16[1024,256]{1,0:T(8,128)(2,1)S(1)}, u32[]{:S(2)}, u32[]{:S(2)}) collective-permute-start(bf16[1024,256]{1,0:T(8,128)(2,1)} %attend_halo.2.m0), channel_id=1, source_target_pairs={{0,2},{1,3},{2,0},{3,1},{4,6},{5,7},{6,4},{7,5},{8,10},{9,11},{10,... | collective-permute-start | bytes 1572872 | tf_op jit(solution)/shard_map/ppermute | solution.py:396
  229.1 4.2 %collective-permute-start.8 = (bf16[1024,256]{1,0:T(8,128)(2,1)S(1)}, bf16[1024,256]{1,0:T(8,128)(2,1)S(1)}, u32[]{:S(2)}, u32[]{:S(2)}) collective-permute-start(bf16[1024,256]{1,0:T(8,128)(2,1)S(1)} %copy-done.15), channel_id=1, source_target_pairs={{0,1},{1,0},{2,3},{3,2},{4,5},{5,4},{6,7},{7,6},{8,9},{9,8},{10,11... | collective-permute-start | bytes 1572872 | tf_op jit(solution)/shard_map/ppermute | solution.py:396
  229.5 4.8 %copy-start.16 = (bf16[1024,256]{1,0:T(8,128)(2,1)}, bf16[1024,256]{1,0:T(8,128)(2,1)S(1)}, u32[]{:S(2)}) copy-start(bf16[1024,256]{1,0:T(8,128)(2,1)S(1)} %collective-permute-done.7.m1) | copy-start | bytes 1572868
  229.5 3.9 collective-permute-start.9
  231.8 18.7 %collective-permute-start.10 = (bf16[1024,256]{1,0:T(8,128)(2,1)}, bf16[1024,256]{1,0:T(8,128)(2,1)S(1)}, u32[]{:S(2)}, u32[]{:S(2)}) collective-permute-start(bf16[1024,256]{1,0:T(8,128)(2,1)} %attend_halo.3.m0), channel_id=1, source_target_pairs={{0,2},{1,3},{2,0},{3,1},{4,6},{5,7},{6,4},{7,5},{8,10},{9,11},{10,... | collective-permute-start | bytes 1572872 | tf_op jit(solution)/shard_map/ppermute | solution.py:396
  232.7 17.9 %collective-permute-start.11 = (bf16[1024,256]{1,0:T(8,128)(2,1)}, bf16[1024,256]{1,0:T(8,128)(2,1)S(1)}, u32[]{:S(2)}, u32[]{:S(2)}) collective-permute-start(bf16[1024,256]{1,0:T(8,128)(2,1)} %attend_halo.3.m0), channel_id=1, source_target_pairs={{0,1},{1,0},{2,3},{3,2},{4,5},{5,4},{6,7},{7,6},{8,9},{9,8},{10,11... | collective-permute-start | bytes 1572872 | tf_op jit(solution)/shard_map/ppermute | solution.py:396
  233.3 0.9 copy-start.18
  233.3 1.1 copy-start.20
  250.5 2.0 copy-start.17
  250.5 2.0 collective-permute-start.12
  250.6 1.9 copy-start.19
  252.5 0.8 copy-start.21
  253.3 104.5 %copy-start.14 = (bf16[1024,512]{1,0:T(8,128)(2,1)S(1)}, bf16[1024,512]{1,0:T(8,128)(2,1)}, u32[]{:S(2)}) copy-start(bf16[1024,512]{1,0:T(8,128)(2,1)} %get-tuple-element.59) | copy-start | bytes 3145732
  270.5 1.3 collective-permute-start.13
  271.9 2.8 collective-permute-start.14
  351.6 16.3 %all-to-all-start.2 = ((bf16[128,2,256]{2,1,0:T(2,128)(2,1)}), bf16[128,2,256]{2,1,0:T(2,128)(2,1)S(1)}, u32[]{:S(2)}, u32[]{:S(2)}) async-start(bf16[128,2,256]{2,1,0:T(2,128)(2,1)} %broadcast_in_dim.55), calls=%async_computation.2 | async-start | bytes 262144 | tf_op jit(solution)/shard_map/all_to_all | solution.py:422
  357.8 11.4 %collective-permute-start.15 = (bf16[1024,512]{1,0:T(8,128)(2,1)S(1)}, bf16[1024,512]{1,0:T(8,128)(2,1)}, u32[]{:S(2)}, u32[]{:S(2)}) collective-permute-start(bf16[1024,512]{1,0:T(8,128)(2,1)S(1)} %copy-done.14), channel_id=1, source_target_pairs={{0,1},{1,0},{2,3},{3,2},{4,5},{5,4},{6,7},{7,6},{8,9},{9,8},{10,11... | collective-permute-start | bytes 3145736 | tf_op jit(solution)/shard_map/ppermute | solution.py:396
  359.1 13.2 %collective-permute-start.17 = (bf16[1024,512]{1,0:T(8,128)(2,1)}, bf16[1024,512]{1,0:T(8,128)(2,1)S(1)}, u32[]{:S(2)}, u32[]{:S(2)}) collective-permute-start(bf16[1024,512]{1,0:T(8,128)(2,1)} %get-tuple-element.61), channel_id=1, source_target_pairs={{0,1},{1,0},{2,3},{3,2},{4,5},{5,4},{6,7},{7,6},{8,9},{9,8},{10,11... | collective-permute-start | bytes 3145736 | tf_op jit(solution)/shard_map/ppermute | solution.py:396
  368.5 2.2 copy-start.6
  371.7 1.6 copy-start.7
  371.7 26.8 %collective-permute-start.16 = (bf16[1024,256]{1,0:T(8,128)(2,1)}, bf16[1024,256]{1,0:T(8,128)(2,1)}, u32[]{:S(2)}, u32[]{:S(2)}) collective-permute-start(bf16[1024,256]{1,0:T(8,128)(2,1)} %fusion.6), channel_id=1, source_target_pairs={{0,2},{1,3},{2,0},{3,1},{4,6},{5,7},{6,4},{7,5},{8,10},{9,11},{10,... | collective-permute-start | bytes 1572872 | tf_op jit(solution)/shard_map/ppermute | solution.py:396
  373.3 2.6 copy-start.3
  373.3 1.0 copy-start.13
  373.3 2.2 copy-start.8
  373.6 26.7 %collective-permute-start.18 = (bf16[1024,256]{1,0:T(8,128)(2,1)S(1)}, bf16[1024,256]{1,0:T(8,128)(2,1)S(1)}, u32[]{:S(2)}, u32[]{:S(2)}) collective-permute-start(bf16[1024,256]{1,0:T(8,128)(2,1)S(1)} %fusion.3), channel_id=1, source_target_pairs={{0,2},{1,3},{2,0},{3,1},{4,6},{5,7},{6,4},{7,5},{8,10},{9,11},{10,... | collective-permute-start | bytes 1572872 | tf_op jit(solution)/shard_map/ppermute | solution.py:396
  398.5 2.1 copy-start.4
Sparse Core Ops, SparseCore 0:
  25.6 66.3 all-gather.2
  93.7 111.5 all-gather.4

commit v6 on v4

--- a/solution.py
+++ b/solution.py
@@ -353,6 +353,10 @@
     return lax.ppermute(x, "tp", [(i, i ^ bit) for i in range(4)])
 
 
+def turn_bits(n):
+    return n % 2 * 2 + n // 2
+
+
 def gather_tp(x, after=None):
     far = swap(x, 2)
     near = swap(x, 1)
@@ -368,18 +372,6 @@
 
 def reduce_far(mine, send):
     return (mine + swap(send, 2).astype(F32)).astype(BF)
-
-
-def from_offset(x, dx, dy, dz=0):
-    pairs = []
-    for i in range(32):
-        far = (i // 16 + dz) % 2 * 16 + (i // 4 + dx) % 4 * 4 + (i + dy) % 4
-        pairs.append((far, i))
-    return lax.ppermute(x, "req", pairs)
-
-
-def sum_req(x, moves):
-    return sum([from_offset(x, *move) for move in moves], x)
 
 
 def shift(x, by):
@@ -416,13 +408,18 @@
     slots, width = hidden_in.shape
     requests = lengths.shape[0]
 
-    tp_order = jnp.array([0, 2, 1, 3], jnp.int32)
-    place_of = tp_order[jnp.arange(4, dtype=jnp.int32) ^ tp_index]
+    four = jnp.arange(4, dtype=jnp.int32)
+    place_of = turn_bits(four ^ tp_index)
     qkv_block, rest_block = prep(req_count, place_of, wq, wk, wv, wo, wi_in, wi_gate, wo2)
     place = jnp.arange(count, dtype=jnp.int32)
     source = jnp.sum(
         jnp.where(shard_map[None, :] == place[:, None], place[None, :], 0), axis=1
     )
+    rest_rows = jnp.concatenate(
+        [rest_block[0], swap(rest_block[1], 2), swap(rest_block[2], 1), swap(rest_block[3], 3)], axis=0
+    )
+    hidden, lengths, rest_rows = lax.optimization_barrier((hidden_in, lengths, rest_rows))
+
     ends = jnp.cumsum(lengths)
     base = req_index * slots
     index = base - slots + jnp.arange(3 * slots, dtype=jnp.int32)
@@ -431,12 +428,10 @@
     own = base + jnp.arange(slots, dtype=jnp.int32)
     start_of = jnp.max(jnp.where(ends[None, :] <= own[:, None], ends[None, :], 0), axis=1)
     position = (own - start_of).astype(F32)
-    half = HEAD_DIM // 2
-    lane = jnp.arange(128, dtype=jnp.int32) % half
+    lane = jnp.arange(128, dtype=jnp.int32) % (HEAD_DIM // 2)
     freq = THETA ** (-(2.0 * lane.astype(F32)) / HEAD_DIM)
     angle = position[:, None] * freq[None, :]
-    cos = jnp.cos(angle)
-    sin = jnp.sin(angle)
+    turn = (jnp.cos(angle), jnp.sin(angle))
     begin = base + jnp.arange(slots // QB, dtype=jnp.int32) * QB
     close = begin + QB - 1
     low = jnp.max(jnp.where(ends[None, :] <= begin[:, None], ends[None, :], 0), axis=1) - base
@@ -453,49 +448,24 @@
     segs = segment.reshape(3, slots, 1)
     qseg = segment[slots : 2 * slots].reshape(1, slots)
 
-    later, qkv_block = lax.optimization_barrier((hidden_in, qkv_block))
-    normed = norm(later, attn_gain)
-    rest_block, normed = lax.optimization_barrier((rest_block, normed))
-    rest_rows = jnp.concatenate(
-        [rest_block[0], swap(rest_block[1], 2), swap(rest_block[2], 1), swap(rest_block[3], 3)], axis=0
-    )
-    level = jnp.concatenate([rest_rows, from_offset(rest_rows, 0, 0, 1)], axis=0)
-    level = jnp.concatenate([level] + [from_offset(level, 0, d) for d in (1, 3, 2)], axis=0)
-    ahead = from_offset(level, 1, 0)
-    behind = from_offset(level, 3, 0)
-    far = jnp.arange(count, dtype=jnp.int32)
-    slot_x, slot_y = (jnp.array([0, 1, 3, 2], jnp.int32)[n] for n in (far // 32, far // 8 % 4))
-    from_req = (
-        (req_index // 16 + far // 4) % 2 * 16
-        + (req_index // 4 + slot_x) % 4 * 4
-        + (req_index + slot_y) % 4
-    )
-    rest_target = shard_map[from_req * tp_count + (tp_index ^ tp_order[far % 4])]
+    normed = norm(hidden, attn_gain)
     qkv_all = exchange(qkv_block.reshape(count, 8, 768), BOTH)
     qkv_w = qkv_all[source].reshape(width, 768)
-    query, kv, cache = qkv_project(normed, qkv_w, cos, sin)
+    rest = [lax.all_gather(rest_rows, "req", axis=0, tiled=True).reshape(count, 8, REST)]
+    far = jnp.arange(count, dtype=jnp.int32)
+    rest_target = shard_map[far // 4 * tp_count + (tp_index ^ turn_bits(far % 4))]
+    query, kv, cache = qkv_project(normed, qkv_w, *turn)
     left = shift(kv, 1)
     right = shift(kv, -1)
     parts = 2
     state = attend(0, 1, table, query, qseg, (kv, segs[1]), ())
-    ahead, behind, state = lax.optimization_barrier((ahead, behind, state))
-    rest = [
-        piece.reshape(-1, 8, REST)
-        for piece in (
-            level,
-            ahead,
-            behind,
-            from_offset(ahead[:128], 1, 0),
-            from_offset(behind[128:], 3, 0),
-        )
-    ]
     mixed = [
         attend(part, parts, table, query, qseg, (left, segs[0], right, segs[2]), state)
         for part in range(parts)
     ]
 
     last_slot = (ends - 1 - base).reshape(requests, 1)
-    order = jnp.concatenate([tp_index ^ tp_order, rest_target])
+    order = jnp.concatenate([tp_index ^ turn_bits(four), rest_target])
     picked = jnp.zeros((2, requests, 512), F32)
     bulk = []
     after = mixed[1]
@@ -513,14 +483,18 @@
         after = (keep, send)
         bulk.append((keep, send))
 
-    pieces = gather_tp(reduce_far(*reduce_core(picked[0], picked[1].astype(BF))))
-    wide = jnp.stack(pieces)[place_of].transpose(1, 0, 2).reshape(requests, width)
-    wide = sum_req(wide, ((0, 0, 1),))
-    bulk, wide = lax.optimization_barrier((bulk, wide))
+    each = requests // req_count
+    last_mine = reduce_far(*reduce_core(picked[0], picked[1].astype(BF)))
+    bulk, last_mine = lax.optimization_barrier((bulk, last_mine))
+    taken = exchange(last_mine.reshape(req_count, each, 256), "req").astype(F32).sum(axis=0)
+    spread = exchange(jnp.broadcast_to(taken.astype(BF)[None], (count, each, 256)), BOTH)
     hidden_out = jnp.concatenate([reduce_far(*reduce_core(*pair)) for pair in bulk], axis=0)
-    wide = sum_req(wide, tuple((0, d, 0) for d in (1, 3, 2)))
-    wide = sum_req(wide, tuple((d, 0, 0) for d in (1, 3, 2)))
-    last = wide.astype(F32)
+    last = (
+        spread.reshape(req_count, tp_count, each, 256)
+        .transpose(0, 2, 1, 3)
+        .reshape(requests, width)
+        .astype(F32)
+    )
     last_rms = jnp.sqrt(jnp.mean(last * last, axis=-1))
     choose = (tenant[:, None] == jnp.arange(final_gain.shape[0], dtype=jnp.int32)[None, :]).astype(
         F32

time: 327 us -> 310 us (0.948); the launches traced: 322 us -> 309 us
  starting transfers between devices: 74.9 us -> 36.4 us
  blocking collectives: 21 us -> 36.8 us
  between operations: 1.23 us -> 14.5 us
  local copies, waits for them, and re-layouts: 24.8 us -> 15.2 us
  waiting for transfers between devices: 91.7 us -> 95.4 us
    ppermute x15 -> x0, waiting for transfers between devices: 87.5 us -> none  [from_offset(): return lax.ppermute(x, 'req', pairs)]
    all_gather x0 -> x1, waiting for transfers between devices: none -> 35.7 us  [body(): lax.all_gather(rest_rows, 'req', axis=0, tiled=True).reshape(count, 8, REST)]
    ppermute x15 -> x0, starting transfers between devices: 25.5 us -> none  [from_offset(): return lax.ppermute(x, 'req', pairs)]
    ppermute x2, waiting for transfers between devices: 0.01 us -> 21.7 us  [shift(): lax.ppermute(x, 'req', [(i, i + by) for i in range(count) if 0 <= i + by...]
    all_to_all x1 -> x2, waiting for transfers between devices: 0.01 us -> 21.6 us  [exchange(): return lax.all_to_all(x, axes, split_axis=0, concat_axis=0, tiled=True)]
    ppermute x18 -> x15, starting transfers between devices: 35.2 us -> 15 us  [swap(): return lax.ppermute(x, 'tp', [(i, i ^ bit) for i in range(4)])]
    all_to_all x1 -> x2, blocking collectives: 21 us -> 36.8 us  [exchange(): return lax.all_to_all(x, axes, split_axis=0, concat_axis=0, tiled=True)]
    ppermute x18 -> x15, waiting for transfers between devices: 4.27 us -> 16.4 us  [swap(): return lax.ppermute(x, 'tp', [(i, i ^ bit) for i in range(4)])]
  transfers between devices with their start and end apart: 36 -> 20, of which waited for: 14 -> 11; matrix products, arithmetic and copies ran while one was open for 9% -> 8% of each run, Pallas kernels for 21% -> 24%
where the time goes in v6:
time: 310 us; the launch traced here: 309 us
  waiting for transfers between devices  95.4 us (31%)
  Pallas kernels  91.8 us (30%)
  blocking collectives  36.8 us (12%)
  starting transfers between devices  36.4 us (12%)
  other arithmetic  18.1 us (6%)
  local copies, waits for them, and re-layouts  15.2 us (5%)
  between operations  14.5 us (5%)
    pallas_call x3, Pallas kernels, attend(): pl.pallas_call(kernel, grid_spec=pltpu.PrefetchScalarGridSpec(num_scalar_...  42.8 us
    all_to_all x2, blocking collectives, exchange(): return lax.all_to_all(x, axes, split_axis=0, concat_axis=0, tiled=True)  36.8 us
    all_gather x1, waiting for transfers between devices, body(): lax.all_gather(rest_rows, 'req', axis=0, tiled=True).reshape(count, 8, REST)  35.7 us
    pallas_call x2, Pallas kernels, mlp(): pl.pallas_call(functools.partial(mlp_kernel, base), grid_spec=pltpu.Prefe...  32.3 us
    ppermute x2, waiting for transfers between devices, shift(): lax.ppermute(x, 'req', [(i, i + by) for i in range(count) if 0 <= i + by...  21.7 us
    all_to_all x2, waiting for transfers between devices, exchange(): return lax.all_to_all(x, axes, split_axis=0, concat_axis=0, tiled=True)  21.6 us
    ppermute x15, waiting for transfers between devices, swap(): return lax.ppermute(x, 'tp', [(i, i ^ bit) for i in range(4)])  16.4 us
    all_to_all x2, starting transfers between devices, exchange(): return lax.all_to_all(x, axes, split_axis=0, concat_axis=0, tiled=True)  15.9 us
  transfers between devices with their start and end apart: 20, of which 11 were waited for; matrix products, arithmetic and copies ran while one was open for 8% of the time, Pallas kernels for 24%

profile of v6, /device:TPU:1, one launch (start us, length us, event | category | flops | bytes accessed | tf_op | source)
XLA Modules:
  0.0 308.9 jit_solution(4079488829051164836)
XLA Ops:
  7.2 0.5 fusion.22.order
  7.8 2.6 prep.1
  10.4 0.9 slice_bitcast_fusion.4
  11.3 2.5 collective-permute-start
  13.9 1.0 collective-permute-start.1
  14.8 0.6 collective-permute-done
  15.4 0.3 collective-permute-done.1
  15.7 2.7 collective-permute-done.2
  18.4 0.7 pad_maximum_fusion.1
  19.1 9.7 %all-to-all-start = ((bf16[128,8,768]{2,1,0:T(8,128)(2,1)}), bf16[128,8,768]{2,1,0:T(8,128)(2,1)S(1)}, u32[]{:S(2)}, u32[]{:S(2)}) async-start(bf16[128,8,768]{2,1,0:T(8,128)(2,1)} %bitcast.77), calls=%async_computation | async-start | bytes 3145728 | tf_op jit(solution)/shard_map/all_to_all | solution.py:383
  29.2 5.9 %norm.1.x = bf16[2048,1024]{1,0:T(8,128)(2,1)} custom-call(bf16[2048,1024]{1,0:T(8,128)(2,1)} %h.4, f32[1,1024]{1,0:T(1,128)} %bitcast.88), custom_call_target="tpu_custom_call" | custom-call | flops 16777216 | bytes 8388608 | tf_op jit(solution)/shard_map/norm/pallas_call | solution.py:87
  35.1 0.7 add_subtract_fusion
  36.0 5.5 %multiply_sine_fusion = (f32[2048,128]{1,0:T(8,128)}, f32[2048,128]{1,0:T(8,128)}) fusion(f32[128]{0:T(128)S(1)} %fusion.27, f32[2048]{0:T(1024)S(1)} %subtract_convert_fusion), kind=kLoop, calls=%fused_computation.3 | loop fusion | flops 262144 | bytes 2105856 | tf_op jit(solution)/shard_map/sin | solution.py:434
  41.6 12.9 %all-to-all-done = bf16[128,8,768]{2,1,0:T(8,128)(2,1)S(1)} async-done(((bf16[128,8,768]{2,1,0:T(8,128)(2,1)}), bf16[128,8,768]{2,1,0:T(8,128)(2,1)S(1)}, u32[]{:S(2)}, u32[]{:S(2)}) %all-to-all-start) | async-done | bytes 1572896 | tf_op jit(solution)/shard_map/all_to_all | solution.py:383
  54.4 1.8 gather_fusion.1
  56.2 8.2 %qkv.1 = (bf16[2048,256]{1,0:T(8,128)(2,1)}, bf16[8,2,256,256]{3,2,1,0:T(8,128)(2,1)}, bf16[2,2048,256]{2,1,0:T(8,128)(2,1)}) custom-call(bf16[2048,1024]{1,0:T(8,128)(2,1)} %norm.1.x, bf16[1024,768]{1,0:T(8,128)(2,1)} %bitcast.78, f32[2048,128]{1,0:T(8,128)} %get-tuple-element.66.cos, f32[2048,128]{1,0:T(8,128)} %get-tuple-element.65.sin), custom_call_target="tpu_custom_call" | custom-call | flops 3221225472 | bytes 12582912 | tf_op jit(solution)/shard_map/qkv/pallas_call | solution.py:126
  64.4 4.2 %collective-permute-start.3 = (bf16[8,2,256,256]{3,2,1,0:T(8,128)(2,1)}, bf16[8,2,256,256]{3,2,1,0:T(8,128)(2,1)}, u32[]{:S(2)}, u32[]{:S(2)}) collective-permute-start(bf16[8,2,256,256]{3,2,1,0:T(8,128)(2,1)} %get-tuple-element.32.kv), channel_id=1, source_target_pairs={{0,4},{4,8},{8,12},{12,16},{16,20},{20,24},{24,28},{28,32},{32,36}... | collective-permute-start | bytes 6291464 | tf_op jit(solution)/shard_map/ppermute | solution.py:379
  68.6 1.3 collective-permute-start.4
  70.2 1.4 copy.41.kseg
  71.6 1.3 copy.42.lseg
  72.9 1.4 copy.43.rseg
  74.5 0.6 stack.2.table
  75.1 26.6 %attend_own.1 = (f32[4,72,2048]{2,1,0:T(8,128)}, f32[4,1,2048]{2,1,0:T(1,128)}) custom-call(s32[6,8]{1,0:T(8,128)} %stack.2.table, bf16[2048,256]{1,0:T(8,128)(2,1)} %get-tuple-element.31.q, s32[1,2048]{1,0:T(1,128)} %bitcast.83, bf16[8,2,256,256]{3,2,1,0:T(8,128)(2,1)} %get-tuple-element.32.kv, s32[2048,1]{1,0:T(8,128)} %copy.41.kseg), custom_call_target="tpu_custom_call" | custom-call | flops 12884901888 | bytes 8388608 | tf_op jit(solution)/shard_map/attend_own/pallas_call | solution.py:233
  101.7 18.0 %collective-permute-done.3.lkv = bf16[8,2,256,256]{3,2,1,0:T(8,128)(2,1)} collective-permute-done((bf16[8,2,256,256]{3,2,1,0:T(8,128)(2,1)}, bf16[8,2,256,256]{3,2,1,0:T(8,128)(2,1)}, u32[]{:S(2)}, u32[]{:S(2)}) %collective-permute-start.3) | collective-permute-done | bytes 2097184 | tf_op jit(solution)/shard_map/ppermute | solution.py:379
  119.7 3.7 %collective-permute-done.4.rkv = bf16[8,2,256,256]{3,2,1,0:T(8,128)(2,1)} collective-permute-done((bf16[8,2,256,256]{3,2,1,0:T(8,128)(2,1)}, bf16[8,2,256,256]{3,2,1,0:T(8,128)(2,1)}, u32[]{:S(2)}, u32[]{:S(2)}) %collective-permute-start.4) | collective-permute-done | bytes 2097184 | tf_op jit(solution)/shard_map/ppermute | solution.py:379
  123.4 7.5 %attend_halo.2.m0 = bf16[1024,256]{1,0:T(8,128)(2,1)} custom-call(s32[6,8]{1,0:T(8,128)} %stack.2.table, bf16[2048,256]{1,0:T(8,128)(2,1)} %get-tuple-element.31.q, s32[1,2048]{1,0:T(1,128)} %bitcast.84, bf16[8,2,256,256]{3,2,1,0:T(8,128)(2,1)} %collective-permute-done.3.lkv, s32[2048,1]{1,0:T(8,128)} %copy.42.lseg, ...), custom_call_target="tpu_custom_call" | custom-call | flops 12884901888 | bytes 8388608 | tf_op jit(solution)/shard_map/attend_halo/pallas_call | solution.py:233
  130.9 0.7 collective-permute-start.5
  131.6 0.9 collective-permute-start.6
  132.5 8.7 %attend_halo.3.m0 = bf16[1024,256]{1,0:T(8,128)(2,1)} custom-call(s32[6,8]{1,0:T(8,128)} %stack.2.table, bf16[2048,256]{1,0:T(8,128)(2,1)} %get-tuple-element.31.q, s32[1,2048]{1,0:T(1,128)} %bitcast.85, bf16[8,2,256,256]{3,2,1,0:T(8,128)(2,1)} %collective-permute-done.3.lkv, s32[2048,1]{1,0:T(8,128)} %copy.42.lseg, ...), custom_call_target="tpu_custom_call" | custom-call | flops 12884901888 | bytes 8388608 | tf_op jit(solution)/shard_map/attend_halo/pallas_call | solution.py:233
  141.2 8.8 %collective-permute-done.5.m1 = bf16[1024,256]{1,0:T(8,128)(2,1)S(1)} collective-permute-done((bf16[1024,256]{1,0:T(8,128)(2,1)}, bf16[1024,256]{1,0:T(8,128)(2,1)S(1)}, u32[]{:S(2)}, u32[]{:S(2)}) %collective-permute-start.5) | collective-permute-done | bytes 524320 | tf_op jit(solution)/shard_map/ppermute | solution.py:353
  150.0 4.2 %collective-permute-start.7 = (bf16[1024,256]{1,0:T(8,128)(2,1)S(1)}, bf16[1024,256]{1,0:T(8,128)(2,1)S(1)}, u32[]{:S(2)}, u32[]{:S(2)}) collective-permute-start(bf16[1024,256]{1,0:T(8,128)(2,1)S(1)} %collective-permute-done.5.m1), channel_id=1, source_target_pairs={{0,1},{1,0},{2,3},{3,2},{4,5},{5,4},{6,7},{7,6},{8,9},{9,8},{10,11... | collective-permute-start | bytes 1572872 | tf_op jit(solution)/shard_map/ppermute | solution.py:353
  154.3 1.2 gather_fusion
  155.5 0.6 pad_add_fusion.table
  156.2 1.2 collective-permute-start.8
  157.7 35.7 %all-gather.2.cloned.1.call-done = bf16[1024,3328]{1,0:T(8,128)(2,1)} async-done(((bf16[32,3328]{1,0:T(8,128)(2,1)}), bf16[1024,3328]{1,0:T(8,128)(2,1)}) %all-gather.2.cloned.1.call-update) | async-done | bytes 6815760 | tf_op jit(solution)/shard_map/all_gather | solution.py:454
  193.4 0.7 broadcast_in_dim.54.before
  194.2 16.1 %mlp.2 = (f32[1024,512]{1,0:T(8,128)}, bf16[1024,512]{1,0:T(8,128)(2,1)}, f32[2,64,512]{2,1,0:T(8,128)}) custom-call(s32[132]{0:T(256)} %pad_add_fusion.table, bf16[1024,256]{1,0:T(8,128)(2,1)} %attend_halo.2.m0, bf16[1024,256]{1,0:T(8,128)(2,1)} %copy-done.11, bf16[1024,256]{1,0:T(8,128)(2,1)} %copy-done.12, bf16[1024,256]{1,0:T(8,128)(2,1)} %copy-done.15, ...), custom_call_target="tpu_custom_call" | custom-call | flops 6979321856 | bytes 12582912 | tf_op jit(solution)/shard_map/mlp/pallas_call | solution.py:329
  210.2 0.9 collective-permute-start.10
  211.2 1.5 collective-permute-done.10.m3
  212.7 0.8 copy-done.16
  213.5 16.2 %mlp.3 = (f32[1024,512]{1,0:T(8,128)}, bf16[1024,512]{1,0:T(8,128)(2,1)}, f32[2,64,512]{2,1,0:T(8,128)}) custom-call(s32[132]{0:T(256)} %pad_add_fusion.table, bf16[1024,256]{1,0:T(8,128)(2,1)} %attend_halo.3.m0, bf16[1024,256]{1,0:T(8,128)(2,1)} %copy-done.13, bf16[1024,256]{1,0:T(8,128)(2,1)} %copy-done.14, bf16[1024,256]{1,0:T(8,128)(2,1)} %copy-done.16, ...), custom_call_target="tpu_custom_call" | custom-call | flops 6979321856 | bytes 12582912 | tf_op jit(solution)/shard_map/mlp/pallas_call | solution.py:329
  229.7 0.9 fusion.9
  230.7 0.5 collective-permute-start.11
  231.1 0.9 slice_bitcast_fusion
  232.1 0.4 collective-permute-start.12
  232.5 2.5 collective-permute-done.12
  235.0 15.0 %all_to_all.21 = bf16[32,2,256]{2,1,0:T(2,128)(2,1)S(1)} all-to-all(bf16[32,2,256]{2,1,0:T(2,128)(2,1)S(1)} %reshape.544), channel_id=1, replica_groups=mesh['req'=32,'tp'=4] {'req'}, dimensions={0} | all-to-all | bytes 65536 | tf_op jit(solution)/shard_map/all_to_all | solution.py:383
  250.0 0.7 broadcast_in_dim.55
  250.7 6.2 %all-to-all-start.2 = ((bf16[128,2,256]{2,1,0:T(2,128)(2,1)}), bf16[128,2,256]{2,1,0:T(2,128)(2,1)S(1)}, u32[]{:S(2)}, u32[]{:S(2)}) async-start(bf16[128,2,256]{2,1,0:T(2,128)(2,1)} %broadcast_in_dim.55), calls=%async_computation.2 | async-start | bytes 262144 | tf_op jit(solution)/shard_map/all_to_all | solution.py:383
  256.9 1.1 collective-permute-start.13
  258.2 8.7 %all-to-all-done.2 = bf16[128,2,256]{2,1,0:T(2,128)(2,1)S(1)} async-done(((bf16[128,2,256]{2,1,0:T(2,128)(2,1)}), bf16[128,2,256]{2,1,0:T(2,128)(2,1)S(1)}, u32[]{:S(2)}, u32[]{:S(2)}) %all-to-all-start.2) | async-done | bytes 131104 | tf_op jit(solution)/shard_map/all_to_all | solution.py:383
  267.7 0.5 add_rsqrt_fusion
  268.2 1.5 convert_element_type.92
  269.7 1.0 fusion.4
  270.7 0.6 collective-permute-start.14
  271.5 0.7 copy-done.5
  272.6 0.6 collective-permute-start.16
  273.5 0.9 copy-done.6
  274.5 0.5 convolution_reduce_fusion
  275.0 21.8 %all_to_all.22 = f32[128,1,64]{2,1,0:T(1,128)S(1)} all-to-all(f32[128,1,64]{2,1,0:T(1,128)S(1)} %broadcast_in_dim.56), channel_id=1, replica_groups=mesh['req'=32,'tp'=4] {'req','tp'}, dimensions={0} | all-to-all | bytes 65536 | tf_op jit(solution)/shard_map/all_to_all | solution.py:383
  296.8 0.7 reduce_max.39
  297.4 1.8 fusion.6
  299.5 1.5 fusion.3
  301.0 1.0 pad_maximum_fusion
  (82 shorter events, 3.5 us)
Async XLA Ops:
  7.2 266.0 %copy-start = (f32[4,1024]{1,0:T(4,128)S(1)}, f32[4,1024]{1,0:T(4,128)}, u32[]{:S(2)}) copy-start(f32[4,1024]{1,0:T(4,128)} %param.29) | copy-start | bytes 49156
  7.2 186.2 %all-gather.2.cloned.1.call-start = ((), (), s32[]{:S(2)}) async-start(), calls=%async_computation.4 | async-start | bytes 7028736 | tf_op jit(solution)/shard_map/all_gather | solution.py:454
  10.4 18.4 %copy-start.1 = (s32[128]{0:T(128)S(1)}, s32[128]{0:T(128)}, u32[]{:S(2)}) copy-start(s32[128]{0:T(128)} %param.18) | copy-start | bytes 1540
  10.4 18.6 %copy-start.8 = (s32[64]{0:T(128)S(1)}, s32[64]{0:T(128)}, u32[]{:S(2)}) copy-start(s32[64]{0:T(128)} %param.16) | copy-start | bytes 772
  11.3 4.1 %collective-permute-start = (bf16[8,3328]{1,0:T(8,128)(2,1)S(1)}, bf16[8,3328]{1,0:T(8,128)(2,1)S(1)}, u32[]{:S(2)}, u32[]{:S(2)}) collective-permute-start(bf16[8,3328]{1,0:T(8,128)(2,1)S(1)} %get-tuple-element.59), channel_id=1, source_target_pairs={{0,2},{1,3},{2,0},{3,1},{4,6},{5,7},{6,4},{7,5},{8,10},{9,11},{10,... | collective-permute-start | bytes 159752 | tf_op jit(solution)/shard_map/ppermute | solution.py:353
  13.9 1.8 collective-permute-start.1
  14.8 3.6 %collective-permute-start.2 = (bf16[8,3328]{1,0:T(8,128)(2,1)S(1)}, bf16[8,3328]{1,0:T(8,128)(2,1)S(1)}, u32[]{:S(2)}, u32[]{:S(2)}) collective-permute-start(bf16[8,3328]{1,0:T(8,128)(2,1)S(1)} %get-tuple-element.57), channel_id=1, source_target_pairs={{0,3},{1,2},{2,1},{3,0},{4,7},{5,6},{6,5},{7,4},{8,11},{9,10},{10,... | collective-permute-start | bytes 159752 | tf_op jit(solution)/shard_map/ppermute | solution.py:353
  19.1 35.3 %all-to-all-start = ((bf16[128,8,768]{2,1,0:T(8,128)(2,1)}), bf16[128,8,768]{2,1,0:T(8,128)(2,1)S(1)}, u32[]{:S(2)}, u32[]{:S(2)}) async-start(bf16[128,8,768]{2,1,0:T(8,128)(2,1)} %bitcast.77), calls=%async_computation | async-start | bytes 3145728 | tf_op jit(solution)/shard_map/all_to_all | solution.py:383
  64.4 55.3 %collective-permute-start.3 = (bf16[8,2,256,256]{3,2,1,0:T(8,128)(2,1)}, bf16[8,2,256,256]{3,2,1,0:T(8,128)(2,1)}, u32[]{:S(2)}, u32[]{:S(2)}) collective-permute-start(bf16[8,2,256,256]{3,2,1,0:T(8,128)(2,1)} %get-tuple-element.32.kv), channel_id=1, source_target_pairs={{0,4},{4,8},{8,12},{12,16},{16,20},{20,24},{24,28},{28,32},{32,36}... | collective-permute-start | bytes 6291464 | tf_op jit(solution)/shard_map/ppermute | solution.py:379
  68.6 54.8 %collective-permute-start.4 = (bf16[8,2,256,256]{3,2,1,0:T(8,128)(2,1)}, bf16[8,2,256,256]{3,2,1,0:T(8,128)(2,1)}, u32[]{:S(2)}, u32[]{:S(2)}) collective-permute-start(bf16[8,2,256,256]{3,2,1,0:T(8,128)(2,1)} %get-tuple-element.32.kv), channel_id=1, source_target_pairs={{4,0},{8,4},{12,8},{16,12},{20,16},{24,20},{28,24},{32,28},{36,32}... | collective-permute-start | bytes 6291464 | tf_op jit(solution)/shard_map/ppermute | solution.py:379
  70.2 4.9 %copy-start.7 = (s32[2048]{0:T(1024)}, s32[2048]{0:T(1024)S(1)}, u32[]{:S(2)}) copy-start(s32[2048]{0:T(1024)S(1)} %get-tuple-element.64) | copy-start | bytes 24580
  130.9 19.1 %collective-permute-start.5 = (bf16[1024,256]{1,0:T(8,128)(2,1)}, bf16[1024,256]{1,0:T(8,128)(2,1)S(1)}, u32[]{:S(2)}, u32[]{:S(2)}) collective-permute-start(bf16[1024,256]{1,0:T(8,128)(2,1)} %attend_halo.2.m0), channel_id=1, source_target_pairs={{0,2},{1,3},{2,0},{3,1},{4,6},{5,7},{6,4},{7,5},{8,10},{9,11},{10,... | collective-permute-start | bytes 1572872 | tf_op jit(solution)/shard_map/ppermute | solution.py:353
  131.6 26.0 %collective-permute-start.6 = (bf16[1024,256]{1,0:T(8,128)(2,1)}, bf16[1024,256]{1,0:T(8,128)(2,1)S(1)}, u32[]{:S(2)}, u32[]{:S(2)}) collective-permute-start(bf16[1024,256]{1,0:T(8,128)(2,1)} %attend_halo.2.m0), channel_id=1, source_target_pairs={{0,1},{1,0},{2,3},{3,2},{4,5},{5,4},{6,7},{7,6},{8,9},{9,8},{10,11... | collective-permute-start | bytes 1572872 | tf_op jit(solution)/shard_map/ppermute | solution.py:353
  150.0 44.1 %copy-start.11 = (bf16[1024,256]{1,0:T(8,128)(2,1)}, bf16[1024,256]{1,0:T(8,128)(2,1)S(1)}, u32[]{:S(2)}) copy-start(bf16[1024,256]{1,0:T(8,128)(2,1)S(1)} %collective-permute-done.5.m1) | copy-start | bytes 1572868
  150.0 7.6 %collective-permute-start.7 = (bf16[1024,256]{1,0:T(8,128)(2,1)S(1)}, bf16[1024,256]{1,0:T(8,128)(2,1)S(1)}, u32[]{:S(2)}, u32[]{:S(2)}) collective-permute-start(bf16[1024,256]{1,0:T(8,128)(2,1)S(1)} %collective-permute-done.5.m1), channel_id=1, source_target_pairs={{0,1},{1,0},{2,3},{3,2},{4,5},{5,4},{6,7},{7,6},{8,9},{9,8},{10,11... | collective-permute-start | bytes 1572872 | tf_op jit(solution)/shard_map/ppermute | solution.py:353
  156.2 54.0 %collective-permute-start.8 = (bf16[1024,256]{1,0:T(8,128)(2,1)}, bf16[1024,256]{1,0:T(8,128)(2,1)S(1)}, u32[]{:S(2)}, u32[]{:S(2)}) collective-permute-start(bf16[1024,256]{1,0:T(8,128)(2,1)} %attend_halo.3.m0), channel_id=1, source_target_pairs={{0,2},{1,3},{2,0},{3,1},{4,6},{5,7},{6,4},{7,5},{8,10},{9,11},{10,... | collective-permute-start | bytes 1572872 | tf_op jit(solution)/shard_map/ppermute | solution.py:353
  157.4 53.8 %collective-permute-start.9 = (bf16[1024,256]{1,0:T(8,128)(2,1)}, bf16[1024,256]{1,0:T(8,128)(2,1)S(1)}, u32[]{:S(2)}, u32[]{:S(2)}) collective-permute-start(bf16[1024,256]{1,0:T(8,128)(2,1)} %attend_halo.3.m0), channel_id=1, source_target_pairs={{0,1},{1,0},{2,3},{3,2},{4,5},{5,4},{6,7},{7,6},{8,9},{9,8},{10,11... | collective-permute-start | bytes 1572872 | tf_op jit(solution)/shard_map/ppermute | solution.py:353
  157.7 36.5 %copy-start.12 = (bf16[1024,256]{1,0:T(8,128)(2,1)}, bf16[1024,256]{1,0:T(8,128)(2,1)S(1)}, u32[]{:S(2)}) copy-start(bf16[1024,256]{1,0:T(8,128)(2,1)S(1)} %collective-permute-done.6.m2) | copy-start | bytes 1572868
  157.7 36.5 %copy-start.15 = (bf16[1024,256]{1,0:T(8,128)(2,1)}, bf16[1024,256]{1,0:T(8,128)(2,1)S(1)}, u32[]{:S(2)}) copy-start(bf16[1024,256]{1,0:T(8,128)(2,1)S(1)} %collective-permute-done.7.m3) | copy-start | bytes 1572868
  210.2 2.5 copy-start.13
  210.2 2.4 collective-permute-start.10
  211.2 1.5 copy-start.14
  212.7 0.8 copy-start.16
  213.5 43.4 %copy-start.10 = (bf16[1024,512]{1,0:T(8,128)(2,1)S(1)}, bf16[1024,512]{1,0:T(8,128)(2,1)}, u32[]{:S(2)}) copy-start(bf16[1024,512]{1,0:T(8,128)(2,1)} %get-tuple-element.45) | copy-start | bytes 3145732
  230.7 1.4 collective-permute-start.11
  232.1 2.8 collective-permute-start.12
  250.7 16.2 %all-to-all-start.2 = ((bf16[128,2,256]{2,1,0:T(2,128)(2,1)}), bf16[128,2,256]{2,1,0:T(2,128)(2,1)S(1)}, u32[]{:S(2)}, u32[]{:S(2)}) async-start(bf16[128,2,256]{2,1,0:T(2,128)(2,1)} %broadcast_in_dim.55), calls=%async_computation.2 | async-start | bytes 262144 | tf_op jit(solution)/shard_map/all_to_all | solution.py:383
  256.9 11.2 %collective-permute-start.13 = (bf16[1024,512]{1,0:T(8,128)(2,1)S(1)}, bf16[1024,512]{1,0:T(8,128)(2,1)}, u32[]{:S(2)}, u32[]{:S(2)}) collective-permute-start(bf16[1024,512]{1,0:T(8,128)(2,1)S(1)} %copy-done.10), channel_id=1, source_target_pairs={{0,1},{1,0},{2,3},{3,2},{4,5},{5,4},{6,7},{7,6},{8,9},{9,8},{10,11... | collective-permute-start | bytes 3145736 | tf_op jit(solution)/shard_map/ppermute | solution.py:353
  258.1 13.2 %collective-permute-start.15 = (bf16[1024,512]{1,0:T(8,128)(2,1)}, bf16[1024,512]{1,0:T(8,128)(2,1)S(1)}, u32[]{:S(2)}, u32[]{:S(2)}) collective-permute-start(bf16[1024,512]{1,0:T(8,128)(2,1)} %get-tuple-element.47), channel_id=1, source_target_pairs={{0,1},{1,0},{2,3},{3,2},{4,5},{5,4},{6,7},{7,6},{8,9},{9,8},{10,11... | collective-permute-start | bytes 3145736 | tf_op jit(solution)/shard_map/ppermute | solution.py:353
  267.5 2.2 copy-start.4
  270.7 1.6 copy-start.5
  270.7 26.8 %collective-permute-start.14 = (bf16[1024,256]{1,0:T(8,128)(2,1)}, bf16[1024,256]{1,0:T(8,128)(2,1)}, u32[]{:S(2)}, u32[]{:S(2)}) collective-permute-start(bf16[1024,256]{1,0:T(8,128)(2,1)} %fusion.4), channel_id=1, source_target_pairs={{0,2},{1,3},{2,0},{3,1},{4,6},{5,7},{6,4},{7,5},{8,10},{9,11},{10,... | collective-permute-start | bytes 1572872 | tf_op jit(solution)/shard_map/ppermute | solution.py:353
  272.3 2.6 copy-start.2
  272.3 0.9 copy-start.9
  272.3 2.2 copy-start.6
  272.6 26.7 %collective-permute-start.16 = (bf16[1024,256]{1,0:T(8,128)(2,1)S(1)}, bf16[1024,256]{1,0:T(8,128)(2,1)S(1)}, u32[]{:S(2)}, u32[]{:S(2)}) collective-permute-start(bf16[1024,256]{1,0:T(8,128)(2,1)S(1)} %fusion.1), channel_id=1, source_target_pairs={{0,2},{1,3},{2,0},{3,1},{4,6},{5,7},{6,4},{7,5},{8,10},{9,11},{10,... | collective-permute-start | bytes 1572872 | tf_op jit(solution)/shard_map/ppermute | solution.py:353
  297.4 2.1 copy-start.3
Sparse Core Ops, SparseCore 0:
  19.2 174.1 all-gather.1

commit v7 on v6

--- a/solution.py
+++ b/solution.py
@@ -16,7 +16,7 @@
 BOTH = ("req", "tp")
 NEG = -1e30
 FFP = 768
-REST = 3 * FFP + 1024
+REST = 3 * FFP
 QB = 256
 KB = 256
 
@@ -33,7 +33,7 @@
     return pl.CostEstimate(flops=flops, bytes_accessed=moved, transcendentals=transcendentals)
 
 
-def prep_kernel(order, wq, wk, wv, wo, wi, wg, w2, qkv, rest):
+def prep_kernel(order, wq, wk, wv, wo, wi, wg, w2, first, rest):
     row = lax.broadcasted_iota(jnp.int32, (256, 256), 0)
     col = lax.broadcasted_iota(jnp.int32, (256, 256), 1)
     source = (col % 128) // 32 * 64 + col // 128 * 32 + col % 32
@@ -46,9 +46,9 @@
             jnp.dot(w[:, at].astype(BF), turn, preferred_element_type=F32).astype(BF)
             for w in (wq, wk)
         )
-        mine = jnp.concatenate([q, k, wv[:, at].astype(BF)], axis=1)
-        for r in range(qkv.shape[0]):
-            qkv[r, t] = mine
+        mine = jnp.concatenate([q, k, wv[:, at].astype(BF), wo[:, at].astype(BF)], axis=1)
+        for r in range(first.shape[0]):
+            first[r, t] = mine
         pick = jnp.where((trow == tcol + 16 * t) & (tcol < 16), 1.0, 0.0).astype(BF)
         to = order[t]
         for n, w in enumerate((wi, wg, w2)):
@@ -56,7 +56,6 @@
             rest[to, :, FFP * n + 640 : FFP * n + 768] = jnp.dot(
                 w[:, 2560:2624].astype(BF), pick, preferred_element_type=F32
             ).astype(BF)
-        rest[to, :, 3 * FFP :] = wo[...].astype(BF)
 
 
 def prep(req_count, order, *weights):
@@ -64,7 +63,7 @@
         prep_kernel,
         in_specs=[pl.BlockSpec(memory_space=pltpu.SMEM)] + [vmem(*w.shape) for w in weights],
         out_shape=(
-            jax.ShapeDtypeStruct((req_count, 4, 8, 768), BF),
+            jax.ShapeDtypeStruct((req_count, 4, 8, 1024), BF),
             jax.ShapeDtypeStruct((4, 8, REST), BF),
         ),
         compiler_params=params(),
@@ -259,7 +258,7 @@
     return lax.dot_general(a, b, (((1,), (1,)), ((), ())), preferred_element_type=F32)
 
 
-def mlp_kernel(base, table, m0, m1, m2, m3, h, gain, last, before, *refs):
+def mlp_kernel(base, table, m0, m1, m2, m3, o0, o1, o2, o3, h, gain, last, before, *refs):
     *pieces, keep, send, picked, w, sem = refs
     count = w.shape[0]
 
@@ -281,9 +280,8 @@
     n = h.shape[0]
     wide = h[...].astype(F32)
     total = None
-    for j, m in enumerate((m0, m1, m2, m3)):
-        lo = pl.multiple_of(3 * FFP + 256 * table[j], 128)
-        piece = contract_last(m[...], rows(0, count, lo, 256))
+    for m, o in ((m0, o0), (m1, o1), (m2, o2), (m3, o3)):
+        piece = contract_last(m[...], o[...])
         total = piece if total is None else total + piece
     first = (wide + total).astype(BF)
     wide = first.astype(F32)
@@ -318,7 +316,7 @@
     picked[1] += pick(sent)
 
 
-def mlp(table, mixed, h, base, gain, last, before, pieces):
+def mlp(table, mixed, out_w, h, base, gain, last, before, pieces):
     n = 256
     rows = mixed[0].shape[0]
     count = sum(piece.shape[0] for piece in pieces)
@@ -332,6 +330,7 @@
             num_scalar_prefetch=1,
             grid=(rows // n,),
             in_specs=[block(256)] * 4
+            + [vmem(1024, 256)] * 4
             + [pl.BlockSpec((n, 1024), lambda i, *_: (i + base, 0))]
             + [vmem(1, 1024), vmem(*last.shape), vmem(*before.shape)]
             + [pl.BlockSpec(memory_space=pl.ANY)] * len(pieces),
@@ -346,7 +345,7 @@
         compiler_params=params(),
         cost_estimate=cost(rows * 1024 * (1024 + 3 * FFP) * 2, 12 << 20, rows * FFP),
         name="mlp",
-    )(table, *mixed, h, gain.reshape(1, 1024), last, before, *pieces)
+    )(table, *mixed, *out_w, h, gain.reshape(1, 1024), last, before, *pieces)
 
 
 def swap(x, bit):
@@ -355,14 +354,6 @@
 
 def turn_bits(n):
     return n % 2 * 2 + n // 2
-
-
-def gather_tp(x, after=None):
-    far = swap(x, 2)
-    near = swap(x, 1)
-    if after is not None:
-        far, _ = lax.optimization_barrier((far, after))
-    return x, far, near, swap(far, 1)
 
 
 def reduce_core(keep, send):
@@ -410,7 +401,7 @@
 
     four = jnp.arange(4, dtype=jnp.int32)
     place_of = turn_bits(four ^ tp_index)
-    qkv_block, rest_block = prep(req_count, place_of, wq, wk, wv, wo, wi_in, wi_gate, wo2)
+    first_block, rest_block = prep(req_count, place_of, wq, wk, wv, wo, wi_in, wi_gate, wo2)
     place = jnp.arange(count, dtype=jnp.int32)
     source = jnp.sum(
         jnp.where(shard_map[None, :] == place[:, None], place[None, :], 0), axis=1
@@ -419,6 +410,9 @@
         [rest_block[0], swap(rest_block[1], 2), swap(rest_block[2], 1), swap(rest_block[3], 3)], axis=0
     )
     hidden, lengths, rest_rows = lax.optimization_barrier((hidden_in, lengths, rest_rows))
+    rest = lax.all_gather(rest_rows, "req", axis=0, tiled=True).reshape(count, 8, REST)
+    far = jnp.arange(count, dtype=jnp.int32)
+    rest_target = shard_map[far // 4 * tp_count + (tp_index ^ turn_bits(far % 4))]
 
     ends = jnp.cumsum(lengths)
     base = req_index * slots
@@ -449,16 +443,17 @@
     qseg = segment[slots : 2 * slots].reshape(1, slots)
 
     normed = norm(hidden, attn_gain)
-    qkv_all = exchange(qkv_block.reshape(count, 8, 768), BOTH)
-    qkv_w = qkv_all[source].reshape(width, 768)
-    rest = [lax.all_gather(rest_rows, "req", axis=0, tiled=True).reshape(count, 8, REST)]
-    far = jnp.arange(count, dtype=jnp.int32)
-    rest_target = shard_map[far // 4 * tp_count + (tp_index ^ turn_bits(far % 4))]
-    query, kv, cache = qkv_project(normed, qkv_w, *turn)
+    first_all = exchange(first_block.reshape(count, 8, width), BOTH)
+    first_w = first_all[source].reshape(width, width)
+    query, kv, cache = qkv_project(normed, first_w, *turn)
     left = shift(kv, 1)
     right = shift(kv, -1)
+    out_w, kv = lax.optimization_barrier((first_w[:, 768:], kv))
+    out_far, out_near = swap(out_w, 2), swap(out_w, 1)
     parts = 2
     state = attend(0, 1, table, query, qseg, (kv, segs[1]), ())
+    out_far, out_near, state = lax.optimization_barrier((out_far, out_near, state))
+    out_w = (out_w, out_far, out_near, swap(out_far, 1))
     mixed = [
         attend(part, parts, table, query, qseg, (left, segs[0], right, segs[2]), state)
         for part in range(parts)
@@ -466,29 +461,34 @@
 
     last_slot = (ends - 1 - base).reshape(requests, 1)
     order = jnp.concatenate([tp_index ^ turn_bits(four), rest_target])
-    picked = jnp.zeros((2, requests, 512), F32)
-    bulk = []
-    after = mixed[1]
-    for part in range(parts):
-        keep, send, picked = mlp(
-            order,
-            gather_tp(mixed[part], after),
-            hidden_in,
-            part * (slots // parts // 256),
-            mlp_gain,
-            last_slot,
-            picked,
-            rest,
+    steps = slots // parts // 256
+
+    def feed(part, pieces, picked):
+        return mlp(
+            order, pieces, out_w, hidden_in, part * steps, mlp_gain, last_slot, picked, [rest]
         )
-        after = (keep, send)
-        bulk.append((keep, send))
+
+    far = [swap(m, 2) for m in mixed]
+    near = [swap(m, 1) for m in mixed]
+    far[0], _ = lax.optimization_barrier((far[0], mixed[1]))
+    keep, send, picked = feed(
+        0, (mixed[0], far[0], near[0], swap(far[0], 1)), jnp.zeros((2, requests, 512), F32)
+    )
+    keep, send, far[1] = lax.optimization_barrier((keep, send, far[1]))
+    last_piece = swap(far[1], 1)
+    pair, picked, last_piece = lax.optimization_barrier(
+        (reduce_core(keep, send), picked, last_piece)
+    )
+    top = reduce_far(*pair)
+    keep, send, picked = feed(1, (mixed[1], far[1], near[1], last_piece), picked)
+    picked, top = lax.optimization_barrier((picked, top))
 
     each = requests // req_count
     last_mine = reduce_far(*reduce_core(picked[0], picked[1].astype(BF)))
-    bulk, last_mine = lax.optimization_barrier((bulk, last_mine))
+    (keep, send), last_mine = lax.optimization_barrier(((keep, send), last_mine))
     taken = exchange(last_mine.reshape(req_count, each, 256), "req").astype(F32).sum(axis=0)
     spread = exchange(jnp.broadcast_to(taken.astype(BF)[None], (count, each, 256)), BOTH)
-    hidden_out = jnp.concatenate([reduce_far(*reduce_core(*pair)) for pair in bulk], axis=0)
+    hidden_out = jnp.concatenate([top, reduce_far(*reduce_core(keep, send))], axis=0)
     last = (
         spread.reshape(req_count, tp_count, each, 256)
         .transpose(0, 2, 1, 3)

time: 310 us -> 288 us (0.929)
  waiting for transfers between devices: 95.4 us -> 67.5 us
  Pallas kernels: 91.8 us -> 101 us
  starting transfers between devices: 36.4 us -> 28.5 us
  blocking collectives: 36.8 us -> 44.2 us
    all_gather x1, waiting for transfers between devices: 35.7 us -> 8.52 us  [body(): lax.all_gather(rest_rows, 'req', axis=0, tiled=True).reshape(count, 8, REST)]
    ppermute x15 -> x18, waiting for transfers between devices: 16.4 us -> 40.9 us  [swap(): return lax.ppermute(x, 'tp', [(i, i ^ bit) for i in range(4)])]
    ppermute x2, waiting for transfers between devices: 21.7 us -> 0.01 us  [shift(): lax.ppermute(x, 'req', [(i, i + by) for i in range(count) if 0 <= i + by...]
    pallas_call x3, Pallas kernels: 42.8 us -> 51.5 us  [attend(): pl.pallas_call(kernel, grid_spec=pltpu.PrefetchScalarGridSpec(num_scalar_...]
    all_to_all x2 -> x3, blocking collectives: 36.8 us -> 44.2 us  [exchange(): return lax.all_to_all(x, axes, split_axis=0, concat_axis=0, tiled=True)]
    all_to_all x2 -> x1, starting transfers between devices: 15.9 us -> 9.66 us  [exchange(): return lax.all_to_all(x, axes, split_axis=0, concat_axis=0, tiled=True)]
    all_to_all x2 -> x1, waiting for transfers between devices: 21.6 us -> 18.1 us  [exchange(): return lax.all_to_all(x, axes, split_axis=0, concat_axis=0, tiled=True)]
    ppermute x15 -> x18, starting transfers between devices: 15 us -> 13 us  [swap(): return lax.ppermute(x, 'tp', [(i, i ^ bit) for i in range(4)])]
  transfers between devices with their start and end apart: 20 -> 22, of which waited for: 11 -> 11; matrix products, arithmetic and copies ran while one was open for 8% -> 7% of each run, Pallas kernels for 24% -> 34%
where the time goes in v7:
time: 288 us; the launch traced here: 286 us
  Pallas kernels  101 us (35%)
  waiting for transfers between devices  67.5 us (23%)
  blocking collectives  44.2 us (15%)
  starting transfers between devices  28.5 us (10%)
  other arithmetic  17.1 us (6%)
  between operations  14.6 us (5%)
  local copies, waits for them, and re-layouts  12.6 us (4%)
    pallas_call x3, Pallas kernels, attend(): pl.pallas_call(kernel, grid_spec=pltpu.PrefetchScalarGridSpec(num_scalar_...  51.5 us
    all_to_all x3, blocking collectives, exchange(): return lax.all_to_all(x, axes, split_axis=0, concat_axis=0, tiled=True)  44.2 us
    ppermute x18, waiting for transfers between devices, swap(): return lax.ppermute(x, 'tp', [(i, i ^ bit) for i in range(4)])  40.9 us
    pallas_call x2, Pallas kernels, mlp(): pl.pallas_call(functools.partial(mlp_kernel, base), grid_spec=pltpu.Prefe...  32.6 us
    all_to_all x1, waiting for transfers between devices, exchange(): return lax.all_to_all(x, axes, split_axis=0, concat_axis=0, tiled=True)  18.1 us
    ppermute x18, starting transfers between devices, swap(): return lax.ppermute(x, 'tp', [(i, i ^ bit) for i in range(4)])  13 us
    all_to_all x1, starting transfers between devices, exchange(): return lax.all_to_all(x, axes, split_axis=0, concat_axis=0, tiled=True)  9.66 us
    all_gather x1, waiting for transfers between devices, body(): lax.all_gather(rest_rows, 'req', axis=0, tiled=True).reshape(count, 8, REST)  8.52 us
  transfers between devices with their start and end apart: 22, of which 11 were waited for; matrix products, arithmetic and copies ran while one was open for 7% of the time, Pallas kernels for 34%

profile of v7, /device:TPU:1, one launch (start us, length us, event | category | flops | bytes accessed | tf_op | source)
XLA Modules:
  0.0 286.3 jit_solution(1276864620532549628)
XLA Ops:
  7.2 0.5 fusion.20.order
  7.8 2.8 prep.1
  10.6 0.8 slice_bitcast_fusion.4
  11.4 2.5 collective-permute-start
  14.0 1.0 collective-permute-start.1
  14.9 0.4 collective-permute-done
  15.3 0.5 collective-permute-done.1
  15.8 2.5 collective-permute-done.2
  18.3 0.7 pad_maximum_fusion.1
  19.0 9.7 %all-to-all-start = ((bf16[128,8,1024]{2,1,0:T(8,128)(2,1)}), bf16[128,8,1024]{2,1,0:T(8,128)(2,1)S(1)}, u32[]{:S(2)}, u32[]{:S(2)}) async-start(bf16[128,8,1024]{2,1,0:T(8,128)(2,1)} %bitcast.79), calls=%async_computation | async-start | bytes 4194304 | tf_op jit(solution)/shard_map/all_to_all | solution.py:374
  29.1 5.9 %norm.1.x = bf16[2048,1024]{1,0:T(8,128)(2,1)} custom-call(bf16[2048,1024]{1,0:T(8,128)(2,1)} %h.4, f32[1,1024]{1,0:T(1,128)} %bitcast.89), custom_call_target="tpu_custom_call" | custom-call | flops 16777216 | bytes 8388608 | tf_op jit(solution)/shard_map/norm/pallas_call | solution.py:86
  35.0 0.7 add_subtract_fusion
  35.9 5.5 %multiply_sine_fusion = (f32[2048,128]{1,0:T(8,128)}, f32[2048,128]{1,0:T(8,128)}) fusion(f32[128]{0:T(128)S(1)} %fusion.25, f32[2048]{0:T(1024)S(1)} %subtract_convert_fusion), kind=kLoop, calls=%fused_computation.3 | loop fusion | flops 262144 | bytes 2105856 | tf_op jit(solution)/shard_map/sin | solution.py:428
  41.4 18.1 %all-to-all-done = bf16[128,8,1024]{2,1,0:T(8,128)(2,1)S(1)} async-done(((bf16[128,8,1024]{2,1,0:T(8,128)(2,1)}), bf16[128,8,1024]{2,1,0:T(8,128)(2,1)S(1)}, u32[]{:S(2)}, u32[]{:S(2)}) %all-to-all-start) | async-done | bytes 2097184 | tf_op jit(solution)/shard_map/all_to_all | solution.py:374
  59.5 2.0 gather_fusion.1
  61.5 8.2 %qkv.1 = (bf16[2048,256]{1,0:T(8,128)(2,1)}, bf16[8,2,256,256]{3,2,1,0:T(8,128)(2,1)}, bf16[2,2048,256]{2,1,0:T(8,128)(2,1)}) custom-call(bf16[2048,1024]{1,0:T(8,128)(2,1)} %norm.1.x, bf16[1024,1024]{1,0:T(8,128)(2,1)} %bitcast.77, f32[2048,128]{1,0:T(8,128)} %get-tuple-element.92.cos, f32[2048,128]{1,0:T(8,128)} %get-tuple-element.91.sin), custom_call_target="tpu_custom_call" | custom-call | flops 3221225472 | bytes 12582912 | tf_op jit(solution)/shard_map/qkv/pallas_call | solution.py:125
  69.6 4.5 %collective-permute-start.3 = (bf16[8,2,256,256]{3,2,1,0:T(8,128)(2,1)}, bf16[8,2,256,256]{3,2,1,0:T(8,128)(2,1)}, u32[]{:S(2)}, u32[]{:S(2)}) collective-permute-start(bf16[8,2,256,256]{3,2,1,0:T(8,128)(2,1)} %get-tuple-element.46.kv), channel_id=1, source_target_pairs={{0,4},{4,8},{8,12},{12,16},{16,20},{20,24},{24,28},{28,32},{32,36}... | collective-permute-start | bytes 6291464 | tf_op jit(solution)/shard_map/ppermute | solution.py:370
  74.2 1.3 collective-permute-start.4
  75.8 1.4 copy.41.kseg
  77.1 1.3 copy.42.lseg
  78.5 1.4 copy.43.rseg
  80.1 0.6 stack.2.table
  80.7 1.1 slice.102.o0
  82.1 0.5 collective-permute-start.6
  82.6 36.3 %attend_own.1 = (f32[4,72,2048]{2,1,0:T(8,128)}, f32[4,1,2048]{2,1,0:T(1,128)}) custom-call(s32[6,8]{1,0:T(8,128)} %stack.2.table, bf16[2048,256]{1,0:T(8,128)(2,1)} %get-tuple-element.43.q, s32[1,2048]{1,0:T(1,128)} %bitcast.84, bf16[8,2,256,256]{3,2,1,0:T(8,128)(2,1)} %get-tuple-element.46.kv, s32[2048,1]{1,0:T(8,128)} %copy.41.kseg), custom_call_target="tpu_custom_call" | custom-call | flops 12884901888 | bytes 8388608 | tf_op jit(solution)/shard_map/attend_own/pallas_call | solution.py:232
  118.9 16.6 %collective-permute-done.5.o1 = bf16[1024,256]{1,0:T(8,128)(2,1)S(1)} collective-permute-done((bf16[1024,256]{1,0:T(8,128)(2,1)S(1)}, bf16[1024,256]{1,0:T(8,128)(2,1)S(1)}, u32[]{:S(2)}, u32[]{:S(2)}) %collective-permute-start.5) | collective-permute-done | bytes 524320 | tf_op jit(solution)/shard_map/ppermute | solution.py:352
  135.5 0.7 collective-permute-start.10
  136.3 6.7 %attend_halo.3.m0 = bf16[1024,256]{1,0:T(8,128)(2,1)} custom-call(s32[6,8]{1,0:T(8,128)} %stack.2.table, bf16[2048,256]{1,0:T(8,128)(2,1)} %get-tuple-element.43.q, s32[1,2048]{1,0:T(1,128)} %bitcast.85, bf16[8,2,256,256]{3,2,1,0:T(8,128)(2,1)} %collective-permute-done.3.lkv, s32[2048,1]{1,0:T(8,128)} %copy.42.lseg, ...), custom_call_target="tpu_custom_call" | custom-call | flops 12884901888 | bytes 8388608 | tf_op jit(solution)/shard_map/attend_halo/pallas_call | solution.py:232
  143.0 0.9 collective-permute-start.7
  143.9 0.3 collective-permute-start.8
  144.3 8.5 %attend_halo.2.m0 = bf16[1024,256]{1,0:T(8,128)(2,1)} custom-call(s32[6,8]{1,0:T(8,128)} %stack.2.table, bf16[2048,256]{1,0:T(8,128)(2,1)} %get-tuple-element.43.q, s32[1,2048]{1,0:T(1,128)} %bitcast.86, bf16[8,2,256,256]{3,2,1,0:T(8,128)(2,1)} %collective-permute-done.3.lkv, s32[2048,1]{1,0:T(8,128)} %copy.42.lseg, ...), custom_call_target="tpu_custom_call" | custom-call | flops 12884901888 | bytes 8388608 | tf_op jit(solution)/shard_map/attend_halo/pallas_call | solution.py:232
  152.8 15.7 %collective-permute-done.7.m1 = bf16[1024,256]{1,0:T(8,128)(2,1)S(1)} collective-permute-done((bf16[1024,256]{1,0:T(8,128)(2,1)}, bf16[1024,256]{1,0:T(8,128)(2,1)S(1)}, u32[]{:S(2)}, u32[]{:S(2)}) %collective-permute-start.7) | collective-permute-done | bytes 524320 | tf_op jit(solution)/shard_map/ppermute | solution.py:352
  168.4 0.6 collective-permute-start.9
  169.1 1.2 gather_fusion
  170.3 0.6 pad_add_fusion.table
  171.0 0.8 collective-permute-start.11
  171.8 8.5 %all-gather.2.cloned.1.call-done = bf16[1024,2304]{1,0:T(8,128)(2,1)} async-done(((bf16[32,2304]{1,0:T(8,128)(2,1)}), bf16[1024,2304]{1,0:T(8,128)(2,1)}) %all-gather.2.cloned.1.call-update) | async-done | bytes 4718608 | tf_op jit(solution)/shard_map/all_gather | solution.py:413
  180.3 0.8 broadcast_in_dim.54.before
  181.1 16.4 %mlp.2 = (f32[1024,512]{1,0:T(8,128)}, bf16[1024,512]{1,0:T(8,128)(2,1)}, f32[2,64,512]{2,1,0:T(8,128)}) custom-call(s32[132]{0:T(256)} %pad_add_fusion.table, bf16[1024,256]{1,0:T(8,128)(2,1)} %attend_halo.3.m0, bf16[1024,256]{1,0:T(8,128)(2,1)} %copy-done.14, bf16[1024,256]{1,0:T(8,128)(2,1)} %copy-done.15, bf16[1024,256]{1,0:T(8,128)(2,1)} %copy-done.17, ...), custom_call_target="tpu_custom_call" | custom-call | flops 6979321856 | bytes 12582912 | tf_op jit(solution)/shard_map/mlp/pallas_call | solution.py:327
  197.5 0.9 collective-permute-start.13
  198.5 0.4 collective-permute-start.12
  198.9 2.6 collective-permute-done.13
  201.5 0.3 convert_element_type.87
  201.8 0.3 fusion.4
  202.3 0.6 copy-done.16
  202.9 16.2 %mlp.3 = (f32[1024,512]{1,0:T(8,128)}, bf16[1024,512]{1,0:T(8,128)(2,1)}, f32[2,64,512]{2,1,0:T(8,128)}) custom-call(s32[132]{0:T(256)} %pad_add_fusion.table, bf16[1024,256]{1,0:T(8,128)(2,1)} %attend_halo.2.m0, bf16[1024,256]{1,0:T(8,128)(2,1)} %copy-done.13, bf16[1024,256]{1,0:T(8,128)(2,1)} %collective-permute-done.12.m2, bf16[1024,256]{1,0:T(8,128)(2,1)} %copy-done.16, ...), custom_call_target="tpu_custom_call" | custom-call | flops 6979321856 | bytes 12582912 | tf_op jit(solution)/shard_map/mlp/pallas_call | solution.py:327
  219.3 0.8 copy-done.5
  220.1 0.5 collective-permute-start.16
  220.6 0.9 collective-permute-done.16
  221.5 1.1 collective-permute-start.17
  222.6 1.7 collective-permute-done.17
  224.4 1.6 collective-permute-start.18
  226.0 15.7 %all_to_all.21 = bf16[32,2,256]{2,1,0:T(2,128)(2,1)S(1)} all-to-all(bf16[32,2,256]{2,1,0:T(2,128)(2,1)S(1)} %reshape.544), channel_id=1, replica_groups=mesh['req'=32,'tp'=4] {'req'}, dimensions={0} | all-to-all | bytes 65536 | tf_op jit(solution)/shard_map/all_to_all | solution.py:374
  241.8 14.5 %all_to_all.22 = bf16[128,2,256]{2,1,0:T(2,128)(2,1)S(1)} all-to-all(bf16[128,2,256]{2,1,0:T(2,128)(2,1)S(1)} %broadcast_in_dim.55), channel_id=1, replica_groups=mesh['req'=32,'tp'=4] {'req','tp'}, dimensions={0} | all-to-all | bytes 262144 | tf_op jit(solution)/shard_map/all_to_all | solution.py:374
  256.8 1.5 convert_element_type.96
  258.4 1.5 fusion.1
  259.9 0.6 collective-permute-start.19
  260.5 0.5 add_rsqrt_fusion
  261.2 0.3 fusion
  261.5 0.5 convolution_reduce_fusion
  262.0 14.1 %all_to_all.23 = f32[128,1,64]{2,1,0:T(1,128)S(1)} all-to-all(f32[128,1,64]{2,1,0:T(1,128)S(1)} %broadcast_in_dim.56), channel_id=1, replica_groups=mesh['req'=32,'tp'=4] {'req','tp'}, dimensions={0} | all-to-all | bytes 65536 | tf_op jit(solution)/shard_map/all_to_all | solution.py:374
  276.1 0.7 reduce_max.39
  276.8 1.6 fusion.3
  278.4 1.0 pad_maximum_fusion
  (90 shorter events, 2.9 us)
Async XLA Ops:
  7.2 254.0 %copy-start = (f32[4,1024]{1,0:T(4,128)S(1)}, f32[4,1024]{1,0:T(4,128)}, u32[]{:S(2)}) copy-start(f32[4,1024]{1,0:T(4,128)} %param.29) | copy-start | bytes 49156
  7.2 173.1 %all-gather.2.cloned.1.call-start = ((), (), s32[]{:S(2)}) async-start(), calls=%async_computation.4 | async-start | bytes 4866048 | tf_op jit(solution)/shard_map/all_gather | solution.py:413
  11.4 3.9 %collective-permute-start = (bf16[8,2304]{1,0:T(8,128)(2,1)S(1)}, bf16[8,2304]{1,0:T(8,128)(2,1)S(1)}, u32[]{:S(2)}, u32[]{:S(2)}) collective-permute-start(bf16[8,2304]{1,0:T(8,128)(2,1)S(1)} %get-tuple-element.85), channel_id=1, source_target_pairs={{0,2},{1,3},{2,0},{3,1},{4,6},{5,7},{6,4},{7,5},{8,10},{9,11},{10,... | collective-permute-start | bytes 110600 | tf_op jit(solution)/shard_map/ppermute | solution.py:352
  14.0 1.8 collective-permute-start.1
  14.9 3.4 %collective-permute-start.2 = (bf16[8,2304]{1,0:T(8,128)(2,1)S(1)}, bf16[8,2304]{1,0:T(8,128)(2,1)S(1)}, u32[]{:S(2)}, u32[]{:S(2)}) collective-permute-start(bf16[8,2304]{1,0:T(8,128)(2,1)S(1)} %get-tuple-element.83), channel_id=1, source_target_pairs={{0,3},{1,2},{2,1},{3,0},{4,7},{5,6},{6,5},{7,4},{8,11},{9,10},{10,... | collective-permute-start | bytes 110600 | tf_op jit(solution)/shard_map/ppermute | solution.py:352
  19.0 9.7 %copy-start.1 = (s32[128]{0:T(128)S(1)}, s32[128]{0:T(128)}, u32[]{:S(2)}) copy-start(s32[128]{0:T(128)} %param.18) | copy-start | bytes 1540
  19.0 9.9 %copy-start.7 = (s32[64]{0:T(128)S(1)}, s32[64]{0:T(128)}, u32[]{:S(2)}) copy-start(s32[64]{0:T(128)} %param.16) | copy-start | bytes 772
  19.0 40.5 %all-to-all-start = ((bf16[128,8,1024]{2,1,0:T(8,128)(2,1)}), bf16[128,8,1024]{2,1,0:T(8,128)(2,1)S(1)}, u32[]{:S(2)}, u32[]{:S(2)}) async-start(bf16[128,8,1024]{2,1,0:T(8,128)(2,1)} %bitcast.79), calls=%async_computation | async-start | bytes 4194304 | tf_op jit(solution)/shard_map/all_to_all | solution.py:374
  69.6 66.6 %collective-permute-start.3 = (bf16[8,2,256,256]{3,2,1,0:T(8,128)(2,1)}, bf16[8,2,256,256]{3,2,1,0:T(8,128)(2,1)}, u32[]{:S(2)}, u32[]{:S(2)}) collective-permute-start(bf16[8,2,256,256]{3,2,1,0:T(8,128)(2,1)} %get-tuple-element.46.kv), channel_id=1, source_target_pairs={{0,4},{4,8},{8,12},{12,16},{16,20},{20,24},{24,28},{28,32},{32,36}... | collective-permute-start | bytes 6291464 | tf_op jit(solution)/shard_map/ppermute | solution.py:370
  74.2 62.1 %collective-permute-start.4 = (bf16[8,2,256,256]{3,2,1,0:T(8,128)(2,1)}, bf16[8,2,256,256]{3,2,1,0:T(8,128)(2,1)}, u32[]{:S(2)}, u32[]{:S(2)}) collective-permute-start(bf16[8,2,256,256]{3,2,1,0:T(8,128)(2,1)} %get-tuple-element.46.kv), channel_id=1, source_target_pairs={{4,0},{8,4},{12,8},{16,12},{20,16},{24,20},{28,24},{32,28},{36,32}... | collective-permute-start | bytes 6291464 | tf_op jit(solution)/shard_map/ppermute | solution.py:370
  75.8 6.1 %copy-start.6 = (s32[2048]{0:T(1024)}, s32[2048]{0:T(1024)S(1)}, u32[]{:S(2)}) copy-start(s32[2048]{0:T(1024)S(1)} %get-tuple-element.90) | copy-start | bytes 24580
  81.8 37.1 %copy-start.4 = (bf16[1024,256]{1,0:T(8,128)(2,1)}, bf16[1024,256]{1,0:T(8,128)(2,1)S(1)}, u32[]{:S(2)}) copy-start(bf16[1024,256]{1,0:T(8,128)(2,1)S(1)} %slice.102.o0) | copy-start | bytes 1572868
  81.8 53.7 %collective-permute-start.5 = (bf16[1024,256]{1,0:T(8,128)(2,1)S(1)}, bf16[1024,256]{1,0:T(8,128)(2,1)S(1)}, u32[]{:S(2)}, u32[]{:S(2)}) collective-permute-start(bf16[1024,256]{1,0:T(8,128)(2,1)S(1)} %slice.102.o0), channel_id=1, source_target_pairs={{0,2},{1,3},{2,0},{3,1},{4,6},{5,7},{6,4},{7,5},{8,10},{9,11},{10,... | collective-permute-start | bytes 1572872 | tf_op jit(solution)/shard_map/ppermute | solution.py:352
  82.1 53.4 %collective-permute-start.6 = (bf16[1024,256]{1,0:T(8,128)(2,1)S(1)}, bf16[1024,256]{1,0:T(8,128)(2,1)S(1)}, u32[]{:S(2)}, u32[]{:S(2)}) collective-permute-start(bf16[1024,256]{1,0:T(8,128)(2,1)S(1)} %slice.102.o0), channel_id=1, source_target_pairs={{0,1},{1,0},{2,3},{3,2},{4,5},{5,4},{6,7},{7,6},{8,9},{9,8},{10,11... | collective-permute-start | bytes 1572872 | tf_op jit(solution)/shard_map/ppermute | solution.py:352
  135.5 7.5 %copy-start.9 = (bf16[1024,256]{1,0:T(8,128)(2,1)}, bf16[1024,256]{1,0:T(8,128)(2,1)S(1)}, u32[]{:S(2)}) copy-start(bf16[1024,256]{1,0:T(8,128)(2,1)S(1)} %collective-permute-done.5.o1) | copy-start | bytes 1572868
  135.5 7.5 %copy-start.10 = (bf16[1024,256]{1,0:T(8,128)(2,1)}, bf16[1024,256]{1,0:T(8,128)(2,1)S(1)}, u32[]{:S(2)}) copy-start(bf16[1024,256]{1,0:T(8,128)(2,1)S(1)} %collective-permute-done.6.o2) | copy-start | bytes 1572868
  135.5 36.2 %collective-permute-start.10 = (bf16[1024,256]{1,0:T(8,128)(2,1)S(1)}, bf16[1024,256]{1,0:T(8,128)(2,1)S(1)}, u32[]{:S(2)}, u32[]{:S(2)}) collective-permute-start(bf16[1024,256]{1,0:T(8,128)(2,1)S(1)} %collective-permute-done.5.o1), channel_id=1, source_target_pairs={{0,1},{1,0},{2,3},{3,2},{4,5},{5,4},{6,7},{7,6},{8,9},{9,8},{10,11... | collective-permute-start | bytes 1572872 | tf_op jit(solution)/shard_map/ppermute | solution.py:352
  143.0 25.4 %collective-permute-start.7 = (bf16[1024,256]{1,0:T(8,128)(2,1)}, bf16[1024,256]{1,0:T(8,128)(2,1)S(1)}, u32[]{:S(2)}, u32[]{:S(2)}) collective-permute-start(bf16[1024,256]{1,0:T(8,128)(2,1)} %attend_halo.3.m0), channel_id=1, source_target_pairs={{0,2},{1,3},{2,0},{3,1},{4,6},{5,7},{6,4},{7,5},{8,10},{9,11},{10,... | collective-permute-start | bytes 1572872 | tf_op jit(solution)/shard_map/ppermute | solution.py:352
  143.9 27.8 %collective-permute-start.8 = (bf16[1024,256]{1,0:T(8,128)(2,1)}, bf16[1024,256]{1,0:T(8,128)(2,1)S(1)}, u32[]{:S(2)}, u32[]{:S(2)}) collective-permute-start(bf16[1024,256]{1,0:T(8,128)(2,1)} %attend_halo.3.m0), channel_id=1, source_target_pairs={{0,1},{1,0},{2,3},{3,2},{4,5},{5,4},{6,7},{7,6},{8,9},{9,8},{10,11... | collective-permute-start | bytes 1572872 | tf_op jit(solution)/shard_map/ppermute | solution.py:352
  168.4 12.6 %copy-start.14 = (bf16[1024,256]{1,0:T(8,128)(2,1)}, bf16[1024,256]{1,0:T(8,128)(2,1)S(1)}, u32[]{:S(2)}) copy-start(bf16[1024,256]{1,0:T(8,128)(2,1)S(1)} %collective-permute-done.7.m1) | copy-start | bytes 1572868
  168.4 3.3 %collective-permute-start.9 = (bf16[1024,256]{1,0:T(8,128)(2,1)S(1)}, bf16[1024,256]{1,0:T(8,128)(2,1)S(1)}, u32[]{:S(2)}, u32[]{:S(2)}) collective-permute-start(bf16[1024,256]{1,0:T(8,128)(2,1)S(1)} %collective-permute-done.7.m1), channel_id=1, source_target_pairs={{0,1},{1,0},{2,3},{3,2},{4,5},{5,4},{6,7},{7,6},{8,9},{9,8},{10,11... | collective-permute-start | bytes 1572872 | tf_op jit(solution)/shard_map/ppermute | solution.py:352
  171.0 26.5 %collective-permute-start.11 = (bf16[1024,256]{1,0:T(8,128)(2,1)}, bf16[1024,256]{1,0:T(8,128)(2,1)S(1)}, u32[]{:S(2)}, u32[]{:S(2)}) collective-permute-start(bf16[1024,256]{1,0:T(8,128)(2,1)} %attend_halo.2.m0), channel_id=1, source_target_pairs={{0,2},{1,3},{2,0},{3,1},{4,6},{5,7},{6,4},{7,5},{8,10},{9,11},{10,... | collective-permute-start | bytes 1572872 | tf_op jit(solution)/shard_map/ppermute | solution.py:352
  171.7 9.3 %copy-start.11 = (bf16[1024,256]{1,0:T(8,128)(2,1)}, bf16[1024,256]{1,0:T(8,128)(2,1)S(1)}, u32[]{:S(2)}) copy-start(bf16[1024,256]{1,0:T(8,128)(2,1)S(1)} %collective-permute-done.10.o3) | copy-start | bytes 1572868
  171.7 9.3 %copy-start.15 = (bf16[1024,256]{1,0:T(8,128)(2,1)}, bf16[1024,256]{1,0:T(8,128)(2,1)S(1)}, u32[]{:S(2)}) copy-start(bf16[1024,256]{1,0:T(8,128)(2,1)S(1)} %collective-permute-done.8.m2) | copy-start | bytes 1572868
  171.8 9.3 %copy-start.17 = (bf16[1024,256]{1,0:T(8,128)(2,1)}, bf16[1024,256]{1,0:T(8,128)(2,1)S(1)}, u32[]{:S(2)}) copy-start(bf16[1024,256]{1,0:T(8,128)(2,1)S(1)} %collective-permute-done.9.m3) | copy-start | bytes 1572868
  181.1 17.4 %copy-start.12 = (bf16[1024,256]{1,0:T(8,128)(2,1)S(1)}, bf16[1024,256]{1,0:T(8,128)(2,1)}, u32[]{:S(2)}) copy-start(bf16[1024,256]{1,0:T(8,128)(2,1)} %attend_halo.2.m0) | copy-start | bytes 1572868
  197.4 4.3 %copy-start.2 = (f32[1024,512]{1,0:T(8,128)S(1)}, f32[1024,512]{1,0:T(8,128)}, u32[]{:S(2)}) copy-start(f32[1024,512]{1,0:T(8,128)} %get-tuple-element.58) | copy-start | bytes 6291460
  197.5 4.6 %copy-start.13 = (bf16[1024,256]{1,0:T(8,128)(2,1)}, bf16[1024,256]{1,0:T(8,128)(2,1)S(1)}, u32[]{:S(2)}) copy-start(bf16[1024,256]{1,0:T(8,128)(2,1)S(1)} %collective-permute-done.11.m1) | copy-start | bytes 1572868
  197.5 4.0 %collective-permute-start.13 = (bf16[1024,512]{1,0:T(8,128)(2,1)}, bf16[1024,512]{1,0:T(8,128)(2,1)S(1)}, u32[]{:S(2)}, u32[]{:S(2)}) collective-permute-start(bf16[1024,512]{1,0:T(8,128)(2,1)} %get-tuple-element.59), channel_id=1, source_target_pairs={{0,1},{1,0},{2,3},{3,2},{4,5},{5,4},{6,7},{7,6},{8,9},{9,8},{10,11... | collective-permute-start | bytes 3145736 | tf_op jit(solution)/shard_map/ppermute | solution.py:352
  198.4 3.7 %collective-permute-start.14 = (bf16[1024,256]{1,0:T(8,128)(2,1)S(1)}, bf16[1024,256]{1,0:T(8,128)(2,1)S(1)}, u32[]{:S(2)}, u32[]{:S(2)}) collective-permute-start(bf16[1024,256]{1,0:T(8,128)(2,1)S(1)} %collective-permute-done.11.m1), channel_id=1, source_target_pairs={{0,1},{1,0},{2,3},{3,2},{4,5},{5,4},{6,7},{7,6},{8,9},{9,8},{10,11... | collective-permute-start | bytes 1572872 | tf_op jit(solution)/shard_map/ppermute | solution.py:352
  198.5 3.8 %collective-permute-start.12 = (bf16[1024,256]{1,0:T(8,128)(2,1)S(1)}, bf16[1024,256]{1,0:T(8,128)(2,1)}, u32[]{:S(2)}, u32[]{:S(2)}) collective-permute-start(bf16[1024,256]{1,0:T(8,128)(2,1)S(1)} %copy-done.12), channel_id=1, source_target_pairs={{0,1},{1,0},{2,3},{3,2},{4,5},{5,4},{6,7},{7,6},{8,9},{9,8},{10,11... | collective-permute-start | bytes 1572872 | tf_op jit(solution)/shard_map/ppermute | solution.py:352
  202.1 0.8 copy-start.16
  202.1 17.0 %collective-permute-start.15 = (bf16[1024,256]{1,0:T(8,128)(2,1)S(1)}, bf16[1024,256]{1,0:T(8,128)(2,1)S(1)}, u32[]{:S(2)}, u32[]{:S(2)}) collective-permute-start(bf16[1024,256]{1,0:T(8,128)(2,1)S(1)} %get-tuple-element.65), channel_id=1, source_target_pairs={{0,2},{1,3},{2,0},{3,1},{4,6},{5,7},{6,4},{7,5},{8,10},{9,11},{10,... | collective-permute-start | bytes 1572872 | tf_op jit(solution)/shard_map/ppermute | solution.py:352
  219.1 1.0 copy-start.5
  220.1 1.4 collective-permute-start.16
  221.5 2.8 collective-permute-start.17
  224.4 32.5 %collective-permute-start.18 = (bf16[1024,512]{1,0:T(8,128)(2,1)}, bf16[1024,512]{1,0:T(8,128)(2,1)}, u32[]{:S(2)}, u32[]{:S(2)}) collective-permute-start(bf16[1024,512]{1,0:T(8,128)(2,1)} %get-tuple-element.71), channel_id=1, source_target_pairs={{0,1},{1,0},{2,3},{3,2},{4,5},{5,4},{6,7},{7,6},{8,9},{9,8},{10,11... | collective-permute-start | bytes 3145736 | tf_op jit(solution)/shard_map/ppermute | solution.py:352
  258.4 2.8 copy-start.8
  258.4 3.1 %copy-start.3 = (f32[384,1024]{1,0:T(8,128)S(1)}, f32[384,1024]{1,0:T(8,128)}, u32[]{:S(2)}) copy-start(f32[384,1024]{1,0:T(8,128)} %param.26) | copy-start | bytes 4718596
  259.9 16.9 %collective-permute-start.19 = (bf16[1024,256]{1,0:T(8,128)(2,1)S(1)}, bf16[1024,256]{1,0:T(8,128)(2,1)}, u32[]{:S(2)}, u32[]{:S(2)}) collective-permute-start(bf16[1024,256]{1,0:T(8,128)(2,1)S(1)} %fusion.1), channel_id=1, source_target_pairs={{0,2},{1,3},{2,0},{3,1},{4,6},{5,7},{6,4},{7,5},{8,10},{9,11},{10,... | collective-permute-start | bytes 1572872 | tf_op jit(solution)/shard_map/ppermute | solution.py:352
Sparse Core Ops, SparseCore 0:
  19.1 161.1 all-gather.1

commit v8 on v7

--- a/solution.py
+++ b/solution.py
@@ -199,7 +199,9 @@
     m_out[...] = m_sc[...]
 
 
-def halo_kernel(base, table, q, qseg, lkv, lseg, rkv, rseg, acc_in, m_in, out, qm, m_sc, acc):
+def halo_kernel(
+    base, table, q, qseg, lkv, lseg, rkv, rseg, last, acc_in, m_in, out, picked, qm, m_sc, acc
+):
     i = pl.program_id(0) + base
     spread_heads(q, qm)
     m_sc[...] = m_in[...]
@@ -207,7 +209,16 @@
     attend_span(table, 2, i, qm, lkv, lseg, qseg, m_sc, acc)
     attend_span(table, 4, i, qm, rkv, rseg, qseg, m_sc, acc)
     heads = [acc[h, :HEAD_DIM] / acc[h, HEAD_DIM : HEAD_DIM + 1] for h in range(4)]
-    out[...] = jnp.transpose(jnp.concatenate(heads, axis=0)).astype(BF)
+    mixed = jnp.transpose(jnp.concatenate(heads, axis=0)).astype(BF)
+    out[...] = mixed
+    slot = lax.broadcasted_iota(jnp.int32, (last.shape[0], QB), 1) + i * QB
+    ends_here = jnp.where(last[...] == slot, 1.0, 0.0).astype(BF)
+
+    @pl.when(pl.program_id(0) == 0)
+    def _():
+        picked[...] = jnp.zeros_like(picked)
+
+    picked[...] += jnp.dot(ends_here, mixed, preferred_element_type=F32)
 
 
 def attend(part, parts, table, q, qseg, sources, state):
@@ -220,8 +231,12 @@
     ]
     if state:
         kernel = functools.partial(halo_kernel, base)
-        out_specs = pl.BlockSpec((QB, 256), lambda i, *_: (i, 0))
-        out_shape = jax.ShapeDtypeStruct((rows // parts, 256), BF)
+        requests = sources[-1].shape[0]
+        out_specs = [pl.BlockSpec((QB, 256), lambda i, *_: (i, 0)), vmem(requests, 256)]
+        out_shape = (
+            jax.ShapeDtypeStruct((rows // parts, 256), BF),
+            jax.ShapeDtypeStruct((requests, 256), F32),
+        )
     else:
         kernel = own_kernel
         out_specs = state_specs
@@ -258,30 +273,38 @@
     return lax.dot_general(a, b, (((1,), (1,)), ((), ())), preferred_element_type=F32)
 
 
-def mlp_kernel(base, table, m0, m1, m2, m3, o0, o1, o2, o3, h, gain, last, before, *refs):
-    *pieces, keep, send, picked, w, sem = refs
+def mlp_kernel(extra, table, m0, m1, m2, m3, o0, o1, o2, o3, h, gain, weights, *refs):
+    lasts = refs[: 5 * extra]
+    outs = refs[5 * extra :]
+    *outs, w, sem = outs
+    keep, send = outs[:2]
     count = w.shape[0]
+    step = pl.program_id(0)
+
+    def load(ref, n):
+        x = ref[...]
+        if extra:
+            last = lasts[n][...]
+            fill = jnp.zeros((x.shape[0] - last.shape[0], x.shape[1]), BF)
+            x = jnp.where(step == 0, jnp.concatenate([last, fill], axis=0), x)
+        return x
 
     @pl.when(pl.program_id(0) == 0)
     def _():
-        done = 4
-        for piece in pieces:
-
-            @pl.loop(0, piece.shape[0])
-            def _(n, piece=piece, done=done):
-                pltpu.make_async_copy(piece.at[n], w.at[table[done + n]], sem).start()
-
-            done += piece.shape[0]
+        @pl.loop(0, count)
+        def _(k):
+            pltpu.make_async_copy(weights.at[k], w.at[table[4 + k]], sem).start()
+
         pltpu.make_async_copy(w, w, sem).wait()
 
     def rows(at, size, lo, width):
         return w[pl.ds(at, size), :, pl.ds(lo, width)].reshape(8 * size, width)
 
     n = h.shape[0]
-    wide = h[...].astype(F32)
+    wide = load(h, 4).astype(F32)
     total = None
-    for m, o in ((m0, o0), (m1, o1), (m2, o2), (m3, o3)):
-        piece = contract_last(m[...], o[...])
+    for j, (m, o) in enumerate(((m0, o0), (m1, o1), (m2, o2), (m3, o3))):
+        piece = contract_last(load(m, j), o[...])
         total = piece if total is None else total + piece
     first = (wide + total).astype(BF)
     wide = first.astype(F32)
@@ -300,60 +323,61 @@
     sent = jnp.concatenate([down(2), down(3)], axis=1).astype(BF)
     keep[...] = kept
     send[...] = sent
-    slot = lax.broadcasted_iota(jnp.int32, (last.shape[0], n), 1) + (pl.program_id(0) + base) * n
-    ends_here = jnp.where(last[...] == slot, 1.0, 0.0).astype(BF)
-    coarse = kept.astype(BF)
-    fine = (kept - coarse.astype(F32)).astype(BF)
-
-    def pick(x):
-        return jnp.dot(ends_here, x, preferred_element_type=F32)
-
-    @pl.when(pl.program_id(0) == 0)
-    def _():
-        picked[...] = before[...]
-
-    picked[0] += pick(coarse) + pick(fine)
-    picked[1] += pick(sent)
-
-
-def mlp(table, mixed, out_w, h, base, gain, last, before, pieces):
+    if extra:
+
+        @pl.when(step == 0)
+        def _():
+            rows = lasts[0].shape[0]
+            outs[2][...] = kept[:rows]
+            outs[3][...] = sent[:rows]
+
+
+def mlp(table, mixed, out_w, h, base, gain, weights, lasts=()):
     n = 256
     rows = mixed[0].shape[0]
-    count = sum(piece.shape[0] for piece in pieces)
-
-    def block(width):
-        return pl.BlockSpec((n, width), lambda i, *_: (i, 0))
-
+    count = weights.shape[0]
+    extra = 1 if lasts else 0
+
+    def block(width, base=0):
+        return pl.BlockSpec((n, width), lambda i, *_: (jnp.maximum(i - extra, 0) + base, 0))
+
+    out_specs = [block(512), block(512)]
+    out_shape = [
+        jax.ShapeDtypeStruct((rows, 512), F32),
+        jax.ShapeDtypeStruct((rows, 512), BF),
+    ]
+    if lasts:
+        held = lasts[0].shape[0]
+        out_specs += [vmem(held, 512), vmem(held, 512)]
+        out_shape += [
+            jax.ShapeDtypeStruct((held, 512), F32),
+            jax.ShapeDtypeStruct((held, 512), BF),
+        ]
     return pl.pallas_call(
-        functools.partial(mlp_kernel, base),
+        functools.partial(mlp_kernel, extra),
         grid_spec=pltpu.PrefetchScalarGridSpec(
             num_scalar_prefetch=1,
-            grid=(rows // n,),
+            grid=(rows // n + extra,),
             in_specs=[block(256)] * 4
             + [vmem(1024, 256)] * 4
-            + [pl.BlockSpec((n, 1024), lambda i, *_: (i + base, 0))]
-            + [vmem(1, 1024), vmem(*last.shape), vmem(*before.shape)]
-            + [pl.BlockSpec(memory_space=pl.ANY)] * len(pieces),
-            out_specs=[block(512), block(512), vmem(*before.shape)],
+            + [block(1024, base), vmem(1, 1024), pl.BlockSpec(memory_space=pl.ANY)]
+            + [vmem(*x.shape) for x in lasts],
+            out_specs=out_specs,
             scratch_shapes=[pltpu.VMEM((count, 8, REST), BF), pltpu.SemaphoreType.DMA(())],
         ),
-        out_shape=(
-            jax.ShapeDtypeStruct((rows, 512), F32),
-            jax.ShapeDtypeStruct((rows, 512), BF),
-            jax.ShapeDtypeStruct(before.shape, F32),
-        ),
+        out_shape=tuple(out_shape),
         compiler_params=params(),
         cost_estimate=cost(rows * 1024 * (1024 + 3 * FFP) * 2, 12 << 20, rows * FFP),
         name="mlp",
-    )(table, *mixed, *out_w, h, gain.reshape(1, 1024), last, before, *pieces)
+    )(table, *mixed, *out_w, h, gain.reshape(1, 1024), weights, *lasts)
+
+
+def turn_bits(n):
+    return n % 2 * 2 + n // 2
 
 
 def swap(x, bit):
     return lax.ppermute(x, "tp", [(i, i ^ bit) for i in range(4)])
-
-
-def turn_bits(n):
-    return n % 2 * 2 + n // 2
 
 
 def reduce_core(keep, send):
@@ -454,39 +478,45 @@
     state = attend(0, 1, table, query, qseg, (kv, segs[1]), ())
     out_far, out_near, state = lax.optimization_barrier((out_far, out_near, state))
     out_w = (out_w, out_far, out_near, swap(out_far, 1))
-    mixed = [
-        attend(part, parts, table, query, qseg, (left, segs[0], right, segs[2]), state)
-        for part in range(parts)
-    ]
-
     last_slot = (ends - 1 - base).reshape(requests, 1)
+    halo = (left, segs[0], right, segs[2], last_slot)
+    mixed, picked = zip(
+        *[attend(part, parts, table, query, qseg, halo, state) for part in range(parts)]
+    )
+
+    holds = (last_slot >= 0) & (last_slot < slots)
+    last_in = jnp.where(holds, hidden[jnp.clip(last_slot[:, 0], 0, slots - 1)], 0)
+    last_mixed = sum(picked).astype(BF)
+    last_far = swap(last_mixed, 2)
+    lasts = (last_mixed, last_far, swap(last_mixed, 1), swap(last_far, 1), last_in)
+
     order = jnp.concatenate([tp_index ^ turn_bits(four), rest_target])
     steps = slots // parts // 256
 
-    def feed(part, pieces, picked):
+    def feed(part, pieces, *lasts):
         return mlp(
-            order, pieces, out_w, hidden_in, part * steps, mlp_gain, last_slot, picked, [rest]
+            order, pieces, out_w, hidden_in, part * steps, mlp_gain, rest, *lasts
         )
 
     far = [swap(m, 2) for m in mixed]
     near = [swap(m, 1) for m in mixed]
     far[0], _ = lax.optimization_barrier((far[0], mixed[1]))
-    keep, send, picked = feed(
-        0, (mixed[0], far[0], near[0], swap(far[0], 1)), jnp.zeros((2, requests, 512), F32)
-    )
-    keep, send, far[1] = lax.optimization_barrier((keep, send, far[1]))
+    keep, send, last_keep, last_send = feed(
+        0, (mixed[0], far[0], near[0], swap(far[0], 1)), lasts
+    )
+    last_keep, last_send, keep, send, far[1] = lax.optimization_barrier(
+        (last_keep, last_send, keep, send, far[1])
+    )
     last_piece = swap(far[1], 1)
-    pair, picked, last_piece = lax.optimization_barrier(
-        (reduce_core(keep, send), picked, last_piece)
+    last_mine = reduce_far(*reduce_core(last_keep, last_send))
+    pair, last_mine, last_piece, piece = lax.optimization_barrier(
+        (reduce_core(keep, send), last_mine, last_piece, mixed[1])
     )
     top = reduce_far(*pair)
-    keep, send, picked = feed(1, (mixed[1], far[1], near[1], last_piece), picked)
-    picked, top = lax.optimization_barrier((picked, top))
-
     each = requests // req_count
-    last_mine = reduce_far(*reduce_core(picked[0], picked[1].astype(BF)))
-    (keep, send), last_mine = lax.optimization_barrier(((keep, send), last_mine))
     taken = exchange(last_mine.reshape(req_count, each, 256), "req").astype(F32).sum(axis=0)
+    keep, send = feed(1, (piece, far[1], near[1], last_piece))
+    taken, keep, send, top = lax.optimization_barrier((taken, keep, send, top))
     spread = exchange(jnp.broadcast_to(taken.astype(BF)[None], (count, each, 256)), BOTH)
     hidden_out = jnp.concatenate([top, reduce_far(*reduce_core(keep, send))], axis=0)
     last = (

time: 288 us -> 284 us (0.986)
  blocking collectives: 44.2 us -> 32.9 us
  starting transfers between devices: 28.5 us -> 37.6 us
  waiting for transfers between devices: 67.5 us -> 61.8 us
  other arithmetic: 17.1 us -> 20.3 us
  local copies, waits for them, and re-layouts: 12.6 us -> 15.7 us
    all_to_all x3 -> x2, blocking collectives: 44.2 us -> 32.9 us  [exchange(): return lax.all_to_all(x, axes, split_axis=0, concat_axis=0, tiled=True)]
    all_to_all x1 -> x2, starting transfers between devices: 9.66 us -> 17.6 us  [exchange(): return lax.all_to_all(x, axes, split_axis=0, concat_axis=0, tiled=True)]
    all_gather x1, waiting for transfers between devices: 8.52 us -> 3.73 us  [body(): lax.all_gather(rest_rows, 'req', axis=0, tiled=True).reshape(count, 8, REST)]
    gather x0 -> x1, local copies, waits for them, and re-layouts: none -> 3.79 us  [body(): hidden[jnp.clip(last_slot[:, 0], 0, slots - 1)]]
    all_to_all x1 -> x2, waiting for transfers between devices: 18.1 us -> 15.9 us  [exchange(): return lax.all_to_all(x, axes, split_axis=0, concat_axis=0, tiled=True)]
    ppermute x18 -> x21, waiting for transfers between devices: 40.9 us -> 42.1 us  [swap(): return lax.ppermute(x, 'tp', [(i, i ^ bit) for i in range(4)])]
    ppermute x18 -> x21, starting transfers between devices: 13 us -> 14.1 us  [swap(): return lax.ppermute(x, 'tp', [(i, i ^ bit) for i in range(4)])]
  transfers between devices with their start and end apart: 22 -> 26, of which waited for: 11 -> 9; matrix products, arithmetic and copies ran while one was open for 7% -> 10% of each run, Pallas kernels for 34% -> 34%
where the time goes in v8:
time: 284 us; the launch traced here: 283 us
  Pallas kernels  99.4 us (35%)
  waiting for transfers between devices  61.8 us (22%)
  starting transfers between devices  37.6 us (13%)
  blocking collectives  32.9 us (12%)
  other arithmetic  20.3 us (7%)
  local copies, waits for them, and re-layouts  15.7 us (6%)
  between operations  14.7 us (5%)
    pallas_call x3, Pallas kernels, attend(): pl.pallas_call(kernel, grid_spec=pltpu.PrefetchScalarGridSpec(num_scalar_...  49.7 us
    ppermute x21, waiting for transfers between devices, swap(): return lax.ppermute(x, 'tp', [(i, i ^ bit) for i in range(4)])  42.1 us
    all_to_all x2, blocking collectives, exchange(): return lax.all_to_all(x, axes, split_axis=0, concat_axis=0, tiled=True)  32.9 us
    pallas_call x2, Pallas kernels, mlp(): pl.pallas_call(functools.partial(mlp_kernel, extra), grid_spec=pltpu.Pref...  32.7 us
    all_to_all x2, starting transfers between devices, exchange(): return lax.all_to_all(x, axes, split_axis=0, concat_axis=0, tiled=True)  17.6 us
    all_to_all x2, waiting for transfers between devices, exchange(): return lax.all_to_all(x, axes, split_axis=0, concat_axis=0, tiled=True)  15.9 us
    ppermute x21, starting transfers between devices, swap(): return lax.ppermute(x, 'tp', [(i, i ^ bit) for i in range(4)])  14.1 us
    pallas_call x1, Pallas kernels, qkv_project(): pl.pallas_call(qkv_kernel, grid=(rows // n,), in_specs=[pl.BlockSpec((n,...  8.16 us
  transfers between devices with their start and end apart: 26, of which 9 were waited for; matrix products, arithmetic and copies ran while one was open for 10% of the time, Pallas kernels for 34%

profile of v8, /device:TPU:1, one launch (start us, length us, event | category | flops | bytes accessed | tf_op | source)
XLA Modules:
  0.0 283.0 jit_solution(15483227450085033271)
XLA Ops:
  7.2 0.5 fusion.20.order
  7.8 2.8 prep.1
  10.6 0.8 slice_bitcast_fusion.3
  11.4 2.5 collective-permute-start
  14.0 1.0 collective-permute-start.1
  14.9 0.4 collective-permute-done
  15.3 0.5 collective-permute-done.1
  15.8 2.5 collective-permute-done.2
  18.3 0.7 pad_maximum_fusion.1
  19.0 9.7 %all-to-all-start = ((bf16[128,8,1024]{2,1,0:T(8,128)(2,1)}), bf16[128,8,1024]{2,1,0:T(8,128)(2,1)S(1)}, u32[]{:S(2)}, u32[]{:S(2)}) async-start(bf16[128,8,1024]{2,1,0:T(8,128)(2,1)} %bitcast.75), calls=%async_computation | async-start | bytes 4194304 | tf_op jit(solution)/shard_map/all_to_all | solution.py:398
  28.7 1.2 gather_fusion
  30.0 0.6 pad_add_fusion.table
  31.0 6.0 %norm.1.x = bf16[2048,1024]{1,0:T(8,128)(2,1)} custom-call(bf16[2048,1024]{1,0:T(8,128)(2,1)} %h.4, f32[1,1024]{1,0:T(1,128)} %bitcast.85), custom_call_target="tpu_custom_call" | custom-call | flops 16777216 | bytes 8388608 | tf_op jit(solution)/shard_map/norm/pallas_call | solution.py:86
  37.0 0.7 fusion.10
  38.1 5.5 %multiply_sine_fusion = (f32[2048,128]{1,0:T(8,128)}, f32[2048,128]{1,0:T(8,128)}) fusion(f32[128]{0:T(128)S(1)} %fusion.25, f32[2048]{0:T(1024)S(1)} %subtract_convert_fusion), kind=kLoop, calls=%fused_computation.4 | loop fusion | flops 262144 | bytes 2105856 | tf_op jit(solution)/shard_map/sin | solution.py:452
  43.6 15.9 %all-to-all-done = bf16[128,8,1024]{2,1,0:T(8,128)(2,1)S(1)} async-done(((bf16[128,8,1024]{2,1,0:T(8,128)(2,1)}), bf16[128,8,1024]{2,1,0:T(8,128)(2,1)S(1)}, u32[]{:S(2)}, u32[]{:S(2)}) %all-to-all-start) | async-done | bytes 2097184 | tf_op jit(solution)/shard_map/all_to_all | solution.py:398
  59.5 2.0 gather_fusion.1
  61.5 8.2 %qkv.1 = (bf16[2048,256]{1,0:T(8,128)(2,1)}, bf16[8,2,256,256]{3,2,1,0:T(8,128)(2,1)}, bf16[2,2048,256]{2,1,0:T(8,128)(2,1)}) custom-call(bf16[2048,1024]{1,0:T(8,128)(2,1)} %norm.1.x, bf16[1024,1024]{1,0:T(8,128)(2,1)} %bitcast.73, f32[2048,128]{1,0:T(8,128)} %get-tuple-element.105.cos, f32[2048,128]{1,0:T(8,128)} %get-tuple-element.104.sin), custom_call_target="tpu_custom_call" | custom-call | flops 3221225472 | bytes 12582912 | tf_op jit(solution)/shard_map/qkv/pallas_call | solution.py:125
  69.7 4.5 %collective-permute-start.3 = (bf16[8,2,256,256]{3,2,1,0:T(8,128)(2,1)}, bf16[8,2,256,256]{3,2,1,0:T(8,128)(2,1)}, u32[]{:S(2)}, u32[]{:S(2)}) collective-permute-start(bf16[8,2,256,256]{3,2,1,0:T(8,128)(2,1)} %get-tuple-element.52.kv), channel_id=1, source_target_pairs={{0,4},{4,8},{8,12},{12,16},{16,20},{20,24},{24,28},{28,32},{32,36}... | collective-permute-start | bytes 6291464 | tf_op jit(solution)/shard_map/ppermute | solution.py:394
  74.2 1.3 collective-permute-start.4
  75.5 1.4 copy.41.kseg
  76.9 1.3 copy.42.lseg
  78.2 1.4 copy.43.rseg
  79.9 0.6 stack.2.table
  80.5 1.1 slice.93.o0
  81.8 0.6 collective-permute-start.6
  82.4 36.1 %attend_own.1 = (f32[4,72,2048]{2,1,0:T(8,128)}, f32[4,1,2048]{2,1,0:T(1,128)}) custom-call(s32[6,8]{1,0:T(8,128)} %stack.2.table, bf16[2048,256]{1,0:T(8,128)(2,1)} %get-tuple-element.49.q, s32[1,2048]{1,0:T(1,128)} %bitcast.80, bf16[8,2,256,256]{3,2,1,0:T(8,128)(2,1)} %get-tuple-element.52.kv, s32[2048,1]{1,0:T(8,128)} %copy.41.kseg), custom_call_target="tpu_custom_call" | custom-call | flops 12884901888 | bytes 8388608 | tf_op jit(solution)/shard_map/attend_own/pallas_call | solution.py:247
  118.5 16.9 %collective-permute-done.5.o1 = bf16[1024,256]{1,0:T(8,128)(2,1)S(1)} collective-permute-done((bf16[1024,256]{1,0:T(8,128)(2,1)S(1)}, bf16[1024,256]{1,0:T(8,128)(2,1)S(1)}, u32[]{:S(2)}, u32[]{:S(2)}) %collective-permute-start.5) | collective-permute-done | bytes 524320 | tf_op jit(solution)/shard_map/ppermute | solution.py:380
  135.4 0.7 collective-permute-start.10
  136.2 6.9 %attend_halo.2 = (bf16[1024,256]{1,0:T(8,128)(2,1)}, f32[64,256]{1,0:T(8,128)}) custom-call(s32[6,8]{1,0:T(8,128)} %stack.2.table, bf16[2048,256]{1,0:T(8,128)(2,1)} %get-tuple-element.49.q, s32[1,2048]{1,0:T(1,128)} %bitcast.81, bf16[8,2,256,256]{3,2,1,0:T(8,128)(2,1)} %collective-permute-done.3.lkv, s32[2048,1]{1,0:T(8,128)} %copy.42.lseg, ...), custom_call_target="tpu_custom_call" | custom-call | flops 12884901888 | bytes 8388608 | tf_op jit(solution)/shard_map/attend_halo/pallas_call | solution.py:247
  143.0 1.1 collective-permute-start.7
  144.2 0.3 collective-permute-start.8
  144.5 6.8 %attend_halo.3 = (bf16[1024,256]{1,0:T(8,128)(2,1)}, f32[64,256]{1,0:T(8,128)}) custom-call(s32[6,8]{1,0:T(8,128)} %stack.2.table, bf16[2048,256]{1,0:T(8,128)(2,1)} %get-tuple-element.49.q, s32[1,2048]{1,0:T(1,128)} %bitcast.82, bf16[8,2,256,256]{3,2,1,0:T(8,128)(2,1)} %collective-permute-done.3.lkv, s32[2048,1]{1,0:T(8,128)} %copy.42.lseg, ...), custom_call_target="tpu_custom_call" | custom-call | flops 12884901888 | bytes 8388608 | tf_op jit(solution)/shard_map/attend_halo/pallas_call | solution.py:247
  151.3 17.1 %collective-permute-done.7.m1 = bf16[1024,256]{1,0:T(8,128)(2,1)S(1)} collective-permute-done((bf16[1024,256]{1,0:T(8,128)(2,1)}, bf16[1024,256]{1,0:T(8,128)(2,1)S(1)}, u32[]{:S(2)}, u32[]{:S(2)}) %collective-permute-start.7) | collective-permute-done | bytes 524320 | tf_op jit(solution)/shard_map/ppermute | solution.py:380
  168.4 0.7 collective-permute-start.9
  169.2 0.8 add_convert_fusion.1.refs_0_
  170.0 0.9 collective-permute-start.11
  170.9 3.8 %gather_fusion.2 = bf16[64,1024]{1,0:T(8,128)(2,1)S(1)} fusion(bf16[2048,1024]{1,0:T(8,128)(2,1)} %h.4, s32[1024]{0:T(1024)S(1)} %pad_clamp_fusion), kind=kCustom, calls=%fused_computation.2 | custom fusion | bytes 262400 | tf_op jit(solution)/shard_map/gather | solution.py:488
  174.7 0.3 collective-permute-start.12
  175.3 0.7 broadcast_select_fusion.refs_4_
  176.0 0.7 collective-permute-start.14
  176.8 3.7 %all-gather.2.cloned.1.call-done = bf16[1024,2304]{1,0:T(8,128)(2,1)} async-done(((bf16[32,2304]{1,0:T(8,128)(2,1)}), bf16[1024,2304]{1,0:T(8,128)(2,1)}) %all-gather.2.cloned.1.call-update) | async-done | bytes 4718608 | tf_op jit(solution)/shard_map/all_gather | solution.py:437
  180.6 17.7 %mlp.2 = (f32[1024,512]{1,0:T(8,128)}, bf16[1024,512]{1,0:T(8,128)(2,1)}, f32[64,512]{1,0:T(8,128)}, bf16[64,512]{1,0:T(8,128)(2,1)}) custom-call(s32[132]{0:T(256)} %pad_add_fusion.table, bf16[1024,256]{1,0:T(8,128)(2,1)} %get-tuple-element.57.m0, bf16[1024,256]{1,0:T(8,128)(2,1)} %copy-done.15, bf16[1024,256]{1,0:T(8,128)(2,1)} %copy-done.16, ...), custom_call_target="tpu_custom_call" | custom-call | flops 6979321856 | bytes 12582912 | tf_op jit(solution)/shard_map/mlp/pallas_call | solution.py:356
  198.4 1.0 collective-permute-start.15
  199.4 2.5 collective-permute-done.16
  202.0 0.9 fusion.7
  202.9 0.5 collective-permute-start.19
  203.5 2.2 collective-permute-done.17
  205.7 0.9 fusion.9
  207.2 0.8 copy-done.17
  208.1 0.6 reshape.562
  208.8 8.0 %all-to-all-start.1 = ((bf16[32,2,256]{2,1,0:T(2,128)(2,1)}), bf16[32,2,256]{2,1,0:T(2,128)(2,1)S(1)}, u32[]{:S(2)}, u32[]{:S(2)}) async-start(bf16[32,2,256]{2,1,0:T(2,128)(2,1)} %reshape.562), calls=%async_computation.1 | async-start | bytes 65536 | tf_op jit(solution)/shard_map/all_to_all | solution.py:398
  216.7 14.9 %mlp.3 = (f32[1024,512]{1,0:T(8,128)}, bf16[1024,512]{1,0:T(8,128)(2,1)}) custom-call(s32[132]{0:T(256)} %pad_add_fusion.table, bf16[1024,256]{1,0:T(8,128)(2,1)} %get-tuple-element.75.m0, bf16[1024,256]{1,0:T(8,128)(2,1)} %copy-done.14, bf16[1024,256]{1,0:T(8,128)(2,1)} %collective-permute-done.19.m2, bf16[1024,256]{1,0:T(8,128)(2,1)} %copy-done.17, ...), custom_call_target="tpu_custom_call" | custom-call | flops 6979321856 | bytes 12582912 | tf_op jit(solution)/shard_map/mlp/pallas_call | solution.py:356
  231.9 2.2 collective-permute-start.21
  234.1 18.8 %all_to_all.21 = bf16[128,2,256]{2,1,0:T(2,128)(2,1)S(1)} all-to-all(bf16[128,2,256]{2,1,0:T(2,128)(2,1)S(1)} %broadcast_in_dim.97), channel_id=1, replica_groups=mesh['req'=32,'tp'=4] {'req','tp'}, dimensions={0} | all-to-all | bytes 262144 | tf_op jit(solution)/shard_map/all_to_all | solution.py:398
  253.6 1.5 convert_element_type.102
  255.1 1.5 fusion.1
  256.6 0.6 collective-permute-start.22
  257.2 0.5 add_rsqrt_fusion
  258.2 0.5 convolution_reduce_fusion
  258.7 14.1 %all_to_all.22 = f32[128,1,64]{2,1,0:T(1,128)S(1)} all-to-all(f32[128,1,64]{2,1,0:T(1,128)S(1)} %broadcast_in_dim.98), channel_id=1, replica_groups=mesh['req'=32,'tp'=4] {'req','tp'}, dimensions={0} | all-to-all | bytes 65536 | tf_op jit(solution)/shard_map/all_to_all | solution.py:398
  272.8 0.7 reduce_max.39
  273.5 1.6 fusion.3
  275.1 1.0 pad_maximum_fusion
  (105 shorter events, 4.1 us)
Async XLA Ops:
  7.2 250.7 %copy-start = (f32[4,1024]{1,0:T(4,128)S(1)}, f32[4,1024]{1,0:T(4,128)}, u32[]{:S(2)}) copy-start(f32[4,1024]{1,0:T(4,128)} %param.29) | copy-start | bytes 49156
  7.2 173.3 %all-gather.2.cloned.1.call-start = ((), (), s32[]{:S(2)}) async-start(), calls=%async_computation.4 | async-start | bytes 4866048 | tf_op jit(solution)/shard_map/all_gather | solution.py:437
  11.4 3.9 %collective-permute-start = (bf16[8,2304]{1,0:T(8,128)(2,1)S(1)}, bf16[8,2304]{1,0:T(8,128)(2,1)S(1)}, u32[]{:S(2)}, u32[]{:S(2)}) collective-permute-start(bf16[8,2304]{1,0:T(8,128)(2,1)S(1)} %get-tuple-element.99), channel_id=1, source_target_pairs={{0,2},{1,3},{2,0},{3,1},{4,6},{5,7},{6,4},{7,5},{8,10},{9,11},{10,... | collective-permute-start | bytes 110600 | tf_op jit(solution)/shard_map/ppermute | solution.py:380
  14.0 1.8 collective-permute-start.1
  14.9 3.4 %collective-permute-start.2 = (bf16[8,2304]{1,0:T(8,128)(2,1)S(1)}, bf16[8,2304]{1,0:T(8,128)(2,1)S(1)}, u32[]{:S(2)}, u32[]{:S(2)}) collective-permute-start(bf16[8,2304]{1,0:T(8,128)(2,1)S(1)} %get-tuple-element.97), channel_id=1, source_target_pairs={{0,3},{1,2},{2,1},{3,0},{4,7},{5,6},{6,5},{7,4},{8,11},{9,10},{10,... | collective-permute-start | bytes 110600 | tf_op jit(solution)/shard_map/ppermute | solution.py:380
  19.0 9.7 %copy-start.1 = (s32[128]{0:T(128)S(1)}, s32[128]{0:T(128)}, u32[]{:S(2)}) copy-start(s32[128]{0:T(128)} %param.18) | copy-start | bytes 1540
  19.0 11.8 %copy-start.8 = (s32[64]{0:T(128)S(1)}, s32[64]{0:T(128)}, u32[]{:S(2)}) copy-start(s32[64]{0:T(128)} %param.16) | copy-start | bytes 772
  19.0 40.5 %all-to-all-start = ((bf16[128,8,1024]{2,1,0:T(8,128)(2,1)}), bf16[128,8,1024]{2,1,0:T(8,128)(2,1)S(1)}, u32[]{:S(2)}, u32[]{:S(2)}) async-start(bf16[128,8,1024]{2,1,0:T(8,128)(2,1)} %bitcast.75), calls=%async_computation | async-start | bytes 4194304 | tf_op jit(solution)/shard_map/all_to_all | solution.py:398
  69.7 66.5 %collective-permute-start.3 = (bf16[8,2,256,256]{3,2,1,0:T(8,128)(2,1)}, bf16[8,2,256,256]{3,2,1,0:T(8,128)(2,1)}, u32[]{:S(2)}, u32[]{:S(2)}) collective-permute-start(bf16[8,2,256,256]{3,2,1,0:T(8,128)(2,1)} %get-tuple-element.52.kv), channel_id=1, source_target_pairs={{0,4},{4,8},{8,12},{12,16},{16,20},{20,24},{24,28},{28,32},{32,36}... | collective-permute-start | bytes 6291464 | tf_op jit(solution)/shard_map/ppermute | solution.py:394
  74.2 61.9 %collective-permute-start.4 = (bf16[8,2,256,256]{3,2,1,0:T(8,128)(2,1)}, bf16[8,2,256,256]{3,2,1,0:T(8,128)(2,1)}, u32[]{:S(2)}, u32[]{:S(2)}) collective-permute-start(bf16[8,2,256,256]{3,2,1,0:T(8,128)(2,1)} %get-tuple-element.52.kv), channel_id=1, source_target_pairs={{4,0},{8,4},{12,8},{16,12},{20,16},{24,20},{28,24},{32,28},{36,32}... | collective-permute-start | bytes 6291464 | tf_op jit(solution)/shard_map/ppermute | solution.py:394
  75.5 6.0 %copy-start.6 = (s32[2048]{0:T(1024)}, s32[2048]{0:T(1024)S(1)}, u32[]{:S(2)}) copy-start(s32[2048]{0:T(1024)S(1)} %get-tuple-element.103) | copy-start | bytes 24580
  81.6 36.9 %copy-start.4 = (bf16[1024,256]{1,0:T(8,128)(2,1)}, bf16[1024,256]{1,0:T(8,128)(2,1)S(1)}, u32[]{:S(2)}) copy-start(bf16[1024,256]{1,0:T(8,128)(2,1)S(1)} %slice.93.o0) | copy-start | bytes 1572868
  81.6 53.8 %collective-permute-start.5 = (bf16[1024,256]{1,0:T(8,128)(2,1)S(1)}, bf16[1024,256]{1,0:T(8,128)(2,1)S(1)}, u32[]{:S(2)}, u32[]{:S(2)}) collective-permute-start(bf16[1024,256]{1,0:T(8,128)(2,1)S(1)} %slice.93.o0), channel_id=1, source_target_pairs={{0,2},{1,3},{2,0},{3,1},{4,6},{5,7},{6,4},{7,5},{8,10},{9,11},{10,... | collective-permute-start | bytes 1572872 | tf_op jit(solution)/shard_map/ppermute | solution.py:380
  81.8 53.6 %collective-permute-start.6 = (bf16[1024,256]{1,0:T(8,128)(2,1)S(1)}, bf16[1024,256]{1,0:T(8,128)(2,1)S(1)}, u32[]{:S(2)}, u32[]{:S(2)}) collective-permute-start(bf16[1024,256]{1,0:T(8,128)(2,1)S(1)} %slice.93.o0), channel_id=1, source_target_pairs={{0,1},{1,0},{2,3},{3,2},{4,5},{5,4},{6,7},{7,6},{8,9},{9,8},{10,11... | collective-permute-start | bytes 1572872 | tf_op jit(solution)/shard_map/ppermute | solution.py:380
  135.4 7.6 %copy-start.10 = (bf16[1024,256]{1,0:T(8,128)(2,1)}, bf16[1024,256]{1,0:T(8,128)(2,1)S(1)}, u32[]{:S(2)}) copy-start(bf16[1024,256]{1,0:T(8,128)(2,1)S(1)} %collective-permute-done.5.o1) | copy-start | bytes 1572868
  135.4 7.6 %copy-start.11 = (bf16[1024,256]{1,0:T(8,128)(2,1)}, bf16[1024,256]{1,0:T(8,128)(2,1)S(1)}, u32[]{:S(2)}) copy-start(bf16[1024,256]{1,0:T(8,128)(2,1)S(1)} %collective-permute-done.6.o2) | copy-start | bytes 1572868
  135.4 40.6 %collective-permute-start.10 = (bf16[1024,256]{1,0:T(8,128)(2,1)S(1)}, bf16[1024,256]{1,0:T(8,128)(2,1)S(1)}, u32[]{:S(2)}, u32[]{:S(2)}) collective-permute-start(bf16[1024,256]{1,0:T(8,128)(2,1)S(1)} %collective-permute-done.5.o1), channel_id=1, source_target_pairs={{0,1},{1,0},{2,3},{3,2},{4,5},{5,4},{6,7},{7,6},{8,9},{9,8},{10,11... | collective-permute-start | bytes 1572872 | tf_op jit(solution)/shard_map/ppermute | solution.py:380
  143.0 26.1 %copy-start.5 = (f32[64,256]{1,0:T(8,128)S(1)}, f32[64,256]{1,0:T(8,128)}, u32[]{:S(2)}) copy-start(f32[64,256]{1,0:T(8,128)} %get-tuple-element.63) | copy-start | bytes 196612
  143.0 25.4 %collective-permute-start.7 = (bf16[1024,256]{1,0:T(8,128)(2,1)}, bf16[1024,256]{1,0:T(8,128)(2,1)S(1)}, u32[]{:S(2)}, u32[]{:S(2)}) collective-permute-start(bf16[1024,256]{1,0:T(8,128)(2,1)} %get-tuple-element.57.m0), channel_id=1, source_target_pairs={{0,2},{1,3},{2,0},{3,1},{4,6},{5,7},{6,4},{7,5},{8,10},{9,11},{10,... | collective-permute-start | bytes 1572872 | tf_op jit(solution)/shard_map/ppermute | solution.py:380
  144.2 32.6 %collective-permute-start.8 = (bf16[1024,256]{1,0:T(8,128)(2,1)}, bf16[1024,256]{1,0:T(8,128)(2,1)S(1)}, u32[]{:S(2)}, u32[]{:S(2)}) collective-permute-start(bf16[1024,256]{1,0:T(8,128)(2,1)} %get-tuple-element.57.m0), channel_id=1, source_target_pairs={{0,1},{1,0},{2,3},{3,2},{4,5},{5,4},{6,7},{7,6},{8,9},{9,8},{10,11... | collective-permute-start | bytes 1572872 | tf_op jit(solution)/shard_map/ppermute | solution.py:380
  168.4 12.1 %copy-start.15 = (bf16[1024,256]{1,0:T(8,128)(2,1)}, bf16[1024,256]{1,0:T(8,128)(2,1)S(1)}, u32[]{:S(2)}) copy-start(bf16[1024,256]{1,0:T(8,128)(2,1)S(1)} %collective-permute-done.7.m1) | copy-start | bytes 1572868
  168.4 8.3 %collective-permute-start.9 = (bf16[1024,256]{1,0:T(8,128)(2,1)S(1)}, bf16[1024,256]{1,0:T(8,128)(2,1)}, u32[]{:S(2)}, u32[]{:S(2)}) collective-permute-start(bf16[1024,256]{1,0:T(8,128)(2,1)S(1)} %collective-permute-done.7.m1), channel_id=1, source_target_pairs={{0,1},{1,0},{2,3},{3,2},{4,5},{5,4},{6,7},{7,6},{8,9},{9,8},{10,11... | collective-permute-start | bytes 1572872 | tf_op jit(solution)/shard_map/ppermute | solution.py:380
  170.0 10.5 %copy-start.7 = (bf16[64,256]{1,0:T(8,128)(2,1)}, bf16[64,256]{1,0:T(8,128)(2,1)S(1)}, u32[]{:S(2)}) copy-start(bf16[64,256]{1,0:T(8,128)(2,1)S(1)} %add_convert_fusion.1.refs_0_) | copy-start | bytes 98308
  170.0 5.0 %collective-permute-start.11 = (bf16[64,256]{1,0:T(8,128)(2,1)S(1)}, bf16[64,256]{1,0:T(8,128)(2,1)S(1)}, u32[]{:S(2)}, u32[]{:S(2)}) collective-permute-start(bf16[64,256]{1,0:T(8,128)(2,1)S(1)} %add_convert_fusion.1.refs_0_), channel_id=1, source_target_pairs={{0,2},{1,3},{2,0},{3,1},{4,6},{5,7},{6,4},{7,5},{8,10},{9,11},{10,... | collective-permute-start | bytes 98312 | tf_op jit(solution)/shard_map/ppermute | solution.py:380
  174.7 2.0 collective-permute-start.12
  175.0 5.5 %copy-start.18 = (bf16[64,256]{1,0:T(8,128)(2,1)}, bf16[64,256]{1,0:T(8,128)(2,1)S(1)}, u32[]{:S(2)}) copy-start(bf16[64,256]{1,0:T(8,128)(2,1)S(1)} %collective-permute-done.11.refs_1_) | copy-start | bytes 98308
  175.0 1.7 collective-permute-start.13
  176.0 4.5 %copy-start.12 = (bf16[1024,256]{1,0:T(8,128)(2,1)}, bf16[1024,256]{1,0:T(8,128)(2,1)S(1)}, u32[]{:S(2)}) copy-start(bf16[1024,256]{1,0:T(8,128)(2,1)S(1)} %collective-permute-done.10.o3) | copy-start | bytes 1572868
  176.0 22.3 %collective-permute-start.14 = (bf16[1024,256]{1,0:T(8,128)(2,1)}, bf16[1024,256]{1,0:T(8,128)(2,1)S(1)}, u32[]{:S(2)}, u32[]{:S(2)}) collective-permute-start(bf16[1024,256]{1,0:T(8,128)(2,1)} %get-tuple-element.75.m0), channel_id=1, source_target_pairs={{0,2},{1,3},{2,0},{3,1},{4,6},{5,7},{6,4},{7,5},{8,10},{9,11},{10,... | collective-permute-start | bytes 1572872 | tf_op jit(solution)/shard_map/ppermute | solution.py:380
  176.7 3.8 %copy-start.19 = (bf16[64,256]{1,0:T(8,128)(2,1)}, bf16[64,256]{1,0:T(8,128)(2,1)S(1)}, u32[]{:S(2)}) copy-start(bf16[64,256]{1,0:T(8,128)(2,1)S(1)} %collective-permute-done.12.refs_2_) | copy-start | bytes 98308
  176.7 3.8 %copy-start.20 = (bf16[64,256]{1,0:T(8,128)(2,1)}, bf16[64,256]{1,0:T(8,128)(2,1)S(1)}, u32[]{:S(2)}) copy-start(bf16[64,256]{1,0:T(8,128)(2,1)S(1)} %collective-permute-done.13.refs_3_) | copy-start | bytes 98308
  176.8 3.8 %copy-start.16 = (bf16[1024,256]{1,0:T(8,128)(2,1)}, bf16[1024,256]{1,0:T(8,128)(2,1)S(1)}, u32[]{:S(2)}) copy-start(bf16[1024,256]{1,0:T(8,128)(2,1)S(1)} %collective-permute-done.8.m2) | copy-start | bytes 1572868
  180.6 22.3 %copy-start.13 = (bf16[1024,256]{1,0:T(8,128)(2,1)S(1)}, bf16[1024,256]{1,0:T(8,128)(2,1)}, u32[]{:S(2)}) copy-start(bf16[1024,256]{1,0:T(8,128)(2,1)} %get-tuple-element.75.m0) | copy-start | bytes 1572868
  198.3 8.5 %copy-start.2 = (f32[1024,512]{1,0:T(8,128)S(1)}, f32[1024,512]{1,0:T(8,128)}, u32[]{:S(2)}) copy-start(f32[1024,512]{1,0:T(8,128)} %get-tuple-element.69) | copy-start | bytes 6291460
  198.3 8.8 %copy-start.14 = (bf16[1024,256]{1,0:T(8,128)(2,1)}, bf16[1024,256]{1,0:T(8,128)(2,1)S(1)}, u32[]{:S(2)}) copy-start(bf16[1024,256]{1,0:T(8,128)(2,1)S(1)} %collective-permute-done.14.m1) | copy-start | bytes 1572868
  198.4 8.2 %collective-permute-start.15 = (bf16[1024,512]{1,0:T(8,128)(2,1)}, bf16[1024,512]{1,0:T(8,128)(2,1)S(1)}, u32[]{:S(2)}, u32[]{:S(2)}) collective-permute-start(bf16[1024,512]{1,0:T(8,128)(2,1)} %get-tuple-element.70), channel_id=1, source_target_pairs={{0,1},{1,0},{2,3},{3,2},{4,5},{5,4},{6,7},{7,6},{8,9},{9,8},{10,11... | collective-permute-start | bytes 3145736 | tf_op jit(solution)/shard_map/ppermute | solution.py:380
  199.3 2.6 collective-permute-start.16
  202.8 2.8 %collective-permute-start.17 = (bf16[64,256]{1,0:T(8,128)(2,1)S(1)}, bf16[64,256]{1,0:T(8,128)(2,1)S(1)}, u32[]{:S(2)}, u32[]{:S(2)}) collective-permute-start(bf16[64,256]{1,0:T(8,128)(2,1)S(1)} %fusion.7), channel_id=1, source_target_pairs={{0,2},{1,3},{2,0},{3,1},{4,6},{5,7},{6,4},{7,5},{8,10},{9,11},{10,... | collective-permute-start | bytes 98312 | tf_op jit(solution)/shard_map/ppermute | solution.py:380
  202.9 13.8 %collective-permute-start.19 = (bf16[1024,256]{1,0:T(8,128)(2,1)S(1)}, bf16[1024,256]{1,0:T(8,128)(2,1)}, u32[]{:S(2)}, u32[]{:S(2)}) collective-permute-start(bf16[1024,256]{1,0:T(8,128)(2,1)S(1)} %copy-done.13), channel_id=1, source_target_pairs={{0,1},{1,0},{2,3},{3,2},{4,5},{5,4},{6,7},{7,6},{8,9},{9,8},{10,11... | collective-permute-start | bytes 1572872 | tf_op jit(solution)/shard_map/ppermute | solution.py:380
  203.4 3.8 %collective-permute-start.18 = (bf16[1024,256]{1,0:T(8,128)(2,1)S(1)}, bf16[1024,256]{1,0:T(8,128)(2,1)S(1)}, u32[]{:S(2)}, u32[]{:S(2)}) collective-permute-start(bf16[1024,256]{1,0:T(8,128)(2,1)S(1)} %collective-permute-done.14.m1), channel_id=1, source_target_pairs={{0,1},{1,0},{2,3},{3,2},{4,5},{5,4},{6,7},{7,6},{8,9},{9,8},{10,11... | collective-permute-start | bytes 1572872 | tf_op jit(solution)/shard_map/ppermute | solution.py:380
  207.2 0.8 copy-start.17
  208.0 23.8 %collective-permute-start.20 = (bf16[1024,256]{1,0:T(8,128)(2,1)S(1)}, bf16[1024,256]{1,0:T(8,128)(2,1)S(1)}, u32[]{:S(2)}, u32[]{:S(2)}) collective-permute-start(bf16[1024,256]{1,0:T(8,128)(2,1)S(1)} %get-tuple-element.80), channel_id=1, source_target_pairs={{0,2},{1,3},{2,0},{3,1},{4,6},{5,7},{6,4},{7,5},{8,10},{9,11},{10,... | collective-permute-start | bytes 1572872 | tf_op jit(solution)/shard_map/ppermute | solution.py:380
  208.8 22.9 %all-to-all-start.1 = ((bf16[32,2,256]{2,1,0:T(2,128)(2,1)}), bf16[32,2,256]{2,1,0:T(2,128)(2,1)S(1)}, u32[]{:S(2)}, u32[]{:S(2)}) async-start(bf16[32,2,256]{2,1,0:T(2,128)(2,1)} %reshape.562), calls=%async_computation.1 | async-start | bytes 65536 | tf_op jit(solution)/shard_map/all_to_all | solution.py:398
  231.9 21.7 %collective-permute-start.21 = (bf16[1024,512]{1,0:T(8,128)(2,1)}, bf16[1024,512]{1,0:T(8,128)(2,1)}, u32[]{:S(2)}, u32[]{:S(2)}) collective-permute-start(bf16[1024,512]{1,0:T(8,128)(2,1)} %get-tuple-element.83), channel_id=1, source_target_pairs={{0,1},{1,0},{2,3},{3,2},{4,5},{5,4},{6,7},{7,6},{8,9},{9,8},{10,11... | collective-permute-start | bytes 3145736 | tf_op jit(solution)/shard_map/ppermute | solution.py:380
  255.1 2.8 copy-start.9
  255.1 3.1 %copy-start.3 = (f32[384,1024]{1,0:T(8,128)S(1)}, f32[384,1024]{1,0:T(8,128)}, u32[]{:S(2)}) copy-start(f32[384,1024]{1,0:T(8,128)} %param.26) | copy-start | bytes 4718596
  256.6 16.9 %collective-permute-start.22 = (bf16[1024,256]{1,0:T(8,128)(2,1)S(1)}, bf16[1024,256]{1,0:T(8,128)(2,1)}, u32[]{:S(2)}, u32[]{:S(2)}) collective-permute-start(bf16[1024,256]{1,0:T(8,128)(2,1)S(1)} %fusion.1), channel_id=1, source_target_pairs={{0,2},{1,3},{2,0},{3,1},{4,6},{5,7},{6,4},{7,5},{8,10},{9,11},{10,... | collective-permute-start | bytes 1572872 | tf_op jit(solution)/shard_map/ppermute | solution.py:380
Sparse Core Ops, SparseCore 0:
  19.1 161.3 all-gather.1

commit v9 on v8

--- a/solution.py
+++ b/solution.py
@@ -33,7 +33,7 @@
     return pl.CostEstimate(flops=flops, bytes_accessed=moved, transcendentals=transcendentals)
 
 
-def prep_kernel(order, wq, wk, wv, wo, wi, wg, w2, first, rest):
+def prep_kernel(order, wq, wk, wv, wo, wi, wg, w2, first, *rest):
     row = lax.broadcasted_iota(jnp.int32, (256, 256), 0)
     col = lax.broadcasted_iota(jnp.int32, (256, 256), 1)
     source = (col % 128) // 32 * 64 + col // 128 * 32 + col % 32
@@ -49,11 +49,13 @@
         mine = jnp.concatenate([q, k, wv[:, at].astype(BF), wo[:, at].astype(BF)], axis=1)
         for r in range(first.shape[0]):
             first[r, t] = mine
+    for piece, out in enumerate(rest):
+        t = order[piece]
         pick = jnp.where((trow == tcol + 16 * t) & (tcol < 16), 1.0, 0.0).astype(BF)
-        to = order[t]
         for n, w in enumerate((wi, wg, w2)):
-            rest[to, :, FFP * n : FFP * n + 640] = w[:, 640 * t : 640 * t + 640].astype(BF)
-            rest[to, :, FFP * n + 640 : FFP * n + 768] = jnp.dot(
+            main = pl.ds(pl.multiple_of(640 * t, 128), 640)
+            out[:, FFP * n : FFP * n + 640] = w[:, main].astype(BF)
+            out[:, FFP * n + 640 : FFP * n + 768] = jnp.dot(
                 w[:, 2560:2624].astype(BF), pick, preferred_element_type=F32
             ).astype(BF)
 
@@ -64,8 +66,8 @@
         in_specs=[pl.BlockSpec(memory_space=pltpu.SMEM)] + [vmem(*w.shape) for w in weights],
         out_shape=(
             jax.ShapeDtypeStruct((req_count, 4, 8, 1024), BF),
-            jax.ShapeDtypeStruct((4, 8, REST), BF),
-        ),
+        )
+        + (jax.ShapeDtypeStruct((8, REST), BF),) * 4,
         compiler_params=params(),
         name="prep",
     )(order, *weights)
@@ -295,8 +297,6 @@
         def _(k):
             pltpu.make_async_copy(weights.at[k], w.at[table[4 + k]], sem).start()
 
-        pltpu.make_async_copy(w, w, sem).wait()
-
     def rows(at, size, lo, width):
         return w[pl.ds(at, size), :, pl.ds(lo, width)].reshape(8 * size, width)
 
@@ -309,6 +309,11 @@
     first = (wide + total).astype(BF)
     wide = first.astype(F32)
     normed = layer_norm(wide, gain[...]).astype(BF)
+
+    @pl.when(step == 0)
+    def _():
+        pltpu.make_async_copy(w, w, sem).wait()
+
     a = jnp.dot(normed, rows(0, count, 0, FFP), preferred_element_type=F32)
     b = jnp.dot(normed, rows(0, count, FFP, FFP), preferred_element_type=F32)
     inner = (0.5 * a * (1.0 + lax.erf(a * (0.5**0.5))) * b).astype(BF)
@@ -320,16 +325,18 @@
         return contract_last(inner, rows(table[j] * (count // 4), count // 4, 2 * FFP, FFP))
 
     kept = jnp.concatenate([down(0) + mine, down(1)], axis=1)
-    sent = jnp.concatenate([down(2), down(3)], axis=1).astype(BF)
+    sent = jnp.concatenate([down(2), down(3)], axis=1)
     keep[...] = kept
-    send[...] = sent
+    send[...] = sent.astype(BF)
     if extra:
 
         @pl.when(step == 0)
         def _():
-            rows = lasts[0].shape[0]
-            outs[2][...] = kept[:rows]
-            outs[3][...] = sent[:rows]
+            held = lasts[0].shape[0]
+            for j, x in enumerate((kept, sent)):
+                for n in range(2):
+                    at = pl.ds(pl.multiple_of(256 * table[2 * j + n], 128), 256)
+                    outs[2][:, at] = x[:held, 256 * n : 256 * n + 256]
 
 
 def mlp(table, mixed, out_w, h, base, gain, weights, lasts=()):
@@ -348,11 +355,8 @@
     ]
     if lasts:
         held = lasts[0].shape[0]
-        out_specs += [vmem(held, 512), vmem(held, 512)]
-        out_shape += [
-            jax.ShapeDtypeStruct((held, 512), F32),
-            jax.ShapeDtypeStruct((held, 512), BF),
-        ]
+        out_specs.append(vmem(held, 1024))
+        out_shape.append(jax.ShapeDtypeStruct((held, 1024), F32))
     return pl.pallas_call(
         functools.partial(mlp_kernel, extra),
         grid_spec=pltpu.PrefetchScalarGridSpec(
@@ -424,8 +428,8 @@
     requests = lengths.shape[0]
 
     four = jnp.arange(4, dtype=jnp.int32)
-    place_of = turn_bits(four ^ tp_index)
-    first_block, rest_block = prep(req_count, place_of, wq, wk, wv, wo, wi_in, wi_gate, wo2)
+    near_first = tp_index ^ turn_bits(four)
+    first_block, *rest_block = prep(req_count, near_first, wq, wk, wv, wo, wi_in, wi_gate, wo2)
     place = jnp.arange(count, dtype=jnp.int32)
     source = jnp.sum(
         jnp.where(shard_map[None, :] == place[:, None], place[None, :], 0), axis=1
@@ -490,7 +494,7 @@
     last_far = swap(last_mixed, 2)
     lasts = (last_mixed, last_far, swap(last_mixed, 1), swap(last_far, 1), last_in)
 
-    order = jnp.concatenate([tp_index ^ turn_bits(four), rest_target])
+    order = jnp.concatenate([near_first, rest_target])
     steps = slots // parts // 256
 
     def feed(part, pieces, *lasts):
@@ -501,20 +505,16 @@
     far = [swap(m, 2) for m in mixed]
     near = [swap(m, 1) for m in mixed]
     far[0], _ = lax.optimization_barrier((far[0], mixed[1]))
-    keep, send, last_keep, last_send = feed(
-        0, (mixed[0], far[0], near[0], swap(far[0], 1)), lasts
-    )
-    last_keep, last_send, keep, send, far[1] = lax.optimization_barrier(
-        (last_keep, last_send, keep, send, far[1])
-    )
+    keep, send, last_part = feed(0, (mixed[0], far[0], near[0], swap(far[0], 1)), lasts)
+    keep, send, far[1] = lax.optimization_barrier((keep, send, far[1]))
     last_piece = swap(far[1], 1)
-    last_mine = reduce_far(*reduce_core(last_keep, last_send))
-    pair, last_mine, last_piece, piece = lax.optimization_barrier(
-        (reduce_core(keep, send), last_mine, last_piece, mixed[1])
+    each = requests // req_count
+    last_part = last_part.reshape(req_count, each, tp_count, 256).transpose(0, 2, 1, 3)
+    pair, last_part, last_piece, piece = lax.optimization_barrier(
+        (reduce_core(keep, send), last_part, last_piece, mixed[1])
     )
     top = reduce_far(*pair)
-    each = requests // req_count
-    taken = exchange(last_mine.reshape(req_count, each, 256), "req").astype(F32).sum(axis=0)
+    taken = exchange(last_part.reshape(count, each, 256), BOTH).sum(axis=0)
     keep, send = feed(1, (piece, far[1], near[1], last_piece))
     taken, keep, send, top = lax.optimization_barrier((taken, keep, send, top))
     spread = exchange(jnp.broadcast_to(taken.astype(BF)[None], (count, each, 256)), BOTH)

time: 284 us -> 278 us (0.979)
  Pallas kernels: 99.4 us -> 94.5 us
    pallas_call x3, Pallas kernels: 49.7 us -> 45.5 us  [attend(): pl.pallas_call(kernel, grid_spec=pltpu.PrefetchScalarGridSpec(num_scalar_...]
    ppermute x21 -> x19, starting transfers between devices: 14.1 us -> 13.2 us  [swap(): return lax.ppermute(x, 'tp', [(i, i ^ bit) for i in range(4)])]
    ppermute x21 -> x19, waiting for transfers between devices: 42.1 us -> 42.5 us  [swap(): return lax.ppermute(x, 'tp', [(i, i ^ bit) for i in range(4)])]
  transfers between devices with their start and end apart: 26 -> 24, of which waited for: 9 -> 8; matrix products, arithmetic and copies ran while one was open for 10% -> 10% of each run, Pallas kernels for 34% -> 33%
where the time goes in v9:
time: 278 us; the launch traced here: 276 us
  Pallas kernels  94.5 us (34%)
  waiting for transfers between devices  61.2 us (22%)
  starting transfers between devices  37 us (13%)
  blocking collectives  32.7 us (12%)
  other arithmetic  20.3 us (7%)
  local copies, waits for them, and re-layouts  15.4 us (6%)
  between operations  14.6 us (5%)
    pallas_call x3, Pallas kernels, attend(): pl.pallas_call(kernel, grid_spec=pltpu.PrefetchScalarGridSpec(num_scalar_...  45.5 us
    ppermute x19, waiting for transfers between devices, swap(): return lax.ppermute(x, 'tp', [(i, i ^ bit) for i in range(4)])  42.5 us
    all_to_all x2, blocking collectives, exchange(): return lax.all_to_all(x, axes, split_axis=0, concat_axis=0, tiled=True)  32.7 us
    pallas_call x2, Pallas kernels, mlp(): pl.pallas_call(functools.partial(mlp_kernel, extra), grid_spec=pltpu.Pref...  32.1 us
    all_to_all x2, starting transfers between devices, exchange(): return lax.all_to_all(x, axes, split_axis=0, concat_axis=0, tiled=True)  17.9 us
    all_to_all x2, waiting for transfers between devices, exchange(): return lax.all_to_all(x, axes, split_axis=0, concat_axis=0, tiled=True)  15.8 us
    ppermute x19, starting transfers between devices, swap(): return lax.ppermute(x, 'tp', [(i, i ^ bit) for i in range(4)])  13.2 us
    pallas_call x1, Pallas kernels, qkv_project(): pl.pallas_call(qkv_kernel, grid=(rows // n,), in_specs=[pl.BlockSpec((n,...  8.16 us
  transfers between devices with their start and end apart: 24, of which 8 were waited for; matrix products, arithmetic and copies ran while one was open for 10% of the time, Pallas kernels for 33%

profile of v9, /device:TPU:1, one launch (start us, length us, event | category | flops | bytes accessed | tf_op | source)
XLA Modules:
  0.0 276.5 jit_solution(17853017227688896836)
XLA Ops:
  7.2 0.5 fusion.11.order
  7.7 2.8 %prep.1 = (bf16[32,4,8,1024]{3,2,1,0:T(8,128)(2,1)}, bf16[8,2304]{1,0:T(8,128)(2,1)}, bf16[8,2304]{1,0:T(8,128)(2,1)}, bf16[8,2304]{1,0:T(8,128)(2,1)}, bf16[8,2304]{1,0:T(8,128)(2,1)}) custom-call(s32[4]{0:T(128)} %fusion.11.order, f32[8,1024]{1,0:T(8,128)} %wq.1, f32[8,1024]{1,0:T(8,128)} %wk.1, f32[8,1024]{1,0:T(8,128)} %wv.1, f32[8,1024]{1,0:T(8,128)} %wo.1, ...), custom_call_target="tpu_custom_call" | custom-call | tf_op jit(solution)/shard_map/prep/pallas_call | solution.py:64
  10.6 2.5 collective-permute-start
  13.0 1.0 collective-permute-start.1
  14.0 0.6 collective-permute-done
  14.6 0.5 collective-permute-done.1
  15.1 2.5 collective-permute-done.2
  17.6 1.4 pad_maximum_fusion.1
  19.1 9.7 %all-to-all-start = ((bf16[128,8,1024]{2,1,0:T(8,128)(2,1)}), bf16[128,8,1024]{2,1,0:T(8,128)(2,1)S(1)}, u32[]{:S(2)}, u32[]{:S(2)}) async-start(bf16[128,8,1024]{2,1,0:T(8,128)(2,1)} %bitcast.71), calls=%async_computation | async-start | bytes 4194304 | tf_op jit(solution)/shard_map/all_to_all | solution.py:402
  28.8 1.2 gather_fusion
  30.1 0.7 pad_add_fusion.table
  31.1 6.0 %norm.1.x = bf16[2048,1024]{1,0:T(8,128)(2,1)} custom-call(bf16[2048,1024]{1,0:T(8,128)(2,1)} %h.4, f32[1,1024]{1,0:T(1,128)} %bitcast.81), custom_call_target="tpu_custom_call" | custom-call | flops 16777216 | bytes 8388608 | tf_op jit(solution)/shard_map/norm/pallas_call | solution.py:88
  37.1 0.7 fusion.7
  38.2 5.5 %multiply_sine_fusion = (f32[2048,128]{1,0:T(8,128)}, f32[2048,128]{1,0:T(8,128)}) fusion(f32[128]{0:T(128)S(1)} %fusion.20, f32[2048]{0:T(1024)S(1)} %subtract_convert_fusion), kind=kLoop, calls=%fused_computation.4 | loop fusion | flops 262144 | bytes 2105856 | tf_op jit(solution)/shard_map/sin | solution.py:456
  43.8 15.8 %all-to-all-done = bf16[128,8,1024]{2,1,0:T(8,128)(2,1)S(1)} async-done(((bf16[128,8,1024]{2,1,0:T(8,128)(2,1)}), bf16[128,8,1024]{2,1,0:T(8,128)(2,1)S(1)}, u32[]{:S(2)}, u32[]{:S(2)}) %all-to-all-start) | async-done | bytes 2097184 | tf_op jit(solution)/shard_map/all_to_all | solution.py:402
  59.6 2.0 gather_fusion.1
  61.6 8.2 %qkv.1 = (bf16[2048,256]{1,0:T(8,128)(2,1)}, bf16[8,2,256,256]{3,2,1,0:T(8,128)(2,1)}, bf16[2,2048,256]{2,1,0:T(8,128)(2,1)}) custom-call(bf16[2048,1024]{1,0:T(8,128)(2,1)} %norm.1.x, bf16[1024,1024]{1,0:T(8,128)(2,1)} %bitcast.69, f32[2048,128]{1,0:T(8,128)} %get-tuple-element.101.cos, f32[2048,128]{1,0:T(8,128)} %get-tuple-element.100.sin), custom_call_target="tpu_custom_call" | custom-call | flops 3221225472 | bytes 12582912 | tf_op jit(solution)/shard_map/qkv/pallas_call | solution.py:127
  69.7 4.6 %collective-permute-start.3 = (bf16[8,2,256,256]{3,2,1,0:T(8,128)(2,1)}, bf16[8,2,256,256]{3,2,1,0:T(8,128)(2,1)}, u32[]{:S(2)}, u32[]{:S(2)}) collective-permute-start(bf16[8,2,256,256]{3,2,1,0:T(8,128)(2,1)} %get-tuple-element.55.kv), channel_id=1, source_target_pairs={{0,4},{4,8},{8,12},{12,16},{16,20},{20,24},{24,28},{28,32},{32,36}... | collective-permute-start | bytes 6291464 | tf_op jit(solution)/shard_map/ppermute | solution.py:398
  74.3 1.3 collective-permute-start.4
  75.7 1.4 copy.44.kseg
  77.1 1.3 copy.45.lseg
  78.4 1.4 copy.46.rseg
  80.0 0.6 stack.2.table
  80.6 1.1 slice.61.o0
  82.0 0.6 collective-permute-start.6
  82.6 26.5 %attend_own.1 = (f32[4,72,2048]{2,1,0:T(8,128)}, f32[4,1,2048]{2,1,0:T(1,128)}) custom-call(s32[6,8]{1,0:T(8,128)} %stack.2.table, bf16[2048,256]{1,0:T(8,128)(2,1)} %get-tuple-element.52.q, s32[1,2048]{1,0:T(1,128)} %bitcast.76, bf16[8,2,256,256]{3,2,1,0:T(8,128)(2,1)} %get-tuple-element.55.kv, s32[2048,1]{1,0:T(8,128)} %copy.44.kseg), custom_call_target="tpu_custom_call" | custom-call | flops 12884901888 | bytes 8388608 | tf_op jit(solution)/shard_map/attend_own/pallas_call | solution.py:249
  109.1 26.4 %collective-permute-done.5.o1 = bf16[1024,256]{1,0:T(8,128)(2,1)S(1)} collective-permute-done((bf16[1024,256]{1,0:T(8,128)(2,1)S(1)}, bf16[1024,256]{1,0:T(8,128)(2,1)S(1)}, u32[]{:S(2)}, u32[]{:S(2)}) %collective-permute-start.5) | collective-permute-done | bytes 524320 | tf_op jit(solution)/shard_map/ppermute | solution.py:384
  135.5 0.8 collective-permute-start.10
  136.3 6.9 %attend_halo.2 = (bf16[1024,256]{1,0:T(8,128)(2,1)}, f32[64,256]{1,0:T(8,128)}) custom-call(s32[6,8]{1,0:T(8,128)} %stack.2.table, bf16[2048,256]{1,0:T(8,128)(2,1)} %get-tuple-element.52.q, s32[1,2048]{1,0:T(1,128)} %bitcast.77, bf16[8,2,256,256]{3,2,1,0:T(8,128)(2,1)} %collective-permute-done.3.lkv, s32[2048,1]{1,0:T(8,128)} %copy.45.lseg, ...), custom_call_target="tpu_custom_call" | custom-call | flops 12884901888 | bytes 8388608 | tf_op jit(solution)/shard_map/attend_halo/pallas_call | solution.py:249
  143.2 1.1 collective-permute-start.7
  144.3 0.3 collective-permute-start.8
  144.6 12.0 %attend_halo.3 = (bf16[1024,256]{1,0:T(8,128)(2,1)}, f32[64,256]{1,0:T(8,128)}) custom-call(s32[6,8]{1,0:T(8,128)} %stack.2.table, bf16[2048,256]{1,0:T(8,128)(2,1)} %get-tuple-element.52.q, s32[1,2048]{1,0:T(1,128)} %bitcast.78, bf16[8,2,256,256]{3,2,1,0:T(8,128)(2,1)} %collective-permute-done.3.lkv, s32[2048,1]{1,0:T(8,128)} %copy.45.lseg, ...), custom_call_target="tpu_custom_call" | custom-call | flops 12884901888 | bytes 8388608 | tf_op jit(solution)/shard_map/attend_halo/pallas_call | solution.py:249
  156.6 12.0 %collective-permute-done.7.m1 = bf16[1024,256]{1,0:T(8,128)(2,1)S(1)} collective-permute-done((bf16[1024,256]{1,0:T(8,128)(2,1)}, bf16[1024,256]{1,0:T(8,128)(2,1)S(1)}, u32[]{:S(2)}, u32[]{:S(2)}) %collective-permute-start.7) | collective-permute-done | bytes 524320 | tf_op jit(solution)/shard_map/ppermute | solution.py:384
  168.6 0.7 collective-permute-start.9
  169.3 0.8 add_convert_fusion.1.refs_0_
  170.2 0.8 collective-permute-start.11
  171.0 3.7 %gather_fusion.2 = bf16[64,1024]{1,0:T(8,128)(2,1)S(1)} fusion(bf16[2048,1024]{1,0:T(8,128)(2,1)} %h.4, s32[1024]{0:T(1024)S(1)} %pad_clamp_fusion), kind=kCustom, calls=%fused_computation.2 | custom fusion | bytes 262400 | tf_op jit(solution)/shard_map/gather | solution.py:492
  175.0 0.3 collective-permute-start.13
  175.3 0.8 broadcast_select_fusion.refs_4_
  176.1 0.6 collective-permute-start.14
  176.7 2.9 %all-gather.2.cloned.1.call-done = bf16[1024,2304]{1,0:T(8,128)(2,1)} async-done(((bf16[32,2304]{1,0:T(8,128)(2,1)}), bf16[1024,2304]{1,0:T(8,128)(2,1)}) %all-gather.2.cloned.1.call-update) | async-done | bytes 4718608 | tf_op jit(solution)/shard_map/all_gather | solution.py:441
  179.7 17.5 %mlp.2 = (f32[1024,512]{1,0:T(8,128)}, bf16[1024,512]{1,0:T(8,128)(2,1)}, f32[64,1024]{1,0:T(8,128)}) custom-call(s32[132]{0:T(256)} %pad_add_fusion.table, bf16[1024,256]{1,0:T(8,128)(2,1)} %get-tuple-element.60.m0, bf16[1024,256]{1,0:T(8,128)(2,1)} %copy-done.14, bf16[1024,256]{1,0:T(8,128)(2,1)} %copy-done.15, ...), custom_call_target="tpu_custom_call" | custom-call | flops 6979321856 | bytes 12582912 | tf_op jit(solution)/shard_map/mlp/pallas_call | solution.py:360
  197.2 1.6 collective-permute-start.15
  198.9 0.4 collective-permute-start.17
  199.3 1.2 reshape.565
  200.5 0.8 copy.55
  201.4 0.5 collective-permute-done.15
  201.9 0.3 convert_element_type.78
  202.2 1.1 fusion.4
  203.3 8.3 %all-to-all-start.1 = ((f32[128,2,256]{2,1,0:T(2,128)}), f32[128,2,256]{2,1,0:T(2,128)S(1)}, u32[]{:S(2)}, u32[]{:S(2)}) async-start(f32[128,2,256]{2,1,0:T(2,128)} %bitcast.19), calls=%async_computation.1 | async-start | bytes 524288 | tf_op jit(solution)/shard_map/all_to_all | solution.py:402
  211.6 14.6 %mlp.3 = (f32[1024,512]{1,0:T(8,128)}, bf16[1024,512]{1,0:T(8,128)(2,1)}) custom-call(s32[132]{0:T(256)} %pad_add_fusion.table, bf16[1024,256]{1,0:T(8,128)(2,1)} %get-tuple-element.75.m0, bf16[1024,256]{1,0:T(8,128)(2,1)} %collective-permute-done.14.m1, bf16[1024,256]{1,0:T(8,128)(2,1)} %collective-permute-done.17.m2, ...), custom_call_target="tpu_custom_call" | custom-call | flops 6979321856 | bytes 12582912 | tf_op jit(solution)/shard_map/mlp/pallas_call | solution.py:360
  226.4 1.4 collective-permute-start.19
  227.9 18.6 %all_to_all.21 = bf16[128,2,256]{2,1,0:T(2,128)(2,1)S(1)} all-to-all(bf16[128,2,256]{2,1,0:T(2,128)(2,1)S(1)} %broadcast_in_dim.97), channel_id=1, replica_groups=mesh['req'=32,'tp'=4] {'req','tp'}, dimensions={0} | all-to-all | bytes 262144 | tf_op jit(solution)/shard_map/all_to_all | solution.py:402
  246.4 0.3 fusion.6
  247.0 1.5 convert_element_type.82
  248.6 1.5 fusion.1
  250.1 0.6 collective-permute-start.20
  250.7 0.5 add_rsqrt_fusion
  251.4 0.3 fusion
  251.7 0.5 convolution_reduce_fusion
  252.2 14.1 %all_to_all.22 = f32[128,1,64]{2,1,0:T(1,128)S(1)} all-to-all(f32[128,1,64]{2,1,0:T(1,128)S(1)} %broadcast_in_dim.98), channel_id=1, replica_groups=mesh['req'=32,'tp'=4] {'req','tp'}, dimensions={0} | all-to-all | bytes 65536 | tf_op jit(solution)/shard_map/all_to_all | solution.py:402
  266.3 0.7 reduce_max.39
  267.0 1.6 fusion.3
  268.6 1.0 pad_maximum_fusion
  (93 shorter events, 2.7 us)
Async XLA Ops:
  7.2 244.2 %copy-start = (f32[4,1024]{1,0:T(4,128)S(1)}, f32[4,1024]{1,0:T(4,128)}, u32[]{:S(2)}) copy-start(f32[4,1024]{1,0:T(4,128)} %param.29) | copy-start | bytes 49156
  7.2 172.5 %all-gather.2.cloned.1.call-start = ((), (), s32[]{:S(2)}) async-start(), calls=%async_computation.4 | async-start | bytes 4866048 | tf_op jit(solution)/shard_map/all_gather | solution.py:441
  10.6 4.0 %collective-permute-start = (bf16[8,2304]{1,0:T(8,128)(2,1)}, bf16[8,2304]{1,0:T(8,128)(2,1)S(1)}, u32[]{:S(2)}, u32[]{:S(2)}) collective-permute-start(bf16[8,2304]{1,0:T(8,128)(2,1)} %get-tuple-element.46), channel_id=1, source_target_pairs={{0,2},{1,3},{2,0},{3,1},{4,6},{5,7},{6,4},{7,5},{8,10},{9,11},{10,... | collective-permute-start | bytes 110600 | tf_op jit(solution)/shard_map/ppermute | solution.py:384
  13.0 2.0 collective-permute-start.1
  14.0 3.6 %collective-permute-start.2 = (bf16[8,2304]{1,0:T(8,128)(2,1)}, bf16[8,2304]{1,0:T(8,128)(2,1)S(1)}, u32[]{:S(2)}, u32[]{:S(2)}) collective-permute-start(bf16[8,2304]{1,0:T(8,128)(2,1)} %get-tuple-element.48), channel_id=1, source_target_pairs={{0,3},{1,2},{2,1},{3,0},{4,7},{5,6},{6,5},{7,4},{8,11},{9,10},{10,... | collective-permute-start | bytes 110600 | tf_op jit(solution)/shard_map/ppermute | solution.py:384
  19.0 9.7 %copy-start.1 = (s32[128]{0:T(128)S(1)}, s32[128]{0:T(128)}, u32[]{:S(2)}) copy-start(s32[128]{0:T(128)} %param.18) | copy-start | bytes 1540
  19.1 11.0 %copy-start.8 = (s32[4]{0:T(128)S(1)}, s32[4]{0:T(128)}, u32[]{:S(2)}) copy-start(s32[4]{0:T(128)} %fusion.11.order) | copy-start | bytes 52
  19.1 11.8 %copy-start.9 = (s32[64]{0:T(128)S(1)}, s32[64]{0:T(128)}, u32[]{:S(2)}) copy-start(s32[64]{0:T(128)} %param.16) | copy-start | bytes 772
  19.1 40.5 %all-to-all-start = ((bf16[128,8,1024]{2,1,0:T(8,128)(2,1)}), bf16[128,8,1024]{2,1,0:T(8,128)(2,1)S(1)}, u32[]{:S(2)}, u32[]{:S(2)}) async-start(bf16[128,8,1024]{2,1,0:T(8,128)(2,1)} %bitcast.71), calls=%async_computation | async-start | bytes 4194304 | tf_op jit(solution)/shard_map/all_to_all | solution.py:402
  69.7 66.5 %collective-permute-start.3 = (bf16[8,2,256,256]{3,2,1,0:T(8,128)(2,1)}, bf16[8,2,256,256]{3,2,1,0:T(8,128)(2,1)}, u32[]{:S(2)}, u32[]{:S(2)}) collective-permute-start(bf16[8,2,256,256]{3,2,1,0:T(8,128)(2,1)} %get-tuple-element.55.kv), channel_id=1, source_target_pairs={{0,4},{4,8},{8,12},{12,16},{16,20},{20,24},{24,28},{28,32},{32,36}... | collective-permute-start | bytes 6291464 | tf_op jit(solution)/shard_map/ppermute | solution.py:398
  74.3 61.9 %collective-permute-start.4 = (bf16[8,2,256,256]{3,2,1,0:T(8,128)(2,1)}, bf16[8,2,256,256]{3,2,1,0:T(8,128)(2,1)}, u32[]{:S(2)}, u32[]{:S(2)}) collective-permute-start(bf16[8,2,256,256]{3,2,1,0:T(8,128)(2,1)} %get-tuple-element.55.kv), channel_id=1, source_target_pairs={{4,0},{8,4},{12,8},{16,12},{20,16},{24,20},{28,24},{32,28},{36,32}... | collective-permute-start | bytes 6291464 | tf_op jit(solution)/shard_map/ppermute | solution.py:398
  75.7 6.1 %copy-start.6 = (s32[2048]{0:T(1024)}, s32[2048]{0:T(1024)S(1)}, u32[]{:S(2)}) copy-start(s32[2048]{0:T(1024)S(1)} %get-tuple-element.99) | copy-start | bytes 24580
  81.7 27.4 %copy-start.4 = (bf16[1024,256]{1,0:T(8,128)(2,1)}, bf16[1024,256]{1,0:T(8,128)(2,1)S(1)}, u32[]{:S(2)}) copy-start(bf16[1024,256]{1,0:T(8,128)(2,1)S(1)} %slice.61.o0) | copy-start | bytes 1572868
  81.7 53.7 %collective-permute-start.5 = (bf16[1024,256]{1,0:T(8,128)(2,1)S(1)}, bf16[1024,256]{1,0:T(8,128)(2,1)S(1)}, u32[]{:S(2)}, u32[]{:S(2)}) collective-permute-start(bf16[1024,256]{1,0:T(8,128)(2,1)S(1)} %slice.61.o0), channel_id=1, source_target_pairs={{0,2},{1,3},{2,0},{3,1},{4,6},{5,7},{6,4},{7,5},{8,10},{9,11},{10,... | collective-permute-start | bytes 1572872 | tf_op jit(solution)/shard_map/ppermute | solution.py:384
  82.0 53.5 %collective-permute-start.6 = (bf16[1024,256]{1,0:T(8,128)(2,1)S(1)}, bf16[1024,256]{1,0:T(8,128)(2,1)S(1)}, u32[]{:S(2)}, u32[]{:S(2)}) collective-permute-start(bf16[1024,256]{1,0:T(8,128)(2,1)S(1)} %slice.61.o0), channel_id=1, source_target_pairs={{0,1},{1,0},{2,3},{3,2},{4,5},{5,4},{6,7},{7,6},{8,9},{9,8},{10,11... | collective-permute-start | bytes 1572872 | tf_op jit(solution)/shard_map/ppermute | solution.py:384
  135.5 7.7 %copy-start.11 = (bf16[1024,256]{1,0:T(8,128)(2,1)}, bf16[1024,256]{1,0:T(8,128)(2,1)S(1)}, u32[]{:S(2)}) copy-start(bf16[1024,256]{1,0:T(8,128)(2,1)S(1)} %collective-permute-done.5.o1) | copy-start | bytes 1572868
  135.5 7.7 %copy-start.12 = (bf16[1024,256]{1,0:T(8,128)(2,1)}, bf16[1024,256]{1,0:T(8,128)(2,1)S(1)}, u32[]{:S(2)}) copy-start(bf16[1024,256]{1,0:T(8,128)(2,1)S(1)} %collective-permute-done.6.o2) | copy-start | bytes 1572868
  135.5 40.6 %collective-permute-start.10 = (bf16[1024,256]{1,0:T(8,128)(2,1)S(1)}, bf16[1024,256]{1,0:T(8,128)(2,1)S(1)}, u32[]{:S(2)}, u32[]{:S(2)}) collective-permute-start(bf16[1024,256]{1,0:T(8,128)(2,1)S(1)} %collective-permute-done.5.o1), channel_id=1, source_target_pairs={{0,1},{1,0},{2,3},{3,2},{4,5},{5,4},{6,7},{7,6},{8,9},{9,8},{10,11... | collective-permute-start | bytes 1572872 | tf_op jit(solution)/shard_map/ppermute | solution.py:384
  143.2 26.1 %copy-start.5 = (f32[64,256]{1,0:T(8,128)S(1)}, f32[64,256]{1,0:T(8,128)}, u32[]{:S(2)}) copy-start(f32[64,256]{1,0:T(8,128)} %get-tuple-element.66) | copy-start | bytes 196612
  143.2 25.4 %collective-permute-start.7 = (bf16[1024,256]{1,0:T(8,128)(2,1)}, bf16[1024,256]{1,0:T(8,128)(2,1)S(1)}, u32[]{:S(2)}, u32[]{:S(2)}) collective-permute-start(bf16[1024,256]{1,0:T(8,128)(2,1)} %get-tuple-element.60.m0), channel_id=1, source_target_pairs={{0,2},{1,3},{2,0},{3,1},{4,6},{5,7},{6,4},{7,5},{8,10},{9,11},{10,... | collective-permute-start | bytes 1572872 | tf_op jit(solution)/shard_map/ppermute | solution.py:384
  144.3 32.4 %collective-permute-start.8 = (bf16[1024,256]{1,0:T(8,128)(2,1)}, bf16[1024,256]{1,0:T(8,128)(2,1)S(1)}, u32[]{:S(2)}, u32[]{:S(2)}) collective-permute-start(bf16[1024,256]{1,0:T(8,128)(2,1)} %get-tuple-element.60.m0), channel_id=1, source_target_pairs={{0,1},{1,0},{2,3},{3,2},{4,5},{5,4},{6,7},{7,6},{8,9},{9,8},{10,11... | collective-permute-start | bytes 1572872 | tf_op jit(solution)/shard_map/ppermute | solution.py:384
  168.6 11.1 %copy-start.14 = (bf16[1024,256]{1,0:T(8,128)(2,1)}, bf16[1024,256]{1,0:T(8,128)(2,1)S(1)}, u32[]{:S(2)}) copy-start(bf16[1024,256]{1,0:T(8,128)(2,1)S(1)} %collective-permute-done.7.m1) | copy-start | bytes 1572868
  168.6 8.1 %collective-permute-start.9 = (bf16[1024,256]{1,0:T(8,128)(2,1)S(1)}, bf16[1024,256]{1,0:T(8,128)(2,1)}, u32[]{:S(2)}, u32[]{:S(2)}) collective-permute-start(bf16[1024,256]{1,0:T(8,128)(2,1)S(1)} %collective-permute-done.7.m1), channel_id=1, source_target_pairs={{0,1},{1,0},{2,3},{3,2},{4,5},{5,4},{6,7},{7,6},{8,9},{9,8},{10,11... | collective-permute-start | bytes 1572872 | tf_op jit(solution)/shard_map/ppermute | solution.py:384
  170.2 9.5 %copy-start.7 = (bf16[64,256]{1,0:T(8,128)(2,1)}, bf16[64,256]{1,0:T(8,128)(2,1)S(1)}, u32[]{:S(2)}) copy-start(bf16[64,256]{1,0:T(8,128)(2,1)S(1)} %add_convert_fusion.1.refs_0_) | copy-start | bytes 98308
  170.2 4.8 %collective-permute-start.11 = (bf16[64,256]{1,0:T(8,128)(2,1)S(1)}, bf16[64,256]{1,0:T(8,128)(2,1)S(1)}, u32[]{:S(2)}, u32[]{:S(2)}) collective-permute-start(bf16[64,256]{1,0:T(8,128)(2,1)S(1)} %add_convert_fusion.1.refs_0_), channel_id=1, source_target_pairs={{0,2},{1,3},{2,0},{3,1},{4,6},{5,7},{6,4},{7,5},{8,10},{9,11},{10,... | collective-permute-start | bytes 98312 | tf_op jit(solution)/shard_map/ppermute | solution.py:384
  174.7 2.0 collective-permute-start.12
  175.0 4.7 %copy-start.16 = (bf16[64,256]{1,0:T(8,128)(2,1)}, bf16[64,256]{1,0:T(8,128)(2,1)S(1)}, u32[]{:S(2)}) copy-start(bf16[64,256]{1,0:T(8,128)(2,1)S(1)} %collective-permute-done.11.refs_1_) | copy-start | bytes 98308
  175.0 1.7 collective-permute-start.13
  176.1 3.6 %copy-start.13 = (bf16[1024,256]{1,0:T(8,128)(2,1)}, bf16[1024,256]{1,0:T(8,128)(2,1)S(1)}, u32[]{:S(2)}) copy-start(bf16[1024,256]{1,0:T(8,128)(2,1)S(1)} %collective-permute-done.10.o3) | copy-start | bytes 1572868
  176.1 21.2 %collective-permute-start.14 = (bf16[1024,256]{1,0:T(8,128)(2,1)}, bf16[1024,256]{1,0:T(8,128)(2,1)}, u32[]{:S(2)}, u32[]{:S(2)}) collective-permute-start(bf16[1024,256]{1,0:T(8,128)(2,1)} %get-tuple-element.75.m0), channel_id=1, source_target_pairs={{0,2},{1,3},{2,0},{3,1},{4,6},{5,7},{6,4},{7,5},{8,10},{9,11},{10,... | collective-permute-start | bytes 1572872 | tf_op jit(solution)/shard_map/ppermute | solution.py:384
  176.7 3.0 %copy-start.17 = (bf16[64,256]{1,0:T(8,128)(2,1)}, bf16[64,256]{1,0:T(8,128)(2,1)S(1)}, u32[]{:S(2)}) copy-start(bf16[64,256]{1,0:T(8,128)(2,1)S(1)} %collective-permute-done.12.refs_2_) | copy-start | bytes 98308
  176.7 3.0 %copy-start.18 = (bf16[64,256]{1,0:T(8,128)(2,1)}, bf16[64,256]{1,0:T(8,128)(2,1)S(1)}, u32[]{:S(2)}) copy-start(bf16[64,256]{1,0:T(8,128)(2,1)S(1)} %collective-permute-done.13.refs_3_) | copy-start | bytes 98308
  176.7 3.0 %copy-start.15 = (bf16[1024,256]{1,0:T(8,128)(2,1)}, bf16[1024,256]{1,0:T(8,128)(2,1)S(1)}, u32[]{:S(2)}) copy-start(bf16[1024,256]{1,0:T(8,128)(2,1)S(1)} %collective-permute-done.8.m2) | copy-start | bytes 1572868
  197.2 4.6 %collective-permute-start.15 = (bf16[1024,512]{1,0:T(8,128)(2,1)}, bf16[1024,512]{1,0:T(8,128)(2,1)S(1)}, u32[]{:S(2)}, u32[]{:S(2)}) collective-permute-start(bf16[1024,512]{1,0:T(8,128)(2,1)} %get-tuple-element.71), channel_id=1, source_target_pairs={{0,1},{1,0},{2,3},{3,2},{4,5},{5,4},{6,7},{7,6},{8,9},{9,8},{10,11... | collective-permute-start | bytes 3145736 | tf_op jit(solution)/shard_map/ppermute | solution.py:384
  198.8 4.4 %collective-permute-start.16 = (bf16[1024,256]{1,0:T(8,128)(2,1)}, bf16[1024,256]{1,0:T(8,128)(2,1)}, u32[]{:S(2)}, u32[]{:S(2)}) collective-permute-start(bf16[1024,256]{1,0:T(8,128)(2,1)} %collective-permute-done.14.m1), channel_id=1, source_target_pairs={{0,1},{1,0},{2,3},{3,2},{4,5},{5,4},{6,7},{7,6},{8,9},{9,8},{10,11... | collective-permute-start | bytes 1572872 | tf_op jit(solution)/shard_map/ppermute | solution.py:384
  198.9 12.7 %collective-permute-start.17 = (bf16[1024,256]{1,0:T(8,128)(2,1)}, bf16[1024,256]{1,0:T(8,128)(2,1)}, u32[]{:S(2)}, u32[]{:S(2)}) collective-permute-start(bf16[1024,256]{1,0:T(8,128)(2,1)} %get-tuple-element.75.m0), channel_id=1, source_target_pairs={{0,1},{1,0},{2,3},{3,2},{4,5},{5,4},{6,7},{7,6},{8,9},{9,8},{10,11... | collective-permute-start | bytes 1572872 | tf_op jit(solution)/shard_map/ppermute | solution.py:384
  199.3 2.8 %copy-start.2 = (f32[1024,512]{1,0:T(8,128)S(1)}, f32[1024,512]{1,0:T(8,128)}, u32[]{:S(2)}) copy-start(f32[1024,512]{1,0:T(8,128)} %get-tuple-element.70) | copy-start | bytes 6291460
  203.3 23.1 %collective-permute-start.18 = (bf16[1024,256]{1,0:T(8,128)(2,1)}, bf16[1024,256]{1,0:T(8,128)(2,1)S(1)}, u32[]{:S(2)}, u32[]{:S(2)}) collective-permute-start(bf16[1024,256]{1,0:T(8,128)(2,1)} %get-tuple-element.80), channel_id=1, source_target_pairs={{0,2},{1,3},{2,0},{3,1},{4,6},{5,7},{6,4},{7,5},{8,10},{9,11},{10,... | collective-permute-start | bytes 1572872 | tf_op jit(solution)/shard_map/ppermute | solution.py:384
  203.3 22.9 %all-to-all-start.1 = ((f32[128,2,256]{2,1,0:T(2,128)}), f32[128,2,256]{2,1,0:T(2,128)S(1)}, u32[]{:S(2)}, u32[]{:S(2)}) async-start(f32[128,2,256]{2,1,0:T(2,128)} %bitcast.19), calls=%async_computation.1 | async-start | bytes 524288 | tf_op jit(solution)/shard_map/all_to_all | solution.py:402
  226.4 20.6 %collective-permute-start.19 = (bf16[1024,512]{1,0:T(8,128)(2,1)}, bf16[1024,512]{1,0:T(8,128)(2,1)}, u32[]{:S(2)}, u32[]{:S(2)}) collective-permute-start(bf16[1024,512]{1,0:T(8,128)(2,1)} %get-tuple-element.83), channel_id=1, source_target_pairs={{0,1},{1,0},{2,3},{3,2},{4,5},{5,4},{6,7},{7,6},{8,9},{9,8},{10,11... | collective-permute-start | bytes 3145736 | tf_op jit(solution)/shard_map/ppermute | solution.py:384
  248.6 2.8 %copy-start.10 = (s32[64]{0:T(128)S(1)}, s32[64]{0:T(128)}, u32[]{:S(2)}) copy-start(s32[64]{0:T(128)} %param.17) | copy-start | bytes 772
  248.6 3.1 %copy-start.3 = (f32[384,1024]{1,0:T(8,128)S(1)}, f32[384,1024]{1,0:T(8,128)}, u32[]{:S(2)}) copy-start(f32[384,1024]{1,0:T(8,128)} %param.26) | copy-start | bytes 4718596
  250.1 16.9 %collective-permute-start.20 = (bf16[1024,256]{1,0:T(8,128)(2,1)S(1)}, bf16[1024,256]{1,0:T(8,128)(2,1)}, u32[]{:S(2)}, u32[]{:S(2)}) collective-permute-start(bf16[1024,256]{1,0:T(8,128)(2,1)S(1)} %fusion.1), channel_id=1, source_target_pairs={{0,2},{1,3},{2,0},{3,1},{4,6},{5,7},{6,4},{7,5},{8,10},{9,11},{10,... | collective-permute-start | bytes 1572872 | tf_op jit(solution)/shard_map/ppermute | solution.py:384
Sparse Core Ops, SparseCore 0:
  19.2 160.4 all-gather.1

commit v10 on v9

--- a/solution.py
+++ b/solution.py
@@ -279,7 +279,6 @@
     lasts = refs[: 5 * extra]
     outs = refs[5 * extra :]
     *outs, w, sem = outs
-    keep, send = outs[:2]
     count = w.shape[0]
     step = pl.program_id(0)
 
@@ -324,19 +323,16 @@
     def down(j):
         return contract_last(inner, rows(table[j] * (count // 4), count // 4, 2 * FFP, FFP))
 
-    kept = jnp.concatenate([down(0) + mine, down(1)], axis=1)
-    sent = jnp.concatenate([down(2), down(3)], axis=1)
-    keep[...] = kept
-    send[...] = sent.astype(BF)
+    quarters = (down(0) + mine, down(1), down(2), down(3))
+    for out, x in zip(outs, quarters):
+        out[...] = x.astype(out.dtype)
     if extra:
 
         @pl.when(step == 0)
         def _():
             held = lasts[0].shape[0]
-            for j, x in enumerate((kept, sent)):
-                for n in range(2):
-                    at = pl.ds(pl.multiple_of(256 * table[2 * j + n], 128), 256)
-                    outs[2][:, at] = x[:held, 256 * n : 256 * n + 256]
+            for j, x in enumerate(quarters):
+                outs[4][:, pl.ds(pl.multiple_of(256 * table[j], 128), 256)] = x[:held]
 
 
 def mlp(table, mixed, out_w, h, base, gain, weights, lasts=()):
@@ -348,10 +344,9 @@
     def block(width, base=0):
         return pl.BlockSpec((n, width), lambda i, *_: (jnp.maximum(i - extra, 0) + base, 0))
 
-    out_specs = [block(512), block(512)]
+    out_specs = [block(256)] * 4
     out_shape = [
-        jax.ShapeDtypeStruct((rows, 512), F32),
-        jax.ShapeDtypeStruct((rows, 512), BF),
+        jax.ShapeDtypeStruct((rows, 256), kind) for kind in (F32, F32, BF, BF)
     ]
     if lasts:
         held = lasts[0].shape[0]
@@ -384,13 +379,12 @@
     return lax.ppermute(x, "tp", [(i, i ^ bit) for i in range(4)])
 
 
-def reduce_core(keep, send):
-    got = swap(send, 1).astype(F32)
-    return keep[:, :256] + got[:, :256], (keep[:, 256:] + got[:, 256:]).astype(BF)
-
-
-def reduce_far(mine, send):
-    return (mine + swap(send, 2).astype(F32)).astype(BF)
+def reduce_core(mine, over, add, add_over):
+    return mine, swap(add, 1), (over + swap(add_over, 1).astype(F32)).astype(BF)
+
+
+def reduce_far(mine, got, over):
+    return (mine + got.astype(F32) + swap(over, 2).astype(F32)).astype(BF)
 
 
 def shift(x, by):
@@ -480,16 +474,18 @@
     out_far, out_near = swap(out_w, 2), swap(out_w, 1)
     parts = 2
     state = attend(0, 1, table, query, qseg, (kv, segs[1]), ())
-    out_far, out_near, state = lax.optimization_barrier((out_far, out_near, state))
+    last_slot = (ends - 1 - base).reshape(requests, 1)
+    holds = (last_slot >= 0) & (last_slot < slots)
+    last_in = jnp.where(holds, hidden[jnp.clip(last_slot[:, 0], 0, slots - 1)], 0)
+    out_far, out_near, last_in, state = lax.optimization_barrier(
+        (out_far, out_near, last_in, state)
+    )
     out_w = (out_w, out_far, out_near, swap(out_far, 1))
-    last_slot = (ends - 1 - base).reshape(requests, 1)
     halo = (left, segs[0], right, segs[2], last_slot)
     mixed, picked = zip(
         *[attend(part, parts, table, query, qseg, halo, state) for part in range(parts)]
     )
 
-    holds = (last_slot >= 0) & (last_slot < slots)
-    last_in = jnp.where(holds, hidden[jnp.clip(last_slot[:, 0], 0, slots - 1)], 0)
     last_mixed = sum(picked).astype(BF)
     last_far = swap(last_mixed, 2)
     lasts = (last_mixed, last_far, swap(last_mixed, 1), swap(last_far, 1), last_in)
@@ -505,20 +501,20 @@
     far = [swap(m, 2) for m in mixed]
     near = [swap(m, 1) for m in mixed]
     far[0], _ = lax.optimization_barrier((far[0], mixed[1]))
-    keep, send, last_part = feed(0, (mixed[0], far[0], near[0], swap(far[0], 1)), lasts)
-    keep, send, far[1] = lax.optimization_barrier((keep, send, far[1]))
+    *sums, last_part = feed(0, (mixed[0], far[0], near[0], swap(far[0], 1)), lasts)
+    sums, far[1] = lax.optimization_barrier((sums, far[1]))
     last_piece = swap(far[1], 1)
     each = requests // req_count
     last_part = last_part.reshape(req_count, each, tp_count, 256).transpose(0, 2, 1, 3)
     pair, last_part, last_piece, piece = lax.optimization_barrier(
-        (reduce_core(keep, send), last_part, last_piece, mixed[1])
+        (reduce_core(*sums), last_part, last_piece, mixed[1])
     )
     top = reduce_far(*pair)
     taken = exchange(last_part.reshape(count, each, 256), BOTH).sum(axis=0)
-    keep, send = feed(1, (piece, far[1], near[1], last_piece))
-    taken, keep, send, top = lax.optimization_barrier((taken, keep, send, top))
+    sums = feed(1, (piece, far[1], near[1], last_piece))
+    taken, sums, top = lax.optimization_barrier((taken, sums, top))
     spread = exchange(jnp.broadcast_to(taken.astype(BF)[None], (count, each, 256)), BOTH)
-    hidden_out = jnp.concatenate([top, reduce_far(*reduce_core(keep, send))], axis=0)
+    hidden_out = jnp.concatenate([top, reduce_far(*reduce_core(*sums))], axis=0)
     last = (
         spread.reshape(req_count, tp_count, each, 256)
         .transpose(0, 2, 1, 3)

time: 278 us -> 279 us (level)
  blocking collectives: 32.7 us -> 13.9 us
  waiting for transfers between devices: 61.2 us -> 71.4 us
  starting transfers between devices: 37 us -> 46.2 us
    all_to_all x2 -> x1, blocking collectives: 32.7 us -> 13.9 us  [exchange(): return lax.all_to_all(x, axes, split_axis=0, concat_axis=0, tiled=True)]
    all_to_all x2 -> x3, starting transfers between devices: 17.9 us -> 27.5 us  [exchange(): return lax.all_to_all(x, axes, split_axis=0, concat_axis=0, tiled=True)]
    all_to_all x2 -> x3, waiting for transfers between devices: 15.8 us -> 25.1 us  [exchange(): return lax.all_to_all(x, axes, split_axis=0, concat_axis=0, tiled=True)]
    convert_element_type x6 -> x4, other arithmetic: 6.09 us -> 6.8 us  [the longest x2 4.11 us: reduce_core(): (over + swap(add_over, 1).astype(F32)).astype(BF)]
    ppermute x19 -> x21, waiting for transfers between devices: 42.5 us -> 43.2 us  [swap(): return lax.ppermute(x, 'tp', [(i, i ^ bit) for i in range(4)])]
    ppermute x19 -> x21, starting transfers between devices: 13.2 us -> 12.8 us  [swap(): return lax.ppermute(x, 'tp', [(i, i ^ bit) for i in range(4)])]
  transfers between devices with their start and end apart: 24 -> 27, of which waited for: 8 -> 10; matrix products, arithmetic and copies ran while one was open for 10% -> 11% of each run, Pallas kernels for 33% -> 33%
where the time goes in v10:
time: 279 us; the launch traced here: 278 us
  Pallas kernels  93.7 us (34%)
  waiting for transfers between devices  71.4 us (26%)
  starting transfers between devices  46.2 us (17%)
  other arithmetic  20.9 us (7%)
  local copies, waits for them, and re-layouts  16.1 us (6%)
  between operations  14.6 us (5%)
  blocking collectives  13.9 us (5%)
    pallas_call x3, Pallas kernels, attend(): pl.pallas_call(kernel, grid_spec=pltpu.PrefetchScalarGridSpec(num_scalar_...  44.3 us
    ppermute x21, waiting for transfers between devices, swap(): return lax.ppermute(x, 'tp', [(i, i ^ bit) for i in range(4)])  43.2 us
    pallas_call x2, Pallas kernels, mlp(): pl.pallas_call(functools.partial(mlp_kernel, extra), grid_spec=pltpu.Pref...  32.4 us
    all_to_all x3, starting transfers between devices, exchange(): return lax.all_to_all(x, axes, split_axis=0, concat_axis=0, tiled=True)  27.5 us
    all_to_all x3, waiting for transfers between devices, exchange(): return lax.all_to_all(x, axes, split_axis=0, concat_axis=0, tiled=True)  25.1 us
    all_to_all x1, blocking collectives, exchange(): return lax.all_to_all(x, axes, split_axis=0, concat_axis=0, tiled=True)  13.9 us
    ppermute x21, starting transfers between devices, swap(): return lax.ppermute(x, 'tp', [(i, i ^ bit) for i in range(4)])  12.8 us
    pallas_call x1, Pallas kernels, qkv_project(): pl.pallas_call(qkv_kernel, grid=(rows // n,), in_specs=[pl.BlockSpec((n,...  8.16 us
  transfers between devices with their start and end apart: 27, of which 10 were waited for; matrix products, arithmetic and copies ran while one was open for 11% of the time, Pallas kernels for 33%

profile of v10, /device:TPU:1, one launch (start us, length us, event | category | flops | bytes accessed | tf_op | source)
XLA Modules:
  0.0 277.6 jit_solution(15190506158170755319)
XLA Ops:
  7.2 0.5 fusion.7.order
  7.7 2.8 %prep.1 = (bf16[32,4,8,1024]{3,2,1,0:T(8,128)(2,1)}, bf16[8,2304]{1,0:T(8,128)(2,1)}, bf16[8,2304]{1,0:T(8,128)(2,1)}, bf16[8,2304]{1,0:T(8,128)(2,1)}, bf16[8,2304]{1,0:T(8,128)(2,1)}) custom-call(s32[4]{0:T(128)} %fusion.7.order, f32[8,1024]{1,0:T(8,128)} %wq.1, f32[8,1024]{1,0:T(8,128)} %wk.1, f32[8,1024]{1,0:T(8,128)} %wv.1, f32[8,1024]{1,0:T(8,128)} %wo.1, ...), custom_call_target="tpu_custom_call" | custom-call | tf_op jit(solution)/shard_map/prep/pallas_call | solution.py:64
  10.6 2.5 collective-permute-start
  13.0 1.0 collective-permute-start.1
  14.0 0.6 collective-permute-done
  14.6 0.5 collective-permute-done.1
  15.1 2.5 collective-permute-done.2
  17.6 1.4 pad_maximum_fusion.1
  19.1 9.7 %all-to-all-start = ((bf16[128,8,1024]{2,1,0:T(8,128)(2,1)}), bf16[128,8,1024]{2,1,0:T(8,128)(2,1)S(1)}, u32[]{:S(2)}, u32[]{:S(2)}) async-start(bf16[128,8,1024]{2,1,0:T(8,128)(2,1)} %bitcast.71), calls=%async_computation | async-start | bytes 4194304 | tf_op jit(solution)/shard_map/all_to_all | solution.py:396
  29.1 0.7 fusion.3
  30.2 1.4 copy.44.kseg
  31.5 6.0 %norm.1.x = bf16[2048,1024]{1,0:T(8,128)(2,1)} custom-call(bf16[2048,1024]{1,0:T(8,128)(2,1)} %h.4, f32[1,1024]{1,0:T(1,128)} %bitcast.81), custom_call_target="tpu_custom_call" | custom-call | flops 16777216 | bytes 8388608 | tf_op jit(solution)/shard_map/norm/pallas_call | solution.py:88
  37.7 5.5 %multiply_sine_fusion = (f32[2048,128]{1,0:T(8,128)}, f32[2048,128]{1,0:T(8,128)}) fusion(f32[128]{0:T(128)S(1)} %fusion.16, f32[2048]{0:T(1024)S(1)} %subtract_convert_fusion), kind=kLoop, calls=%fused_computation.4 | loop fusion | flops 262144 | bytes 2105856 | tf_op jit(solution)/shard_map/sin | solution.py:450
  43.2 16.4 %all-to-all-done = bf16[128,8,1024]{2,1,0:T(8,128)(2,1)S(1)} async-done(((bf16[128,8,1024]{2,1,0:T(8,128)(2,1)}), bf16[128,8,1024]{2,1,0:T(8,128)(2,1)S(1)}, u32[]{:S(2)}, u32[]{:S(2)}) %all-to-all-start) | async-done | bytes 2097184 | tf_op jit(solution)/shard_map/all_to_all | solution.py:396
  59.6 2.0 gather_fusion.1
  61.5 8.2 %qkv.1 = (bf16[2048,256]{1,0:T(8,128)(2,1)}, bf16[8,2,256,256]{3,2,1,0:T(8,128)(2,1)}, bf16[2,2048,256]{2,1,0:T(8,128)(2,1)}) custom-call(bf16[2048,1024]{1,0:T(8,128)(2,1)} %norm.1.x, bf16[1024,1024]{1,0:T(8,128)(2,1)} %bitcast.69, f32[2048,128]{1,0:T(8,128)} %get-tuple-element.119.cos, f32[2048,128]{1,0:T(8,128)} %get-tuple-element.118.sin), custom_call_target="tpu_custom_call" | custom-call | flops 3221225472 | bytes 12582912 | tf_op jit(solution)/shard_map/qkv/pallas_call | solution.py:127
  69.7 4.5 %collective-permute-start.3 = (bf16[8,2,256,256]{3,2,1,0:T(8,128)(2,1)}, bf16[8,2,256,256]{3,2,1,0:T(8,128)(2,1)}, u32[]{:S(2)}, u32[]{:S(2)}) collective-permute-start(bf16[8,2,256,256]{3,2,1,0:T(8,128)(2,1)} %get-tuple-element.65.kv), channel_id=1, source_target_pairs={{0,4},{4,8},{8,12},{12,16},{16,20},{20,24},{24,28},{28,32},{32,36}... | collective-permute-start | bytes 6291464 | tf_op jit(solution)/shard_map/ppermute | solution.py:392
  74.3 1.3 collective-permute-start.4
  75.6 3.6 %gather_fusion.2 = bf16[64,1024]{1,0:T(8,128)(2,1)S(1)} fusion(bf16[2048,1024]{1,0:T(8,128)(2,1)} %h.4, s32[1024]{0:T(1024)S(1)} %pad_clamp_fusion), kind=kCustom, calls=%fused_computation.2 | custom fusion | bytes 262400 | tf_op jit(solution)/shard_map/gather | solution.py:479
  79.1 1.3 copy.45.lseg
  80.5 1.3 copy.46.rseg
  82.1 0.6 stack.2.table
  82.7 0.7 broadcast_select_fusion.refs_4_
  83.4 1.1 slice.29.o0
  84.8 0.6 collective-permute-start.6
  85.3 26.6 %attend_own.1 = (f32[4,72,2048]{2,1,0:T(8,128)}, f32[4,1,2048]{2,1,0:T(1,128)}) custom-call(s32[6,8]{1,0:T(8,128)} %stack.2.table, bf16[2048,256]{1,0:T(8,128)(2,1)} %get-tuple-element.62.q, s32[1,2048]{1,0:T(1,128)} %bitcast.76, bf16[8,2,256,256]{3,2,1,0:T(8,128)(2,1)} %get-tuple-element.65.kv, s32[2048,1]{1,0:T(8,128)} %copy.44.kseg), custom_call_target="tpu_custom_call" | custom-call | flops 12884901888 | bytes 8388608 | tf_op jit(solution)/shard_map/attend_own/pallas_call | solution.py:249
  111.9 24.8 %collective-permute-done.5.o1 = bf16[1024,256]{1,0:T(8,128)(2,1)S(1)} collective-permute-done((bf16[1024,256]{1,0:T(8,128)(2,1)S(1)}, bf16[1024,256]{1,0:T(8,128)(2,1)S(1)}, u32[]{:S(2)}, u32[]{:S(2)}) %collective-permute-start.5) | collective-permute-done | bytes 524320 | tf_op jit(solution)/shard_map/ppermute | solution.py:379
  136.6 0.7 collective-permute-start.10
  137.4 7.3 %attend_halo.2 = (bf16[1024,256]{1,0:T(8,128)(2,1)}, f32[64,256]{1,0:T(8,128)}) custom-call(s32[6,8]{1,0:T(8,128)} %stack.2.table, bf16[2048,256]{1,0:T(8,128)(2,1)} %get-tuple-element.62.q, s32[1,2048]{1,0:T(1,128)} %bitcast.77, bf16[8,2,256,256]{3,2,1,0:T(8,128)(2,1)} %collective-permute-done.3.lkv, s32[2048,1]{1,0:T(8,128)} %copy.45.lseg, ...), custom_call_target="tpu_custom_call" | custom-call | flops 12884901888 | bytes 8388608 | tf_op jit(solution)/shard_map/attend_halo/pallas_call | solution.py:249
  144.7 1.2 collective-permute-start.7
  146.2 10.4 %attend_halo.3 = (bf16[1024,256]{1,0:T(8,128)(2,1)}, f32[64,256]{1,0:T(8,128)}) custom-call(s32[6,8]{1,0:T(8,128)} %stack.2.table, bf16[2048,256]{1,0:T(8,128)(2,1)} %get-tuple-element.62.q, s32[1,2048]{1,0:T(1,128)} %bitcast.78, bf16[8,2,256,256]{3,2,1,0:T(8,128)(2,1)} %collective-permute-done.3.lkv, s32[2048,1]{1,0:T(8,128)} %copy.45.lseg, ...), custom_call_target="tpu_custom_call" | custom-call | flops 12884901888 | bytes 8388608 | tf_op jit(solution)/shard_map/attend_halo/pallas_call | solution.py:249
  156.6 13.1 %collective-permute-done.7.m1 = bf16[1024,256]{1,0:T(8,128)(2,1)S(1)} collective-permute-done((bf16[1024,256]{1,0:T(8,128)(2,1)}, bf16[1024,256]{1,0:T(8,128)(2,1)S(1)}, u32[]{:S(2)}, u32[]{:S(2)}) %collective-permute-start.7) | collective-permute-done | bytes 524320 | tf_op jit(solution)/shard_map/ppermute | solution.py:379
  169.7 0.5 collective-permute-start.9
  170.2 0.9 add_convert_fusion.4.refs_0_
  171.2 1.2 gather_fusion
  172.4 0.4 collective-permute-start.12
  172.8 1.5 collective-permute-done.11.refs_1_
  174.3 0.9 collective-permute-start.13
  175.2 0.7 pad_add_fusion.table
  176.1 3.1 %all-gather.2.cloned.1.call-done = bf16[1024,2304]{1,0:T(8,128)(2,1)} async-done(((bf16[32,2304]{1,0:T(8,128)(2,1)}), bf16[1024,2304]{1,0:T(8,128)(2,1)}) %all-gather.2.cloned.1.call-update) | async-done | bytes 4718608 | tf_op jit(solution)/shard_map/all_gather | solution.py:435
  179.2 17.7 %mlp.2 = (f32[1024,256]{1,0:T(8,128)}, f32[1024,256]{1,0:T(8,128)}, bf16[1024,256]{1,0:T(8,128)(2,1)}, bf16[1024,256]{1,0:T(8,128)(2,1)}, f32[64,1024]{1,0:T(8,128)}) custom-call(s32[132]{0:T(256)} %pad_add_fusion.table, bf16[1024,256]{1,0:T(8,128)(2,1)} %get-tuple-element.70.m0, bf16[1024,256]{1,0:T(8,128)(2,1)} %copy-done.18, ...), custom_call_target="tpu_custom_call" | custom-call | flops 6979321856 | bytes 12582912 | tf_op jit(solution)/shard_map/mlp/pallas_call | solution.py:355
  197.0 1.7 collective-permute-start.16
  198.8 0.4 collective-permute-start.17
  199.3 1.1 reshape.565
  200.4 0.8 copy.55
  201.2 2.1 add_convert_fusion.3
  203.4 0.4 collective-permute-start.19
  203.8 0.4 copy-done.20
  204.2 8.1 %all-to-all-start.1 = ((f32[128,2,256]{2,1,0:T(2,128)}), f32[128,2,256]{2,1,0:T(2,128)S(1)}, u32[]{:S(2)}, u32[]{:S(2)}) async-start(f32[128,2,256]{2,1,0:T(2,128)} %bitcast.19), calls=%async_computation.1 | async-start | bytes 524288 | tf_op jit(solution)/shard_map/all_to_all | solution.py:396
  212.3 14.7 %mlp.3 = (f32[1024,256]{1,0:T(8,128)}, f32[1024,256]{1,0:T(8,128)}, bf16[1024,256]{1,0:T(8,128)(2,1)}, bf16[1024,256]{1,0:T(8,128)(2,1)}) custom-call(s32[132]{0:T(256)} %pad_add_fusion.table, bf16[1024,256]{1,0:T(8,128)(2,1)} %get-tuple-element.90.m0, bf16[1024,256]{1,0:T(8,128)(2,1)} %copy-done.17, bf16[1024,256]{1,0:T(8,128)(2,1)} %collective-permute-done.18.m2, ...), custom_call_target="tpu_custom_call" | custom-call | flops 6979321856 | bytes 12582912 | tf_op jit(solution)/shard_map/mlp/pallas_call | solution.py:355
  227.2 1.3 add_convert_fusion.2
  228.6 0.7 broadcast_in_dim.97
  229.3 9.8 %all-to-all-start.2 = ((bf16[128,2,256]{2,1,0:T(2,128)(2,1)}), bf16[128,2,256]{2,1,0:T(2,128)(2,1)S(1)}, u32[]{:S(2)}, u32[]{:S(2)}) async-start(bf16[128,2,256]{2,1,0:T(2,128)(2,1)} %broadcast_in_dim.97), calls=%async_computation.2 | async-start | bytes 262144 | tf_op jit(solution)/shard_map/all_to_all | solution.py:396
  239.1 1.1 collective-permute-start.21
  240.3 8.7 %all-to-all-done.2 = bf16[128,2,256]{2,1,0:T(2,128)(2,1)S(1)} async-done(((bf16[128,2,256]{2,1,0:T(2,128)(2,1)}), bf16[128,2,256]{2,1,0:T(2,128)(2,1)S(1)}, u32[]{:S(2)}, u32[]{:S(2)}) %all-to-all-start.2) | async-done | bytes 131104 | tf_op jit(solution)/shard_map/all_to_all | solution.py:396
  249.7 2.0 add_convert_fusion.1
  251.6 0.6 collective-permute-start.22
  252.2 0.5 add_rsqrt_fusion
  252.9 0.3 fusion
  253.2 0.5 convolution_reduce_fusion
  253.7 13.9 %all_to_all.21 = f32[128,1,64]{2,1,0:T(1,128)S(1)} all-to-all(f32[128,1,64]{2,1,0:T(1,128)S(1)} %broadcast_in_dim.98), channel_id=1, replica_groups=mesh['req'=32,'tp'=4] {'req','tp'}, dimensions={0} | all-to-all | bytes 65536 | tf_op jit(solution)/shard_map/all_to_all | solution.py:396
  267.7 0.7 reduce_max.39
  268.3 1.4 add_convert_fusion
  269.7 1.0 pad_maximum_fusion
  (106 shorter events, 3.2 us)
Async XLA Ops:
  7.2 245.7 %copy-start = (f32[4,1024]{1,0:T(4,128)S(1)}, f32[4,1024]{1,0:T(4,128)}, u32[]{:S(2)}) copy-start(f32[4,1024]{1,0:T(4,128)} %param.29) | copy-start | bytes 49156
  7.2 172.0 %all-gather.2.cloned.1.call-start = ((), (), s32[]{:S(2)}) async-start(), calls=%async_computation.4 | async-start | bytes 4866048 | tf_op jit(solution)/shard_map/all_gather | solution.py:435
  10.6 4.0 %collective-permute-start = (bf16[8,2304]{1,0:T(8,128)(2,1)}, bf16[8,2304]{1,0:T(8,128)(2,1)S(1)}, u32[]{:S(2)}, u32[]{:S(2)}) collective-permute-start(bf16[8,2304]{1,0:T(8,128)(2,1)} %get-tuple-element.56), channel_id=1, source_target_pairs={{0,2},{1,3},{2,0},{3,1},{4,6},{5,7},{6,4},{7,5},{8,10},{9,11},{10,... | collective-permute-start | bytes 110600 | tf_op jit(solution)/shard_map/ppermute | solution.py:379
  13.0 2.0 collective-permute-start.1
  14.0 3.6 %collective-permute-start.2 = (bf16[8,2304]{1,0:T(8,128)(2,1)}, bf16[8,2304]{1,0:T(8,128)(2,1)S(1)}, u32[]{:S(2)}, u32[]{:S(2)}) collective-permute-start(bf16[8,2304]{1,0:T(8,128)(2,1)} %get-tuple-element.58), channel_id=1, source_target_pairs={{0,3},{1,2},{2,1},{3,0},{4,7},{5,6},{6,5},{7,4},{8,11},{9,10},{10,... | collective-permute-start | bytes 110600 | tf_op jit(solution)/shard_map/ppermute | solution.py:379
  19.1 9.7 %copy-start.1 = (s32[128]{0:T(128)S(1)}, s32[128]{0:T(128)}, u32[]{:S(2)}) copy-start(s32[128]{0:T(128)} %param.18) | copy-start | bytes 1540
  19.1 9.9 %copy-start.11 = (s32[64]{0:T(128)S(1)}, s32[64]{0:T(128)}, u32[]{:S(2)}) copy-start(s32[64]{0:T(128)} %param.16) | copy-start | bytes 772
  19.1 40.5 %all-to-all-start = ((bf16[128,8,1024]{2,1,0:T(8,128)(2,1)}), bf16[128,8,1024]{2,1,0:T(8,128)(2,1)S(1)}, u32[]{:S(2)}, u32[]{:S(2)}) async-start(bf16[128,8,1024]{2,1,0:T(8,128)(2,1)} %bitcast.71), calls=%async_computation | async-start | bytes 4194304 | tf_op jit(solution)/shard_map/all_to_all | solution.py:396
  30.2 7.3 %copy-start.8 = (s32[2048]{0:T(1024)}, s32[2048]{0:T(1024)S(1)}, u32[]{:S(2)}) copy-start(s32[2048]{0:T(1024)S(1)} %get-tuple-element.117) | copy-start | bytes 24580
  69.7 67.6 %collective-permute-start.3 = (bf16[8,2,256,256]{3,2,1,0:T(8,128)(2,1)}, bf16[8,2,256,256]{3,2,1,0:T(8,128)(2,1)}, u32[]{:S(2)}, u32[]{:S(2)}) collective-permute-start(bf16[8,2,256,256]{3,2,1,0:T(8,128)(2,1)} %get-tuple-element.65.kv), channel_id=1, source_target_pairs={{0,4},{4,8},{8,12},{12,16},{16,20},{20,24},{24,28},{28,32},{32,36}... | collective-permute-start | bytes 6291464 | tf_op jit(solution)/shard_map/ppermute | solution.py:392
  74.3 63.1 %collective-permute-start.4 = (bf16[8,2,256,256]{3,2,1,0:T(8,128)(2,1)}, bf16[8,2,256,256]{3,2,1,0:T(8,128)(2,1)}, u32[]{:S(2)}, u32[]{:S(2)}) collective-permute-start(bf16[8,2,256,256]{3,2,1,0:T(8,128)(2,1)} %get-tuple-element.65.kv), channel_id=1, source_target_pairs={{4,0},{8,4},{12,8},{16,12},{20,16},{24,20},{28,24},{32,28},{36,32}... | collective-permute-start | bytes 6291464 | tf_op jit(solution)/shard_map/ppermute | solution.py:392
  84.5 27.4 %copy-start.6 = (bf16[1024,256]{1,0:T(8,128)(2,1)}, bf16[1024,256]{1,0:T(8,128)(2,1)S(1)}, u32[]{:S(2)}) copy-start(bf16[1024,256]{1,0:T(8,128)(2,1)S(1)} %slice.29.o0) | copy-start | bytes 1572868
  84.5 52.1 %collective-permute-start.5 = (bf16[1024,256]{1,0:T(8,128)(2,1)S(1)}, bf16[1024,256]{1,0:T(8,128)(2,1)S(1)}, u32[]{:S(2)}, u32[]{:S(2)}) collective-permute-start(bf16[1024,256]{1,0:T(8,128)(2,1)S(1)} %slice.29.o0), channel_id=1, source_target_pairs={{0,2},{1,3},{2,0},{3,1},{4,6},{5,7},{6,4},{7,5},{8,10},{9,11},{10,... | collective-permute-start | bytes 1572872 | tf_op jit(solution)/shard_map/ppermute | solution.py:379
  84.8 51.9 %collective-permute-start.6 = (bf16[1024,256]{1,0:T(8,128)(2,1)S(1)}, bf16[1024,256]{1,0:T(8,128)(2,1)S(1)}, u32[]{:S(2)}, u32[]{:S(2)}) collective-permute-start(bf16[1024,256]{1,0:T(8,128)(2,1)S(1)} %slice.29.o0), channel_id=1, source_target_pairs={{0,1},{1,0},{2,3},{3,2},{4,5},{5,4},{6,7},{7,6},{8,9},{9,8},{10,11... | collective-permute-start | bytes 1572872 | tf_op jit(solution)/shard_map/ppermute | solution.py:379
  136.6 8.1 %copy-start.13 = (bf16[1024,256]{1,0:T(8,128)(2,1)}, bf16[1024,256]{1,0:T(8,128)(2,1)S(1)}, u32[]{:S(2)}) copy-start(bf16[1024,256]{1,0:T(8,128)(2,1)S(1)} %collective-permute-done.5.o1) | copy-start | bytes 1572868
  136.6 8.1 %copy-start.14 = (bf16[1024,256]{1,0:T(8,128)(2,1)}, bf16[1024,256]{1,0:T(8,128)(2,1)S(1)}, u32[]{:S(2)}) copy-start(bf16[1024,256]{1,0:T(8,128)(2,1)S(1)} %collective-permute-done.6.o2) | copy-start | bytes 1572868
  136.6 39.2 %collective-permute-start.10 = (bf16[1024,256]{1,0:T(8,128)(2,1)S(1)}, bf16[1024,256]{1,0:T(8,128)(2,1)S(1)}, u32[]{:S(2)}, u32[]{:S(2)}) collective-permute-start(bf16[1024,256]{1,0:T(8,128)(2,1)S(1)} %collective-permute-done.5.o1), channel_id=1, source_target_pairs={{0,1},{1,0},{2,3},{3,2},{4,5},{5,4},{6,7},{7,6},{8,9},{9,8},{10,11... | collective-permute-start | bytes 1572872 | tf_op jit(solution)/shard_map/ppermute | solution.py:379
  144.7 25.5 %copy-start.7 = (f32[64,256]{1,0:T(8,128)S(1)}, f32[64,256]{1,0:T(8,128)}, u32[]{:S(2)}) copy-start(f32[64,256]{1,0:T(8,128)} %get-tuple-element.76) | copy-start | bytes 196612
  144.7 30.5 %copy-start.10 = (s32[4]{0:T(128)S(1)}, s32[4]{0:T(128)}, u32[]{:S(2)}) copy-start(s32[4]{0:T(128)} %fusion.7.order) | copy-start | bytes 52
  144.7 25.0 %collective-permute-start.7 = (bf16[1024,256]{1,0:T(8,128)(2,1)}, bf16[1024,256]{1,0:T(8,128)(2,1)S(1)}, u32[]{:S(2)}, u32[]{:S(2)}) collective-permute-start(bf16[1024,256]{1,0:T(8,128)(2,1)} %get-tuple-element.70.m0), channel_id=1, source_target_pairs={{0,2},{1,3},{2,0},{3,1},{4,6},{5,7},{6,4},{7,5},{8,10},{9,11},{10,... | collective-permute-start | bytes 1572872 | tf_op jit(solution)/shard_map/ppermute | solution.py:379
  145.9 30.2 %collective-permute-start.8 = (bf16[1024,256]{1,0:T(8,128)(2,1)}, bf16[1024,256]{1,0:T(8,128)(2,1)S(1)}, u32[]{:S(2)}, u32[]{:S(2)}) collective-permute-start(bf16[1024,256]{1,0:T(8,128)(2,1)} %get-tuple-element.70.m0), channel_id=1, source_target_pairs={{0,1},{1,0},{2,3},{3,2},{4,5},{5,4},{6,7},{7,6},{8,9},{9,8},{10,11... | collective-permute-start | bytes 1572872 | tf_op jit(solution)/shard_map/ppermute | solution.py:379
  169.7 9.5 %copy-start.18 = (bf16[1024,256]{1,0:T(8,128)(2,1)}, bf16[1024,256]{1,0:T(8,128)(2,1)S(1)}, u32[]{:S(2)}) copy-start(bf16[1024,256]{1,0:T(8,128)(2,1)S(1)} %collective-permute-done.7.m1) | copy-start | bytes 1572868
  169.7 6.4 %collective-permute-start.9 = (bf16[1024,256]{1,0:T(8,128)(2,1)S(1)}, bf16[1024,256]{1,0:T(8,128)(2,1)}, u32[]{:S(2)}, u32[]{:S(2)}) collective-permute-start(bf16[1024,256]{1,0:T(8,128)(2,1)S(1)} %collective-permute-done.7.m1), channel_id=1, source_target_pairs={{0,1},{1,0},{2,3},{3,2},{4,5},{5,4},{6,7},{7,6},{8,9},{9,8},{10,11... | collective-permute-start | bytes 1572872 | tf_op jit(solution)/shard_map/ppermute | solution.py:379
  171.1 8.1 %copy-start.9 = (bf16[64,256]{1,0:T(8,128)(2,1)}, bf16[64,256]{1,0:T(8,128)(2,1)S(1)}, u32[]{:S(2)}) copy-start(bf16[64,256]{1,0:T(8,128)(2,1)S(1)} %add_convert_fusion.4.refs_0_) | copy-start | bytes 98308
  171.1 3.2 %collective-permute-start.11 = (bf16[64,256]{1,0:T(8,128)(2,1)S(1)}, bf16[64,256]{1,0:T(8,128)(2,1)S(1)}, u32[]{:S(2)}, u32[]{:S(2)}) collective-permute-start(bf16[64,256]{1,0:T(8,128)(2,1)S(1)} %add_convert_fusion.4.refs_0_), channel_id=1, source_target_pairs={{0,2},{1,3},{2,0},{3,1},{4,6},{5,7},{6,4},{7,5},{8,10},{9,11},{10,... | collective-permute-start | bytes 98312 | tf_op jit(solution)/shard_map/ppermute | solution.py:379
  172.4 3.5 %collective-permute-start.12 = (bf16[64,256]{1,0:T(8,128)(2,1)S(1)}, bf16[64,256]{1,0:T(8,128)(2,1)S(1)}, u32[]{:S(2)}, u32[]{:S(2)}) collective-permute-start(bf16[64,256]{1,0:T(8,128)(2,1)S(1)} %add_convert_fusion.4.refs_0_), channel_id=1, source_target_pairs={{0,1},{1,0},{2,3},{3,2},{4,5},{5,4},{6,7},{7,6},{8,9},{9,8},{10,11... | collective-permute-start | bytes 98312 | tf_op jit(solution)/shard_map/ppermute | solution.py:379
  174.3 4.9 %copy-start.21 = (bf16[64,256]{1,0:T(8,128)(2,1)}, bf16[64,256]{1,0:T(8,128)(2,1)S(1)}, u32[]{:S(2)}) copy-start(bf16[64,256]{1,0:T(8,128)(2,1)S(1)} %collective-permute-done.11.refs_1_) | copy-start | bytes 98308
  174.3 1.8 collective-permute-start.13
  175.9 3.3 %copy-start.15 = (bf16[1024,256]{1,0:T(8,128)(2,1)}, bf16[1024,256]{1,0:T(8,128)(2,1)S(1)}, u32[]{:S(2)}) copy-start(bf16[1024,256]{1,0:T(8,128)(2,1)S(1)} %collective-permute-done.10.o3) | copy-start | bytes 1572868
  175.9 21.1 %collective-permute-start.14 = (bf16[1024,256]{1,0:T(8,128)(2,1)}, bf16[1024,256]{1,0:T(8,128)(2,1)S(1)}, u32[]{:S(2)}, u32[]{:S(2)}) collective-permute-start(bf16[1024,256]{1,0:T(8,128)(2,1)} %get-tuple-element.90.m0), channel_id=1, source_target_pairs={{0,2},{1,3},{2,0},{3,1},{4,6},{5,7},{6,4},{7,5},{8,10},{9,11},{10,... | collective-permute-start | bytes 1572872 | tf_op jit(solution)/shard_map/ppermute | solution.py:379
  175.9 3.3 %copy-start.22 = (bf16[64,256]{1,0:T(8,128)(2,1)}, bf16[64,256]{1,0:T(8,128)(2,1)S(1)}, u32[]{:S(2)}) copy-start(bf16[64,256]{1,0:T(8,128)(2,1)S(1)} %collective-permute-done.12.refs_2_) | copy-start | bytes 98308
  176.1 3.1 %copy-start.23 = (bf16[64,256]{1,0:T(8,128)(2,1)}, bf16[64,256]{1,0:T(8,128)(2,1)S(1)}, u32[]{:S(2)}) copy-start(bf16[64,256]{1,0:T(8,128)(2,1)S(1)} %collective-permute-done.13.refs_3_) | copy-start | bytes 98308
  176.1 3.2 %copy-start.19 = (bf16[1024,256]{1,0:T(8,128)(2,1)}, bf16[1024,256]{1,0:T(8,128)(2,1)S(1)}, u32[]{:S(2)}) copy-start(bf16[1024,256]{1,0:T(8,128)(2,1)S(1)} %collective-permute-done.8.m2) | copy-start | bytes 1572868
  179.2 20.0 %copy-start.16 = (bf16[1024,256]{1,0:T(8,128)(2,1)S(1)}, bf16[1024,256]{1,0:T(8,128)(2,1)}, u32[]{:S(2)}) copy-start(bf16[1024,256]{1,0:T(8,128)(2,1)} %get-tuple-element.90.m0) | copy-start | bytes 1572868
  197.0 6.8 %copy-start.17 = (bf16[1024,256]{1,0:T(8,128)(2,1)}, bf16[1024,256]{1,0:T(8,128)(2,1)S(1)}, u32[]{:S(2)}) copy-start(bf16[1024,256]{1,0:T(8,128)(2,1)S(1)} %collective-permute-done.14.m1) | copy-start | bytes 1572868
  197.0 4.2 %collective-permute-start.16 = (bf16[1024,256]{1,0:T(8,128)(2,1)}, bf16[1024,256]{1,0:T(8,128)(2,1)S(1)}, u32[]{:S(2)}, u32[]{:S(2)}) collective-permute-start(bf16[1024,256]{1,0:T(8,128)(2,1)} %get-tuple-element.86), channel_id=1, source_target_pairs={{0,1},{1,0},{2,3},{3,2},{4,5},{5,4},{6,7},{7,6},{8,9},{9,8},{10,11... | collective-permute-start | bytes 1572872 | tf_op jit(solution)/shard_map/ppermute | solution.py:379
  198.7 4.7 %collective-permute-start.15 = (bf16[1024,256]{1,0:T(8,128)(2,1)}, bf16[1024,256]{1,0:T(8,128)(2,1)S(1)}, u32[]{:S(2)}, u32[]{:S(2)}) collective-permute-start(bf16[1024,256]{1,0:T(8,128)(2,1)} %get-tuple-element.84), channel_id=1, source_target_pairs={{0,1},{1,0},{2,3},{3,2},{4,5},{5,4},{6,7},{7,6},{8,9},{9,8},{10,11... | collective-permute-start | bytes 1572872 | tf_op jit(solution)/shard_map/ppermute | solution.py:379
  198.8 4.6 %collective-permute-start.17 = (bf16[1024,256]{1,0:T(8,128)(2,1)S(1)}, bf16[1024,256]{1,0:T(8,128)(2,1)S(1)}, u32[]{:S(2)}, u32[]{:S(2)}) collective-permute-start(bf16[1024,256]{1,0:T(8,128)(2,1)S(1)} %collective-permute-done.14.m1), channel_id=1, source_target_pairs={{0,1},{1,0},{2,3},{3,2},{4,5},{5,4},{6,7},{7,6},{8,9},{9,8},{10,11... | collective-permute-start | bytes 1572872 | tf_op jit(solution)/shard_map/ppermute | solution.py:379
  199.2 13.1 %collective-permute-start.18 = (bf16[1024,256]{1,0:T(8,128)(2,1)S(1)}, bf16[1024,256]{1,0:T(8,128)(2,1)}, u32[]{:S(2)}, u32[]{:S(2)}) collective-permute-start(bf16[1024,256]{1,0:T(8,128)(2,1)S(1)} %copy-done.16), channel_id=1, source_target_pairs={{0,1},{1,0},{2,3},{3,2},{4,5},{5,4},{6,7},{7,6},{8,9},{9,8},{10,11... | collective-permute-start | bytes 1572872 | tf_op jit(solution)/shard_map/ppermute | solution.py:379
  203.4 0.8 copy-start.20
  203.4 23.8 %collective-permute-start.19 = (bf16[1024,256]{1,0:T(8,128)(2,1)}, bf16[1024,256]{1,0:T(8,128)(2,1)}, u32[]{:S(2)}, u32[]{:S(2)}) collective-permute-start(bf16[1024,256]{1,0:T(8,128)(2,1)} %add_convert_fusion.3), channel_id=1, source_target_pairs={{0,2},{1,3},{2,0},{3,1},{4,6},{5,7},{6,4},{7,5},{8,10},{9,11},{10,... | collective-permute-start | bytes 1572872 | tf_op jit(solution)/shard_map/ppermute | solution.py:379
  204.2 22.9 %all-to-all-start.1 = ((f32[128,2,256]{2,1,0:T(2,128)}), f32[128,2,256]{2,1,0:T(2,128)S(1)}, u32[]{:S(2)}, u32[]{:S(2)}) async-start(f32[128,2,256]{2,1,0:T(2,128)} %bitcast.19), calls=%async_computation.1 | async-start | bytes 524288 | tf_op jit(solution)/shard_map/all_to_all | solution.py:396
  212.3 14.9 %copy-start.4 = (f32[1024,256]{1,0:T(8,128)S(1)}, f32[1024,256]{1,0:T(8,128)}, u32[]{:S(2)}) copy-start(f32[1024,256]{1,0:T(8,128)} %get-tuple-element.96) | copy-start | bytes 3145732
  227.0 22.6 %copy-start.5 = (f32[1024,256]{1,0:T(8,128)S(1)}, f32[1024,256]{1,0:T(8,128)}, u32[]{:S(2)}) copy-start(f32[1024,256]{1,0:T(8,128)} %get-tuple-element.102) | copy-start | bytes 3145732
  228.6 24.3 %copy-start.12 = (s32[64]{0:T(128)S(1)}, s32[64]{0:T(128)}, u32[]{:S(2)}) copy-start(s32[64]{0:T(128)} %param.17) | copy-start | bytes 772
  229.3 19.7 %all-to-all-start.2 = ((bf16[128,2,256]{2,1,0:T(2,128)(2,1)}), bf16[128,2,256]{2,1,0:T(2,128)(2,1)S(1)}, u32[]{:S(2)}, u32[]{:S(2)}) async-start(bf16[128,2,256]{2,1,0:T(2,128)(2,1)} %broadcast_in_dim.97), calls=%async_computation.2 | async-start | bytes 262144 | tf_op jit(solution)/shard_map/all_to_all | solution.py:396
  239.1 10.6 %collective-permute-start.21 = (bf16[1024,256]{1,0:T(8,128)(2,1)}, bf16[1024,256]{1,0:T(8,128)(2,1)}, u32[]{:S(2)}, u32[]{:S(2)}) collective-permute-start(bf16[1024,256]{1,0:T(8,128)(2,1)} %get-tuple-element.103), channel_id=1, source_target_pairs={{0,1},{1,0},{2,3},{3,2},{4,5},{5,4},{6,7},{7,6},{8,9},{9,8},{10,11... | collective-permute-start | bytes 1572872 | tf_op jit(solution)/shard_map/ppermute | solution.py:379
  240.2 28.1 %collective-permute-start.20 = (bf16[1024,256]{1,0:T(8,128)(2,1)}, bf16[1024,256]{1,0:T(8,128)(2,1)}, u32[]{:S(2)}, u32[]{:S(2)}) collective-permute-start(bf16[1024,256]{1,0:T(8,128)(2,1)} %get-tuple-element.101), channel_id=1, source_target_pairs={{0,1},{1,0},{2,3},{3,2},{4,5},{5,4},{6,7},{7,6},{8,9},{9,8},{10,11... | collective-permute-start | bytes 1572872 | tf_op jit(solution)/shard_map/ppermute | solution.py:379
  249.0 4.2 %copy-start.2 = (f32[384,1024]{1,0:T(8,128)S(1)}, f32[384,1024]{1,0:T(8,128)}, u32[]{:S(2)}) copy-start(f32[384,1024]{1,0:T(8,128)} %param.26) | copy-start | bytes 4718596
  251.6 16.7 %copy-start.3 = (f32[1024,256]{1,0:T(8,128)S(1)}, f32[1024,256]{1,0:T(8,128)}, u32[]{:S(2)}) copy-start(f32[1024,256]{1,0:T(8,128)} %get-tuple-element.100) | copy-start | bytes 3145732
  251.6 16.7 %collective-permute-start.22 = (bf16[1024,256]{1,0:T(8,128)(2,1)}, bf16[1024,256]{1,0:T(8,128)(2,1)}, u32[]{:S(2)}, u32[]{:S(2)}) collective-permute-start(bf16[1024,256]{1,0:T(8,128)(2,1)} %add_convert_fusion.1), channel_id=1, source_target_pairs={{0,2},{1,3},{2,0},{3,1},{4,6},{5,7},{6,4},{7,5},{8,10},{9,11},{10,... | collective-permute-start | bytes 1572872 | tf_op jit(solution)/shard_map/ppermute | solution.py:379
Sparse Core Ops, SparseCore 0:
  19.2 159.9 all-gather.1

commit v11 on v10

--- a/solution.py
+++ b/solution.py
@@ -432,9 +432,20 @@
         [rest_block[0], swap(rest_block[1], 2), swap(rest_block[2], 1), swap(rest_block[3], 3)], axis=0
     )
     hidden, lengths, rest_rows = lax.optimization_barrier((hidden_in, lengths, rest_rows))
-    rest = lax.all_gather(rest_rows, "req", axis=0, tiled=True).reshape(count, 8, REST)
+    sides = (4, 4)
+    plane = sides[0] * sides[1]
+    group = [
+        z * plane + x * sides[1] + y
+        for z in range(req_count // plane)
+        for y in range(sides[1])
+        for x in range(sides[0])
+    ]
+    rest = lax.all_gather(rest_rows, "req", axis=0, tiled=True, axis_index_groups=[group])
+    rest = rest.reshape(count, 8, REST)
     far = jnp.arange(count, dtype=jnp.int32)
-    rest_target = shard_map[far // 4 * tp_count + (tp_index ^ turn_bits(far % 4))]
+    at = far // tp_count
+    from_req = at // plane * plane + at % sides[0] * sides[1] + at // sides[0] % sides[1]
+    rest_target = shard_map[from_req * tp_count + (tp_index ^ turn_bits(far % tp_count))]
 
     ends = jnp.cumsum(lengths)
     base = req_index * slots

time: 279 us -> 279 us (level)
  transfers between devices with their start and end apart: 27 -> 27, of which waited for: 10 -> 10; matrix products, arithmetic and copies ran while one was open for 11% -> 11% of each run, Pallas kernels for 33% -> 32%
where the time goes in v11:
time: 279 us; the launch traced here: 278 us
  Pallas kernels  92.3 us (33%)
  waiting for transfers between devices  74 us (27%)
  starting transfers between devices  45.4 us (16%)
  other arithmetic  20.9 us (7%)
  local copies, waits for them, and re-layouts  15.8 us (6%)
  between operations  14.6 us (5%)
  blocking collectives  13.9 us (5%)
    ppermute x21, waiting for transfers between devices, swap(): return lax.ppermute(x, 'tp', [(i, i ^ bit) for i in range(4)])  44.5 us
    pallas_call x3, Pallas kernels, attend(): pl.pallas_call(kernel, grid_spec=pltpu.PrefetchScalarGridSpec(num_scalar_...  42.9 us
    pallas_call x2, Pallas kernels, mlp(): pl.pallas_call(functools.partial(mlp_kernel, extra), grid_spec=pltpu.Pref...  32.4 us
    all_to_all x3, starting transfers between devices, exchange(): return lax.all_to_all(x, axes, split_axis=0, concat_axis=0, tiled=True)  26.7 us
    all_to_all x3, waiting for transfers between devices, exchange(): return lax.all_to_all(x, axes, split_axis=0, concat_axis=0, tiled=True)  25.1 us
    all_to_all x1, blocking collectives, exchange(): return lax.all_to_all(x, axes, split_axis=0, concat_axis=0, tiled=True)  13.9 us
    ppermute x21, starting transfers between devices, swap(): return lax.ppermute(x, 'tp', [(i, i ^ bit) for i in range(4)])  12.8 us
    pallas_call x1, Pallas kernels, qkv_project(): pl.pallas_call(qkv_kernel, grid=(rows // n,), in_specs=[pl.BlockSpec((n,...  8.16 us
  transfers between devices with their start and end apart: 27, of which 10 were waited for; matrix products, arithmetic and copies ran while one was open for 11% of the time, Pallas kernels for 32%

profile of v11, /device:TPU:1, one launch (start us, length us, event | category | flops | bytes accessed | tf_op | source)
XLA Modules:
  0.0 277.7 jit_solution(15001247636936813850)
XLA Ops:
  7.2 0.5 fusion.8.order
  7.7 2.8 %prep.1 = (bf16[32,4,8,1024]{3,2,1,0:T(8,128)(2,1)}, bf16[8,2304]{1,0:T(8,128)(2,1)}, bf16[8,2304]{1,0:T(8,128)(2,1)}, bf16[8,2304]{1,0:T(8,128)(2,1)}, bf16[8,2304]{1,0:T(8,128)(2,1)}) custom-call(s32[4]{0:T(128)} %fusion.8.order, f32[8,1024]{1,0:T(8,128)} %wq.1, f32[8,1024]{1,0:T(8,128)} %wk.1, f32[8,1024]{1,0:T(8,128)} %wv.1, f32[8,1024]{1,0:T(8,128)} %wo.1, ...), custom_call_target="tpu_custom_call" | custom-call | tf_op jit(solution)/shard_map/prep/pallas_call | solution.py:64
  10.6 2.5 collective-permute-start
  13.0 1.0 collective-permute-start.1
  14.0 0.6 collective-permute-done
  14.6 0.5 collective-permute-done.1
  15.1 2.5 collective-permute-done.2
  17.6 1.4 pad_maximum_fusion.1
  19.1 9.7 %all-to-all-start = ((bf16[128,8,1024]{2,1,0:T(8,128)(2,1)}), bf16[128,8,1024]{2,1,0:T(8,128)(2,1)S(1)}, u32[]{:S(2)}, u32[]{:S(2)}) async-start(bf16[128,8,1024]{2,1,0:T(8,128)(2,1)} %bitcast.71), calls=%async_computation | async-start | bytes 4194304 | tf_op jit(solution)/shard_map/all_to_all | solution.py:396
  29.1 0.7 fusion.3
  30.2 1.4 copy.44.kseg
  31.5 6.0 %norm.1.x = bf16[2048,1024]{1,0:T(8,128)(2,1)} custom-call(bf16[2048,1024]{1,0:T(8,128)(2,1)} %h.4, f32[1,1024]{1,0:T(1,128)} %bitcast.81), custom_call_target="tpu_custom_call" | custom-call | flops 16777216 | bytes 8388608 | tf_op jit(solution)/shard_map/norm/pallas_call | solution.py:88
  37.7 5.5 %multiply_sine_fusion = (f32[2048,128]{1,0:T(8,128)}, f32[2048,128]{1,0:T(8,128)}) fusion(f32[128]{0:T(128)S(1)} %fusion.17, f32[2048]{0:T(1024)S(1)} %subtract_convert_fusion), kind=kLoop, calls=%fused_computation.4 | loop fusion | flops 262144 | bytes 2105856 | tf_op jit(solution)/shard_map/sin | solution.py:461
  43.2 16.4 %all-to-all-done = bf16[128,8,1024]{2,1,0:T(8,128)(2,1)S(1)} async-done(((bf16[128,8,1024]{2,1,0:T(8,128)(2,1)}), bf16[128,8,1024]{2,1,0:T(8,128)(2,1)S(1)}, u32[]{:S(2)}, u32[]{:S(2)}) %all-to-all-start) | async-done | bytes 2097184 | tf_op jit(solution)/shard_map/all_to_all | solution.py:396
  59.6 2.0 gather_fusion.1
  61.5 8.2 %qkv.1 = (bf16[2048,256]{1,0:T(8,128)(2,1)}, bf16[8,2,256,256]{3,2,1,0:T(8,128)(2,1)}, bf16[2,2048,256]{2,1,0:T(8,128)(2,1)}) custom-call(bf16[2048,1024]{1,0:T(8,128)(2,1)} %norm.1.x, bf16[1024,1024]{1,0:T(8,128)(2,1)} %bitcast.69, f32[2048,128]{1,0:T(8,128)} %get-tuple-element.119.cos, f32[2048,128]{1,0:T(8,128)} %get-tuple-element.118.sin), custom_call_target="tpu_custom_call" | custom-call | flops 3221225472 | bytes 12582912 | tf_op jit(solution)/shard_map/qkv/pallas_call | solution.py:127
  69.7 4.5 %collective-permute-start.3 = (bf16[8,2,256,256]{3,2,1,0:T(8,128)(2,1)}, bf16[8,2,256,256]{3,2,1,0:T(8,128)(2,1)}, u32[]{:S(2)}, u32[]{:S(2)}) collective-permute-start(bf16[8,2,256,256]{3,2,1,0:T(8,128)(2,1)} %get-tuple-element.65.kv), channel_id=1, source_target_pairs={{0,4},{4,8},{8,12},{12,16},{16,20},{20,24},{24,28},{28,32},{32,36}... | collective-permute-start | bytes 6291464 | tf_op jit(solution)/shard_map/ppermute | solution.py:392
  74.3 1.3 collective-permute-start.4
  75.6 3.6 %gather_fusion.2 = bf16[64,1024]{1,0:T(8,128)(2,1)S(1)} fusion(bf16[2048,1024]{1,0:T(8,128)(2,1)} %h.4, s32[1024]{0:T(1024)S(1)} %pad_clamp_fusion), kind=kCustom, calls=%fused_computation.2 | custom fusion | bytes 262400 | tf_op jit(solution)/shard_map/gather | solution.py:490
  79.1 1.3 copy.45.lseg
  80.5 1.3 copy.46.rseg
  82.1 0.6 stack.2.table
  82.7 0.7 broadcast_select_fusion.refs_4_
  83.4 1.1 slice.29.o0
  84.8 0.6 collective-permute-start.6
  85.3 21.6 %attend_own.1 = (f32[4,72,2048]{2,1,0:T(8,128)}, f32[4,1,2048]{2,1,0:T(1,128)}) custom-call(s32[6,8]{1,0:T(8,128)} %stack.2.table, bf16[2048,256]{1,0:T(8,128)(2,1)} %get-tuple-element.62.q, s32[1,2048]{1,0:T(1,128)} %bitcast.76, bf16[8,2,256,256]{3,2,1,0:T(8,128)(2,1)} %get-tuple-element.65.kv, s32[2048,1]{1,0:T(8,128)} %copy.44.kseg), custom_call_target="tpu_custom_call" | custom-call | flops 12884901888 | bytes 8388608 | tf_op jit(solution)/shard_map/attend_own/pallas_call | solution.py:249
  106.9 29.7 %collective-permute-done.5.o1 = bf16[1024,256]{1,0:T(8,128)(2,1)S(1)} collective-permute-done((bf16[1024,256]{1,0:T(8,128)(2,1)S(1)}, bf16[1024,256]{1,0:T(8,128)(2,1)S(1)}, u32[]{:S(2)}, u32[]{:S(2)}) %collective-permute-start.5) | collective-permute-done | bytes 524320 | tf_op jit(solution)/shard_map/ppermute | solution.py:379
  136.6 0.7 collective-permute-start.10
  137.4 7.3 %attend_halo.2 = (bf16[1024,256]{1,0:T(8,128)(2,1)}, f32[64,256]{1,0:T(8,128)}) custom-call(s32[6,8]{1,0:T(8,128)} %stack.2.table, bf16[2048,256]{1,0:T(8,128)(2,1)} %get-tuple-element.62.q, s32[1,2048]{1,0:T(1,128)} %bitcast.77, bf16[8,2,256,256]{3,2,1,0:T(8,128)(2,1)} %collective-permute-done.3.lkv, s32[2048,1]{1,0:T(8,128)} %copy.45.lseg, ...), custom_call_target="tpu_custom_call" | custom-call | flops 12884901888 | bytes 8388608 | tf_op jit(solution)/shard_map/attend_halo/pallas_call | solution.py:249
  144.7 1.1 collective-permute-start.7
  146.1 14.0 %attend_halo.3 = (bf16[1024,256]{1,0:T(8,128)(2,1)}, f32[64,256]{1,0:T(8,128)}) custom-call(s32[6,8]{1,0:T(8,128)} %stack.2.table, bf16[2048,256]{1,0:T(8,128)(2,1)} %get-tuple-element.62.q, s32[1,2048]{1,0:T(1,128)} %bitcast.78, bf16[8,2,256,256]{3,2,1,0:T(8,128)(2,1)} %collective-permute-done.3.lkv, s32[2048,1]{1,0:T(8,128)} %copy.45.lseg, ...), custom_call_target="tpu_custom_call" | custom-call | flops 12884901888 | bytes 8388608 | tf_op jit(solution)/shard_map/attend_halo/pallas_call | solution.py:249
  160.1 9.6 %collective-permute-done.7.m1 = bf16[1024,256]{1,0:T(8,128)(2,1)S(1)} collective-permute-done((bf16[1024,256]{1,0:T(8,128)(2,1)}, bf16[1024,256]{1,0:T(8,128)(2,1)S(1)}, u32[]{:S(2)}, u32[]{:S(2)}) %collective-permute-start.7) | collective-permute-done | bytes 524320 | tf_op jit(solution)/shard_map/ppermute | solution.py:379
  169.7 0.5 collective-permute-start.9
  170.2 0.9 add_convert_fusion.4.refs_0_
  171.1 1.2 gather_fusion
  172.4 0.5 collective-permute-start.12
  172.8 1.5 collective-permute-done.11.refs_1_
  174.3 0.9 collective-permute-start.13
  175.2 0.7 pad_add_fusion.table
  176.0 4.3 %all-gather.2.cloned.1.call-done = bf16[1024,2304]{1,0:T(8,128)(2,1)} async-done(((bf16[32,2304]{1,0:T(8,128)(2,1)}), bf16[1024,2304]{1,0:T(8,128)(2,1)}) %all-gather.2.cloned.1.call-update) | async-done | bytes 4718608 | tf_op jit(solution)/shard_map/all_gather | solution.py:443
  180.4 17.7 %mlp.2 = (f32[1024,256]{1,0:T(8,128)}, f32[1024,256]{1,0:T(8,128)}, bf16[1024,256]{1,0:T(8,128)(2,1)}, bf16[1024,256]{1,0:T(8,128)(2,1)}, f32[64,1024]{1,0:T(8,128)}) custom-call(s32[132]{0:T(256)} %pad_add_fusion.table, bf16[1024,256]{1,0:T(8,128)(2,1)} %get-tuple-element.70.m0, bf16[1024,256]{1,0:T(8,128)(2,1)} %copy-done.18, ...), custom_call_target="tpu_custom_call" | custom-call | flops 6979321856 | bytes 12582912 | tf_op jit(solution)/shard_map/mlp/pallas_call | solution.py:355
  198.1 1.5 collective-permute-start.16
  199.7 0.4 collective-permute-start.17
  200.2 1.1 reshape.704
  201.3 0.8 copy.55
  202.1 2.1 add_convert_fusion.3
  204.3 0.7 collective-permute-start.19
  205.1 7.3 %all-to-all-start.1 = ((f32[128,2,256]{2,1,0:T(2,128)}), f32[128,2,256]{2,1,0:T(2,128)S(1)}, u32[]{:S(2)}, u32[]{:S(2)}) async-start(f32[128,2,256]{2,1,0:T(2,128)} %bitcast.19), calls=%async_computation.1 | async-start | bytes 524288 | tf_op jit(solution)/shard_map/all_to_all | solution.py:396
  212.4 14.7 %mlp.3 = (f32[1024,256]{1,0:T(8,128)}, f32[1024,256]{1,0:T(8,128)}, bf16[1024,256]{1,0:T(8,128)(2,1)}, bf16[1024,256]{1,0:T(8,128)(2,1)}) custom-call(s32[132]{0:T(256)} %pad_add_fusion.table, bf16[1024,256]{1,0:T(8,128)(2,1)} %get-tuple-element.90.m0, bf16[1024,256]{1,0:T(8,128)(2,1)} %copy-done.17, bf16[1024,256]{1,0:T(8,128)(2,1)} %collective-permute-done.18.m2, ...), custom_call_target="tpu_custom_call" | custom-call | flops 6979321856 | bytes 12582912 | tf_op jit(solution)/shard_map/mlp/pallas_call | solution.py:355
  227.3 1.3 add_convert_fusion.2
  228.7 0.7 broadcast_in_dim.97
  229.4 9.8 %all-to-all-start.2 = ((bf16[128,2,256]{2,1,0:T(2,128)(2,1)}), bf16[128,2,256]{2,1,0:T(2,128)(2,1)S(1)}, u32[]{:S(2)}, u32[]{:S(2)}) async-start(bf16[128,2,256]{2,1,0:T(2,128)(2,1)} %broadcast_in_dim.97), calls=%async_computation.2 | async-start | bytes 262144 | tf_op jit(solution)/shard_map/all_to_all | solution.py:396
  239.2 1.1 collective-permute-start.21
  240.4 8.7 %all-to-all-done.2 = bf16[128,2,256]{2,1,0:T(2,128)(2,1)S(1)} async-done(((bf16[128,2,256]{2,1,0:T(2,128)(2,1)}), bf16[128,2,256]{2,1,0:T(2,128)(2,1)S(1)}, u32[]{:S(2)}, u32[]{:S(2)}) %all-to-all-start.2) | async-done | bytes 131104 | tf_op jit(solution)/shard_map/all_to_all | solution.py:396
  249.1 0.3 fusion.2
  249.8 2.0 add_convert_fusion.1
  251.7 0.6 collective-permute-start.22
  252.3 0.5 add_rsqrt_fusion
  253.0 0.3 fusion
  253.3 0.5 convolution_reduce_fusion
  253.8 13.9 %all_to_all.21 = f32[128,1,64]{2,1,0:T(1,128)S(1)} all-to-all(f32[128,1,64]{2,1,0:T(1,128)S(1)} %broadcast_in_dim.98), channel_id=1, replica_groups=mesh['req'=32,'tp'=4] {'req','tp'}, dimensions={0} | all-to-all | bytes 65536 | tf_op jit(solution)/shard_map/all_to_all | solution.py:396
  267.7 0.7 reduce_max.39
  268.4 1.4 add_convert_fusion
  269.8 1.0 pad_maximum_fusion
  (106 shorter events, 3.1 us)
Async XLA Ops:
  7.2 245.8 %copy-start = (f32[4,1024]{1,0:T(4,128)S(1)}, f32[4,1024]{1,0:T(4,128)}, u32[]{:S(2)}) copy-start(f32[4,1024]{1,0:T(4,128)} %param.29) | copy-start | bytes 49156
  7.2 173.2 %all-gather.2.cloned.1.call-start = ((), (), s32[]{:S(2)}) async-start(), calls=%async_computation.4 | async-start | bytes 4866048 | tf_op jit(solution)/shard_map/all_gather | solution.py:443
  10.6 4.0 %collective-permute-start = (bf16[8,2304]{1,0:T(8,128)(2,1)}, bf16[8,2304]{1,0:T(8,128)(2,1)S(1)}, u32[]{:S(2)}, u32[]{:S(2)}) collective-permute-start(bf16[8,2304]{1,0:T(8,128)(2,1)} %get-tuple-element.56), channel_id=1, source_target_pairs={{0,2},{1,3},{2,0},{3,1},{4,6},{5,7},{6,4},{7,5},{8,10},{9,11},{10,... | collective-permute-start | bytes 110600 | tf_op jit(solution)/shard_map/ppermute | solution.py:379
  13.0 2.0 collective-permute-start.1
  14.0 3.6 %collective-permute-start.2 = (bf16[8,2304]{1,0:T(8,128)(2,1)}, bf16[8,2304]{1,0:T(8,128)(2,1)S(1)}, u32[]{:S(2)}, u32[]{:S(2)}) collective-permute-start(bf16[8,2304]{1,0:T(8,128)(2,1)} %get-tuple-element.58), channel_id=1, source_target_pairs={{0,3},{1,2},{2,1},{3,0},{4,7},{5,6},{6,5},{7,4},{8,11},{9,10},{10,... | collective-permute-start | bytes 110600 | tf_op jit(solution)/shard_map/ppermute | solution.py:379
  19.1 9.7 %copy-start.1 = (s32[128]{0:T(128)S(1)}, s32[128]{0:T(128)}, u32[]{:S(2)}) copy-start(s32[128]{0:T(128)} %param.18) | copy-start | bytes 1540
  19.1 9.9 %copy-start.11 = (s32[64]{0:T(128)S(1)}, s32[64]{0:T(128)}, u32[]{:S(2)}) copy-start(s32[64]{0:T(128)} %param.16) | copy-start | bytes 772
  19.1 40.5 %all-to-all-start = ((bf16[128,8,1024]{2,1,0:T(8,128)(2,1)}), bf16[128,8,1024]{2,1,0:T(8,128)(2,1)S(1)}, u32[]{:S(2)}, u32[]{:S(2)}) async-start(bf16[128,8,1024]{2,1,0:T(8,128)(2,1)} %bitcast.71), calls=%async_computation | async-start | bytes 4194304 | tf_op jit(solution)/shard_map/all_to_all | solution.py:396
  30.2 7.3 %copy-start.8 = (s32[2048]{0:T(1024)}, s32[2048]{0:T(1024)S(1)}, u32[]{:S(2)}) copy-start(s32[2048]{0:T(1024)S(1)} %get-tuple-element.117) | copy-start | bytes 24580
  69.7 67.6 %collective-permute-start.3 = (bf16[8,2,256,256]{3,2,1,0:T(8,128)(2,1)}, bf16[8,2,256,256]{3,2,1,0:T(8,128)(2,1)}, u32[]{:S(2)}, u32[]{:S(2)}) collective-permute-start(bf16[8,2,256,256]{3,2,1,0:T(8,128)(2,1)} %get-tuple-element.65.kv), channel_id=1, source_target_pairs={{0,4},{4,8},{8,12},{12,16},{16,20},{20,24},{24,28},{28,32},{32,36}... | collective-permute-start | bytes 6291464 | tf_op jit(solution)/shard_map/ppermute | solution.py:392
  74.3 63.1 %collective-permute-start.4 = (bf16[8,2,256,256]{3,2,1,0:T(8,128)(2,1)}, bf16[8,2,256,256]{3,2,1,0:T(8,128)(2,1)}, u32[]{:S(2)}, u32[]{:S(2)}) collective-permute-start(bf16[8,2,256,256]{3,2,1,0:T(8,128)(2,1)} %get-tuple-element.65.kv), channel_id=1, source_target_pairs={{4,0},{8,4},{12,8},{16,12},{20,16},{24,20},{28,24},{32,28},{36,32}... | collective-permute-start | bytes 6291464 | tf_op jit(solution)/shard_map/ppermute | solution.py:392
  84.5 22.5 %copy-start.6 = (bf16[1024,256]{1,0:T(8,128)(2,1)}, bf16[1024,256]{1,0:T(8,128)(2,1)S(1)}, u32[]{:S(2)}) copy-start(bf16[1024,256]{1,0:T(8,128)(2,1)S(1)} %slice.29.o0) | copy-start | bytes 1572868
  84.5 52.2 %collective-permute-start.5 = (bf16[1024,256]{1,0:T(8,128)(2,1)S(1)}, bf16[1024,256]{1,0:T(8,128)(2,1)S(1)}, u32[]{:S(2)}, u32[]{:S(2)}) collective-permute-start(bf16[1024,256]{1,0:T(8,128)(2,1)S(1)} %slice.29.o0), channel_id=1, source_target_pairs={{0,2},{1,3},{2,0},{3,1},{4,6},{5,7},{6,4},{7,5},{8,10},{9,11},{10,... | collective-permute-start | bytes 1572872 | tf_op jit(solution)/shard_map/ppermute | solution.py:379
  84.8 51.9 %collective-permute-start.6 = (bf16[1024,256]{1,0:T(8,128)(2,1)S(1)}, bf16[1024,256]{1,0:T(8,128)(2,1)S(1)}, u32[]{:S(2)}, u32[]{:S(2)}) collective-permute-start(bf16[1024,256]{1,0:T(8,128)(2,1)S(1)} %slice.29.o0), channel_id=1, source_target_pairs={{0,1},{1,0},{2,3},{3,2},{4,5},{5,4},{6,7},{7,6},{8,9},{9,8},{10,11... | collective-permute-start | bytes 1572872 | tf_op jit(solution)/shard_map/ppermute | solution.py:379
  136.6 8.1 %copy-start.13 = (bf16[1024,256]{1,0:T(8,128)(2,1)}, bf16[1024,256]{1,0:T(8,128)(2,1)S(1)}, u32[]{:S(2)}) copy-start(bf16[1024,256]{1,0:T(8,128)(2,1)S(1)} %collective-permute-done.5.o1) | copy-start | bytes 1572868
  136.6 8.1 %copy-start.14 = (bf16[1024,256]{1,0:T(8,128)(2,1)}, bf16[1024,256]{1,0:T(8,128)(2,1)S(1)}, u32[]{:S(2)}) copy-start(bf16[1024,256]{1,0:T(8,128)(2,1)S(1)} %collective-permute-done.6.o2) | copy-start | bytes 1572868
  136.6 39.2 %collective-permute-start.10 = (bf16[1024,256]{1,0:T(8,128)(2,1)S(1)}, bf16[1024,256]{1,0:T(8,128)(2,1)S(1)}, u32[]{:S(2)}, u32[]{:S(2)}) collective-permute-start(bf16[1024,256]{1,0:T(8,128)(2,1)S(1)} %collective-permute-done.5.o1), channel_id=1, source_target_pairs={{0,1},{1,0},{2,3},{3,2},{4,5},{5,4},{6,7},{7,6},{8,9},{9,8},{10,11... | collective-permute-start | bytes 1572872 | tf_op jit(solution)/shard_map/ppermute | solution.py:379
  144.7 25.4 %copy-start.7 = (f32[64,256]{1,0:T(8,128)S(1)}, f32[64,256]{1,0:T(8,128)}, u32[]{:S(2)}) copy-start(f32[64,256]{1,0:T(8,128)} %get-tuple-element.76) | copy-start | bytes 196612
  144.7 30.5 %copy-start.10 = (s32[4]{0:T(128)S(1)}, s32[4]{0:T(128)}, u32[]{:S(2)}) copy-start(s32[4]{0:T(128)} %fusion.8.order) | copy-start | bytes 52
  144.7 24.9 %collective-permute-start.7 = (bf16[1024,256]{1,0:T(8,128)(2,1)}, bf16[1024,256]{1,0:T(8,128)(2,1)S(1)}, u32[]{:S(2)}, u32[]{:S(2)}) collective-permute-start(bf16[1024,256]{1,0:T(8,128)(2,1)} %get-tuple-element.70.m0), channel_id=1, source_target_pairs={{0,2},{1,3},{2,0},{3,1},{4,6},{5,7},{6,4},{7,5},{8,10},{9,11},{10,... | collective-permute-start | bytes 1572872 | tf_op jit(solution)/shard_map/ppermute | solution.py:379
  145.9 30.2 %collective-permute-start.8 = (bf16[1024,256]{1,0:T(8,128)(2,1)}, bf16[1024,256]{1,0:T(8,128)(2,1)S(1)}, u32[]{:S(2)}, u32[]{:S(2)}) collective-permute-start(bf16[1024,256]{1,0:T(8,128)(2,1)} %get-tuple-element.70.m0), channel_id=1, source_target_pairs={{0,1},{1,0},{2,3},{3,2},{4,5},{5,4},{6,7},{7,6},{8,9},{9,8},{10,11... | collective-permute-start | bytes 1572872 | tf_op jit(solution)/shard_map/ppermute | solution.py:379
  169.7 10.7 %copy-start.18 = (bf16[1024,256]{1,0:T(8,128)(2,1)}, bf16[1024,256]{1,0:T(8,128)(2,1)S(1)}, u32[]{:S(2)}) copy-start(bf16[1024,256]{1,0:T(8,128)(2,1)S(1)} %collective-permute-done.7.m1) | copy-start | bytes 1572868
  169.7 6.4 %collective-permute-start.9 = (bf16[1024,256]{1,0:T(8,128)(2,1)S(1)}, bf16[1024,256]{1,0:T(8,128)(2,1)}, u32[]{:S(2)}, u32[]{:S(2)}) collective-permute-start(bf16[1024,256]{1,0:T(8,128)(2,1)S(1)} %collective-permute-done.7.m1), channel_id=1, source_target_pairs={{0,1},{1,0},{2,3},{3,2},{4,5},{5,4},{6,7},{7,6},{8,9},{9,8},{10,11... | collective-permute-start | bytes 1572872 | tf_op jit(solution)/shard_map/ppermute | solution.py:379
  171.0 9.3 %copy-start.9 = (bf16[64,256]{1,0:T(8,128)(2,1)}, bf16[64,256]{1,0:T(8,128)(2,1)S(1)}, u32[]{:S(2)}) copy-start(bf16[64,256]{1,0:T(8,128)(2,1)S(1)} %add_convert_fusion.4.refs_0_) | copy-start | bytes 98308
  171.0 3.2 %collective-permute-start.11 = (bf16[64,256]{1,0:T(8,128)(2,1)S(1)}, bf16[64,256]{1,0:T(8,128)(2,1)S(1)}, u32[]{:S(2)}, u32[]{:S(2)}) collective-permute-start(bf16[64,256]{1,0:T(8,128)(2,1)S(1)} %add_convert_fusion.4.refs_0_), channel_id=1, source_target_pairs={{0,2},{1,3},{2,0},{3,1},{4,6},{5,7},{6,4},{7,5},{8,10},{9,11},{10,... | collective-permute-start | bytes 98312 | tf_op jit(solution)/shard_map/ppermute | solution.py:379
  172.4 3.5 %collective-permute-start.12 = (bf16[64,256]{1,0:T(8,128)(2,1)S(1)}, bf16[64,256]{1,0:T(8,128)(2,1)S(1)}, u32[]{:S(2)}, u32[]{:S(2)}) collective-permute-start(bf16[64,256]{1,0:T(8,128)(2,1)S(1)} %add_convert_fusion.4.refs_0_), channel_id=1, source_target_pairs={{0,1},{1,0},{2,3},{3,2},{4,5},{5,4},{6,7},{7,6},{8,9},{9,8},{10,11... | collective-permute-start | bytes 98312 | tf_op jit(solution)/shard_map/ppermute | solution.py:379
  174.3 6.1 %copy-start.21 = (bf16[64,256]{1,0:T(8,128)(2,1)}, bf16[64,256]{1,0:T(8,128)(2,1)S(1)}, u32[]{:S(2)}) copy-start(bf16[64,256]{1,0:T(8,128)(2,1)S(1)} %collective-permute-done.11.refs_1_) | copy-start | bytes 98308
  174.3 1.8 collective-permute-start.13
  175.8 4.5 %copy-start.15 = (bf16[1024,256]{1,0:T(8,128)(2,1)}, bf16[1024,256]{1,0:T(8,128)(2,1)S(1)}, u32[]{:S(2)}) copy-start(bf16[1024,256]{1,0:T(8,128)(2,1)S(1)} %collective-permute-done.10.o3) | copy-start | bytes 1572868
  175.8 22.3 %collective-permute-start.14 = (bf16[1024,256]{1,0:T(8,128)(2,1)}, bf16[1024,256]{1,0:T(8,128)(2,1)S(1)}, u32[]{:S(2)}, u32[]{:S(2)}) collective-permute-start(bf16[1024,256]{1,0:T(8,128)(2,1)} %get-tuple-element.90.m0), channel_id=1, source_target_pairs={{0,2},{1,3},{2,0},{3,1},{4,6},{5,7},{6,4},{7,5},{8,10},{9,11},{10,... | collective-permute-start | bytes 1572872 | tf_op jit(solution)/shard_map/ppermute | solution.py:379
  175.9 4.5 %copy-start.22 = (bf16[64,256]{1,0:T(8,128)(2,1)}, bf16[64,256]{1,0:T(8,128)(2,1)S(1)}, u32[]{:S(2)}) copy-start(bf16[64,256]{1,0:T(8,128)(2,1)S(1)} %collective-permute-done.12.refs_2_) | copy-start | bytes 98308
  176.0 4.3 %copy-start.23 = (bf16[64,256]{1,0:T(8,128)(2,1)}, bf16[64,256]{1,0:T(8,128)(2,1)S(1)}, u32[]{:S(2)}) copy-start(bf16[64,256]{1,0:T(8,128)(2,1)S(1)} %collective-permute-done.13.refs_3_) | copy-start | bytes 98308
  176.0 4.3 %copy-start.19 = (bf16[1024,256]{1,0:T(8,128)(2,1)}, bf16[1024,256]{1,0:T(8,128)(2,1)S(1)}, u32[]{:S(2)}) copy-start(bf16[1024,256]{1,0:T(8,128)(2,1)S(1)} %collective-permute-done.8.m2) | copy-start | bytes 1572868
  180.4 19.7 %copy-start.16 = (bf16[1024,256]{1,0:T(8,128)(2,1)S(1)}, bf16[1024,256]{1,0:T(8,128)(2,1)}, u32[]{:S(2)}) copy-start(bf16[1024,256]{1,0:T(8,128)(2,1)} %get-tuple-element.90.m0) | copy-start | bytes 1572868
  198.1 6.8 %copy-start.17 = (bf16[1024,256]{1,0:T(8,128)(2,1)}, bf16[1024,256]{1,0:T(8,128)(2,1)S(1)}, u32[]{:S(2)}) copy-start(bf16[1024,256]{1,0:T(8,128)(2,1)S(1)} %collective-permute-done.14.m1) | copy-start | bytes 1572868
  198.1 4.0 %collective-permute-start.16 = (bf16[1024,256]{1,0:T(8,128)(2,1)}, bf16[1024,256]{1,0:T(8,128)(2,1)S(1)}, u32[]{:S(2)}, u32[]{:S(2)}) collective-permute-start(bf16[1024,256]{1,0:T(8,128)(2,1)} %get-tuple-element.86), channel_id=1, source_target_pairs={{0,1},{1,0},{2,3},{3,2},{4,5},{5,4},{6,7},{7,6},{8,9},{9,8},{10,11... | collective-permute-start | bytes 1572872 | tf_op jit(solution)/shard_map/ppermute | solution.py:379
  199.6 4.7 %collective-permute-start.15 = (bf16[1024,256]{1,0:T(8,128)(2,1)}, bf16[1024,256]{1,0:T(8,128)(2,1)S(1)}, u32[]{:S(2)}, u32[]{:S(2)}) collective-permute-start(bf16[1024,256]{1,0:T(8,128)(2,1)} %get-tuple-element.84), channel_id=1, source_target_pairs={{0,1},{1,0},{2,3},{3,2},{4,5},{5,4},{6,7},{7,6},{8,9},{9,8},{10,11... | collective-permute-start | bytes 1572872 | tf_op jit(solution)/shard_map/ppermute | solution.py:379
  199.7 4.6 %collective-permute-start.17 = (bf16[1024,256]{1,0:T(8,128)(2,1)S(1)}, bf16[1024,256]{1,0:T(8,128)(2,1)S(1)}, u32[]{:S(2)}, u32[]{:S(2)}) collective-permute-start(bf16[1024,256]{1,0:T(8,128)(2,1)S(1)} %collective-permute-done.14.m1), channel_id=1, source_target_pairs={{0,1},{1,0},{2,3},{3,2},{4,5},{5,4},{6,7},{7,6},{8,9},{9,8},{10,11... | collective-permute-start | bytes 1572872 | tf_op jit(solution)/shard_map/ppermute | solution.py:379
  200.1 12.3 %collective-permute-start.18 = (bf16[1024,256]{1,0:T(8,128)(2,1)S(1)}, bf16[1024,256]{1,0:T(8,128)(2,1)}, u32[]{:S(2)}, u32[]{:S(2)}) collective-permute-start(bf16[1024,256]{1,0:T(8,128)(2,1)S(1)} %copy-done.16), channel_id=1, source_target_pairs={{0,1},{1,0},{2,3},{3,2},{4,5},{5,4},{6,7},{7,6},{8,9},{9,8},{10,11... | collective-permute-start | bytes 1572872 | tf_op jit(solution)/shard_map/ppermute | solution.py:379
  204.2 0.8 copy-start.20
  204.3 23.0 %collective-permute-start.19 = (bf16[1024,256]{1,0:T(8,128)(2,1)}, bf16[1024,256]{1,0:T(8,128)(2,1)}, u32[]{:S(2)}, u32[]{:S(2)}) collective-permute-start(bf16[1024,256]{1,0:T(8,128)(2,1)} %add_convert_fusion.3), channel_id=1, source_target_pairs={{0,2},{1,3},{2,0},{3,1},{4,6},{5,7},{6,4},{7,5},{8,10},{9,11},{10,... | collective-permute-start | bytes 1572872 | tf_op jit(solution)/shard_map/ppermute | solution.py:379
  205.1 22.1 %all-to-all-start.1 = ((f32[128,2,256]{2,1,0:T(2,128)}), f32[128,2,256]{2,1,0:T(2,128)S(1)}, u32[]{:S(2)}, u32[]{:S(2)}) async-start(f32[128,2,256]{2,1,0:T(2,128)} %bitcast.19), calls=%async_computation.1 | async-start | bytes 524288 | tf_op jit(solution)/shard_map/all_to_all | solution.py:396
  212.4 14.9 %copy-start.4 = (f32[1024,256]{1,0:T(8,128)S(1)}, f32[1024,256]{1,0:T(8,128)}, u32[]{:S(2)}) copy-start(f32[1024,256]{1,0:T(8,128)} %get-tuple-element.96) | copy-start | bytes 3145732
  227.1 22.6 %copy-start.5 = (f32[1024,256]{1,0:T(8,128)S(1)}, f32[1024,256]{1,0:T(8,128)}, u32[]{:S(2)}) copy-start(f32[1024,256]{1,0:T(8,128)} %get-tuple-element.102) | copy-start | bytes 3145732
  228.6 24.3 %copy-start.12 = (s32[64]{0:T(128)S(1)}, s32[64]{0:T(128)}, u32[]{:S(2)}) copy-start(s32[64]{0:T(128)} %param.17) | copy-start | bytes 772
  229.4 19.7 %all-to-all-start.2 = ((bf16[128,2,256]{2,1,0:T(2,128)(2,1)}), bf16[128,2,256]{2,1,0:T(2,128)(2,1)S(1)}, u32[]{:S(2)}, u32[]{:S(2)}) async-start(bf16[128,2,256]{2,1,0:T(2,128)(2,1)} %broadcast_in_dim.97), calls=%async_computation.2 | async-start | bytes 262144 | tf_op jit(solution)/shard_map/all_to_all | solution.py:396
  239.2 10.6 %collective-permute-start.21 = (bf16[1024,256]{1,0:T(8,128)(2,1)}, bf16[1024,256]{1,0:T(8,128)(2,1)}, u32[]{:S(2)}, u32[]{:S(2)}) collective-permute-start(bf16[1024,256]{1,0:T(8,128)(2,1)} %get-tuple-element.103), channel_id=1, source_target_pairs={{0,1},{1,0},{2,3},{3,2},{4,5},{5,4},{6,7},{7,6},{8,9},{9,8},{10,11... | collective-permute-start | bytes 1572872 | tf_op jit(solution)/shard_map/ppermute | solution.py:379
  240.3 28.1 %collective-permute-start.20 = (bf16[1024,256]{1,0:T(8,128)(2,1)}, bf16[1024,256]{1,0:T(8,128)(2,1)}, u32[]{:S(2)}, u32[]{:S(2)}) collective-permute-start(bf16[1024,256]{1,0:T(8,128)(2,1)} %get-tuple-element.101), channel_id=1, source_target_pairs={{0,1},{1,0},{2,3},{3,2},{4,5},{5,4},{6,7},{7,6},{8,9},{9,8},{10,11... | collective-permute-start | bytes 1572872 | tf_op jit(solution)/shard_map/ppermute | solution.py:379
  249.1 4.2 %copy-start.2 = (f32[384,1024]{1,0:T(8,128)S(1)}, f32[384,1024]{1,0:T(8,128)}, u32[]{:S(2)}) copy-start(f32[384,1024]{1,0:T(8,128)} %param.26) | copy-start | bytes 4718596
  251.7 16.7 %copy-start.3 = (f32[1024,256]{1,0:T(8,128)S(1)}, f32[1024,256]{1,0:T(8,128)}, u32[]{:S(2)}) copy-start(f32[1024,256]{1,0:T(8,128)} %get-tuple-element.100) | copy-start | bytes 3145732
  251.7 16.7 %collective-permute-start.22 = (bf16[1024,256]{1,0:T(8,128)(2,1)}, bf16[1024,256]{1,0:T(8,128)(2,1)}, u32[]{:S(2)}, u32[]{:S(2)}) collective-permute-start(bf16[1024,256]{1,0:T(8,128)(2,1)} %add_convert_fusion.1), channel_id=1, source_target_pairs={{0,2},{1,3},{2,0},{3,1},{4,6},{5,7},{6,4},{7,5},{8,10},{9,11},{10,... | collective-permute-start | bytes 1572872 | tf_op jit(solution)/shard_map/ppermute | solution.py:379
Sparse Core Ops, SparseCore 0:
  19.2 161.1 all-gather.1

commit v12 on v9

--- a/solution.py
+++ b/solution.py
@@ -340,10 +340,11 @@
 
 
 def mlp(table, mixed, out_w, h, base, gain, weights, lasts=()):
-    n = 256
+    n = 256 if lasts else 512
     rows = mixed[0].shape[0]
     count = weights.shape[0]
     extra = 1 if lasts else 0
+    base = base // n
 
     def block(width, base=0):
         return pl.BlockSpec((n, width), lambda i, *_: (jnp.maximum(i - extra, 0) + base, 0))
@@ -495,11 +496,11 @@
     lasts = (last_mixed, last_far, swap(last_mixed, 1), swap(last_far, 1), last_in)
 
     order = jnp.concatenate([near_first, rest_target])
-    steps = slots // parts // 256
+    part_rows = slots // parts
 
     def feed(part, pieces, *lasts):
         return mlp(
-            order, pieces, out_w, hidden_in, part * steps, mlp_gain, rest, *lasts
+            order, pieces, out_w, hidden_in, part * part_rows, mlp_gain, rest, *lasts
         )
 
     far = [swap(m, 2) for m in mixed]

time: 278 us -> 276 us (level)
  Pallas kernels: 94.5 us -> 90.7 us
  transfers between devices with their start and end apart: 24 -> 24, of which waited for: 8 -> 8; matrix products, arithmetic and copies ran while one was open for 10% -> 10% of each run, Pallas kernels for 33% -> 32%
where the time goes in v12:
time: 276 us; the launch traced here: 275 us
  Pallas kernels  90.7 us (33%)
  waiting for transfers between devices  61.3 us (22%)
  starting transfers between devices  39.5 us (14%)
  blocking collectives  32.7 us (12%)
  other arithmetic  20.3 us (7%)
  local copies, waits for them, and re-layouts  15.6 us (6%)
  between operations  14.6 us (5%)
    ppermute x19, waiting for transfers between devices, swap(): return lax.ppermute(x, 'tp', [(i, i ^ bit) for i in range(4)])  45 us
    pallas_call x3, Pallas kernels, attend(): pl.pallas_call(kernel, grid_spec=pltpu.PrefetchScalarGridSpec(num_scalar_...  42.8 us
    all_to_all x2, blocking collectives, exchange(): return lax.all_to_all(x, axes, split_axis=0, concat_axis=0, tiled=True)  32.7 us
    pallas_call x2, Pallas kernels, mlp(): pl.pallas_call(functools.partial(mlp_kernel, extra), grid_spec=pltpu.Pref...  30.9 us
    all_to_all x2, starting transfers between devices, exchange(): return lax.all_to_all(x, axes, split_axis=0, concat_axis=0, tiled=True)  20.3 us
    all_to_all x2, waiting for transfers between devices, exchange(): return lax.all_to_all(x, axes, split_axis=0, concat_axis=0, tiled=True)  15.8 us
    ppermute x19, starting transfers between devices, swap(): return lax.ppermute(x, 'tp', [(i, i ^ bit) for i in range(4)])  13.3 us
    pallas_call x1, Pallas kernels, qkv_project(): pl.pallas_call(qkv_kernel, grid=(rows // n,), in_specs=[pl.BlockSpec((n,...  8.16 us
  transfers between devices with their start and end apart: 24, of which 8 were waited for; matrix products, arithmetic and copies ran while one was open for 10% of the time, Pallas kernels for 32%

profile of v12, /device:TPU:1, one launch (start us, length us, event | category | flops | bytes accessed | tf_op | source)
XLA Modules:
  0.0 275.4 jit_solution(10403313831541224545)
XLA Ops:
  7.2 0.5 fusion.11.order
  7.7 2.8 %prep.1 = (bf16[32,4,8,1024]{3,2,1,0:T(8,128)(2,1)}, bf16[8,2304]{1,0:T(8,128)(2,1)}, bf16[8,2304]{1,0:T(8,128)(2,1)}, bf16[8,2304]{1,0:T(8,128)(2,1)}, bf16[8,2304]{1,0:T(8,128)(2,1)}) custom-call(s32[4]{0:T(128)} %fusion.11.order, f32[8,1024]{1,0:T(8,128)} %wq.1, f32[8,1024]{1,0:T(8,128)} %wk.1, f32[8,1024]{1,0:T(8,128)} %wv.1, f32[8,1024]{1,0:T(8,128)} %wo.1, ...), custom_call_target="tpu_custom_call" | custom-call | tf_op jit(solution)/shard_map/prep/pallas_call | solution.py:64
  10.6 2.5 collective-permute-start
  13.0 1.0 collective-permute-start.1
  14.0 0.6 collective-permute-done
  14.6 0.5 collective-permute-done.1
  15.1 2.5 collective-permute-done.2
  17.6 1.4 pad_maximum_fusion.1
  19.1 9.7 %all-to-all-start = ((bf16[128,8,1024]{2,1,0:T(8,128)(2,1)}), bf16[128,8,1024]{2,1,0:T(8,128)(2,1)S(1)}, u32[]{:S(2)}, u32[]{:S(2)}) async-start(bf16[128,8,1024]{2,1,0:T(8,128)(2,1)} %bitcast.71), calls=%async_computation | async-start | bytes 4194304 | tf_op jit(solution)/shard_map/all_to_all | solution.py:403
  28.8 1.2 gather_fusion
  30.1 0.7 pad_add_fusion.table
  31.1 6.0 %norm.1.x = bf16[2048,1024]{1,0:T(8,128)(2,1)} custom-call(bf16[2048,1024]{1,0:T(8,128)(2,1)} %h.4, f32[1,1024]{1,0:T(1,128)} %bitcast.81), custom_call_target="tpu_custom_call" | custom-call | flops 16777216 | bytes 8388608 | tf_op jit(solution)/shard_map/norm/pallas_call | solution.py:88
  37.1 0.7 fusion.7
  38.2 5.5 %multiply_sine_fusion = (f32[2048,128]{1,0:T(8,128)}, f32[2048,128]{1,0:T(8,128)}) fusion(f32[128]{0:T(128)S(1)} %fusion.20, f32[2048]{0:T(1024)S(1)} %subtract_convert_fusion), kind=kLoop, calls=%fused_computation.4 | loop fusion | flops 262144 | bytes 2105856 | tf_op jit(solution)/shard_map/sin | solution.py:457
  43.8 15.8 %all-to-all-done = bf16[128,8,1024]{2,1,0:T(8,128)(2,1)S(1)} async-done(((bf16[128,8,1024]{2,1,0:T(8,128)(2,1)}), bf16[128,8,1024]{2,1,0:T(8,128)(2,1)S(1)}, u32[]{:S(2)}, u32[]{:S(2)}) %all-to-all-start) | async-done | bytes 2097184 | tf_op jit(solution)/shard_map/all_to_all | solution.py:403
  59.6 2.0 gather_fusion.1
  61.6 8.2 %qkv.1 = (bf16[2048,256]{1,0:T(8,128)(2,1)}, bf16[8,2,256,256]{3,2,1,0:T(8,128)(2,1)}, bf16[2,2048,256]{2,1,0:T(8,128)(2,1)}) custom-call(bf16[2048,1024]{1,0:T(8,128)(2,1)} %norm.1.x, bf16[1024,1024]{1,0:T(8,128)(2,1)} %bitcast.69, f32[2048,128]{1,0:T(8,128)} %get-tuple-element.101.cos, f32[2048,128]{1,0:T(8,128)} %get-tuple-element.100.sin), custom_call_target="tpu_custom_call" | custom-call | flops 3221225472 | bytes 12582912 | tf_op jit(solution)/shard_map/qkv/pallas_call | solution.py:127
  69.7 4.6 %collective-permute-start.3 = (bf16[8,2,256,256]{3,2,1,0:T(8,128)(2,1)}, bf16[8,2,256,256]{3,2,1,0:T(8,128)(2,1)}, u32[]{:S(2)}, u32[]{:S(2)}) collective-permute-start(bf16[8,2,256,256]{3,2,1,0:T(8,128)(2,1)} %get-tuple-element.55.kv), channel_id=1, source_target_pairs={{0,4},{4,8},{8,12},{12,16},{16,20},{20,24},{24,28},{28,32},{32,36}... | collective-permute-start | bytes 6291464 | tf_op jit(solution)/shard_map/ppermute | solution.py:399
  74.3 1.3 collective-permute-start.4
  75.7 1.4 copy.44.kseg
  77.1 1.3 copy.45.lseg
  78.4 1.4 copy.46.rseg
  80.0 0.6 stack.2.table
  80.6 1.1 slice.61.o0
  82.0 0.6 collective-permute-start.6
  82.6 20.9 %attend_own.1 = (f32[4,72,2048]{2,1,0:T(8,128)}, f32[4,1,2048]{2,1,0:T(1,128)}) custom-call(s32[6,8]{1,0:T(8,128)} %stack.2.table, bf16[2048,256]{1,0:T(8,128)(2,1)} %get-tuple-element.52.q, s32[1,2048]{1,0:T(1,128)} %bitcast.76, bf16[8,2,256,256]{3,2,1,0:T(8,128)(2,1)} %get-tuple-element.55.kv, s32[2048,1]{1,0:T(8,128)} %copy.44.kseg), custom_call_target="tpu_custom_call" | custom-call | flops 12884901888 | bytes 8388608 | tf_op jit(solution)/shard_map/attend_own/pallas_call | solution.py:249
  103.5 32.0 %collective-permute-done.5.o1 = bf16[1024,256]{1,0:T(8,128)(2,1)S(1)} collective-permute-done((bf16[1024,256]{1,0:T(8,128)(2,1)S(1)}, bf16[1024,256]{1,0:T(8,128)(2,1)S(1)}, u32[]{:S(2)}, u32[]{:S(2)}) %collective-permute-start.5) | collective-permute-done | bytes 524320 | tf_op jit(solution)/shard_map/ppermute | solution.py:385
  135.5 0.8 collective-permute-start.10
  136.3 6.9 %attend_halo.2 = (bf16[1024,256]{1,0:T(8,128)(2,1)}, f32[64,256]{1,0:T(8,128)}) custom-call(s32[6,8]{1,0:T(8,128)} %stack.2.table, bf16[2048,256]{1,0:T(8,128)(2,1)} %get-tuple-element.52.q, s32[1,2048]{1,0:T(1,128)} %bitcast.77, bf16[8,2,256,256]{3,2,1,0:T(8,128)(2,1)} %collective-permute-done.3.lkv, s32[2048,1]{1,0:T(8,128)} %copy.45.lseg, ...), custom_call_target="tpu_custom_call" | custom-call | flops 12884901888 | bytes 8388608 | tf_op jit(solution)/shard_map/attend_halo/pallas_call | solution.py:249
  143.2 1.1 collective-permute-start.7
  144.3 0.3 collective-permute-start.8
  144.6 15.0 %attend_halo.3 = (bf16[1024,256]{1,0:T(8,128)(2,1)}, f32[64,256]{1,0:T(8,128)}) custom-call(s32[6,8]{1,0:T(8,128)} %stack.2.table, bf16[2048,256]{1,0:T(8,128)(2,1)} %get-tuple-element.52.q, s32[1,2048]{1,0:T(1,128)} %bitcast.78, bf16[8,2,256,256]{3,2,1,0:T(8,128)(2,1)} %collective-permute-done.3.lkv, s32[2048,1]{1,0:T(8,128)} %copy.45.lseg, ...), custom_call_target="tpu_custom_call" | custom-call | flops 12884901888 | bytes 8388608 | tf_op jit(solution)/shard_map/attend_halo/pallas_call | solution.py:249
  159.6 8.9 %collective-permute-done.7.m1 = bf16[1024,256]{1,0:T(8,128)(2,1)S(1)} collective-permute-done((bf16[1024,256]{1,0:T(8,128)(2,1)}, bf16[1024,256]{1,0:T(8,128)(2,1)S(1)}, u32[]{:S(2)}, u32[]{:S(2)}) %collective-permute-start.7) | collective-permute-done | bytes 524320 | tf_op jit(solution)/shard_map/ppermute | solution.py:385
  168.5 0.8 collective-permute-start.9
  169.3 0.8 add_convert_fusion.1.refs_0_
  170.2 0.8 collective-permute-start.11
  171.0 3.6 %gather_fusion.2 = bf16[64,1024]{1,0:T(8,128)(2,1)S(1)} fusion(bf16[2048,1024]{1,0:T(8,128)(2,1)} %h.4, s32[1024]{0:T(1024)S(1)} %pad_clamp_fusion), kind=kCustom, calls=%fused_computation.2 | custom fusion | bytes 262400 | tf_op jit(solution)/shard_map/gather | solution.py:493
  174.5 0.4 collective-permute-start.12
  175.1 0.8 broadcast_select_fusion.refs_4_
  175.9 0.7 collective-permute-start.14
  176.7 0.4 all-gather.2.cloned.1.call-done
  177.5 17.5 %mlp.2 = (f32[1024,512]{1,0:T(8,128)}, bf16[1024,512]{1,0:T(8,128)(2,1)}, f32[64,1024]{1,0:T(8,128)}) custom-call(s32[132]{0:T(256)} %pad_add_fusion.table, bf16[1024,256]{1,0:T(8,128)(2,1)} %get-tuple-element.60.m0, bf16[1024,256]{1,0:T(8,128)(2,1)} %copy-done.14, bf16[1024,256]{1,0:T(8,128)(2,1)} %copy-done.15, ...), custom_call_target="tpu_custom_call" | custom-call | flops 6979321856 | bytes 12582912 | tf_op jit(solution)/shard_map/mlp/pallas_call | solution.py:361
  195.0 0.8 collective-permute-start.15
  195.9 0.4 collective-permute-start.17
  196.3 1.2 reshape.565
  197.5 0.8 copy.55
  198.3 0.5 collective-permute-done.15
  199.1 1.1 fusion.4
  200.2 0.7 collective-permute-start.18
  200.9 10.7 %all-to-all-start.1 = ((f32[128,2,256]{2,1,0:T(2,128)}), f32[128,2,256]{2,1,0:T(2,128)S(1)}, u32[]{:S(2)}, u32[]{:S(2)}) async-start(f32[128,2,256]{2,1,0:T(2,128)} %bitcast.19), calls=%async_computation.1 | async-start | bytes 524288 | tf_op jit(solution)/shard_map/all_to_all | solution.py:403
  211.6 13.4 %mlp.3 = (f32[1024,512]{1,0:T(8,128)}, bf16[1024,512]{1,0:T(8,128)(2,1)}) custom-call(s32[132]{0:T(256)} %pad_add_fusion.table, bf16[1024,256]{1,0:T(8,128)(2,1)} %get-tuple-element.75.m0, bf16[1024,256]{1,0:T(8,128)(2,1)} %collective-permute-done.14.m1, bf16[1024,256]{1,0:T(8,128)(2,1)} %collective-permute-done.17.m2, ...), custom_call_target="tpu_custom_call" | custom-call | flops 6979321856 | bytes 12582912 | tf_op jit(solution)/shard_map/mlp/pallas_call | solution.py:361
  225.3 1.4 collective-permute-start.19
  226.8 18.6 %all_to_all.21 = bf16[128,2,256]{2,1,0:T(2,128)(2,1)S(1)} all-to-all(bf16[128,2,256]{2,1,0:T(2,128)(2,1)S(1)} %broadcast_in_dim.97), channel_id=1, replica_groups=mesh['req'=32,'tp'=4] {'req','tp'}, dimensions={0} | all-to-all | bytes 262144 | tf_op jit(solution)/shard_map/all_to_all | solution.py:403
  245.3 0.3 fusion.6
  245.9 1.5 convert_element_type.82
  247.5 1.5 fusion.1
  249.0 0.6 collective-permute-start.20
  249.6 0.5 add_rsqrt_fusion
  250.3 0.3 fusion
  250.6 0.5 convolution_reduce_fusion
  251.1 14.1 %all_to_all.22 = f32[128,1,64]{2,1,0:T(1,128)S(1)} all-to-all(f32[128,1,64]{2,1,0:T(1,128)S(1)} %broadcast_in_dim.98), channel_id=1, replica_groups=mesh['req'=32,'tp'=4] {'req','tp'}, dimensions={0} | all-to-all | bytes 65536 | tf_op jit(solution)/shard_map/all_to_all | solution.py:403
  265.2 0.7 reduce_max.39
  265.9 1.6 fusion.3
  267.5 1.0 pad_maximum_fusion
  (93 shorter events, 3.2 us)
Async XLA Ops:
  7.2 243.1 %copy-start = (f32[4,1024]{1,0:T(4,128)S(1)}, f32[4,1024]{1,0:T(4,128)}, u32[]{:S(2)}) copy-start(f32[4,1024]{1,0:T(4,128)} %param.29) | copy-start | bytes 49156
  7.2 169.9 %all-gather.2.cloned.1.call-start = ((), (), s32[]{:S(2)}) async-start(), calls=%async_computation.4 | async-start | bytes 4866048 | tf_op jit(solution)/shard_map/all_gather | solution.py:442
  10.6 4.0 %collective-permute-start = (bf16[8,2304]{1,0:T(8,128)(2,1)}, bf16[8,2304]{1,0:T(8,128)(2,1)S(1)}, u32[]{:S(2)}, u32[]{:S(2)}) collective-permute-start(bf16[8,2304]{1,0:T(8,128)(2,1)} %get-tuple-element.46), channel_id=1, source_target_pairs={{0,2},{1,3},{2,0},{3,1},{4,6},{5,7},{6,4},{7,5},{8,10},{9,11},{10,... | collective-permute-start | bytes 110600 | tf_op jit(solution)/shard_map/ppermute | solution.py:385
  13.0 2.0 collective-permute-start.1
  14.0 3.6 %collective-permute-start.2 = (bf16[8,2304]{1,0:T(8,128)(2,1)}, bf16[8,2304]{1,0:T(8,128)(2,1)S(1)}, u32[]{:S(2)}, u32[]{:S(2)}) collective-permute-start(bf16[8,2304]{1,0:T(8,128)(2,1)} %get-tuple-element.48), channel_id=1, source_target_pairs={{0,3},{1,2},{2,1},{3,0},{4,7},{5,6},{6,5},{7,4},{8,11},{9,10},{10,... | collective-permute-start | bytes 110600 | tf_op jit(solution)/shard_map/ppermute | solution.py:385
  19.0 9.7 %copy-start.1 = (s32[128]{0:T(128)S(1)}, s32[128]{0:T(128)}, u32[]{:S(2)}) copy-start(s32[128]{0:T(128)} %param.18) | copy-start | bytes 1540
  19.1 11.0 %copy-start.8 = (s32[4]{0:T(128)S(1)}, s32[4]{0:T(128)}, u32[]{:S(2)}) copy-start(s32[4]{0:T(128)} %fusion.11.order) | copy-start | bytes 52
  19.1 11.8 %copy-start.9 = (s32[64]{0:T(128)S(1)}, s32[64]{0:T(128)}, u32[]{:S(2)}) copy-start(s32[64]{0:T(128)} %param.16) | copy-start | bytes 772
  19.1 40.5 %all-to-all-start = ((bf16[128,8,1024]{2,1,0:T(8,128)(2,1)}), bf16[128,8,1024]{2,1,0:T(8,128)(2,1)S(1)}, u32[]{:S(2)}, u32[]{:S(2)}) async-start(bf16[128,8,1024]{2,1,0:T(8,128)(2,1)} %bitcast.71), calls=%async_computation | async-start | bytes 4194304 | tf_op jit(solution)/shard_map/all_to_all | solution.py:403
  69.7 66.5 %collective-permute-start.3 = (bf16[8,2,256,256]{3,2,1,0:T(8,128)(2,1)}, bf16[8,2,256,256]{3,2,1,0:T(8,128)(2,1)}, u32[]{:S(2)}, u32[]{:S(2)}) collective-permute-start(bf16[8,2,256,256]{3,2,1,0:T(8,128)(2,1)} %get-tuple-element.55.kv), channel_id=1, source_target_pairs={{0,4},{4,8},{8,12},{12,16},{16,20},{20,24},{24,28},{28,32},{32,36}... | collective-permute-start | bytes 6291464 | tf_op jit(solution)/shard_map/ppermute | solution.py:399
  74.3 61.9 %collective-permute-start.4 = (bf16[8,2,256,256]{3,2,1,0:T(8,128)(2,1)}, bf16[8,2,256,256]{3,2,1,0:T(8,128)(2,1)}, u32[]{:S(2)}, u32[]{:S(2)}) collective-permute-start(bf16[8,2,256,256]{3,2,1,0:T(8,128)(2,1)} %get-tuple-element.55.kv), channel_id=1, source_target_pairs={{4,0},{8,4},{12,8},{16,12},{20,16},{24,20},{28,24},{32,28},{36,32}... | collective-permute-start | bytes 6291464 | tf_op jit(solution)/shard_map/ppermute | solution.py:399
  75.7 6.1 %copy-start.6 = (s32[2048]{0:T(1024)}, s32[2048]{0:T(1024)S(1)}, u32[]{:S(2)}) copy-start(s32[2048]{0:T(1024)S(1)} %get-tuple-element.99) | copy-start | bytes 24580
  81.7 21.8 %copy-start.4 = (bf16[1024,256]{1,0:T(8,128)(2,1)}, bf16[1024,256]{1,0:T(8,128)(2,1)S(1)}, u32[]{:S(2)}) copy-start(bf16[1024,256]{1,0:T(8,128)(2,1)S(1)} %slice.61.o0) | copy-start | bytes 1572868
  81.7 53.7 %collective-permute-start.5 = (bf16[1024,256]{1,0:T(8,128)(2,1)S(1)}, bf16[1024,256]{1,0:T(8,128)(2,1)S(1)}, u32[]{:S(2)}, u32[]{:S(2)}) collective-permute-start(bf16[1024,256]{1,0:T(8,128)(2,1)S(1)} %slice.61.o0), channel_id=1, source_target_pairs={{0,2},{1,3},{2,0},{3,1},{4,6},{5,7},{6,4},{7,5},{8,10},{9,11},{10,... | collective-permute-start | bytes 1572872 | tf_op jit(solution)/shard_map/ppermute | solution.py:385
  82.0 53.5 %collective-permute-start.6 = (bf16[1024,256]{1,0:T(8,128)(2,1)S(1)}, bf16[1024,256]{1,0:T(8,128)(2,1)S(1)}, u32[]{:S(2)}, u32[]{:S(2)}) collective-permute-start(bf16[1024,256]{1,0:T(8,128)(2,1)S(1)} %slice.61.o0), channel_id=1, source_target_pairs={{0,1},{1,0},{2,3},{3,2},{4,5},{5,4},{6,7},{7,6},{8,9},{9,8},{10,11... | collective-permute-start | bytes 1572872 | tf_op jit(solution)/shard_map/ppermute | solution.py:385
  135.5 7.7 %copy-start.11 = (bf16[1024,256]{1,0:T(8,128)(2,1)}, bf16[1024,256]{1,0:T(8,128)(2,1)S(1)}, u32[]{:S(2)}) copy-start(bf16[1024,256]{1,0:T(8,128)(2,1)S(1)} %collective-permute-done.5.o1) | copy-start | bytes 1572868
  135.5 7.7 %copy-start.12 = (bf16[1024,256]{1,0:T(8,128)(2,1)}, bf16[1024,256]{1,0:T(8,128)(2,1)S(1)}, u32[]{:S(2)}) copy-start(bf16[1024,256]{1,0:T(8,128)(2,1)S(1)} %collective-permute-done.6.o2) | copy-start | bytes 1572868
  135.5 40.4 %collective-permute-start.10 = (bf16[1024,256]{1,0:T(8,128)(2,1)S(1)}, bf16[1024,256]{1,0:T(8,128)(2,1)S(1)}, u32[]{:S(2)}, u32[]{:S(2)}) collective-permute-start(bf16[1024,256]{1,0:T(8,128)(2,1)S(1)} %collective-permute-done.5.o1), channel_id=1, source_target_pairs={{0,1},{1,0},{2,3},{3,2},{4,5},{5,4},{6,7},{7,6},{8,9},{9,8},{10,11... | collective-permute-start | bytes 1572872 | tf_op jit(solution)/shard_map/ppermute | solution.py:385
  143.2 26.1 %copy-start.5 = (f32[64,256]{1,0:T(8,128)S(1)}, f32[64,256]{1,0:T(8,128)}, u32[]{:S(2)}) copy-start(f32[64,256]{1,0:T(8,128)} %get-tuple-element.66) | copy-start | bytes 196612
  143.2 25.3 %collective-permute-start.7 = (bf16[1024,256]{1,0:T(8,128)(2,1)}, bf16[1024,256]{1,0:T(8,128)(2,1)S(1)}, u32[]{:S(2)}, u32[]{:S(2)}) collective-permute-start(bf16[1024,256]{1,0:T(8,128)(2,1)} %get-tuple-element.60.m0), channel_id=1, source_target_pairs={{0,2},{1,3},{2,0},{3,1},{4,6},{5,7},{6,4},{7,5},{8,10},{9,11},{10,... | collective-permute-start | bytes 1572872 | tf_op jit(solution)/shard_map/ppermute | solution.py:385
  144.3 32.4 %collective-permute-start.8 = (bf16[1024,256]{1,0:T(8,128)(2,1)}, bf16[1024,256]{1,0:T(8,128)(2,1)S(1)}, u32[]{:S(2)}, u32[]{:S(2)}) collective-permute-start(bf16[1024,256]{1,0:T(8,128)(2,1)} %get-tuple-element.60.m0), channel_id=1, source_target_pairs={{0,1},{1,0},{2,3},{3,2},{4,5},{5,4},{6,7},{7,6},{8,9},{9,8},{10,11... | collective-permute-start | bytes 1572872 | tf_op jit(solution)/shard_map/ppermute | solution.py:385
  168.5 8.6 %copy-start.14 = (bf16[1024,256]{1,0:T(8,128)(2,1)}, bf16[1024,256]{1,0:T(8,128)(2,1)S(1)}, u32[]{:S(2)}) copy-start(bf16[1024,256]{1,0:T(8,128)(2,1)S(1)} %collective-permute-done.7.m1) | copy-start | bytes 1572868
  168.5 8.2 %collective-permute-start.9 = (bf16[1024,256]{1,0:T(8,128)(2,1)S(1)}, bf16[1024,256]{1,0:T(8,128)(2,1)}, u32[]{:S(2)}, u32[]{:S(2)}) collective-permute-start(bf16[1024,256]{1,0:T(8,128)(2,1)S(1)} %collective-permute-done.7.m1), channel_id=1, source_target_pairs={{0,1},{1,0},{2,3},{3,2},{4,5},{5,4},{6,7},{7,6},{8,9},{9,8},{10,11... | collective-permute-start | bytes 1572872 | tf_op jit(solution)/shard_map/ppermute | solution.py:385
  170.2 7.0 %copy-start.7 = (bf16[64,256]{1,0:T(8,128)(2,1)}, bf16[64,256]{1,0:T(8,128)(2,1)S(1)}, u32[]{:S(2)}) copy-start(bf16[64,256]{1,0:T(8,128)(2,1)S(1)} %add_convert_fusion.1.refs_0_) | copy-start | bytes 98308
  170.2 4.8 %collective-permute-start.11 = (bf16[64,256]{1,0:T(8,128)(2,1)S(1)}, bf16[64,256]{1,0:T(8,128)(2,1)S(1)}, u32[]{:S(2)}, u32[]{:S(2)}) collective-permute-start(bf16[64,256]{1,0:T(8,128)(2,1)S(1)} %add_convert_fusion.1.refs_0_), channel_id=1, source_target_pairs={{0,2},{1,3},{2,0},{3,1},{4,6},{5,7},{6,4},{7,5},{8,10},{9,11},{10,... | collective-permute-start | bytes 98312 | tf_op jit(solution)/shard_map/ppermute | solution.py:385
  174.5 2.1 collective-permute-start.12
  174.9 2.2 copy-start.16
  174.9 1.7 collective-permute-start.13
  175.9 1.2 copy-start.13
  175.9 19.1 %collective-permute-start.14 = (bf16[1024,256]{1,0:T(8,128)(2,1)}, bf16[1024,256]{1,0:T(8,128)(2,1)}, u32[]{:S(2)}, u32[]{:S(2)}) collective-permute-start(bf16[1024,256]{1,0:T(8,128)(2,1)} %get-tuple-element.75.m0), channel_id=1, source_target_pairs={{0,2},{1,3},{2,0},{3,1},{4,6},{5,7},{6,4},{7,5},{8,10},{9,11},{10,... | collective-permute-start | bytes 1572872 | tf_op jit(solution)/shard_map/ppermute | solution.py:385
  176.6 0.6 copy-start.17
  176.7 0.6 copy-start.18
  176.7 0.8 copy-start.15
  195.0 3.8 %collective-permute-start.15 = (bf16[1024,512]{1,0:T(8,128)(2,1)}, bf16[1024,512]{1,0:T(8,128)(2,1)S(1)}, u32[]{:S(2)}, u32[]{:S(2)}) collective-permute-start(bf16[1024,512]{1,0:T(8,128)(2,1)} %get-tuple-element.71), channel_id=1, source_target_pairs={{0,1},{1,0},{2,3},{3,2},{4,5},{5,4},{6,7},{7,6},{8,9},{9,8},{10,11... | collective-permute-start | bytes 3145736 | tf_op jit(solution)/shard_map/ppermute | solution.py:385
  195.8 4.4 %collective-permute-start.16 = (bf16[1024,256]{1,0:T(8,128)(2,1)}, bf16[1024,256]{1,0:T(8,128)(2,1)}, u32[]{:S(2)}, u32[]{:S(2)}) collective-permute-start(bf16[1024,256]{1,0:T(8,128)(2,1)} %collective-permute-done.14.m1), channel_id=1, source_target_pairs={{0,1},{1,0},{2,3},{3,2},{4,5},{5,4},{6,7},{7,6},{8,9},{9,8},{10,11... | collective-permute-start | bytes 1572872 | tf_op jit(solution)/shard_map/ppermute | solution.py:385
  195.9 15.7 %collective-permute-start.17 = (bf16[1024,256]{1,0:T(8,128)(2,1)}, bf16[1024,256]{1,0:T(8,128)(2,1)}, u32[]{:S(2)}, u32[]{:S(2)}) collective-permute-start(bf16[1024,256]{1,0:T(8,128)(2,1)} %get-tuple-element.75.m0), channel_id=1, source_target_pairs={{0,1},{1,0},{2,3},{3,2},{4,5},{5,4},{6,7},{7,6},{8,9},{9,8},{10,11... | collective-permute-start | bytes 1572872 | tf_op jit(solution)/shard_map/ppermute | solution.py:385
  196.3 2.8 %copy-start.2 = (f32[1024,512]{1,0:T(8,128)S(1)}, f32[1024,512]{1,0:T(8,128)}, u32[]{:S(2)}) copy-start(f32[1024,512]{1,0:T(8,128)} %get-tuple-element.70) | copy-start | bytes 6291460
  200.2 25.0 %collective-permute-start.18 = (bf16[1024,256]{1,0:T(8,128)(2,1)}, bf16[1024,256]{1,0:T(8,128)(2,1)S(1)}, u32[]{:S(2)}, u32[]{:S(2)}) collective-permute-start(bf16[1024,256]{1,0:T(8,128)(2,1)} %get-tuple-element.80), channel_id=1, source_target_pairs={{0,2},{1,3},{2,0},{3,1},{4,6},{5,7},{6,4},{7,5},{8,10},{9,11},{10,... | collective-permute-start | bytes 1572872 | tf_op jit(solution)/shard_map/ppermute | solution.py:385
  200.9 24.1 %all-to-all-start.1 = ((f32[128,2,256]{2,1,0:T(2,128)}), f32[128,2,256]{2,1,0:T(2,128)S(1)}, u32[]{:S(2)}, u32[]{:S(2)}) async-start(f32[128,2,256]{2,1,0:T(2,128)} %bitcast.19), calls=%async_computation.1 | async-start | bytes 524288 | tf_op jit(solution)/shard_map/all_to_all | solution.py:403
  225.3 20.6 %collective-permute-start.19 = (bf16[1024,512]{1,0:T(8,128)(2,1)}, bf16[1024,512]{1,0:T(8,128)(2,1)}, u32[]{:S(2)}, u32[]{:S(2)}) collective-permute-start(bf16[1024,512]{1,0:T(8,128)(2,1)} %get-tuple-element.83), channel_id=1, source_target_pairs={{0,1},{1,0},{2,3},{3,2},{4,5},{5,4},{6,7},{7,6},{8,9},{9,8},{10,11... | collective-permute-start | bytes 3145736 | tf_op jit(solution)/shard_map/ppermute | solution.py:385
  247.5 2.8 %copy-start.10 = (s32[64]{0:T(128)S(1)}, s32[64]{0:T(128)}, u32[]{:S(2)}) copy-start(s32[64]{0:T(128)} %param.17) | copy-start | bytes 772
  247.5 3.1 %copy-start.3 = (f32[384,1024]{1,0:T(8,128)S(1)}, f32[384,1024]{1,0:T(8,128)}, u32[]{:S(2)}) copy-start(f32[384,1024]{1,0:T(8,128)} %param.26) | copy-start | bytes 4718596
  249.0 16.9 %collective-permute-start.20 = (bf16[1024,256]{1,0:T(8,128)(2,1)S(1)}, bf16[1024,256]{1,0:T(8,128)(2,1)}, u32[]{:S(2)}, u32[]{:S(2)}) collective-permute-start(bf16[1024,256]{1,0:T(8,128)(2,1)S(1)} %fusion.1), channel_id=1, source_target_pairs={{0,2},{1,3},{2,0},{3,1},{4,6},{5,7},{6,4},{7,5},{8,10},{9,11},{10,... | collective-permute-start | bytes 1572872 | tf_op jit(solution)/shard_map/ppermute | solution.py:385
Sparse Core Ops, SparseCore 0:
  19.2 157.8 all-gather.1
